TPU v7x, 32 devices: a whole 2x2x4 slice. The times are simulated.
32 devices in a mesh: batch: 8 (over z, core), seq: 4 (over y, x).
Axes of the slice: x: 2, y: 2, z: 4, core: 2. Of those that a mesh axis runs over, the one named last changes fastest.
Arguments:
- tokens: bfloat16 [8, 1024, 1024], P('batch', 'seq'), may hold values from -6 to 6
- teacher: bfloat16 [8, 1024, 1024], P('batch', 'seq'), may hold values from -6 to 6
- piece_starts: int32 [8, 1024], P('batch', 'seq'), may hold values from 0 to 1, as said below
- valid_rows: int32 [8, 1024], P('batch', 'seq'), may hold values 0 or 1
- norm_gain: bfloat16 [1024], P(('batch', 'seq')), may hold values from 0.5 to 1.5
- in_weight: bfloat16 [1024, 4096], P(('batch', 'seq')), may hold values from -0.1875 to 0.1875
- conv_weight: bfloat16 [4, 2048], P(None, ('batch', 'seq')), may hold values from -3 to 3
- conv_bias: bfloat16 [2048], P(('batch', 'seq')), may hold values from -3 to 3
- xproj_weight: bfloat16 [2048, 96], P(('batch', 'seq')), may hold values from -0.125 to 0.125
- dtproj_weight: bfloat16 [64, 2048], P(None, ('batch', 'seq')), may hold values from -0.75 to 0.75
- dt_bias: bfloat16 [2048], P(('batch', 'seq')), may hold values from -7 to -1
- a_log: bfloat16 [2048, 16], P(('batch', 'seq')), may hold values from -3 to 1.5
- skip_weight: bfloat16 [2048], P(('batch', 'seq')), may hold values from 0.5 to 1.5
- out_weight: bfloat16 [2048, 1024], P(('batch', 'seq')), may hold values from -0.25 to 0.25
Outputs:
- output: bfloat16 [8, 1024, 1024], P('batch', 'seq')
- loss: float32 [], replicated
- input_grad: float32 [8, 1024, 1024], P('batch', 'seq')
- norm_gain_grad: float32 [1024], P(('batch', 'seq'))
- in_weight_grad: float32 [1024, 4096], P(('batch', 'seq'))
- conv_weight_grad: float32 [4, 2048], P(None, ('batch', 'seq'))
- conv_bias_grad: float32 [2048], P(('batch', 'seq'))
- xproj_weight_grad: float32 [2048, 96], P(('batch', 'seq'))
- dtproj_weight_grad: float32 [64, 2048], P(None, ('batch', 'seq'))
- dt_bias_grad: float32 [2048], P(('batch', 'seq'))
- a_log_grad: float32 [2048, 16], P(('batch', 'seq'))
- skip_weight_grad: float32 [2048], P(('batch', 'seq'))
- out_weight_grad: float32 [2048, 1024], P(('batch', 'seq'))
Inputs may be any that keep to these rules, and one draw needn't show every extreme that they name: `piece_starts`: each 1 starts a piece of 256 positions that ends within its sequence; pieces of one sequence do not intersect.
All inputs are finite; a program needn't handle non-finite values. No bound on the sum of `valid_rows` on one device may be relied on, other than what follows from the above.
Results may differ from a plain program's by a relative error of at most 0.0075.
Values may be sent and summed in bfloat16 or wider, within the bound.
No kernel may reach another device: no remote copies, remote signals or barrier semaphores. Data moves between devices by JAX's collectives and lax.ppermute only.
A program may use at most 192 MiB of HBM per device.

v0:
```python
import jax
import jax.numpy as jnp
from jax import lax
from jax.experimental import pallas as pl
from jax.experimental.pallas import tpu as pltpu
from jax.sharding import PartitionSpec as P

PIECE = 256
BLOCK = 16
ROWS = 128
LOG2E = 1.4426950408889634
LN2 = 0.6931471805599453
NEVER = 1e9
f32 = jnp.float32
bf16 = jnp.bfloat16


def _row(ref, t, n):
    return jnp.broadcast_to(ref[pl.ds(t, 1), :], (n, ref.shape[1]))

def _col(blk, tt, c):
    return jnp.broadcast_to(blk[:, tt:tt+1], (blk.shape[0], c))

def _nt(a, b):
    return lax.dot_general(a, b, (((1,), (1,)), ((), ())), preferred_element_type=f32)

def piece_back_kernel(stepm_ref, u_ref, b3_ref, r2_ref, g_ref, carry_ref):
    rows, c = u_ref.shape
    n = r2_ref.shape[0]
    @pl.when(pl.program_id(0) == 0)
    def _(): carry_ref[...] = jnp.zeros_like(carry_ref)
    r2 = r2_ref[...]
    def block(i, carry):
        j = rows // BLOCK - 1 - i
        bblk = b3_ref[j]
        for tt in reversed(range(BLOCK)):
            t = j * BLOCK + tt
            g = _row(u_ref, t, n) * _col(bblk, tt, c) + carry
            g_ref[pl.ds(pl.multiple_of(t * n, n), n), :] = g.astype(bf16)
            carry = jnp.exp2(_row(stepm_ref, t, n) * r2) * g
        return carry
    carry_ref[...] = lax.fori_loop(0, rows // BLOCK, block, carry_ref[...])

def ahead_kernel(step_ref, u_ref, b3_ref, cblk_ref, r2_ref, g_ref, y_ref, hp_ref, carry_ref, s_ref):
    rows, c = u_ref.shape
    n = r2_ref.shape[0]
    @pl.when(pl.program_id(0) == 0)
    def _(): carry_ref[...] = jnp.zeros_like(carry_ref)
    r2 = r2_ref[...]
    def block(j, h):
        bblk = b3_ref[j]
        for tt in range(BLOCK):
            t = j * BLOCK + tt
            at = pl.ds(pl.multiple_of(t * n, n), n)
            hp = jnp.exp2(_row(step_ref, t, n) * r2) * h
            h = hp + _row(u_ref, t, n) * _col(bblk, tt, c)
            hpb = hp.astype(bf16)
            hp_ref[at, :] = hpb
            s_ref[tt * n:(tt + 1) * n, :] = (hp + g_ref[at, :].astype(f32)).astype(bf16)
        rows16 = pl.ds(pl.multiple_of(j * BLOCK, BLOCK), BLOCK)
        y_ref[rows16, :] = jnp.dot(cblk_ref[rows16, :], s_ref[...], preferred_element_type=f32)
        return h
    carry_ref[...] = lax.fori_loop(0, rows // BLOCK, block, carry_ref[...])

def piece_grad_kernel(stepm_ref, dm_ref, c3_ref, r2_ref, q_ref, carry_ref):
    rows, c = dm_ref.shape
    n = r2_ref.shape[0]
    @pl.when(pl.program_id(0) == 0)
    def _(): carry_ref[...] = jnp.zeros_like(carry_ref)
    r2 = r2_ref[...]
    def block(j, w):
        cblk = c3_ref[j]
        for tt in range(BLOCK):
            t = j * BLOCK + tt
            q = jnp.exp2(_row(stepm_ref, t, n) * r2) * w
            q_ref[pl.ds(pl.multiple_of(t * n, n), n), :] = q.astype(bf16)
            w = q + _row(dm_ref, t, n) * _col(cblk, tt, c)
        return w
    carry_ref[...] = lax.fori_loop(0, rows // BLOCK, block, carry_ref[...])

def state_grad_kernel(step_ref, u_ref, dm_ref, c3_ref, bblk_ref, oblk_ref, nblk_ref, r2_ref, g_ref, hp_ref, q_ref,
               x_ref, y_ref, db_ref, dc_ref, al_ref, carry_ref, ig_ref, rr_ref, rs_ref, s_ref, sb_ref):
    rows, c = u_ref.shape
    n = r2_ref.shape[0]
    @pl.when(pl.program_id(0) == 0)
    def _():
        carry_ref[...] = jnp.zeros_like(carry_ref)
        al_ref[...] = jnp.zeros_like(al_ref)
    r2 = r2_ref[...]
    sb_ref[...] = step_ref[...]
    def block(i, m):
        j = rows // BLOCK - 1 - i
        cblk = c3_ref[j]
        for tt in reversed(range(BLOCK)):
            t = j * BLOCK + tt
            at = pl.ds(pl.multiple_of(t * n, n), n)
            loc = slice(tt * n, (tt + 1) * n)
            mu = m + _row(dm_ref, t, n) * _col(cblk, tt, c)
            srow = _row(step_ref, t, n)
            m = jnp.exp2(srow * r2) * mu
            mub = mu.astype(bf16)
            q = q_ref[at, :]
            g = g_ref[at, :]
            hp = hp_ref[at, :]
            rg = mub * hp + q * g
            ig_ref[loc, :] = mub + q
            rr_ref[loc, :] = (rg.astype(f32) * r2).astype(bf16)
            rs_ref[loc, :] = rg * srow.astype(bf16)
            s_ref[loc, :] = hp + g
        r16 = pl.ds(pl.multiple_of(j * BLOCK, BLOCK), BLOCK)
        ig = ig_ref[...]
        x_ref[r16, :] = jnp.dot(bblk_ref[r16, :], ig, preferred_element_type=f32)
        y_ref[r16, :] = jnp.dot(oblk_ref[...], rr_ref[...], preferred_element_type=f32)
        al_ref[...] += jnp.dot(nblk_ref[...], rs_ref[...], preferred_element_type=f32)
        db_ref[r16, :] = _nt(u_ref[r16, :].astype(bf16), ig)
        dc_ref[r16, :] = _nt(dm_ref[r16, :].astype(bf16), s_ref[...])
        return m
    carry_ref[...] = lax.fori_loop(0, rows // BLOCK, block, carry_ref[...])

def blocks_of(v):
    t, n = v.shape
    return v.reshape(t // BLOCK, BLOCK, n).transpose(0, 2, 1)

def block_diag(v):
    t, n = v.shape
    wide = jnp.tile(v, (1, BLOCK))
    keep = (jnp.arange(t)[:, None] % BLOCK) == (jnp.arange(BLOCK * n)[None, :] // n)
    return jnp.where(keep, wide, 0.0).astype(bf16)

def call(kernel, rows, total, reverse, ins, in_kinds, outs, out_kinds, scratch):
    steps = total // rows
    where = (lambda i: steps - 1 - i) if reverse else (lambda i: i)
    def spec(shape, kind):
        if kind == "full":
            return pl.BlockSpec(shape, lambda i: (0,) * len(shape))
        per = shape[0] // steps
        return pl.BlockSpec((per,) + shape[1:], lambda i: (where(i),) + (0,) * (len(shape) - 1))
    return pl.pallas_call(kernel,
        out_shape=[jax.ShapeDtypeStruct(s, d) for s, d in outs],
        grid=(steps,),
        in_specs=[spec(a.shape, k) for a, k in zip(ins, in_kinds)],
        out_specs=[spec(s, k) for (s, d), k in zip(outs, out_kinds)],
        scratch_shapes=scratch,
        compiler_params=pltpu.CompilerParams(dimension_semantics=("arbitrary",), vmem_limit_bytes=60<<20),
    )(*ins)

def run_g(stepm,u,b3,r2):
    t,c=u.shape; n=r2.shape[0]
    return call(piece_back_kernel, ROWS, t, True, [stepm,u,b3,r2], ["t","t","t","full"], [((t*n,c),bf16)], ["t"], [pltpu.VMEM((n,c),f32)])[0]
def run_h(step,u,b3,cblk,r2,g):
    t,c=u.shape; n=r2.shape[0]
    return call(ahead_kernel, ROWS, t, False, [step,u,b3,cblk,r2,g], ["t","t","t","t","full","t"], [((t,c),f32),((t*n,c),bf16)], ["t","t"], [pltpu.VMEM((n,c),f32),pltpu.VMEM((BLOCK*n,c),bf16)])
def run_q(stepm,dm,c3,r2):
    t,c=dm.shape; n=r2.shape[0]
    return call(piece_grad_kernel, ROWS, t, False, [stepm,dm,c3,r2], ["t","t","t","full"], [((t*n,c),bf16)], ["t"], [pltpu.VMEM((n,c),f32)])[0]
def run_m(step,u,dm,c3,bblk,oblk,nblk,r2,g,hp,q):
    t,c=u.shape; n=r2.shape[0]
    return call(state_grad_kernel, ROWS, t, True, [step,u,dm,c3,bblk,oblk,nblk,r2,g,hp,q], ["t"]*5+["full"]*3+["t"]*3,
      [((t,c),f32),((t,c),f32),((t,BLOCK*n),f32),((t,BLOCK*n),f32),((n,c),f32)], ["t","t","t","t","full"],
      [pltpu.VMEM((n,c),f32)]+[pltpu.VMEM((BLOCK*n,c),bf16)]*4+[pltpu.VMEM((ROWS,c),f32)])


def partner(value, axis, k):
    return lax.ppermute(value, axis, [(i, i ^ k) for i in range(lax.axis_size(axis))])


def gather_parts(value, axis):
    n = lax.axis_size(axis)
    if n > 4:
        return lax.all_gather(value, axis)
    me = lax.axis_index(axis)
    parts = [value] + [partner(value, axis, k) for k in range(1, n)]
    whole = jnp.zeros((n,) + value.shape, value.dtype)
    for k, part in enumerate(parts):
        whole = lax.dynamic_update_index_in_dim(whole, part, me ^ k, 0)
    return whole


def sum_parts(value, axis):
    n = lax.axis_size(axis)
    if n > 4:
        return lax.psum(value, axis)
    low = value.astype(bf16)
    total = low.astype(f32)
    for k in range(1, n):
        total = total + partner(low, axis, k).astype(f32)
    return total


def scatter_sum(value, axis):
    n = lax.axis_size(axis)
    if n > 4:
        return lax.psum_scatter(value, axis, scatter_dimension=0)
    me = lax.axis_index(axis)
    low = value.astype(bf16)
    total = lax.dynamic_index_in_dim(value, me, 0, False)
    for k in range(1, n):
        total = total + partner(lax.dynamic_index_in_dim(low, me ^ k, 0, False), axis, k).astype(f32)
    return total


def sum_everywhere(value, axes):
    for axis in axes:
        k = 1
        while k < lax.axis_size(axis):
            value = value + partner(value, axis, k)
            k *= 2
    return value


def swish_fn(v):
    return v * jax.nn.sigmoid(v)


def swish_slope(v):
    s = jax.nn.sigmoid(v)
    return s * (1.0 + v * (1.0 - s))


def dot(a, b):
    return jnp.dot(a, b, preferred_element_type=f32)


def dot_t(a, b):
    return lax.dot_general(a, b, (((1,), (1,)), ((), ())), preferred_element_type=f32)


def t_dot(a, b):
    return lax.dot_general(a, b, (((0,), (0,)), ((), ())), preferred_element_type=f32)


def body(
    tokens,
    teacher,
    piece_starts,
    valid_rows,
    norm_gain,
    in_weight,
    conv_weight,
    conv_bias,
    xproj_weight,
    dtproj_weight,
    dt_bias,
    a_log,
    skip_weight,
    out_weight,
):
    seqs = lax.axis_size("seq")
    batches = lax.axis_size("batch")
    _, rows, width = tokens.shape
    total = rows * seqs
    taps, own = conv_weight.shape
    chans = own * batches
    depth = in_weight.shape[0]
    rank = dtproj_weight.shape[0]
    states = a_log.shape[1]
    me = lax.axis_index("seq")

    tok = tokens.reshape(rows, width)
    valid_f = valid_rows.reshape(rows, 1).astype(f32)
    counted = jnp.sum(valid_rows)
    extra = jnp.concatenate(
        [
            norm_gain[:, None],
            jnp.full((depth, 1), counted // 128).astype(bf16),
            jnp.full((depth, 1), counted % 128).astype(bf16),
            jnp.zeros((depth, 125), bf16),
        ],
        axis=1,
    )
    split = in_weight.reshape(depth, 2, batches, seqs, own).transpose(3, 0, 1, 2, 4).reshape(seqs, depth, 2 * chans)
    split = jnp.concatenate([split, jnp.broadcast_to(extra[None], (seqs, depth, 128))], axis=2)
    split = lax.all_to_all(split, "seq", 0, 0).reshape(seqs * depth, 2 * chans + 128)
    gathered = lax.all_gather(split, "batch", axis=0, tiled=True)
    in_w = gathered[:, : 2 * chans]
    gain = gathered[:, 2 * chans].astype(f32)
    total_valid = (
        jnp.sum(gathered[:, 2 * chans + 1].astype(f32)) * 128.0 + jnp.sum(gathered[:, 2 * chans + 2].astype(f32))
    ) / depth
    small = jnp.concatenate(
        [
            out_weight,
            xproj_weight,
            dtproj_weight.T,
            a_log,
            conv_weight.T,
            conv_bias[:, None],
            dt_bias[:, None],
            skip_weight[:, None],
        ],
        axis=1,
    )
    used = small.shape[1]
    small = jnp.pad(small, ((0, 0), (0, -used % 128)))
    small = lax.all_gather(small, "batch", axis=0, tiled=True)
    cuts = [0]
    for size in (width, rank + 2 * states, rank, states, taps, 1, 1, 1):
        cuts.append(cuts[-1] + size)
    out_w, xproj_w, dt_w, alog_w, conv_w, convb_w, dtb_w, skip_w = [
        small[:, a:b] for a, b in zip(cuts[:-1], cuts[1:])
    ]
    r2 = -jnp.exp(alog_w.astype(f32).T) * LOG2E
    conv_f = conv_w.astype(f32).T
    convb_f = convb_w.astype(f32).T
    dtb_f = dtb_w.astype(f32).T
    skip_f = skip_w.astype(f32).T

    flags = jnp.pad(piece_starts.astype(bf16), ((0, 15), (0, width - rows)))
    everything = gather_parts(jnp.concatenate([tok, flags], axis=0), "seq")
    x_all = everything[:, :rows].reshape(total, width).astype(f32)
    starts = everything[:, rows, :rows].reshape(total).astype(f32)
    mean_sq = jnp.mean(x_all * x_all, axis=-1, keepdims=True)
    unit = x_all * lax.rsqrt(mean_sq + 1e-05)
    normed = (unit * gain[None]).astype(bf16)
    joint = dot(normed, in_w)
    stream = joint[:, :chans].astype(bf16)
    gate = joint[:, chans:]
    wide = jnp.pad(stream, ((taps - 1, 0), (0, 0))).astype(f32)
    conv_pre = convb_f
    for tap in range(taps):
        conv_pre = conv_pre + conv_f[tap] * wide[tap : tap + total]
    act = swish_fn(conv_pre).astype(bf16)
    act_f = act.astype(f32)
    proj = sum_parts(dot(act, xproj_w), "seq")
    low = proj[:, :rank].astype(bf16)
    b_in = proj[:, rank : rank + states]
    c_out = proj[:, rank + states :]
    dt_pre = dot_t(low, dt_w) + dtb_f
    step = jax.nn.softplus(dt_pre)
    running = jnp.cumsum(starts)
    lagged = jnp.concatenate([jnp.zeros((PIECE,), f32), running[: total - PIECE]])
    inside = (running - lagged > 0.5).astype(f32)
    carry_on = inside * (1.0 - starts)
    stepm = jnp.where(carry_on[:, None] > 0.5, step, NEVER)
    u = step * act_f
    b3, c3 = blocks_of(b_in), blocks_of(c_out)
    bblk, cblk = block_diag(b_in), block_diag(c_out)
    oblk = block_diag(jnp.ones((BLOCK, states), f32))
    nblk = jnp.tile(jnp.eye(states, dtype=bf16), (1, BLOCK))
    g = run_g(stepm, u, b3, r2)
    y, hp = run_h(step, u, b3, cblk, r2, g)
    mixed = y + skip_f * act_f
    gate_act = swish_fn(gate)
    gated = (mixed * gate_act).astype(bf16)
    branch = scatter_sum(dot(gated, out_w).reshape(seqs, rows, width), "seq")
    tok_f = tok.astype(f32)
    result = tok_f + branch
    output = result.astype(bf16)
    misfit = result - teacher.reshape(rows, width).astype(f32)
    square_sum = sum_everywhere(jnp.sum(valid_f * misfit * misfit).reshape(1, 1), ("batch", "seq"))
    loss = square_sum[0, 0] / (total_valid * width)
    d_result = 2.0 * (total * batches) / total_valid * valid_f * misfit

    d_branch = gather_parts(d_result.astype(bf16), "seq").reshape(total, width)
    d_gated = dot_t(d_branch, out_w)
    out_grad = lax.psum_scatter(t_dot(gated, d_branch), "batch", scatter_dimension=0, tiled=True)
    d_mixed = d_gated * gate_act
    d_gate = (d_gated * mixed * swish_slope(gate)).astype(bf16)
    q = run_q(stepm, d_mixed, c3, r2)
    xs, ys, dbs, dcs, als = run_m(step, u, d_mixed, c3, bblk, oblk, nblk, r2, g, hp, q)
    d_step = ys * LN2 + act_f * xs
    d_act = step * xs + skip_f * d_mixed
    keep = (jnp.arange(total)[:, None] % BLOCK) == (jnp.arange(BLOCK * states)[None, :] // states)
    d_b = jnp.where(keep, dbs, 0.0).reshape(total, BLOCK, states).sum(1)
    d_c = jnp.where(keep, dcs, 0.0).reshape(total, BLOCK, states).sum(1)
    alog_grad = (als * (r2 * LN2)).T
    skip_grad = jnp.sum(d_mixed * act_f, axis=0)
    d_pre = d_step * jax.nn.sigmoid(dt_pre)
    dtb_grad = jnp.sum(d_pre, axis=0)
    d_pre_low = d_pre.astype(bf16)
    dt_grad = t_dot(d_pre_low, low)
    d_low = dot(d_pre_low, dt_w)
    d_proj = sum_parts(jnp.concatenate([d_low, d_b, d_c], axis=1), "seq").astype(bf16)
    xproj_grad = t_dot(act, d_proj)
    d_act_all = d_act + dot_t(d_proj, xproj_w)
    d_conv = d_act_all * swish_slope(conv_pre)
    convb_grad = jnp.sum(d_conv, axis=0)
    longer = jnp.pad(d_conv, ((0, taps - 1), (0, 0)))
    d_stream = jnp.zeros_like(d_conv)
    conv_grads = []
    for tap in range(taps):
        conv_grads.append(jnp.sum(d_conv * wide[tap : tap + total], axis=0))
        back = taps - 1 - tap
        d_stream = d_stream + conv_f[tap] * longer[back : back + total]
    d_joint = jnp.concatenate([d_stream.astype(bf16), d_gate], axis=1)
    in_grad = t_dot(normed, d_joint)
    d_normed = scatter_sum(dot_t(d_joint, in_w).reshape(seqs, rows, width), "seq")
    small_grads = jnp.concatenate(
        [xproj_grad, dt_grad, alog_grad, jnp.stack(conv_grads + [convb_grad, dtb_grad, skip_grad], axis=1)], axis=1
    )
    kept = small_grads.shape[1]
    small_grads = jnp.pad(small_grads, ((0, 0), (0, -kept % 256))).reshape(batches, -1, 2 * chans)
    lines = seqs * depth
    both = jnp.concatenate([in_grad.reshape(batches, lines, 2 * chans), small_grads], axis=1)
    both = lax.psum_scatter(both, "batch", scatter_dimension=0)
    small_out = both[lines:].reshape(own, -1)
    in_out = lax.all_to_all(both[:lines].reshape(seqs, depth, 2 * chans), "seq", 0, 0)
    in_out = in_out.reshape(seqs, depth, 2, batches, own).transpose(1, 2, 3, 0, 4).reshape(depth, -1)
    cuts = [0]
    for size in (rank + 2 * states, rank, states, taps, 1, 1, 1):
        cuts.append(cuts[-1] + size)
    xproj_out, dt_out, alog_out, conv_out, convb_out, dtb_out, skip_out = [
        small_out[:, a:b] for a, b in zip(cuts[:-1], cuts[1:])
    ]
    gain_f = norm_gain.astype(f32)
    gain_out = jnp.sum(in_out * in_weight.astype(f32), axis=1) / gain_f
    own_sq = jnp.mean(tok_f * tok_f, axis=-1, keepdims=True)
    root_inv = lax.rsqrt(own_sq + 1e-05)
    own_unit = tok_f * root_inv
    scaled = d_normed * gain[None]
    input_grad = d_result + root_inv * (scaled - own_unit * jnp.mean(scaled * own_unit, axis=-1, keepdims=True))
    return (
        output[None],
        loss,
        input_grad[None],
        gain_out,
        in_out,
        conv_out.T,
        convb_out[:, 0],
        xproj_out,
        dt_out.T,
        dtb_out[:, 0],
        alog_out,
        skip_out[:, 0],
        out_grad,
    )


def solution(mesh):
    return jax.shard_map(
        body,
        mesh=mesh,
        in_specs=(
            P("batch", "seq", None),
            P("batch", "seq", None),
            P("batch", "seq"),
            P("batch", "seq"),
            P(("batch", "seq")),
            P(("batch", "seq"), None),
            P(None, ("batch", "seq")),
            P(("batch", "seq")),
            P(("batch", "seq"), None),
            P(None, ("batch", "seq")),
            P(("batch", "seq")),
            P(("batch", "seq"), None),
            P(("batch", "seq")),
            P(("batch", "seq"), None),
        ),
        out_specs=(
            P("batch", "seq", None),
            P(),
            P("batch", "seq", None),
            P(("batch", "seq")),
            P(("batch", "seq"), None),
            P(None, ("batch", "seq")),
            P(("batch", "seq")),
            P(("batch", "seq"), None),
            P(None, ("batch", "seq")),
            P(("batch", "seq")),
            P(("batch", "seq"), None),
            P(("batch", "seq")),
            P(("batch", "seq"), None),
        ),
        check_vma=False,
    )
```

profile of v0, /device:TPU:0, one launch (start us, length us, event | category | flops | bytes accessed | tf_op | source)
XLA Modules:
  0.0 420.3 jit_solution(17552290422365747846)
XLA Ops:
  13.7 2.0 fusion.59
  21.2 11.3 %all_to_all.10 = bf16[4,32,1152]{2,1,0:T(8,128)(2,1)S(1)} all-to-all(bf16[4,32,1152]{2,1,0:T(8,128)(2,1)S(1)} %pad_maximum_fusion.4), channel_id=1, replica_groups=mesh['batch'=8,'seq'=4] {'seq'}, dimensions={0} | all-to-all | bytes 589824 | tf_op jit(solution)/shard_map/all_to_all | solution.py:273
  34.8 2.3 collective-permute-start.2
  38.6 10.7 %collective-permute-done = bf16[272,1024]{1,0:T(8,128)(2,1)} collective-permute-done((bf16[272,1024]{1,0:T(8,128)(2,1)S(1)}, bf16[272,1024]{1,0:T(8,128)(2,1)}, u32[]{:S(2)}, u32[]{:S(2)}) %collective-permute-start) | collective-permute-done | bytes 557088 | tf_op jit(solution)/shard_map/ppermute | solution.py:164
  50.4 8.9 %collective-permute-done.1 = bf16[272,1024]{1,0:T(8,128)(2,1)} collective-permute-done((bf16[272,1024]{1,0:T(8,128)(2,1)S(1)}, bf16[272,1024]{1,0:T(8,128)(2,1)}, u32[]{:S(2)}, u32[]{:S(2)}) %collective-permute-start.1) | collective-permute-done | bytes 557088 | tf_op jit(solution)/shard_map/ppermute | solution.py:164
  63.3 2.4 slice_convert_fusion.1
  66.8 2.0 convert_reduce_fusion
  70.4 4.0 all-gather.5.cloned.1.call-done
  75.7 2.7 fusion.1
  78.6 2.4 fusion.12
  83.1 2.7 multiply_convert_fusion.2
  91.3 3.6 collective-permute-done.3
  95.0 4.6 %collective-permute-done.4 = bf16[1024,96]{0,1:T(8,128)(2,1)S(1)} collective-permute-done((bf16[1024,96]{0,1:T(8,128)(2,1)S(1)}, bf16[1024,96]{0,1:T(8,128)(2,1)S(1)}, u32[]{:S(2)}, u32[]{:S(2)}) %collective-permute-start.4) | collective-permute-done | bytes 196640 | tf_op jit(solution)/shard_map/ppermute | solution.py:164
  100.4 4.3 %broadcast_select_fusion = (f32[1024,512]{1,0:T(8,128)}, f32[1024,512]{1,0:T(8,128)S(1)}, f32[1024,512]{1,0:T(8,128)}) fusion(pred[1024]{0:T(1024)(128)(4,1)S(1)} %copy-done.56, f32[512]{0:T(512)S(1)} %copy-done.45, bf16[512,1280]{1,0:T(8,128)(2,1)} %all-gather.3.cloned.1.call-done, f32[1024,96]{0,1:T(8,128)S(1)} %convert_add_fusion.1), kind=kOutput, calls=%fused_computation.71 | convolution fusion | flops 71303168 | bytes 6556672 | tf_op jit(solution)/shard_map/dot_general | solution.py:225
  104.7 1.9 convert_multiply_fusion.3.u_ref
  106.7 1.8 reshape.256
  108.5 2.1 copy.114
  110.7 1.7 tile.14
  112.4 2.0 copy.90
  114.4 1.7 tile.32
  116.1 2.0 copy.93
  118.2 13.0 %shard_map.237.g_ref = bf16[16384,512]{1,0:T(8,128)(2,1)} custom-call(f32[1024,512]{1,0:T(8,128)} %get-tuple-element.103.stepm_ref, f32[1024,512]{1,0:T(8,128)} %convert_multiply_fusion.3.u_ref, f32[64,16,16]{2,1,0:T(8,128)} %bitcast.171, f32[16,512]{1,0:T(8,128)} %bitcast_multiply_fusion.2.r2_ref), custom_call_target="tpu_custom_call" | custom-call | tf_op jit(solution)/shard_map/pallas_call | solution.py:138
  131.1 2.3 fusion.25
  133.4 23.0 %shard_map.238 = (f32[1024,512]{1,0:T(8,128)}, bf16[16384,512]{1,0:T(8,128)(2,1)}) custom-call(f32[1024,512]{1,0:T(8,128)} %copy-done, f32[1024,512]{1,0:T(8,128)} %convert_multiply_fusion.3.u_ref, f32[64,16,16]{2,1,0:T(8,128)} %bitcast.172, bf16[1024,256]{1,0:T(8,128)(2,1)} %get-tuple-element.123.cblk_ref, f32[16,512]{1,0:T(8,128)} %bitcast_multiply_fusion.2.r2_ref, ...), custom_call_target="tpu_custom_call" | custom-call | tf_op jit(solution)/shard_map/pallas_call | solution.py:138
  156.5 3.0 multiply_convert_fusion.1
  171.0 8.1 %collective-permute-done.6 = bf16[256,1024]{1,0:T(8,128)(2,1)} collective-permute-done((bf16[256,1024]{1,0:T(8,128)(2,1)}, bf16[256,1024]{1,0:T(8,128)(2,1)}, u32[]{:S(2)}, u32[]{:S(2)}) %collective-permute-start.6) | collective-permute-done | bytes 524320 | tf_op jit(solution)/shard_map/ppermute | solution.py:164
  179.1 10.5 %collective-permute-done.7 = bf16[256,1024]{1,0:T(8,128)(2,1)} collective-permute-done((bf16[256,1024]{1,0:T(8,128)(2,1)}, bf16[256,1024]{1,0:T(8,128)(2,1)}, u32[]{:S(2)}, u32[]{:S(2)}) %collective-permute-start.7) | collective-permute-done | bytes 524320 | tf_op jit(solution)/shard_map/ppermute | solution.py:164
  190.0 3.5 bitcast_dynamic-update-slice_fusion.7
  197.2 1.8 collective-permute-start.16
  201.1 3.9 copy.102
  205.1 1.9 reshape.261
  207.0 2.3 copy.113
  210.0 1.9 bitcast_dynamic-update-slice_fusion.6
  211.8 6.7 %collective-permute-done.15 = bf16[256,1024]{1,0:T(8,128)(2,1)} collective-permute-done((bf16[256,1024]{1,0:T(8,128)(2,1)}, bf16[256,1024]{1,0:T(8,128)(2,1)}, u32[]{:S(2)}, u32[]{:S(2)}) %collective-permute-start.15) | collective-permute-done | bytes 524320 | tf_op jit(solution)/shard_map/ppermute | solution.py:164
  218.5 1.9 bitcast_dynamic-update-slice_fusion.5
  220.4 1.9 bitcast_dynamic-update-slice_fusion.4
  222.3 7.1 %fusion.5 = (f32[512]{0:T(512)}, f32[1024,512]{1,0:T(8,128)}, bf16[1024,512]{1,0:T(8,128)(2,1)}) fusion(bf16[1024,512]{1,0:T(8,128)(2,1)S(1)} %get-tuple-element.105, f32[1024,1024]{1,0:T(8,128)S(1)} %copy-done.14, f32[1024,512]{1,0:T(8,128)} %get-tuple-element.20, f32[512]{0:T(512)S(1)} %copy-done.53, bf16[1024,1024]{1,0:T(8,128)(2,1)} %bitcast.167, ...), kind=kOutput, calls=%fused_computation.13 | convolution fusion | flops 1082654208 | bytes 11538432 | tf_op jit(solution)/shard_map/dot_general | solution.py:225
  229.3 12.7 %shard_map.239.q_ref = bf16[16384,512]{1,0:T(8,128)(2,1)} custom-call(f32[1024,512]{1,0:T(8,128)} %get-tuple-element.103.stepm_ref, f32[1024,512]{1,0:T(8,128)} %get-tuple-element.97.dm_ref, f32[64,16,16]{2,1,0:T(8,128)} %bitcast.173, f32[16,512]{1,0:T(8,128)} %bitcast_multiply_fusion.2.r2_ref), custom_call_target="tpu_custom_call" | custom-call | tf_op jit(solution)/shard_map/pallas_call | solution.py:138
  242.0 39.3 %shard_map.240 = (f32[1024,512]{1,0:T(8,128)}, f32[1024,512]{1,0:T(8,128)}, f32[1024,256]{1,0:T(8,128)}, f32[1024,256]{1,0:T(8,128)}, f32[16,512]{1,0:T(8,128)}) custom-call(f32[1024,512]{1,0:T(8,128)} %copy-done, f32[1024,512]{1,0:T(8,128)} %convert_multiply_fusion.3.u_ref, f32[1024,512]{1,0:T(8,128)} %get-tuple-element.97.dm_ref, f32[64,16,16]{2,1,0:T(8,128)} %bitcast.174, ...), custom_call_target="tpu_custom_call" | custom-call | tf_op jit(solution)/shard_map/pallas_call | solution.py:138
  281.4 3.1 compare_select_fusion.2
  284.4 2.6 copy.94
  287.0 1.9 reduce_sum.159
  288.9 2.6 copy.95
  291.5 1.9 reduce_sum.160
  293.4 4.5 %fusion.56 = (f32[512]{0:T(512)}, bf16[1024,512]{1,0:T(8,128)(2,1)S(1)}) fusion(f32[1024,512]{1,0:T(8,128)} %get-tuple-element.126, f32[512]{0:T(512)} %get-tuple-element.87, f32[1024,512]{1,0:T(8,128)} %get-tuple-element.22, bf16[1024,512]{1,0:T(8,128)(2,1)S(1)} %get-tuple-element.105, f32[1024,512]{1,0:T(8,128)} %get-tuple-element.23), kind=kLoop, calls=%fused_computation.162 | loop fusion | flops 5766656 | bytes 8392704 | tf_op jit(solution)/shard_map/reduce_sum | solution.py:369
  299.5 2.0 collective-permute-start.18
  308.8 2.0 multiply_multiply_fusion
  310.9 2.8 multiply_reduce_fusion.1
  315.3 3.9 fusion.6
  319.2 2.5 pad_maximum_fusion
  323.5 2.6 fusion.60
  327.9 5.9 %bitcast_convert_fusion = (bf16[4,256,1024]{2,1,0:T(8,128)(2,1)S(1)}, f32[1024,1024]{1,0:T(8,128)}) fusion(bf16[1024,1152]{0,1:T(8,128)(2,1)} %all-gather.5.cloned.1.call-done, bf16[1024,512]{1,0:T(8,128)(2,1)S(1)} %copy-done.61, bf16[1024,512]{1,0:T(8,128)(2,1)S(1)} %copy-done.24), kind=kOutput, calls=%fused_computation.161 | convolution fusion | flops 2152726528 | bytes 10485760 | tf_op jit(solution)/shard_map/dot_general | solution.py:225
  338.4 10.3 %collective-permute-done.20 = bf16[256,1024]{1,0:T(8,128)(2,1)S(1)} collective-permute-done((bf16[256,1024]{1,0:T(8,128)(2,1)}, bf16[256,1024]{1,0:T(8,128)(2,1)S(1)}, u32[]{:S(2)}, u32[]{:S(2)}) %collective-permute-start.20) | collective-permute-done | bytes 524320 | tf_op jit(solution)/shard_map/ppermute | solution.py:164
  348.7 6.1 %collective-permute-done.21 = bf16[256,1024]{1,0:T(8,128)(2,1)S(1)} collective-permute-done((bf16[256,1024]{1,0:T(8,128)(2,1)S(1)}, bf16[256,1024]{1,0:T(8,128)(2,1)S(1)}, u32[]{:S(2)}, u32[]{:S(2)}) %collective-permute-start.21) | collective-permute-done | bytes 524320 | tf_op jit(solution)/shard_map/ppermute | solution.py:164
  355.7 2.0 fusion.17
  357.7 18.1 %reduce-scatter.3.cloned.1.call-done = f32[1,144,1024]{2,1,0:T(8,128)} async-done(((f32[8,144,1024]{2,1,0:T(8,128)}), f32[1,144,1024]{2,1,0:T(8,128)}) %reduce-scatter.3.cloned.1.call-update) | async-done | bytes 589840 | tf_op jit(solution)/shard_map/reduce_scatter | solution.py:395
  375.8 1.9 slice.214
  377.7 3.7 all-to-all-start.1
  381.5 4.2 fusion.21
  389.5 2.2 collective-permute-done.10
  392.3 1.7 collective-permute-start.11
  394.1 2.7 collective-permute-done.11
  397.4 3.4 collective-permute-start.12
  401.6 3.4 collective-permute-start.13
  (257 shorter events, 76.8 us)
Async XLA Ops:
  7.2 58.5 %all-gather.3.cloned.1.call-start = ((), (), s32[]{:S(2)}) async-start(), calls=%async_computation.4 | async-start | bytes 1474560 | tf_op jit(solution)/shard_map/all_gather | solution.py:295
  13.6 60.8 %all-gather.5.cloned.1.call-start = ((), (), s32[]{:S(2)}) async-start(), calls=%async_computation.5 | async-start | bytes 2654208 | tf_op jit(solution)/shard_map/all_gather | solution.py:274
  20.7 12.8 %copy-start.58 = (s32[1,256]{1,0:T(1,128)S(1)}, s32[1,256]{1,0:T(1,128)}, u32[]{:S(2)}) copy-start(s32[1,256]{1,0:T(1,128)} %param.16) | copy-start | bytes 3076
  20.7 12.8 %copy-start.2 = (bf16[1,256,1024]{2,1,0:T(8,128)(2,1)S(1)}, bf16[1,256,1024]{2,1,0:T(8,128)(2,1)}, u32[]{:S(2)}) copy-start(bf16[1,256,1024]{2,1,0:T(8,128)(2,1)} %param.14) | copy-start | bytes 1572868
  33.4 342.3 %reduce-scatter.3.cloned.1.call-start = ((), (), s32[]{:S(2)}) async-start(), calls=%async_computation.6 | async-start | bytes 5308416 | tf_op jit(solution)/shard_map/reduce_scatter | solution.py:395
  33.6 15.7 %collective-permute-start = (bf16[272,1024]{1,0:T(8,128)(2,1)S(1)}, bf16[272,1024]{1,0:T(8,128)(2,1)}, u32[]{:S(2)}, u32[]{:S(2)}) collective-permute-start(bf16[272,1024]{1,0:T(8,128)(2,1)S(1)} %fusion.35), channel_id=1, source_target_pairs={{0,1},{1,0},{2,3},{3,2},{4,5},{5,4},{6,7},{7,6},{8,9},{9,8},{10,11... | collective-permute-start | bytes 1671176 | tf_op jit(solution)/shard_map/ppermute | solution.py:164
  34.3 25.0 %collective-permute-start.1 = (bf16[272,1024]{1,0:T(8,128)(2,1)S(1)}, bf16[272,1024]{1,0:T(8,128)(2,1)}, u32[]{:S(2)}, u32[]{:S(2)}) collective-permute-start(bf16[272,1024]{1,0:T(8,128)(2,1)S(1)} %fusion.35), channel_id=1, source_target_pairs={{0,2},{1,3},{2,0},{3,1},{4,6},{5,7},{6,4},{7,5},{8,10},{9,11},{10,... | collective-permute-start | bytes 1671176 | tf_op jit(solution)/shard_map/ppermute | solution.py:164
  34.8 25.6 %collective-permute-start.2 = (bf16[272,1024]{1,0:T(8,128)(2,1)S(1)}, bf16[272,1024]{1,0:T(8,128)(2,1)}, u32[]{:S(2)}, u32[]{:S(2)}) collective-permute-start(bf16[272,1024]{1,0:T(8,128)(2,1)S(1)} %fusion.35), channel_id=1, source_target_pairs={{0,3},{1,2},{2,1},{3,0},{4,7},{5,6},{6,5},{7,4},{8,11},{9,10},{10,... | collective-permute-start | bytes 1671176 | tf_op jit(solution)/shard_map/ppermute | solution.py:164
  66.8 23.9 %copy-start.30 = (bf16[512,16]{0,1:T(8,128)(2,1)}, bf16[512,16]{0,1:T(8,128)(2,1)S(1)}, u32[]{:S(2)}) copy-start(bf16[512,16]{0,1:T(8,128)(2,1)S(1)} %copy.103) | copy-start | bytes 49156
  70.4 12.8 %copy-start.37 = (f32[512]{0:T(512)}, f32[512]{0:T(512)S(1)}, u32[]{:S(2)}) copy-start(f32[512]{0:T(512)S(1)} %get-tuple-element.89) | copy-start | bytes 6148
  70.4 12.8 %copy-start.39 = (f32[512]{0:T(512)}, f32[512]{0:T(512)S(1)}, u32[]{:S(2)}) copy-start(f32[512]{0:T(512)S(1)} %get-tuple-element.90) | copy-start | bytes 6148
  70.4 12.7 %copy-start.41 = (f32[512]{0:T(512)}, f32[512]{0:T(512)S(1)}, u32[]{:S(2)}) copy-start(f32[512]{0:T(512)S(1)} %get-tuple-element.91) | copy-start | bytes 6148
  70.4 12.7 %copy-start.43 = (f32[512]{0:T(512)}, f32[512]{0:T(512)S(1)}, u32[]{:S(2)}) copy-start(f32[512]{0:T(512)S(1)} %get-tuple-element.92) | copy-start | bytes 6148
  85.8 14.6 %copy-start.45 = (f32[512]{0:T(512)S(1)}, f32[512]{0:T(512)}, u32[]{:S(2)}) copy-start(f32[512]{0:T(512)} %get-tuple-element.87) | copy-start | bytes 6148
  85.8 14.6 %copy-start.56 = (pred[1024]{0:T(1024)(128)(4,1)S(1)}, pred[1024]{0:T(1024)(128)(4,1)}, u32[]{:S(2)}) copy-start(pred[1024]{0:T(1024)(128)(4,1)} %select_compare_fusion) | copy-start | bytes 3076
  87.2 7.8 %collective-permute-start.3 = (bf16[1024,96]{0,1:T(8,128)(2,1)S(1)}, bf16[1024,96]{0,1:T(8,128)(2,1)S(1)}, u32[]{:S(2)}, u32[]{:S(2)}) collective-permute-start(bf16[1024,96]{0,1:T(8,128)(2,1)S(1)} %convolution_convert_fusion), channel_id=1, source_target_pairs={{0,1},{1,0},{2,3},{3,2},{4,5},{5,4},{6,7},{7,6},{8,9},{9,8},{10,11... | collective-permute-start | bytes 589832 | tf_op jit(solution)/shard_map/ppermute | solution.py:164
  88.6 11.0 %collective-permute-start.4 = (bf16[1024,96]{0,1:T(8,128)(2,1)S(1)}, bf16[1024,96]{0,1:T(8,128)(2,1)S(1)}, u32[]{:S(2)}, u32[]{:S(2)}) collective-permute-start(bf16[1024,96]{0,1:T(8,128)(2,1)S(1)} %convolution_convert_fusion), channel_id=1, source_target_pairs={{0,2},{1,3},{2,0},{3,1},{4,6},{5,7},{6,4},{7,5},{8,10},{9,11},{10,... | collective-permute-start | bytes 589832 | tf_op jit(solution)/shard_map/ppermute | solution.py:164
  90.1 9.5 %collective-permute-start.5 = (bf16[1024,96]{0,1:T(8,128)(2,1)S(1)}, bf16[1024,96]{0,1:T(8,128)(2,1)S(1)}, u32[]{:S(2)}, u32[]{:S(2)}) collective-permute-start(bf16[1024,96]{0,1:T(8,128)(2,1)S(1)} %convolution_convert_fusion), channel_id=1, source_target_pairs={{0,3},{1,2},{2,1},{3,0},{4,7},{5,6},{6,5},{7,4},{8,11},{9,10},{10,... | collective-permute-start | bytes 589832 | tf_op jit(solution)/shard_map/ppermute | solution.py:164
  118.2 13.0 %copy-start.17 = (bf16[1024,256]{1,0:T(8,128)(2,1)S(1)}, bf16[1024,256]{1,0:T(8,128)(2,1)}, u32[]{:S(2)}) copy-start(bf16[1024,256]{1,0:T(8,128)(2,1)} %copy.90) | copy-start | bytes 1572868
  118.2 13.0 %copy-start.34 = (s32[1024]{0:T(1024)S(1)}, s32[1024]{0:T(1024)}, u32[]{:S(2)}) copy-start(s32[1024]{0:T(1024)} %add_select_fusion) | copy-start | bytes 12292
  118.2 13.0 %copy-start.46 = (s32[256]{0:T(256)S(1)}, s32[256]{0:T(256)}, u32[]{:S(2)}) copy-start(s32[256]{0:T(256)} %and_select_fusion.1) | copy-start | bytes 3076
  133.4 23.1 %copy-start.52 = (f32[512]{0:T(512)S(1)}, f32[512]{0:T(512)}, u32[]{:S(2)}) copy-start(f32[512]{0:T(512)} %get-tuple-element.86) | copy-start | bytes 6148
  163.9 15.2 %collective-permute-start.6 = (bf16[256,1024]{1,0:T(8,128)(2,1)}, bf16[256,1024]{1,0:T(8,128)(2,1)}, u32[]{:S(2)}, u32[]{:S(2)}) collective-permute-start(bf16[256,1024]{1,0:T(8,128)(2,1)} %get-tuple-element.112), channel_id=1, source_target_pairs={{0,1},{1,0},{2,3},{3,2},{4,5},{5,4},{6,7},{7,6},{8,9},{9,8},{10,11... | collective-permute-start | bytes 1572872 | tf_op jit(solution)/shard_map/ppermute | solution.py:164
  165.1 24.5 %collective-permute-start.7 = (bf16[256,1024]{1,0:T(8,128)(2,1)}, bf16[256,1024]{1,0:T(8,128)(2,1)}, u32[]{:S(2)}, u32[]{:S(2)}) collective-permute-start(bf16[256,1024]{1,0:T(8,128)(2,1)} %get-tuple-element.114), channel_id=1, source_target_pairs={{0,2},{1,3},{2,0},{3,1},{4,6},{5,7},{6,4},{7,5},{8,10},{9,11},{10,... | collective-permute-start | bytes 1572872 | tf_op jit(solution)/shard_map/ppermute | solution.py:164
  166.0 23.7 %collective-permute-start.8 = (bf16[256,1024]{1,0:T(8,128)(2,1)}, bf16[256,1024]{1,0:T(8,128)(2,1)}, u32[]{:S(2)}, u32[]{:S(2)}) collective-permute-start(bf16[256,1024]{1,0:T(8,128)(2,1)} %get-tuple-element.113), channel_id=1, source_target_pairs={{0,3},{1,2},{2,1},{3,0},{4,7},{5,6},{6,5},{7,4},{8,11},{9,10},{10,... | collective-permute-start | bytes 1572872 | tf_op jit(solution)/shard_map/ppermute | solution.py:164
  170.2 19.7 %copy-start.3 = (bf16[1,256,1024]{2,1,0:T(8,128)(2,1)S(1)}, bf16[1,256,1024]{2,1,0:T(8,128)(2,1)}, u32[]{:S(2)}) copy-start(bf16[1,256,1024]{2,1,0:T(8,128)(2,1)} %param.14) | copy-start | bytes 1572868
  170.2 19.7 %copy-start.20 = (bf16[1,256,1024]{2,1,0:T(8,128)(2,1)S(1)}, bf16[1,256,1024]{2,1,0:T(8,128)(2,1)}, u32[]{:S(2)}) copy-start(bf16[1,256,1024]{2,1,0:T(8,128)(2,1)} %param.15) | copy-start | bytes 1572868
  171.0 22.5 %copy-start.49 = (f32[256]{0:T(256)}, f32[256]{0:T(256)S(1)}, u32[]{:S(2)}) copy-start(f32[256]{0:T(256)S(1)} %broadcast_multiply_fusion.1) | copy-start | bytes 3076
  189.9 6.6 %copy-start.47 = (s32[256]{0:T(256)S(1)}, s32[256]{0:T(256)}, u32[]{:S(2)}) copy-start(s32[256]{0:T(256)} %and_select_fusion.1) | copy-start | bytes 3076
  194.8 15.2 %collective-permute-start.14 = (bf16[256,1024]{1,0:T(8,128)(2,1)}, bf16[256,1024]{1,0:T(8,128)(2,1)}, u32[]{:S(2)}, u32[]{:S(2)}) collective-permute-start(bf16[256,1024]{1,0:T(8,128)(2,1)} %get-tuple-element.101), channel_id=1, source_target_pairs={{0,1},{1,0},{2,3},{3,2},{4,5},{5,4},{6,7},{7,6},{8,9},{9,8},{10,11... | collective-permute-start | bytes 1572872 | tf_op jit(solution)/shard_map/ppermute | solution.py:164
  195.4 23.1 %collective-permute-start.15 = (bf16[256,1024]{1,0:T(8,128)(2,1)}, bf16[256,1024]{1,0:T(8,128)(2,1)}, u32[]{:S(2)}, u32[]{:S(2)}) collective-permute-start(bf16[256,1024]{1,0:T(8,128)(2,1)} %get-tuple-element.101), channel_id=1, source_target_pairs={{0,2},{1,3},{2,0},{3,1},{4,6},{5,7},{6,4},{7,5},{8,10},{9,11},{10,... | collective-permute-start | bytes 1572872 | tf_op jit(solution)/shard_map/ppermute | solution.py:164
  197.2 23.2 %collective-permute-start.16 = (bf16[256,1024]{1,0:T(8,128)(2,1)}, bf16[256,1024]{1,0:T(8,128)(2,1)}, u32[]{:S(2)}, u32[]{:S(2)}) collective-permute-start(bf16[256,1024]{1,0:T(8,128)(2,1)} %get-tuple-element.101), channel_id=1, source_target_pairs={{0,3},{1,2},{2,1},{3,0},{4,7},{5,6},{6,5},{7,4},{8,11},{9,10},{10,... | collective-permute-start | bytes 1572872 | tf_op jit(solution)/shard_map/ppermute | solution.py:164
  207.0 15.3 %copy-start.14 = (f32[1024,1024]{1,0:T(8,128)S(1)}, f32[1024,1024]{1,0:T(8,128)}, u32[]{:S(2)}) copy-start(f32[1024,1024]{1,0:T(8,128)} %copy-done.13) | copy-start | bytes 12582916
  207.0 15.3 %copy-start.53 = (f32[512]{0:T(512)S(1)}, f32[512]{0:T(512)}, u32[]{:S(2)}) copy-start(f32[512]{0:T(512)} %get-tuple-element.86) | copy-start | bytes 6148
  242.0 39.3 %copy-start.35 = (s32[1024]{0:T(1024)S(1)}, s32[1024]{0:T(1024)}, u32[]{:S(2)}) copy-start(s32[1024]{0:T(1024)} %add_select_fusion) | copy-start | bytes 12292
  242.0 39.3 %copy-start.48 = (s32[256]{0:T(256)S(1)}, s32[256]{0:T(256)}, u32[]{:S(2)}) copy-start(s32[256]{0:T(256)} %and_select_fusion.1) | copy-start | bytes 3076
  293.4 6.0 %copy-start.29 = (bf16[1024,16]{0,1:T(8,128)(2,1)S(1)}, bf16[1024,16]{0,1:T(8,128)(2,1)}, u32[]{:S(2)}) copy-start(bf16[1024,16]{0,1:T(8,128)(2,1)} %reduce_sum.160) | copy-start | bytes 98308
  293.4 15.4 %copy-start.18 = (f32[1024,512]{1,0:T(8,128)S(1)}, f32[1024,512]{1,0:T(8,128)}, u32[]{:S(2)}) copy-start(f32[1024,512]{1,0:T(8,128)} %get-tuple-element.106) | copy-start | bytes 6291460
  293.4 15.4 %copy-start.19 = (f32[1024,512]{1,0:T(8,128)S(1)}, f32[1024,512]{1,0:T(8,128)}, u32[]{:S(2)}) copy-start(f32[1024,512]{1,0:T(8,128)} %get-tuple-element.22) | copy-start | bytes 6291460
  297.9 6.1 %copy-start.31 = (bf16[512,16]{0,1:T(8,128)(2,1)S(1)}, bf16[512,16]{0,1:T(8,128)(2,1)}, u32[]{:S(2)}) copy-start(bf16[512,16]{0,1:T(8,128)(2,1)} %copy-done.30) | copy-start | bytes 49156
  297.9 6.1 %copy-start.36 = (f32[16,512]{1,0:T(8,128)S(1)}, f32[16,512]{1,0:T(8,128)}, u32[]{:S(2)}) copy-start(f32[16,512]{1,0:T(8,128)} %get-tuple-element.26) | copy-start | bytes 98308
  299.4 9.4 %copy-start.1 = (f32[1024,512]{1,0:T(8,128)S(1)}, f32[1024,512]{1,0:T(8,128)}, u32[]{:S(2)}) copy-start(f32[1024,512]{1,0:T(8,128)} %copy-done) | copy-start | bytes 6291460
  299.4 9.4 %copy-start.8 = (f32[1024,512]{1,0:T(8,128)S(1)}, f32[1024,512]{1,0:T(8,128)}, u32[]{:S(2)}) copy-start(f32[1024,512]{1,0:T(8,128)} %get-tuple-element.97.dm_ref) | copy-start | bytes 6291460
  299.4 9.4 %copy-start.54 = (f32[512]{0:T(512)S(1)}, f32[512]{0:T(512)}, u32[]{:S(2)}) copy-start(f32[512]{0:T(512)} %get-tuple-element.86) | copy-start | bytes 6148
  299.4 5.7 %collective-permute-start.17 = (bf16[1024,96]{0,1:T(8,128)(2,1)S(1)}, bf16[1024,96]{0,1:T(8,128)(2,1)S(1)}, u32[]{:S(2)}, u32[]{:S(2)}) collective-permute-start(bf16[1024,96]{0,1:T(8,128)(2,1)S(1)} %pad_maximum_fusion.5), channel_id=1, source_target_pairs={{0,1},{1,0},{2,3},{3,2},{4,5},{5,4},{6,7},{7,6},{8,9},{9,8},{10,11... | collective-permute-start | bytes 589832 | tf_op jit(solution)/shard_map/ppermute | solution.py:164
  299.5 7.3 %collective-permute-start.18 = (bf16[1024,96]{0,1:T(8,128)(2,1)S(1)}, bf16[1024,96]{0,1:T(8,128)(2,1)S(1)}, u32[]{:S(2)}, u32[]{:S(2)}) collective-permute-start(bf16[1024,96]{0,1:T(8,128)(2,1)S(1)} %pad_maximum_fusion.5), channel_id=1, source_target_pairs={{0,2},{1,3},{2,0},{3,1},{4,6},{5,7},{6,4},{7,5},{8,10},{9,11},{10,... | collective-permute-start | bytes 589832 | tf_op jit(solution)/shard_map/ppermute | solution.py:164
  301.5 6.8 %collective-permute-start.19 = (bf16[1024,96]{0,1:T(8,128)(2,1)S(1)}, bf16[1024,96]{0,1:T(8,128)(2,1)S(1)}, u32[]{:S(2)}, u32[]{:S(2)}) collective-permute-start(bf16[1024,96]{0,1:T(8,128)(2,1)S(1)} %pad_maximum_fusion.5), channel_id=1, source_target_pairs={{0,3},{1,2},{2,1},{3,0},{4,7},{5,6},{6,5},{7,4},{8,11},{9,10},{10,... | collective-permute-start | bytes 589832 | tf_op jit(solution)/shard_map/ppermute | solution.py:164
  321.7 90.9 %reduce-scatter.5.cloned.1.call-start = ((), (), s32[]{:S(2)}) async-start(), calls=%async_computation.7 | async-start | bytes 2359296 | tf_op jit(solution)/shard_map/reduce_scatter | solution.py:356
  333.8 21.9 %copy-start.33 = (f32[1024,1]{0,1:T(1,128)S(1)}, f32[1024,1]{0,1:T(1,128)}, u32[]{:S(2)}) copy-start(f32[1024,1]{0,1:T(1,128)} %copy-done.32) | copy-start | bytes 12292
  334.7 14.0 %collective-permute-start.20 = (bf16[256,1024]{1,0:T(8,128)(2,1)}, bf16[256,1024]{1,0:T(8,128)(2,1)S(1)}, u32[]{:S(2)}, u32[]{:S(2)}) collective-permute-start(bf16[256,1024]{1,0:T(8,128)(2,1)} %get-tuple-element.109), channel_id=1, source_target_pairs={{0,1},{1,0},{2,3},{3,2},{4,5},{5,4},{6,7},{7,6},{8,9},{9,8},{10,11... | collective-permute-start | bytes 1572872 | tf_op jit(solution)/shard_map/ppermute | solution.py:164
  336.3 18.6 %collective-permute-start.21 = (bf16[256,1024]{1,0:T(8,128)(2,1)S(1)}, bf16[256,1024]{1,0:T(8,128)(2,1)S(1)}, u32[]{:S(2)}, u32[]{:S(2)}) collective-permute-start(bf16[256,1024]{1,0:T(8,128)(2,1)S(1)} %get-tuple-element.111), channel_id=1, source_target_pairs={{0,2},{1,3},{2,0},{3,1},{4,6},{5,7},{6,4},{7,5},{8,10},{9,11},{10,... | collective-permute-start | bytes 1572872 | tf_op jit(solution)/shard_map/ppermute | solution.py:164
  337.3 17.5 %collective-permute-start.22 = (bf16[256,1024]{1,0:T(8,128)(2,1)S(1)}, bf16[256,1024]{1,0:T(8,128)(2,1)S(1)}, u32[]{:S(2)}, u32[]{:S(2)}) collective-permute-start(bf16[256,1024]{1,0:T(8,128)(2,1)S(1)} %get-tuple-element.110), channel_id=1, source_target_pairs={{0,3},{1,2},{2,1},{3,0},{4,7},{5,6},{6,5},{7,4},{8,11},{9,10},{10,... | collective-permute-start | bytes 1572872 | tf_op jit(solution)/shard_map/ppermute | solution.py:164
  354.8 22.8 %copy-start.22 = (bf16[256,1024]{1,0:T(8,128)(2,1)}, bf16[256,1024]{1,0:T(8,128)(2,1)S(1)}, u32[]{:S(2)}) copy-start(bf16[256,1024]{1,0:T(8,128)(2,1)S(1)} %collective-permute-done.21) | copy-start | bytes 1572868
  355.7 25.7 %copy-start.10 = (f32[256,1024]{1,0:T(8,128)S(1)}, f32[256,1024]{1,0:T(8,128)}, u32[]{:S(2)}) copy-start(f32[256,1024]{1,0:T(8,128)} %get-tuple-element.102) | copy-start | bytes 3145732
  355.7 25.8 %copy-start.21 = (bf16[1,256,1024]{2,1,0:T(8,128)(2,1)S(1)}, bf16[1,256,1024]{2,1,0:T(8,128)(2,1)}, u32[]{:S(2)}) copy-start(bf16[1,256,1024]{2,1,0:T(8,128)(2,1)} %param.15) | copy-start | bytes 1572868
  355.7 25.8 %copy-start.50 = (f32[256]{0:T(256)S(1)}, f32[256]{0:T(256)}, u32[]{:S(2)}) copy-start(f32[256]{0:T(256)} %copy-done.49) | copy-start | bytes 3076
  355.7 25.8 %copy-start.51 = (f32[1,256]{1,0:T(1,128)S(1)}, f32[1,256]{1,0:T(1,128)}, u32[]{:S(2)}) copy-start(f32[1,256]{1,0:T(1,128)} %get-tuple-element.125) | copy-start | bytes 3076
  377.7 31.8 %all-to-all-start.1 = ((f32[4,32,1024]{2,1,0:T(8,128)}), f32[4,32,1024]{2,1,0:T(8,128)S(1)}, u32[]{:S(2)}, u32[]{:S(2)}) async-start(f32[4,32,1024]{2,1,0:T(8,128)} %bitcast.59), calls=%async_computation.2 | async-start | bytes 1048576 | tf_op jit(solution)/shard_map/all_to_all | solution.py:397
  381.5 24.4 %slice-start = ((f32[1,144,1024]{2,1,0:T(8,128)}), f32[1,16,1024]{2,1,0:T(8,128)S(1)}, s32[]{:S(2)}) async-start(f32[1,144,1024]{2,1,0:T(8,128)} %reduce-scatter.3.cloned.1.call-done), calls=%async_computation.8 | async-start | bytes 131072 | tf_op jit(solution)/shard_map/slice | solution.py:396
  385.6 1.2 collective-permute-start.9
  388.1 3.6 collective-permute-start.10
  392.3 4.5 %collective-permute-start.11 = (f32[1,1]{1,0:T(1,128)}, f32[1,1]{1,0:T(1,128)}, u32[]{:S(2)}, u32[]{:S(2)}) collective-permute-start(f32[1,1]{1,0:T(1,128)} %add.278), channel_id=1, source_target_pairs={{0,16},{4,20},{8,24},{12,28},{16,0},{20,4},{24,8},{28,12},{1,17},{... | collective-permute-start | bytes 20 | tf_op jit(solution)/shard_map/ppermute | solution.py:164
  397.4 3.6 collective-permute-start.12
  401.6 3.6 collective-permute-start.13
  (27 other events, 58.2 us)
Sparse Core Ops, SparseCore 0:
  13.7 26.1 all-gather.2
  42.1 32.2 all-gather.4
  321.8 53.8 reduce-scatter.2
  378.5 34.0 reduce-scatter.4
where the time goes:
time: 423 us; the launch traced here: 420 us
  waiting for transfers between devices  104 us (25%)
  Pallas kernels  88 us (21%)
  local copies, waits for them, and re-layouts  70 us (17%)
  other arithmetic  55 us (13%)
  starting transfers between devices  34.9 us (8%)
  matrix products  33.5 us (8%)
  between operations  23.5 us (6%)
  blocking collectives  11.3 us (3%)
    pallas_call x4, Pallas kernels, call(): pl.pallas_call(kernel, out_shape=[jax.ShapeDtypeStruct(s, d) for s, d in...  88 us
    ppermute x23, waiting for transfers between devices, partner(): lax.ppermute(value, axis, [(i, i ^ k) for i in range(lax.axis_size(axis))])  81.3 us
    ppermute x23, starting transfers between devices, partner(): lax.ppermute(value, axis, [(i, i ^ k) for i in range(lax.axis_size(axis))])  31 us
    dot_general x4, matrix products, dot_t(): lax.dot_general(a, b, (((1,), (1,)), ((), ())), preferred_element_type=f32)  19.3 us
    reduce_scatter x1, waiting for transfers between devices, body(): both = lax.psum_scatter(both, 'batch', scatter_dimension=0)  18.1 us
    unnamed x133, local copies, waits for them, and re-layouts  15.8 us
    all_to_all x1, blocking collectives, body(): lax.all_to_all(split, 'seq', 0, 0).reshape(seqs * depth, 2 * chans + 128)  11.3 us
    dynamic_update_slice x6, local copies, waits for them, and re-layouts, gather_parts(): whole = lax.dynamic_update_index_in_dim(whole, part, me ^ k, 0)  8.89 us
  transfers between devices with their start and end apart: 28, of which 21 were waited for; matrix products, arithmetic and copies ran while one was open for 15% of the time, Pallas kernels for 0%

commit v1 on v0

v1 whole, which is shorter than its diff:
```python
import jax
import jax.numpy as jnp
from jax import lax
from jax.experimental import pallas as pl
from jax.experimental.pallas import tpu as pltpu
from jax.sharding import PartitionSpec as P

PIECE = 256
BLOCK = 16
ROWS = 128
LOG2E = 1.4426950408889634
LN2 = 0.6931471805599453
NEVER = 1e9
LANES = 128
f32 = jnp.float32
bf16 = jnp.bfloat16

ALOG, CONV, CONVB, DTB, SKIP = 64, 80, 84, 85, 86
INTO, OUT, CARRY = 64, 80, 96


def dot(a, b):
    return jnp.dot(a, b, preferred_element_type=f32)


def dot_t(a, b):
    return lax.dot_general(a, b, (((1,), (1,)), ((), ())), preferred_element_type=f32)


def t_dot(a, b):
    return lax.dot_general(a, b, (((0,), (0,)), ((), ())), preferred_element_type=f32)


def sigmoid(v):
    return 1.0 / (1.0 + jnp.exp(-v))


def row_of(ref, t, n):
    return jnp.broadcast_to(ref[pl.ds(t, 1), :], (n, ref.shape[1]))


def col_of(block, tt, c):
    return jnp.broadcast_to(block[:, tt : tt + 1], (block.shape[0], c))


def rates_of(vec_ref, n):
    return -jnp.exp(vec_ref[ALOG : ALOG + n, :]) * LOG2E


def dt_of(proj, vec_ref, rank):
    low = proj[:, :rank].astype(bf16)
    return low, dot(low, vec_ref[:rank, :].astype(bf16)) + vec_ref[DTB : DTB + 1, :]


def softplus(v):
    return jnp.maximum(v, 0.0) + jnp.log1p(jnp.exp(-jnp.abs(v)))


def columns(proj_t, first, n, into_ref):
    for j in range(into_ref.shape[0]):
        into_ref[j] = proj_t[first : first + n, j * BLOCK : (j + 1) * BLOCK]


def block_diag(values, n):
    rows, wide = values.shape[0], BLOCK * n
    spread = (
        lax.broadcasted_iota(jnp.int32, (n, wide), 1) % n == lax.broadcasted_iota(jnp.int32, (n, wide), 0)
    ).astype(f32).astype(bf16)
    keep = lax.broadcasted_iota(jnp.int32, (rows, wide), 1) // n == lax.broadcasted_iota(
        jnp.int32, (rows, wide), 0
    ) % BLOCK
    return jnp.where(keep, dot(values, spread), 0.0).astype(bf16)


def unit_of(x):
    return x * lax.rsqrt(jnp.mean(x * x, axis=-1, keepdims=True) + 1e-05)


def start_kernel(
    me_ref, x_ref, *refs,
):
    parts = refs[:-13]
    (
        normed_ref, stream_ref, pre_ref, act_ref, proj_ref, w_ref, vec_ref, xproj_ref, gain_ref, marks_ref,
        wide_ref, ext_ref, cols_ref,
    ) = refs[-13:]
    rows, chans = stream_ref.shape
    taps = CONVB - CONV

    @pl.when(pl.program_id(0) == 0)
    def _():
        wide_ref[:8, :] = jnp.zeros((8, chans), f32)
        place = 1
        for part in parts:
            count, lines, _ = part.shape
            own = chans * lines // w_ref.shape[0]
            for k in range(count):
                block = me_ref[place]
                place += 1
                at = pl.ds(pl.multiple_of(block * lines, lines), lines)
                w_ref[at, :] = part[k, :, :chans]
                ext = part[k, :, chans:].astype(f32)
                ext_ref[at, :] = ext
                at = pl.ds(pl.multiple_of(block * own, own), own)
                cols_ref[at, :] = ext[:own]
                used = lax.broadcasted_iota(jnp.int32, (own, LANES), 1) < CARRY
                xproj_ref[at, :] = jnp.where(used, ext[own : 2 * own], 0.0).astype(bf16)
        for k in range(w_ref.shape[0] // LANES):
            at = slice(k * LANES, (k + 1) * LANES)
            gain_ref[:, at] = ext_ref[at, :].T[LANES - 3 : LANES - 2]
        for k in range(chans // LANES):
            at = slice(k * LANES, (k + 1) * LANES)
            vec_ref[:, at] = cols_ref[at, :].T
        marks_ref[...] = jnp.sum(ext_ref[...], axis=0, keepdims=True)

    normed = (unit_of(x_ref[...].astype(f32)) * gain_ref[...]).astype(bf16)
    normed_ref[...] = normed
    stream = dot(normed, w_ref[...]).astype(bf16)
    stream_ref[...] = stream
    wide_ref[8:, :] = stream.astype(f32)
    pre = jnp.broadcast_to(vec_ref[CONVB : CONVB + 1, :], (rows, chans))
    for tap in range(taps):
        first = 8 - taps + 1 + tap
        pre = pre + vec_ref[CONV + tap : CONV + tap + 1, :] * wide_ref[first : first + rows, :]
    wide_ref[:8, :] = wide_ref[rows:, :]
    pre_ref[...] = pre
    act = (pre * sigmoid(pre)).astype(bf16)
    act_ref[...] = act
    proj_ref[...] = dot(act, xproj_ref[...]).astype(bf16)


def piece_kernel(me_ref, proj_ref, act_ref, vec_ref, g_ref, carry_ref, u_ref, stepm_ref, col_ref):
    rows, c = act_ref.shape
    n = carry_ref.shape[0]

    @pl.when(pl.program_id(0) == 0)
    def _():
        carry_ref[...] = jnp.zeros_like(carry_ref)

    proj = proj_ref[...]
    _, pre = dt_of(proj, vec_ref, INTO)
    step = softplus(pre)
    u_ref[...] = step * act_ref[...].astype(f32)
    stepm_ref[...] = jnp.where(proj[:, CARRY : CARRY + 1] > 0.5, step, NEVER)
    columns(proj.T, INTO, n, col_ref)
    r2 = rates_of(vec_ref, n)

    def block(i, carry):
        j = rows // BLOCK - 1 - i
        into = col_ref[j]
        for tt in reversed(range(BLOCK)):
            t = j * BLOCK + tt
            g = row_of(u_ref, t, n) * col_of(into, tt, c) + carry
            g_ref[pl.ds(pl.multiple_of(t * n, n), n), :] = g.astype(bf16)
            carry = jnp.exp2(row_of(stepm_ref, t, n) * r2) * g
        return carry

    carry_ref[...] = lax.fori_loop(0, rows // BLOCK, block, carry_ref[...])


def ahead_kernel(
    me_ref, proj_ref, act_ref, normed_ref, g_ref, vec_ref, second_ref,
    hp_ref, mixed_ref, gate_ref, gated_ref, branch_ref, wgate_ref, outw_ref,
    carry_ref, u_ref, step_ref, col_ref, diag_ref, s_ref, y_ref,
):
    rows, c = act_ref.shape
    n = carry_ref.shape[0]

    @pl.when(pl.program_id(0) == 0)
    def _():
        carry_ref[...] = jnp.zeros_like(carry_ref)
        blocks = second_ref.shape[0]
        lines, own = wgate_ref.shape[0] // blocks, outw_ref.shape[0] // blocks
        for b in range(blocks):
            wgate_ref[b * lines : (b + 1) * lines, :] = second_ref[b, :lines, :]
            for k in range(outw_ref.shape[1] // c):
                outw_ref[b * own : (b + 1) * own, k * c : (k + 1) * c] = second_ref[
                    b, lines + k * own : lines + (k + 1) * own, :
                ]

    proj = proj_ref[...]
    act = act_ref[...].astype(f32)
    _, pre = dt_of(proj, vec_ref, INTO)
    step = softplus(pre)
    step_ref[...] = step
    u_ref[...] = step * act
    columns(proj.T, INTO, n, col_ref)
    read = proj[:, OUT : OUT + n]
    high = read.astype(bf16)
    diag_ref[0, BLOCK:] = block_diag(high, n)
    diag_ref[1, BLOCK:] = block_diag((read - high.astype(f32)).astype(bf16), n)
    r2 = rates_of(vec_ref, n)

    def read_out(j):
        r16 = pl.ds(pl.multiple_of(j * BLOCK, BLOCK), BLOCK)
        both = dot(jnp.concatenate([diag_ref[0, r16, :], diag_ref[1, r16, :]], axis=0), s_ref[...])
        y_ref[r16, :] = both[:BLOCK] + both[BLOCK:]

    def block(j, h):
        read_out(j)
        into = col_ref[j]
        for tt in range(BLOCK):
            t = j * BLOCK + tt
            at = pl.ds(pl.multiple_of(t * n, n), n)
            hp = jnp.exp2(row_of(step_ref, t, n) * r2) * h
            h = hp + row_of(u_ref, t, n) * col_of(into, tt, c)
            hp_ref[at, :] = hp.astype(bf16)
            s_ref[tt * n : (tt + 1) * n, :] = (hp + g_ref[at, :].astype(f32)).astype(bf16)
        return h

    carry_ref[...] = lax.fori_loop(0, rows // BLOCK, block, carry_ref[...])
    read_out(rows // BLOCK)
    mixed = y_ref[BLOCK:] + vec_ref[SKIP : SKIP + 1, :] * act
    mixed_ref[...] = mixed
    gate = dot(normed_ref[...], wgate_ref[...])
    gate_ref[...] = gate
    gated = (mixed * (gate * sigmoid(gate))).astype(bf16)
    gated_ref[...] = gated
    branch_ref[...] = dot(gated, outw_ref[...]).astype(bf16)


def piece_grad_kernel(
    me_ref, proj_ref, act_ref, mixed_ref, gate_ref, db_ref, vec_ref, outw_ref,
    q_ref, dm_ref, dg_ref, sgrad_ref,
    carry_ref, stepm_ref, col_ref,
):
    rows, c = act_ref.shape
    n = carry_ref.shape[0]

    @pl.when(pl.program_id(0) == 0)
    def _():
        carry_ref[...] = jnp.zeros_like(carry_ref)
        sgrad_ref[...] = jnp.zeros_like(sgrad_ref)

    proj = proj_ref[...]
    _, pre = dt_of(proj, vec_ref, INTO)
    stepm_ref[...] = jnp.where(proj[:, CARRY : CARRY + 1] > 0.5, softplus(pre), NEVER)
    columns(proj.T, OUT, n, col_ref)
    db = db_ref[...]
    dgated = dot_t(db, outw_ref[...])
    gate = gate_ref[...]
    s = sigmoid(gate)
    dm = dgated * (gate * s)
    dm_ref[...] = dm
    dg = (dgated * mixed_ref[...] * (s * (1.0 + gate * (1.0 - s)))).astype(bf16)
    dg_ref[...] = dg
    sgrad_ref[...] += jnp.sum(dm * act_ref[...].astype(f32), axis=0, keepdims=True)
    r2 = rates_of(vec_ref, n)

    def block(j, w):
        read = col_ref[j]
        for tt in range(BLOCK):
            t = j * BLOCK + tt
            q = jnp.exp2(row_of(stepm_ref, t, n) * r2) * w
            q_ref[pl.ds(pl.multiple_of(t * n, n), n), :] = q.astype(bf16)
            w = q + row_of(dm_ref, t, n) * col_of(read, tt, c)
        return w

    carry_ref[...] = lax.fori_loop(0, rows // BLOCK, block, carry_ref[...])


def state_grad_kernel(
    me_ref, proj_ref, act_ref, dm_ref, g_ref, hp_ref, q_ref, vec_ref, sgrad_ref,
    dact_ref, dproj_ref, table_ref,
    carry_ref, u_ref, step_ref, col_ref, diag_ref, ig_ref, rr_ref, rs_ref, pair_ref, own_ref, x_ref, y_ref, dp_ref,
):
    rows, c = act_ref.shape
    n = carry_ref.shape[0]
    wide = BLOCK * n

    @pl.when(pl.program_id(0) == 0)
    def _():
        carry_ref[...] = jnp.zeros_like(carry_ref)
        table_ref[...] = jnp.zeros_like(table_ref)
        table_ref[SKIP : SKIP + 1, :] = sgrad_ref[...]
        rs_ref[...] = jnp.zeros_like(rs_ref)

    proj = proj_ref[...]
    act = act_ref[...].astype(f32)
    low, pre = dt_of(proj, vec_ref, INTO)
    step = softplus(pre)
    step_ref[...] = step
    u_ref[...] = step * act
    columns(proj.T, OUT, n, col_ref)
    diag_ref[:rows] = block_diag(proj[:, INTO : INTO + n].astype(bf16), n)
    r2 = rates_of(vec_ref, n)
    iota = lambda shape, axis: lax.broadcasted_iota(jnp.int32, shape, axis)
    mask = lambda v: v.astype(f32).astype(bf16)
    by_row = mask(iota((BLOCK, wide), 1) // n == iota((BLOCK, wide), 0))
    by_state = mask(iota((n, wide), 1) % n == iota((n, wide), 0))
    part = min(c, 2 * LANES)
    which = mask(iota((2 * part, LANES), 0) // part == iota((2 * part, LANES), 1) // n % 2)
    own_lane = iota((wide, LANES), 1) % n == iota((wide, LANES), 0) % n

    def sums(j):
        r16 = pl.ds(pl.multiple_of(j * BLOCK, BLOCK), BLOCK)
        x_ref[r16, :] = dot(diag_ref[r16, :], ig_ref[...])
        y_ref[r16, :] = dot(by_row, rr_ref[...])
        table_ref[ALOG : ALOG + n, :] += dot(by_state, rs_ref[...])
        dp_ref[pl.ds(pl.multiple_of((j + 1) * BLOCK, BLOCK), BLOCK), :] = dot(by_row, own_ref[...])
        own_ref[...] = jnp.where(own_lane, dot(pair_ref[...], which), 0.0).astype(bf16)

    def block(i, m):
        j = rows // BLOCK - 1 - i
        sums(j + 1)
        read = col_ref[j]
        for tt in reversed(range(BLOCK)):
            t = j * BLOCK + tt
            at = pl.ds(pl.multiple_of(t * n, n), n)
            loc = slice(tt * n, (tt + 1) * n)
            drow = row_of(dm_ref, t, n)
            mu = m + drow * col_of(read, tt, c)
            srow = row_of(step_ref, t, n)
            m = jnp.exp2(srow * r2) * mu
            low_mu = mu.astype(bf16)
            q = q_ref[at, :]
            g = g_ref[at, :]
            hp = hp_ref[at, :]
            rg = low_mu * hp + q * g
            ig = low_mu + q
            ig_ref[loc, :] = ig
            rr_ref[loc, :] = (rg.astype(f32) * r2).astype(bf16)
            rs_ref[loc, :] = rg * srow.astype(bf16)
            pb = ig * row_of(u_ref, t, n).astype(bf16)
            pc = (hp + g) * drow.astype(bf16)
            sb, sc = pb[:, :part], pc[:, :part]
            for k in range(1, c // part):
                sb = sb + pb[:, k * part : (k + 1) * part]
                sc = sc + pc[:, k * part : (k + 1) * part]
            pair_ref[loc, :part] = sb
            pair_ref[loc, part:] = sc
        return m

    carry_ref[...] = lax.fori_loop(0, rows // BLOCK, block, carry_ref[...])
    sums(0)
    dp_ref[:BLOCK, :] = dot(by_row, own_ref[...])
    rs_ref[...] = jnp.zeros_like(rs_ref)
    xs = x_ref[:rows]
    dact_ref[...] = step_ref[...] * xs + vec_ref[SKIP : SKIP + 1, :] * dm_ref[...]
    dpre = (y_ref[:rows] * LN2 + act * xs) * sigmoid(pre)
    table_ref[DTB : DTB + 1, :] += jnp.sum(dpre, axis=0, keepdims=True)
    dpre_low = dpre.astype(bf16)
    table_ref[:INTO, :] += t_dot(low, dpre_low)
    dproj_ref[...] = dp_ref[:rows].astype(bf16)
    dproj_ref[:, :INTO] = dot_t(dpre_low, vec_ref[:INTO, :].astype(bf16)).astype(bf16)

    @pl.when(pl.program_id(0) == pl.num_programs(0) - 1)
    def _():
        table_ref[ALOG : ALOG + n, :] *= -jnp.exp(vec_ref[ALOG : ALOG + n, :])


def end_kernel(own, me_ref, *refs):
    parts = refs[:-17]
    (
        dact_ref, pre_ref, stream_ref, act_ref, dg_ref, vec_ref, xproj_ref, ws_ref, wg_ref, table_ref,
        dn_ref, ds_ref, small_ref,
        wide_ref, xgrad_ref, cgrad_ref, turned_ref,
    ) = refs[-17:]
    rows, c = act_ref.shape
    taps = CONVB - CONV

    @pl.when(pl.program_id(0) == 0)
    def _():
        wide_ref[rows:, :] = jnp.zeros((8, c), f32)
        xgrad_ref[...] = jnp.zeros_like(xgrad_ref)
        cgrad_ref[...] = table_ref[...]

    dproj = parts[0][...].astype(f32)
    for part in parts[1:]:
        dproj = dproj + part[...].astype(f32)
    used = lax.broadcasted_iota(jnp.int32, dproj.shape, 1) < CARRY
    dproj = jnp.where(used, dproj, 0.0).astype(bf16)
    pre = pre_ref[...]
    s = sigmoid(pre)
    dconv = (dact_ref[...] + dot_t(dproj, xproj_ref[...])) * (s * (1.0 + pre * (1.0 - s)))
    wide_ref[:rows, :] = dconv
    xgrad_ref[...] += t_dot(act_ref[...], dproj)
    cgrad_ref[CONVB : CONVB + 1, :] += jnp.sum(dconv, axis=0, keepdims=True)
    stream = stream_ref[...].astype(f32)
    dstream = jnp.zeros((rows, c), f32)
    for tap in range(taps):
        back = taps - 1 - tap
        moved = wide_ref[back : back + rows, :]
        cgrad_ref[CONV + tap : CONV + tap + 1, :] += jnp.sum(stream * moved, axis=0, keepdims=True)
        dstream = dstream + vec_ref[CONV + tap : CONV + tap + 1, :] * moved
    wide_ref[rows:, :] = dconv[:8, :]
    dstream_low = dstream.astype(bf16)
    dn_ref[...] = (dot_t(dstream_low, ws_ref[...]) + dot_t(dg_ref[...], wg_ref[...])).astype(bf16)
    ds_ref[...] = dstream_low

    @pl.when(pl.program_id(0) == pl.num_programs(0) - 1)
    def _():
        for k in range(c // LANES):
            at = slice(k * LANES, (k + 1) * LANES)
            turned_ref[at, :] = cgrad_ref[:, at].T
        lines = 2 * own * LANES // c
        for b in range(c // own):
            at = slice(b * own, (b + 1) * own)
            both = jnp.concatenate([xgrad_ref[at, :], turned_ref[at, :]], axis=0)
            for k in range(c // LANES):
                small_ref[b * lines : (b + 1) * lines, k * LANES : (k + 1) * LANES] = both[k * lines : (k + 1) * lines]


def call(kernel, me, ins, outs, scratch, total, local, reverse=False):
    steps = total // ROWS
    per = local // ROWS
    turn = (lambda i: steps - 1 - i) if reverse else (lambda i: i)

    def spec(shape, kind):
        if kind == "f":
            return pl.BlockSpec(shape, lambda i, me_ref: (0,) * len(shape))
        if kind == "x":
            return pl.BlockSpec(
                (None, ROWS, shape[2]), lambda i, me_ref: ((turn(i) // per) ^ me_ref[0], turn(i) % per, 0)
            )
        return pl.BlockSpec((shape[0] // steps, shape[1]), lambda i, me_ref: (turn(i), 0))

    return pl.pallas_call(
        kernel,
        out_shape=[jax.ShapeDtypeStruct(s, d) for s, d, _ in outs],
        grid_spec=pltpu.PrefetchScalarGridSpec(
            num_scalar_prefetch=1,
            grid=(steps,),
            in_specs=[spec(a.shape, k) for a, k in ins],
            out_specs=[spec(s, k) for s, _, k in outs],
            scratch_shapes=scratch,
        ),
        compiler_params=pltpu.CompilerParams(dimension_semantics=("arbitrary",), vmem_limit_bytes=60 << 20),
    )(me, *[a for a, _ in ins])


def split_kernel(seqs, batches, own, w_ref, extra_ref, out_ref):
    half, chans = w_ref.shape[1] // 2, batches * own
    for s in range(seqs):
        for k in range(2):
            pieces = [
                w_ref[:, k * half + (b * seqs + s) * own : k * half + (b * seqs + s + 1) * own].astype(f32)
                for b in range(batches)
            ]
            first = k * (chans + LANES)
            out_ref[s, :, first : first + chans] = jnp.concatenate(pieces, axis=1).astype(bf16)
        out_ref[s, :, chans : chans + LANES] = extra_ref[...]


def split_columns(weight, extra, seqs, batches, own):
    shape = jax.ShapeDtypeStruct((seqs, weight.shape[0], 2 * batches * own + LANES), bf16)
    return pl.pallas_call(lambda *refs: split_kernel(seqs, batches, own, *refs), out_shape=shape)(weight, extra)


def join_kernel(
    batches, stream_ref, gate_ref, small_ref, w_ref, gain_ref,
    out_ref, gain_out_ref, xproj_ref, dt_ref, alog_ref, conv_ref, convb_ref, dtb_ref, skip_ref,
):
    seqs, half = stream_ref.shape[0], w_ref.shape[1] // 2
    chans = half // seqs
    own = chans // batches
    for k, part in enumerate((stream_ref, gate_ref)):
        whole = [part[s] for s in range(seqs)]
        pieces = [whole[s][:, b * own : (b + 1) * own] for b in range(batches) for s in range(seqs)]
        out_ref[:, k * half : (k + 1) * half] = jnp.concatenate(pieces, axis=1)
    products = out_ref[...] * w_ref[...].astype(f32)
    gain_out_ref[...] = jnp.sum(products, axis=1, keepdims=True) / gain_ref[...]
    small = small_ref[...]
    both = jnp.concatenate([small[:, k : k + LANES] for k in range(0, chans, LANES)], axis=0)
    xproj_ref[...] = both[:own, :CARRY]
    table = both[own:]
    alog_ref[...] = table[:, ALOG:CONV]
    table = jnp.concatenate([table, jnp.zeros((LANES - own, LANES), f32)], axis=0).T[:, :own]
    dt_ref[...] = table[:INTO]
    conv_ref[...] = table[CONV:CONVB]
    convb_ref[...] = table[CONVB : CONVB + 1]
    dtb_ref[...] = table[DTB : DTB + 1]
    skip_ref[...] = table[SKIP : SKIP + 1]


def join_columns(stream, gate, small, weight, gain, batches, own):
    depth = weight.shape[0]
    shapes = [weight.shape, (depth, 1), (own, CARRY), (INTO, own), (own, CONV - ALOG), (CONVB - CONV, own)]
    shapes += [(1, own)] * 3
    return pl.pallas_call(
        lambda *refs: join_kernel(batches, *refs), out_shape=[jax.ShapeDtypeStruct(s, f32) for s in shapes]
    )(stream, gate, small, weight, gain)


def partner(value, axis, k):
    return lax.ppermute(value, axis, [(i, i ^ k) for i in range(lax.axis_size(axis))])


def gather_parts(value, axis):
    n = lax.axis_size(axis)
    if n > 4:
        return lax.all_gather(value, axis)
    return jnp.stack([value] + [partner(value, axis, k) for k in range(1, n)])


def gather_batch(value):
    n = lax.axis_size("batch")
    if n > 8:
        return [lax.all_gather(value, "batch")], [jnp.int32(k) for k in range(n)]
    me = lax.axis_index("batch")
    chips = jnp.stack([value] + [partner(value, "batch", 2 * k) for k in range(1, n // 2)])
    other = partner(chips, "batch", 1)
    places = [me ^ (2 * k) for k in range(n // 2)] + [me ^ (2 * k + 1) for k in range(n // 2)]
    return [chips, other], places


def exact(total, rows):
    terms = []
    for _ in range(3):
        term = lax.reduce_precision(total, 8, 7)
        terms.append(term)
        total = total - term
    return jnp.concatenate(terms + [jnp.zeros((rows - 3, total.shape[1]), f32)], axis=0).astype(bf16)


def row_sum(rows):
    a = rows[:3].astype(f32)
    return (a[:1] + a[1:2]) + a[2:]


def tree(values):
    while len(values) > 1:
        values = [a + b for a, b in zip(values[::2], values[1::2])]
    return values[0]


def scatter_batch(value, total):
    n = lax.axis_size("batch")
    if n > 8:
        return lax.psum_scatter(value, "batch", scatter_dimension=0), sum_everywhere(total, ("batch",)), value
    me = lax.axis_index("batch")
    rows, c = value.shape[1:]
    block = lambda t: jnp.broadcast_to(exact(jnp.tile(t, (1, c // LANES)), BLOCK)[None], (n // 2, BLOCK, c))
    pairs = value.reshape((n // 2, 2) + value.shape[1:])
    mine = lax.dynamic_index_in_dim(pairs, me % 2, 1, False)
    theirs = lax.dynamic_index_in_dim(pairs, 1 - me % 2, 1, False).astype(bf16)
    got = partner(jnp.concatenate([theirs, block(total)], axis=1), "batch", 1)
    mine = mine + got[:, :rows].astype(f32)
    total = row_sum(exact(total, BLOCK)) + row_sum(got[0, rows:, :LANES])
    low = jnp.concatenate([mine.astype(bf16), block(total)], axis=1)
    got = [
        partner(lax.dynamic_index_in_dim(low, (me // 2) ^ k, 0, False), "batch", 2 * k) for k in range(1, n // 2)
    ]
    result = lax.dynamic_index_in_dim(mine, me // 2, 0, False)
    for part in got:
        result = result + part[:rows].astype(f32)
    return result, tree([row_sum(exact(total, BLOCK))] + [row_sum(part[rows:, :LANES]) for part in got]), low


def scatter_parts(value, axis):
    n = lax.axis_size(axis)
    if n > 4:
        return [lax.psum_scatter(value.astype(f32), axis, scatter_dimension=0)]
    return [value[0]] + [partner(value[k], axis, k) for k in range(1, n)]


def share_parts(value, axis):
    n = lax.axis_size(axis)
    if n > 4:
        return [lax.psum(value.astype(f32), axis)]
    return [value] + [partner(value, axis, k) for k in range(1, n)]


def added(parts):
    total = parts[0].astype(f32)
    for part in parts[1:]:
        total = total + part.astype(f32)
    return total


def sum_everywhere(value, axes):
    for axis in axes:
        k = 1
        while k < lax.axis_size(axis):
            value = value + partner(value, axis, k)
            k *= 2
    return value


def body(
    tokens,
    teacher,
    piece_starts,
    valid_rows,
    norm_gain,
    in_weight,
    conv_weight,
    conv_bias,
    xproj_weight,
    dtproj_weight,
    dt_bias,
    a_log,
    skip_weight,
    out_weight,
):
    seqs = lax.axis_size("seq")
    batches = lax.axis_size("batch")
    _, rows, width = tokens.shape
    total = rows * seqs
    taps, own = conv_weight.shape
    chans = own * batches
    depth = in_weight.shape[0]
    rank = dtproj_weight.shape[0]
    states = a_log.shape[1]
    lines = depth * seqs
    packed = 2 * LANES * own // chans
    place = lax.axis_index("seq") if seqs <= 4 else jnp.int32(0)
    me = place.astype(jnp.int32).reshape(1)
    tok = tokens.reshape(rows, width)

    counted = jnp.sum(valid_rows, axis=1, keepdims=True)
    extra = jnp.concatenate(
        [
            jnp.zeros((depth, LANES - 3), bf16),
            norm_gain[:, None],
            jnp.broadcast_to((counted // 128).astype(bf16), (depth, 1)),
            jnp.broadcast_to((counted % 128).astype(bf16), (depth, 1)),
        ],
        axis=1,
    )
    split = split_columns(in_weight, extra, seqs, batches, own)
    split = lax.all_to_all(split, "seq", 0, 0).reshape(lines, 2 * chans + LANES)
    vectors = jnp.concatenate(
        [
            dtproj_weight.T,
            a_log,
            conv_weight.T,
            conv_bias[:, None],
            dt_bias[:, None],
            skip_weight[:, None],
        ],
        axis=1,
    )
    vectors = jnp.pad(vectors, ((0, 0), (0, LANES - vectors.shape[1])))
    columns_x = jnp.pad(xproj_weight, ((0, 0), (0, LANES - xproj_weight.shape[1])))
    local = jnp.pad(jnp.concatenate([vectors, columns_x], axis=0), ((0, lines - 2 * own), (chans, 0)))
    blocks, places = gather_batch(split[:, : chans + LANES] + local)
    second = jnp.concatenate(
        [split[:, chans + LANES :]] + [out_weight[:, k : k + chans] for k in range(0, width, chans)], axis=0
    )
    second = lax.all_gather(second, "batch")

    flags = jnp.pad(piece_starts.astype(bf16), ((0, 15), (0, width - rows)))
    held = jnp.concatenate([tok, flags], axis=0)
    held, split = lax.optimization_barrier((held, split))
    everything = gather_parts(held, "seq")

    tile = ((total, chans), f32, "t")
    low_tile = ((total, chans), bf16, "t")
    state = ((total * states, chans), bf16, "t")
    normed, stream, conv_pre, act, proj, w_stream, vec, xproj, gain, marks = call(
        start_kernel,
        jnp.concatenate([me] + [p.astype(jnp.int32).reshape(1) for p in places]),
        [(everything, "x")] + [(block, "f") for block in blocks],
        [
            ((seqs, rows, width), bf16, "x"),
            low_tile,
            tile,
            low_tile,
            ((total, LANES), bf16, "t"),
            ((width, chans), bf16, "f"),
            ((LANES, chans), f32, "f"),
            ((chans, LANES), bf16, "f"),
            ((1, width), f32, "f"),
            ((1, LANES), f32, "f"),
        ],
        [pltpu.VMEM((ROWS + 8, chans), f32), pltpu.VMEM((width, LANES), f32), pltpu.VMEM((chans, LANES), f32)],
        total,
        rows,
    )
    total_valid = (marks[:, LANES - 2 : LANES - 1] * 128.0 + marks[:, LANES - 1 :]) / depth
    slots = jnp.arange(seqs) ^ place
    starts = jnp.take(everything[:, rows, :rows].astype(f32), slots, axis=0).reshape(total)
    running = jnp.cumsum(starts)
    lagged = jnp.concatenate([jnp.zeros((PIECE,), f32), running[: total - PIECE]])
    carry_on = jnp.where(running - lagged > 0.5, 1.0 - starts, 0.0)
    proj = added(share_parts(proj, "seq"))
    proj = jnp.where(jnp.arange(LANES)[None, :] == CARRY, carry_on[:, None], proj)
    groups = (ROWS // BLOCK, states, BLOCK)
    (g,) = call(
        piece_kernel,
        me,
        [(proj, "t"), (act, "t"), (vec, "f")],
        [state],
        [
            pltpu.VMEM((states, chans), f32),
            pltpu.VMEM((ROWS, chans), f32),
            pltpu.VMEM((ROWS, chans), f32),
            pltpu.VMEM(groups, f32),
        ],
        total,
        rows,
        reverse=True,
    )
    hp, mixed, gate, gated, branch, w_gate, out_w = call(
        ahead_kernel,
        me,
        [(proj, "t"), (act, "t"), (normed, "x"), (g, "t"), (vec, "f"), (second, "f")],
        [
            state,
            tile,
            tile,
            ((seqs, rows, chans), bf16, "x"),
            ((seqs, rows, width), bf16, "x"),
            ((width, chans), bf16, "f"),
            ((chans, width), bf16, "f"),
        ],
        [
            pltpu.VMEM((states, chans), f32),
            pltpu.VMEM((ROWS, chans), f32),
            pltpu.VMEM((ROWS, chans), f32),
            pltpu.VMEM(groups, f32),
            pltpu.VMEM((2, ROWS + BLOCK, BLOCK * states), bf16),
            pltpu.VMEM((BLOCK * states, chans), bf16),
            pltpu.VMEM((ROWS + BLOCK, chans), f32),
        ],
        total,
        rows,
    )
    tok_f = tok.astype(f32)
    valid_f = valid_rows.reshape(rows, 1).astype(f32)
    result = tok_f + added(scatter_parts(branch, "seq"))
    output = result.astype(bf16)
    misfit = result - teacher.reshape(rows, width).astype(f32)
    squares = jnp.sum(valid_f * misfit * misfit, axis=0, keepdims=True)
    square_sum = jnp.broadcast_to(jnp.sum(squares, axis=1, keepdims=True), (1, LANES))
    d_result = 2.0 * (total * batches) / total_valid * valid_f * misfit

    d_branch = gather_parts(d_result.astype(bf16), "seq")
    q, d_mixed, d_gate, skip_grad = call(
        piece_grad_kernel,
        me,
        [
            (proj, "t"),
            (act, "t"),
            (mixed, "t"),
            (gate, "t"),
            (d_branch, "x"),
            (vec, "f"),
            (out_w, "f"),
        ],
        [state, tile, ((seqs, rows, chans), bf16, "x"), ((1, chans), f32, "f")],
        [pltpu.VMEM((states, chans), f32), pltpu.VMEM((ROWS, chans), f32), pltpu.VMEM(groups, f32)],
        total,
        rows,
    )
    flat = lambda v: v.reshape(total, v.shape[2])
    gate_grad = t_dot(flat(normed), flat(d_gate))
    out_grad = t_dot(flat(gated), flat(d_branch))
    gate_out = lax.psum_scatter(gate_grad, "batch", scatter_dimension=0, tiled=True)
    out_out = lax.psum_scatter(out_grad, "batch", scatter_dimension=0, tiled=True)
    d_act, d_proj, table = call(
        state_grad_kernel,
        me,
        [(proj, "t"), (act, "t"), (d_mixed, "t"), (g, "t"), (hp, "t"), (q, "t"), (vec, "f"), (skip_grad, "f")],
        [tile, ((total, LANES), bf16, "t"), ((LANES, chans), f32, "f")],
        [
            pltpu.VMEM((states, chans), f32),
            pltpu.VMEM((ROWS, chans), f32),
            pltpu.VMEM((ROWS, chans), f32),
            pltpu.VMEM(groups, f32),
            pltpu.VMEM((ROWS + BLOCK, BLOCK * states), bf16),
        ]
        + [pltpu.VMEM((BLOCK * states, chans), bf16)] * 3
        + [
            pltpu.VMEM((BLOCK * states, 2 * min(chans, 2 * LANES)), bf16),
            pltpu.VMEM((BLOCK * states, LANES), bf16),
        ]
        + [pltpu.VMEM((ROWS + 2 * BLOCK, chans), f32)] * 2
        + [pltpu.VMEM((ROWS + 2 * BLOCK, LANES), f32)],
        total,
        rows,
        reverse=True,
    )
    if seqs <= 4:
        d_proj = lax.dynamic_update_slice(d_proj, exact(square_sum[:, CARRY:], BLOCK), (0, CARRY))
        d_proj = share_parts(d_proj, "seq")
        square_sum = jnp.tile(tree([row_sum(part[:BLOCK, CARRY:]) for part in d_proj]), (1, LANES // (LANES - CARRY)))
    else:
        d_proj = share_parts(d_proj, "seq")
        square_sum = sum_everywhere(square_sum, ("seq",))
    d_normed, d_stream, small = call(
        lambda *refs: end_kernel(own, *refs),
        me,
        [(part, "t") for part in d_proj]
        + [
            (d_act, "t"),
            (conv_pre, "t"),
            (stream, "t"),
            (act, "t"),
            (d_gate, "x"),
            (vec, "f"),
            (xproj, "f"),
            (w_stream, "f"),
            (w_gate, "f"),
            (table, "f"),
        ],
        [
            ((seqs, rows, width), bf16, "x"),
            ((seqs, rows, chans), bf16, "x"),
            ((batches * packed, chans), f32, "f"),
        ],
        [
            pltpu.VMEM((ROWS + 8, chans), f32),
            pltpu.VMEM((chans, LANES), f32),
            pltpu.VMEM((LANES, chans), f32),
            pltpu.VMEM((chans, LANES), f32),
        ],
        total,
        rows,
        reverse=True,
    )
    stream_grad = t_dot(flat(normed), flat(d_stream))
    late = jnp.concatenate(
        [stream_grad.reshape(batches, lines, chans), small.reshape(batches, packed, chans)], axis=1
    )
    d_normed, late = lax.optimization_barrier((d_normed, late))
    late, square_sum, waiting = scatter_batch(late, square_sum)
    loss = (square_sum / (total_valid * width))[0, 0]
    nothing = waiting[0, :1].astype(f32) * 0.0
    gate_out = lax.all_to_all((gate_out + nothing).reshape(seqs, depth, chans), "seq", 0, 0)
    d_normed = [jnp.tile(nothing, (1, width // chans))] + scatter_parts(d_normed, "seq")
    stream_out = lax.all_to_all(late[:lines].reshape(seqs, depth, chans), "seq", 0, 0)
    in_out, gain_out, xproj_out, dt_out, alog_out, conv_out, convb_out, dtb_out, skip_out = join_columns(
        stream_out, gate_out, late[lines:], in_weight, norm_gain.astype(f32)[:, None], batches, own
    )
    d_normed = added(d_normed)
    mean_sq = jnp.mean(tok_f * tok_f, axis=-1, keepdims=True)
    root_inv = lax.rsqrt(mean_sq + 1e-05)
    own_unit = tok_f * root_inv
    scaled = d_normed * gain
    input_grad = d_result + root_inv * (scaled - own_unit * jnp.mean(scaled * own_unit, axis=-1, keepdims=True))
    return (
        output[None],
        loss,
        input_grad[None],
        gain_out[:, 0],
        in_out,
        conv_out,
        convb_out[0],
        xproj_out,
        dt_out,
        dtb_out[0],
        alog_out,
        skip_out[0],
        out_out,
    )


def solution(mesh):
    return jax.shard_map(
        body,
        mesh=mesh,
        in_specs=(
            P("batch", "seq", None),
            P("batch", "seq", None),
            P("batch", "seq"),
            P("batch", "seq"),
            P(("batch", "seq")),
            P(("batch", "seq"), None),
            P(None, ("batch", "seq")),
            P(("batch", "seq")),
            P(("batch", "seq"), None),
            P(None, ("batch", "seq")),
            P(("batch", "seq")),
            P(("batch", "seq"), None),
            P(("batch", "seq")),
            P(("batch", "seq"), None),
        ),
        out_specs=(
            P("batch", "seq", None),
            P(),
            P("batch", "seq", None),
            P(("batch", "seq")),
            P(("batch", "seq"), None),
            P(None, ("batch", "seq")),
            P(("batch", "seq")),
            P(("batch", "seq"), None),
            P(None, ("batch", "seq")),
            P(("batch", "seq")),
            P(("batch", "seq"), None),
            P(("batch", "seq")),
            P(("batch", "seq"), None),
        ),
        check_vma=False,
    )
```

time: 423 us -> 377 us (0.89)
  local copies, waits for them, and re-layouts: 70 us -> 22 us
  Pallas kernels: 88 us -> 133 us
  other arithmetic: 55 us -> 23.2 us
  matrix products: 33.5 us -> 9.04 us
  starting transfers between devices: 34.9 us -> 57.4 us
  blocking collectives: 11.3 us -> 0 us
    pallas_call x4 -> x8, Pallas kernels: 88 us -> 133 us  [the longest x6 129 us: call(): pl.pallas_call(kernel, out_shape=[jax.ShapeDtypeStruct(s, d) for s, d, _...]
    dot_general x8 -> x0, matrix products: 25.8 us -> none  [the longest x4 19.3 us: dot_t(): lax.dot_general(a, b, (((1,), (1,)), ((), ())), preferred_element_type=f32)]
    reduce_scatter x2, waiting for transfers between devices: 18.7 us -> 0.01 us  [the longest x1 0.01 us: body(): lax.psum_scatter(gate_grad, 'batch', scatter_dimension=0, tiled=True)]
    ppermute x23 -> x26, starting transfers between devices: 31 us -> 45.1 us  [partner(): lax.ppermute(value, axis, [(i, i ^ k) for i in range(lax.axis_size(axis))])]
    reshape x13 -> x0, local copies, waits for them, and re-layouts: 12.9 us -> none  [the longest x4 8.2 us: blocks_of(): return v.reshape(t // BLOCK, BLOCK, n).transpose(0, 2, 1)]
    all_to_all x1 -> x3, waiting for transfers between devices: 0.01 us -> 12.5 us  [the longest x1 4.81 us: body(): lax.all_to_all((gate_out + nothing).reshape(seqs, depth, chans), 'seq', 0...]
    convert_element_type x12 -> x13, other arithmetic: 15.3 us -> 3.2 us  [the longest x10 1.61 us: row_sum(): a = rows[:3].astype(f32)]
    reduce_sum x9 -> x2, other arithmetic: 15.3 us -> 3.78 us  [the longest x1 2.39 us: body(): jnp.sum(squares, axis=1, keepdims=True)]
  transfers between devices with their start and end apart: 28 -> 32, of which waited for: 21 -> 17; matrix products, arithmetic and copies ran while one was open for 15% -> 9% of each run, Pallas kernels for 0% -> 23%
where the time goes in v1:
time: 377 us; the launch traced here: 373 us
  Pallas kernels  133 us (35%)
  waiting for transfers between devices  105 us (28%)
  starting transfers between devices  57.4 us (15%)
  between operations  23.9 us (6%)
  other arithmetic  23.2 us (6%)
  local copies, waits for them, and re-layouts  22 us (6%)
  matrix products  9.04 us (2%)
    pallas_call x6, Pallas kernels, call(): pl.pallas_call(kernel, out_shape=[jax.ShapeDtypeStruct(s, d) for s, d, _...  129 us
    ppermute x26, waiting for transfers between devices, partner(): lax.ppermute(value, axis, [(i, i ^ k) for i in range(lax.axis_size(axis))])  92 us
    ppermute x26, starting transfers between devices, partner(): lax.ppermute(value, axis, [(i, i ^ k) for i in range(lax.axis_size(axis))])  45.1 us
    dot_general x3, matrix products, t_dot(): lax.dot_general(a, b, (((0,), (0,)), ((), ())), preferred_element_type=f32)  9.04 us
    unnamed x94, local copies, waits for them, and re-layouts  8.12 us
  transfers between devices with their start and end apart: 32, of which 17 were waited for; matrix products, arithmetic and copies ran while one was open for 9% of the time, Pallas kernels for 23%

profile of v1, /device:TPU:0, one launch (start us, length us, event | category | flops | bytes accessed | tf_op | source)
XLA Modules:
  0.0 372.6 jit_solution(8287801586918552583)
XLA Ops:
  7.3 1.4 fusion.43
  12.9 1.8 shard_map.237
  14.7 5.2 %all-to-all-start = ((bf16[4,32,1152]{2,1,0:T(8,128)(2,1)}), bf16[4,32,1152]{2,1,0:T(8,128)(2,1)S(1)}, u32[]{:S(2)}, u32[]{:S(2)}) async-start(bf16[4,32,1152]{2,1,0:T(8,128)(2,1)} %shard_map.237), calls=%async_computation | async-start | bytes 589824 | tf_op jit(solution)/shard_map/all_to_all | solution.py:622
  20.7 4.7 %all-to-all-done = bf16[4,32,1152]{2,1,0:T(8,128)(2,1)S(1)} async-done(((bf16[4,32,1152]{2,1,0:T(8,128)(2,1)}), bf16[4,32,1152]{2,1,0:T(8,128)(2,1)S(1)}, u32[]{:S(2)}, u32[]{:S(2)}) %all-to-all-start) | async-done | bytes 294944 | tf_op jit(solution)/shard_map/all_to_all | solution.py:622
  27.2 1.4 collective-permute-start.2
  28.6 1.5 collective-permute-start
  30.8 1.6 collective-permute-start.3
  32.4 2.7 collective-permute-start.4
  35.1 3.7 collective-permute-done.3
  38.8 6.6 %collective-permute-start.5 = (bf16[128,640]{1,0:T(8,128)(2,1)S(1)}, bf16[128,640]{1,0:T(8,128)(2,1)S(1)}, u32[]{:S(2)}, u32[]{:S(2)}) collective-permute-start(bf16[128,640]{1,0:T(8,128)(2,1)S(1)} %slice_add_fusion), channel_id=1, source_target_pairs={{0,24},{4,28},{8,16},{12,20},{16,8},{20,12},{24,0},{28,4},{1,25},{... | collective-permute-start | bytes 491528 | tf_op jit(solution)/shard_map/ppermute | solution.py:486
  46.3 7.2 %collective-permute-done.4 = bf16[128,640]{1,0:T(8,128)(2,1)S(1)} collective-permute-done((bf16[128,640]{1,0:T(8,128)(2,1)S(1)}, bf16[128,640]{1,0:T(8,128)(2,1)S(1)}, u32[]{:S(2)}, u32[]{:S(2)}) %collective-permute-start.4) | collective-permute-done | bytes 163872 | tf_op jit(solution)/shard_map/ppermute | solution.py:486
  54.2 1.1 pad_maximum_fusion.4.refs_0_
  56.5 1.9 pad_maximum_fusion.1.x_ref
  59.8 11.1 %shard_map.238 = (bf16[4,256,1024]{2,1,0:T(8,128)(2,1)}, bf16[1024,512]{1,0:T(8,128)(2,1)}, f32[1024,512]{1,0:T(8,128)}, bf16[1024,512]{1,0:T(8,128)(2,1)}, bf16...) custom-call(s32[9]{0:T(128)} %concatenate.68.me_ref, ...), custom_call_target="tpu_custom_call" | custom-call | tf_op jit(solution)/shard_map/pallas_call | solution.py:418
  70.8 1.0 collective-permute-start.7
  72.3 2.1 collective-permute-start.9
  74.5 5.8 %collective-permute-done.7 = bf16[1024,128]{1,0:T(8,128)(2,1)S(1)} collective-permute-done((bf16[1024,128]{1,0:T(8,128)(2,1)}, bf16[1024,128]{1,0:T(8,128)(2,1)S(1)}, u32[]{:S(2)}, u32[]{:S(2)}) %collective-permute-start.7) | collective-permute-done | bytes 262176 | tf_op jit(solution)/shard_map/ppermute | solution.py:486
  80.8 5.3 %collective-permute-done.9 = bf16[1024,128]{1,0:T(8,128)(2,1)S(1)} collective-permute-done((bf16[1024,128]{1,0:T(8,128)(2,1)}, bf16[1024,128]{1,0:T(8,128)(2,1)S(1)}, u32[]{:S(2)}, u32[]{:S(2)}) %collective-permute-start.9) | collective-permute-done | bytes 262176 | tf_op jit(solution)/shard_map/ppermute | solution.py:486
  86.1 1.9 add_select_fusion.proj_ref
  88.1 14.2 %shard_map.239.g_ref = bf16[16384,512]{1,0:T(8,128)(2,1)} custom-call(s32[1]{0:T(128)} %bitcast.1.me_ref.refs_0_, f32[1024,128]{1,0:T(8,128)} %add_select_fusion.proj_ref, bf16[1024,512]{1,0:T(8,128)(2,1)} %get-tuple-element.54.act_ref.refs_8_, f32[128,512]{1,0:T(8,128)} %get-tuple-element.56.vec_ref.refs_10_), custom_call_target="tpu_custom_call" | custom-call | tf_op jit(solution)/shard_map/pallas_call | solution.py:418
  102.2 25.5 %shard_map.240 = (bf16[16384,512]{1,0:T(8,128)(2,1)}, f32[1024,512]{1,0:T(8,128)}, f32[1024,512]{1,0:T(8,128)}, bf16[4,256,512]{2,1,0:T(8,128)(2,1)}, bf16[4,256...) custom-call(s32[1]{0:T(128)} %bitcast.1.me_ref.refs_0_, ...), custom_call_target="tpu_custom_call" | custom-call | tf_op jit(solution)/shard_map/pallas_call | solution.py:418
  127.7 1.5 slice_bitcast_fusion.5
  129.3 0.9 collective-permute-start.10
  130.2 1.4 collective-permute-start.11
  131.6 1.2 collective-permute-start.12
  134.8 9.4 %collective-permute-done.10 = bf16[256,1024]{1,0:T(8,128)(2,1)S(1)} collective-permute-done((bf16[256,1024]{1,0:T(8,128)(2,1)S(1)}, bf16[256,1024]{1,0:T(8,128)(2,1)S(1)}, u32[]{:S(2)}, u32[]{:S(2)}) %collective-permute-start.10) | collective-permute-done | bytes 524320 | tf_op jit(solution)/shard_map/ppermute | solution.py:486
  144.2 10.1 %collective-permute-done.11 = bf16[256,1024]{1,0:T(8,128)(2,1)S(1)} collective-permute-done((bf16[256,1024]{1,0:T(8,128)(2,1)S(1)}, bf16[256,1024]{1,0:T(8,128)(2,1)S(1)}, u32[]{:S(2)}, u32[]{:S(2)}) %collective-permute-start.11) | collective-permute-done | bytes 524320 | tf_op jit(solution)/shard_map/ppermute | solution.py:486
  154.2 2.4 fusion.9
  156.8 1.6 collective-permute-start.13
  159.0 1.3 collective-permute-start.15
  160.4 11.4 %collective-permute-done.13 = bf16[256,1024]{1,0:T(8,128)(2,1)S(1)} collective-permute-done((bf16[256,1024]{1,0:T(8,128)(2,1)S(1)}, bf16[256,1024]{1,0:T(8,128)(2,1)S(1)}, u32[]{:S(2)}, u32[]{:S(2)}) %collective-permute-start.13) | collective-permute-done | bytes 524320 | tf_op jit(solution)/shard_map/ppermute | solution.py:486
  171.7 9.6 %collective-permute-done.15 = bf16[256,1024]{1,0:T(8,128)(2,1)S(1)} collective-permute-done((bf16[256,1024]{1,0:T(8,128)(2,1)S(1)}, bf16[256,1024]{1,0:T(8,128)(2,1)S(1)}, u32[]{:S(2)}, u32[]{:S(2)}) %collective-permute-start.15) | collective-permute-done | bytes 524320 | tf_op jit(solution)/shard_map/ppermute | solution.py:486
  181.4 1.6 pad_maximum_fusion.2.db_ref
  183.0 18.5 %shard_map.241 = (bf16[16384,512]{1,0:T(8,128)(2,1)}, f32[1024,512]{1,0:T(8,128)}, bf16[4,256,512]{2,1,0:T(8,128)(2,1)}, f32[1,512]{1,0:T(1,128)}) custom-call(s32[1]{0:T(128)} %bitcast.1.me_ref.refs_0_, f32[1024,128]{1,0:T(8,128)} %add_select_fusion.proj_ref, bf16[1024,512]{1,0:T(8,128)(2,1)} %get-tuple-element.54.act_ref.refs_8_, ...), custom_call_target="tpu_custom_call" | custom-call | tf_op jit(solution)/shard_map/pallas_call | solution.py:418
  201.5 3.9 %convolution_bitcast_fusion.1 = f32[1024,512]{1,0:T(8,128)} fusion(bf16[4,256,1024]{2,1,0:T(8,128)(2,1)S(1)} %copy-done.1, bf16[4,256,512]{2,1,0:T(8,128)(2,1)} %get-tuple-element.70.refs_9_), kind=kOutput, calls=%fused_computation.5 | convolution fusion | flops 1073741824 | bytes 5242880 | tf_op jit(solution)/shard_map/dot_general | solution.py:31
  206.7 2.5 copy.60
  215.4 47.3 %shard_map.242 = (f32[1024,512]{1,0:T(8,128)}, bf16[1024,128]{1,0:T(8,128)(2,1)}, f32[128,512]{1,0:T(8,128)}) custom-call(s32[1]{0:T(128)} %bitcast.1.me_ref.refs_0_, f32[1024,128]{1,0:T(8,128)} %add_select_fusion.proj_ref, bf16[1024,512]{1,0:T(8,128)(2,1)} %get-tuple-element.54.act_ref.refs_8_, f32[1024,512]{1,0:T(8,128)} %get-tuple-element.62.dm_ref, ...), custom_call_target="tpu_custom_call" | custom-call | tf_op jit(solution)/shard_map/pallas_call | solution.py:418
  262.8 2.2 dynamic_update_slice.3.refs_1_
  265.0 1.8 collective-permute-start.18
  267.4 1.1 collective-permute-start.16
  268.5 6.5 %collective-permute-done.18.refs_4_ = bf16[1024,128]{1,0:T(8,128)(2,1)S(1)} collective-permute-done((bf16[1024,128]{1,0:T(8,128)(2,1)}, bf16[1024,128]{1,0:T(8,128)(2,1)S(1)}, u32[]{:S(2)}, u32[]{:S(2)}) %collective-permute-start.18) | collective-permute-done | bytes 262176 | tf_op jit(solution)/shard_map/ppermute | solution.py:486
  275.1 1.8 collective-permute-done.17.refs_3_
  277.7 12.1 %shard_map.243 = (bf16[4,256,1024]{2,1,0:T(8,128)(2,1)}, bf16[4,256,512]{2,1,0:T(8,128)(2,1)}, f32[256,512]{1,0:T(8,128)}) custom-call(s32[1]{0:T(128)} %bitcast.1.me_ref.refs_0_, bf16[1024,128]{1,0:T(8,128)(2,1)} %dynamic_update_slice.3.refs_1_, bf16[1024,128]{1,0:T(8,128)(2,1)} %copy-done.27, bf16[1024,128]{1,0:T(8,128)(2,1)} %copy-done.26, ...), custom_call_target="tpu_custom_call" | custom-call | tf_op jit(solution)/shard_map/pallas_call | solution.py:418
  289.8 2.5 fusion.45
  292.7 1.4 copy-done.4
  295.3 2.6 convolution_bitcast_fusion
  298.0 1.5 copy-done.8
  300.3 1.1 collective-permute-start.24
  301.4 1.8 collective-permute-start.25
  304.0 1.4 fusion.41
  305.5 8.8 %collective-permute-start.20 = (bf16[176,512]{1,0:T(8,128)(2,1)S(1)}, bf16[176,512]{1,0:T(8,128)(2,1)S(1)}, u32[]{:S(2)}, u32[]{:S(2)}) collective-permute-start(bf16[176,512]{1,0:T(8,128)(2,1)S(1)} %get-tuple-element.144), channel_id=1, source_target_pairs={{0,8},{4,12},{8,0},{12,4},{16,24},{20,28},{24,16},{28,20},{1,9},{5... | collective-permute-start | bytes 540680 | tf_op jit(solution)/shard_map/ppermute | solution.py:486
  314.4 2.4 collective-permute-start.21
  316.8 1.6 collective-permute-start.22
  318.4 7.6 %collective-permute-done.25 = bf16[256,1024]{1,0:T(8,128)(2,1)S(1)} collective-permute-done((bf16[256,1024]{1,0:T(8,128)(2,1)S(1)}, bf16[256,1024]{1,0:T(8,128)(2,1)S(1)}, u32[]{:S(2)}, u32[]{:S(2)}) %collective-permute-start.25) | collective-permute-done | bytes 524320 | tf_op jit(solution)/shard_map/ppermute | solution.py:486
  326.6 1.8 fusion.7
  329.0 12.5 %collective-permute-done.22 = bf16[176,512]{1,0:T(8,128)(2,1)S(1)} collective-permute-done((bf16[176,512]{1,0:T(8,128)(2,1)S(1)}, bf16[176,512]{1,0:T(8,128)(2,1)S(1)}, u32[]{:S(2)}, u32[]{:S(2)}) %collective-permute-start.22) | collective-permute-done | bytes 180256 | tf_op jit(solution)/shard_map/ppermute | solution.py:486
  342.9 3.4 all-to-all-start.1
  347.0 1.7 broadcast_add_fusion
  348.7 3.0 all-to-all-done.1.refs_0_
  351.7 3.4 all-to-all-start.2
  355.6 4.8 %all-to-all-done.2.refs_1_ = f32[4,32,512]{2,1,0:T(8,128)S(1)} async-done(((f32[4,32,512]{2,1,0:T(8,128)}), f32[4,32,512]{2,1,0:T(8,128)S(1)}, u32[]{:S(2)}, u32[]{:S(2)}) %all-to-all-start.2) | async-done | bytes 262176 | tf_op jit(solution)/shard_map/all_to_all | solution.py:821
  361.1 2.1 shard_map.244
  363.3 1.4 copy.65
  364.7 1.3 reduce.5
  (206 shorter events, 22.3 us)
Async XLA Ops:
  7.2 19.1 %copy-start.37 = (s32[1,256]{1,0:T(1,128)S(1)}, s32[1,256]{1,0:T(1,128)}, u32[]{:S(2)}) copy-start(s32[1,256]{1,0:T(1,128)} %param.16) | copy-start | bytes 3076
  7.2 19.1 %copy-start.31 = (bf16[64,64]{1,0:T(8,128)(2,1)S(1)}, bf16[64,64]{1,0:T(8,128)(2,1)}, u32[]{:S(2)}) copy-start(bf16[64,64]{1,0:T(8,128)(2,1)} %param.23) | copy-start | bytes 24580
  7.2 19.2 %copy-start.36 = (bf16[4,64]{1,0:T(4,128)(2,1)S(1)}, bf16[4,64]{1,0:T(4,128)(2,1)}, u32[]{:S(2)}) copy-start(bf16[4,64]{1,0:T(4,128)(2,1)} %param.20) | copy-start | bytes 1540
  7.2 19.3 %copy-start.34 = (bf16[64,16]{0,1:T(8,128)(2,1)S(1)}, bf16[64,16]{0,1:T(8,128)(2,1)}, u32[]{:S(2)}) copy-start(bf16[64,16]{0,1:T(8,128)(2,1)} %param.25) | copy-start | bytes 6148
  7.2 19.4 %copy-start.38 = (bf16[64]{0:T(256)(128)(2,1)S(1)}, bf16[64]{0:T(256)(128)(2,1)}, u32[]{:S(2)}) copy-start(bf16[64]{0:T(256)(128)(2,1)} %param.21) | copy-start | bytes 388
  7.2 19.5 %copy-start.39 = (bf16[64]{0:T(256)(128)(2,1)S(1)}, bf16[64]{0:T(256)(128)(2,1)}, u32[]{:S(2)}) copy-start(bf16[64]{0:T(256)(128)(2,1)} %param.24) | copy-start | bytes 388
  7.2 19.6 %copy-start.40 = (bf16[64]{0:T(256)(128)(2,1)S(1)}, bf16[64]{0:T(256)(128)(2,1)}, u32[]{:S(2)}) copy-start(bf16[64]{0:T(256)(128)(2,1)} %param.26) | copy-start | bytes 388
  7.3 19.9 %copy-start.32 = (bf16[64,96]{1,0:T(8,128)(2,1)S(1)}, bf16[64,96]{1,0:T(8,128)(2,1)}, u32[]{:S(2)}) copy-start(bf16[64,96]{1,0:T(8,128)(2,1)} %param.22) | copy-start | bytes 36868
  7.3 19.9 %copy-start.2 = (bf16[1,256,1024]{2,1,0:T(8,128)(2,1)S(1)}, bf16[1,256,1024]{2,1,0:T(8,128)(2,1)}, u32[]{:S(2)}) copy-start(bf16[1,256,1024]{2,1,0:T(8,128)(2,1)} %param.14) | copy-start | bytes 1572868
  14.7 10.8 %all-to-all-start = ((bf16[4,32,1152]{2,1,0:T(8,128)(2,1)}), bf16[4,32,1152]{2,1,0:T(8,128)(2,1)S(1)}, u32[]{:S(2)}, u32[]{:S(2)}) async-start(bf16[4,32,1152]{2,1,0:T(8,128)(2,1)} %shard_map.237), calls=%async_computation | async-start | bytes 589824 | tf_op jit(solution)/shard_map/all_to_all | solution.py:622
  19.9 82.4 %all-gather.3.cloned.1.call-start = ((), (), s32[]{:S(2)}) async-start(), calls=%async_computation.7 | async-start | bytes 2359296 | tf_op jit(solution)/shard_map/all_gather | solution.py:641
  26.2 320.8 %reduce-scatter.3.cloned.1.call-start = ((), (), s32[]{:S(2)}) async-start(), calls=%async_computation.5 | async-start | bytes 2359296 | tf_op jit(solution)/shard_map/reduce_scatter | solution.py:750
  27.2 28.3 %copy-start.10 = (bf16[272,1024]{1,0:T(8,128)(2,1)}, bf16[272,1024]{1,0:T(8,128)(2,1)S(1)}, u32[]{:S(2)}) copy-start(bf16[272,1024]{1,0:T(8,128)(2,1)S(1)} %fusion.17) | copy-start | bytes 1671172
  27.2 28.2 %collective-permute-start.2 = (bf16[272,1024]{1,0:T(8,128)(2,1)S(1)}, bf16[272,1024]{1,0:T(8,128)(2,1)S(1)}, u32[]{:S(2)}, u32[]{:S(2)}) collective-permute-start(bf16[272,1024]{1,0:T(8,128)(2,1)S(1)} %fusion.17), channel_id=1, source_target_pairs={{0,3},{1,2},{2,1},{3,0},{4,7},{5,6},{6,5},{7,4},{8,11},{9,10},{10,... | collective-permute-start | bytes 1671176 | tf_op jit(solution)/shard_map/ppermute | solution.py:486
  28.6 26.8 %collective-permute-start = (bf16[272,1024]{1,0:T(8,128)(2,1)S(1)}, bf16[272,1024]{1,0:T(8,128)(2,1)S(1)}, u32[]{:S(2)}, u32[]{:S(2)}) collective-permute-start(bf16[272,1024]{1,0:T(8,128)(2,1)S(1)} %fusion.17), channel_id=1, source_target_pairs={{0,1},{1,0},{2,3},{3,2},{4,5},{5,4},{6,7},{7,6},{8,9},{9,8},{10,11... | collective-permute-start | bytes 1671176 | tf_op jit(solution)/shard_map/ppermute | solution.py:486
  30.1 25.4 %collective-permute-start.1 = (bf16[272,1024]{1,0:T(8,128)(2,1)S(1)}, bf16[272,1024]{1,0:T(8,128)(2,1)}, u32[]{:S(2)}, u32[]{:S(2)}) collective-permute-start(bf16[272,1024]{1,0:T(8,128)(2,1)S(1)} %fusion.17), channel_id=1, source_target_pairs={{0,2},{1,3},{2,0},{3,1},{4,6},{5,7},{6,4},{7,5},{8,10},{9,11},{10,... | collective-permute-start | bytes 1671176 | tf_op jit(solution)/shard_map/ppermute | solution.py:486
  30.8 8.0 %collective-permute-start.3 = (bf16[128,640]{1,0:T(8,128)(2,1)S(1)}, bf16[128,640]{1,0:T(8,128)(2,1)S(1)}, u32[]{:S(2)}, u32[]{:S(2)}) collective-permute-start(bf16[128,640]{1,0:T(8,128)(2,1)S(1)} %slice_add_fusion), channel_id=1, source_target_pairs={{0,8},{4,12},{8,0},{12,4},{16,24},{20,28},{24,16},{28,20},{1,9},{5... | collective-permute-start | bytes 491528 | tf_op jit(solution)/shard_map/ppermute | solution.py:486
  32.4 21.0 %collective-permute-start.4 = (bf16[128,640]{1,0:T(8,128)(2,1)S(1)}, bf16[128,640]{1,0:T(8,128)(2,1)S(1)}, u32[]{:S(2)}, u32[]{:S(2)}) collective-permute-start(bf16[128,640]{1,0:T(8,128)(2,1)S(1)} %slice_add_fusion), channel_id=1, source_target_pairs={{0,16},{4,20},{8,24},{12,28},{16,0},{20,4},{24,8},{28,12},{1,17},{... | collective-permute-start | bytes 491528 | tf_op jit(solution)/shard_map/ppermute | solution.py:486
  38.8 14.7 %collective-permute-start.5 = (bf16[128,640]{1,0:T(8,128)(2,1)S(1)}, bf16[128,640]{1,0:T(8,128)(2,1)S(1)}, u32[]{:S(2)}, u32[]{:S(2)}) collective-permute-start(bf16[128,640]{1,0:T(8,128)(2,1)S(1)} %slice_add_fusion), channel_id=1, source_target_pairs={{0,24},{4,28},{8,16},{12,20},{16,8},{20,12},{24,0},{28,4},{1,25},{... | collective-permute-start | bytes 491528 | tf_op jit(solution)/shard_map/ppermute | solution.py:486
  55.3 3.1 copy-start.9
  55.3 4.4 %collective-permute-start.6 = (bf16[4,128,640]{2,1,0:T(8,128)(2,1)S(1)}, bf16[4,128,640]{2,1,0:T(8,128)(2,1)}, u32[]{:S(2)}, u32[]{:S(2)}) collective-permute-start(bf16[4,128,640]{2,1,0:T(8,128)(2,1)S(1)} %pad_maximum_fusion.4.refs_0_), channel_id=1, source_target_pairs={{0,4},{4,0},{8,12},{12,8},{16,20},{20,16},{24,28},{28,24},{1,5},{5... | collective-permute-start | bytes 1966088 | tf_op jit(solution)/shard_map/ppermute | solution.py:486
  70.8 9.4 %collective-permute-start.7 = (bf16[1024,128]{1,0:T(8,128)(2,1)}, bf16[1024,128]{1,0:T(8,128)(2,1)S(1)}, u32[]{:S(2)}, u32[]{:S(2)}) collective-permute-start(bf16[1024,128]{1,0:T(8,128)(2,1)} %get-tuple-element.53), channel_id=1, source_target_pairs={{0,1},{1,0},{2,3},{3,2},{4,5},{5,4},{6,7},{7,6},{8,9},{9,8},{10,11... | collective-permute-start | bytes 786440 | tf_op jit(solution)/shard_map/ppermute | solution.py:486
  71.8 8.9 %collective-permute-start.8 = (bf16[1024,128]{1,0:T(8,128)(2,1)}, bf16[1024,128]{1,0:T(8,128)(2,1)S(1)}, u32[]{:S(2)}, u32[]{:S(2)}) collective-permute-start(bf16[1024,128]{1,0:T(8,128)(2,1)} %get-tuple-element.53), channel_id=1, source_target_pairs={{0,2},{1,3},{2,0},{3,1},{4,6},{5,7},{6,4},{7,5},{8,10},{9,11},{10,... | collective-permute-start | bytes 786440 | tf_op jit(solution)/shard_map/ppermute | solution.py:486
  72.3 13.8 %collective-permute-start.9 = (bf16[1024,128]{1,0:T(8,128)(2,1)}, bf16[1024,128]{1,0:T(8,128)(2,1)S(1)}, u32[]{:S(2)}, u32[]{:S(2)}) collective-permute-start(bf16[1024,128]{1,0:T(8,128)(2,1)} %get-tuple-element.53), channel_id=1, source_target_pairs={{0,3},{1,2},{2,1},{3,0},{4,7},{5,6},{6,5},{7,4},{8,11},{9,10},{10,... | collective-permute-start | bytes 786440 | tf_op jit(solution)/shard_map/ppermute | solution.py:486
  127.7 5.1 %copy-start.35 = (f32[1,128]{1,0:T(1,128)S(1)}, f32[1,128]{1,0:T(1,128)}, u32[]{:S(2)}) copy-start(f32[1,128]{1,0:T(1,128)} %get-tuple-element.60) | copy-start | bytes 1540
  127.7 26.5 %copy-start.6 = (bf16[1,256,1024]{2,1,0:T(8,128)(2,1)S(1)}, bf16[1,256,1024]{2,1,0:T(8,128)(2,1)}, u32[]{:S(2)}) copy-start(bf16[1,256,1024]{2,1,0:T(8,128)(2,1)} %param.15) | copy-start | bytes 1572868
  129.3 14.9 %collective-permute-start.10 = (bf16[256,1024]{1,0:T(8,128)(2,1)S(1)}, bf16[256,1024]{1,0:T(8,128)(2,1)S(1)}, u32[]{:S(2)}, u32[]{:S(2)}) collective-permute-start(bf16[256,1024]{1,0:T(8,128)(2,1)S(1)} %get-tuple-element.139), channel_id=1, source_target_pairs={{0,1},{1,0},{2,3},{3,2},{4,5},{5,4},{6,7},{7,6},{8,9},{9,8},{10,11... | collective-permute-start | bytes 1572872 | tf_op jit(solution)/shard_map/ppermute | solution.py:486
  130.2 24.0 %collective-permute-start.11 = (bf16[256,1024]{1,0:T(8,128)(2,1)S(1)}, bf16[256,1024]{1,0:T(8,128)(2,1)S(1)}, u32[]{:S(2)}, u32[]{:S(2)}) collective-permute-start(bf16[256,1024]{1,0:T(8,128)(2,1)S(1)} %get-tuple-element.141), channel_id=1, source_target_pairs={{0,2},{1,3},{2,0},{3,1},{4,6},{5,7},{6,4},{7,5},{8,10},{9,11},{10,... | collective-permute-start | bytes 1572872 | tf_op jit(solution)/shard_map/ppermute | solution.py:486
  131.6 22.6 %collective-permute-start.12 = (bf16[256,1024]{1,0:T(8,128)(2,1)S(1)}, bf16[256,1024]{1,0:T(8,128)(2,1)S(1)}, u32[]{:S(2)}, u32[]{:S(2)}) collective-permute-start(bf16[256,1024]{1,0:T(8,128)(2,1)S(1)} %get-tuple-element.140), channel_id=1, source_target_pairs={{0,3},{1,2},{2,1},{3,0},{4,7},{5,6},{6,5},{7,4},{8,11},{9,10},{10,... | collective-permute-start | bytes 1572872 | tf_op jit(solution)/shard_map/ppermute | solution.py:486
  156.8 26.2 %copy-start.12 = (bf16[256,1024]{1,0:T(8,128)(2,1)}, bf16[256,1024]{1,0:T(8,128)(2,1)S(1)}, u32[]{:S(2)}) copy-start(bf16[256,1024]{1,0:T(8,128)(2,1)S(1)} %multiply_convert_fusion) | copy-start | bytes 1572868
  156.8 14.9 %collective-permute-start.13 = (bf16[256,1024]{1,0:T(8,128)(2,1)S(1)}, bf16[256,1024]{1,0:T(8,128)(2,1)S(1)}, u32[]{:S(2)}, u32[]{:S(2)}) collective-permute-start(bf16[256,1024]{1,0:T(8,128)(2,1)S(1)} %multiply_convert_fusion), channel_id=1, source_target_pairs={{0,1},{1,0},{2,3},{3,2},{4,5},{5,4},{6,7},{7,6},{8,9},{9,8},{10,11... | collective-permute-start | bytes 1572872 | tf_op jit(solution)/shard_map/ppermute | solution.py:486
  158.4 13.3 %collective-permute-start.14 = (bf16[256,1024]{1,0:T(8,128)(2,1)S(1)}, bf16[256,1024]{1,0:T(8,128)(2,1)S(1)}, u32[]{:S(2)}, u32[]{:S(2)}) collective-permute-start(bf16[256,1024]{1,0:T(8,128)(2,1)S(1)} %multiply_convert_fusion), channel_id=1, source_target_pairs={{0,2},{1,3},{2,0},{3,1},{4,6},{5,7},{6,4},{7,5},{8,10},{9,11},{10,... | collective-permute-start | bytes 1572872 | tf_op jit(solution)/shard_map/ppermute | solution.py:486
  159.0 22.3 %collective-permute-start.15 = (bf16[256,1024]{1,0:T(8,128)(2,1)S(1)}, bf16[256,1024]{1,0:T(8,128)(2,1)S(1)}, u32[]{:S(2)}, u32[]{:S(2)}) collective-permute-start(bf16[256,1024]{1,0:T(8,128)(2,1)S(1)} %multiply_convert_fusion), channel_id=1, source_target_pairs={{0,3},{1,2},{2,1},{3,0},{4,7},{5,6},{6,5},{7,4},{8,11},{9,10},{10,... | collective-permute-start | bytes 1572872 | tf_op jit(solution)/shard_map/ppermute | solution.py:486
  171.7 11.3 %copy-start.19 = (bf16[256,1024]{1,0:T(8,128)(2,1)}, bf16[256,1024]{1,0:T(8,128)(2,1)S(1)}, u32[]{:S(2)}) copy-start(bf16[256,1024]{1,0:T(8,128)(2,1)S(1)} %collective-permute-done.13) | copy-start | bytes 1572868
  171.7 11.3 %copy-start.21 = (bf16[256,1024]{1,0:T(8,128)(2,1)}, bf16[256,1024]{1,0:T(8,128)(2,1)S(1)}, u32[]{:S(2)}) copy-start(bf16[256,1024]{1,0:T(8,128)(2,1)S(1)} %collective-permute-done.14) | copy-start | bytes 1572868
  181.4 1.6 copy-start.23
  183.0 18.5 %copy-start.1 = (bf16[4,256,1024]{2,1,0:T(8,128)(2,1)S(1)}, bf16[4,256,1024]{2,1,0:T(8,128)(2,1)}, u32[]{:S(2)}) copy-start(bf16[4,256,1024]{2,1,0:T(8,128)(2,1)} %get-tuple-element.55.normed_ref) | copy-start | bytes 6291460
  205.4 160.6 %reduce-scatter.5.cloned.1.call-start = ((), (), s32[]{:S(2)}) async-start(), calls=%async_computation.6 | async-start | bytes 2359296 | tf_op jit(solution)/shard_map/reduce_scatter | solution.py:751
  265.0 10.0 %collective-permute-start.18 = (bf16[1024,128]{1,0:T(8,128)(2,1)}, bf16[1024,128]{1,0:T(8,128)(2,1)S(1)}, u32[]{:S(2)}, u32[]{:S(2)}) collective-permute-start(bf16[1024,128]{1,0:T(8,128)(2,1)} %dynamic_update_slice.3.refs_1_), channel_id=1, source_target_pairs={{0,3},{1,2},{2,1},{3,0},{4,7},{5,6},{6,5},{7,4},{8,11},{9,10},{10,... | collective-permute-start | bytes 786440 | tf_op jit(solution)/shard_map/ppermute | solution.py:486
  266.8 10.1 %collective-permute-start.17 = (bf16[1024,128]{1,0:T(8,128)(2,1)}, bf16[1024,128]{1,0:T(8,128)(2,1)S(1)}, u32[]{:S(2)}, u32[]{:S(2)}) collective-permute-start(bf16[1024,128]{1,0:T(8,128)(2,1)} %dynamic_update_slice.3.refs_1_), channel_id=1, source_target_pairs={{0,2},{1,3},{2,0},{3,1},{4,6},{5,7},{6,4},{7,5},{8,10},{9,11},{10,... | collective-permute-start | bytes 786440 | tf_op jit(solution)/shard_map/ppermute | solution.py:486
  267.4 9.6 %collective-permute-start.16 = (bf16[1024,128]{1,0:T(8,128)(2,1)}, bf16[1024,128]{1,0:T(8,128)(2,1)S(1)}, u32[]{:S(2)}, u32[]{:S(2)}) collective-permute-start(bf16[1024,128]{1,0:T(8,128)(2,1)} %dynamic_update_slice.3.refs_1_), channel_id=1, source_target_pairs={{0,1},{1,0},{2,3},{3,2},{4,5},{5,4},{6,7},{7,6},{8,9},{9,8},{10,11... | collective-permute-start | bytes 786440 | tf_op jit(solution)/shard_map/ppermute | solution.py:486
  275.0 2.7 copy-start.25
  277.7 12.1 %copy-start.11 = (bf16[1024,1024]{1,0:T(8,128)(2,1)S(1)}, bf16[1024,1024]{1,0:T(8,128)(2,1)}, u32[]{:S(2)}) copy-start(bf16[1024,1024]{1,0:T(8,128)(2,1)} %copy.60) | copy-start | bytes 6291460
  289.8 2.5 copy-start.18
  292.4 2.9 copy-start.42
  292.6 2.6 copy-start.13
  292.6 2.6 copy-start.20
  292.7 2.6 copy-start.22
  292.7 2.6 copy-start.24
  295.2 8.0 %collective-permute-start.19 = (bf16[4,176,512]{2,1,0:T(8,128)(2,1)}, bf16[4,176,512]{2,1,0:T(8,128)(2,1)}, u32[]{:S(2)}, u32[]{:S(2)}) collective-permute-start(bf16[4,176,512]{2,1,0:T(8,128)(2,1)} %pad_maximum_fusion.3), channel_id=1, source_target_pairs={{0,4},{4,0},{8,12},{12,8},{16,20},{20,16},{24,28},{28,24},{1,5},{5... | collective-permute-start | bytes 2162696 | tf_op jit(solution)/shard_map/ppermute | solution.py:486
  297.9 1.6 copy-start.8
  299.5 4.5 %copy-start.5 = (f32[8,160,512]{2,1,0:T(8,128)S(1)}, f32[8,160,512]{2,1,0:T(8,128)}, u32[]{:S(2)}) copy-start(f32[8,160,512]{2,1,0:T(8,128)} %copy-done.4) | copy-start | bytes 7864324
  299.6 17.1 %collective-permute-start.23 = (bf16[256,1024]{1,0:T(8,128)(2,1)S(1)}, bf16[256,1024]{1,0:T(8,128)(2,1)S(1)}, u32[]{:S(2)}, u32[]{:S(2)}) collective-permute-start(bf16[256,1024]{1,0:T(8,128)(2,1)S(1)} %get-tuple-element.136), channel_id=1, source_target_pairs={{0,1},{1,0},{2,3},{3,2},{4,5},{5,4},{6,7},{7,6},{8,9},{9,8},{10,11... | collective-permute-start | bytes 1572872 | tf_op jit(solution)/shard_map/ppermute | solution.py:486
  300.3 18.1 %collective-permute-start.24 = (bf16[256,1024]{1,0:T(8,128)(2,1)S(1)}, bf16[256,1024]{1,0:T(8,128)(2,1)S(1)}, u32[]{:S(2)}, u32[]{:S(2)}) collective-permute-start(bf16[256,1024]{1,0:T(8,128)(2,1)S(1)} %get-tuple-element.138), channel_id=1, source_target_pairs={{0,2},{1,3},{2,0},{3,1},{4,6},{5,7},{6,4},{7,5},{8,10},{9,11},{10,... | collective-permute-start | bytes 1572872 | tf_op jit(solution)/shard_map/ppermute | solution.py:486
  301.4 24.7 %collective-permute-start.25 = (bf16[256,1024]{1,0:T(8,128)(2,1)S(1)}, bf16[256,1024]{1,0:T(8,128)(2,1)S(1)}, u32[]{:S(2)}, u32[]{:S(2)}) collective-permute-start(bf16[256,1024]{1,0:T(8,128)(2,1)S(1)} %get-tuple-element.137), channel_id=1, source_target_pairs={{0,3},{1,2},{2,1},{3,0},{4,7},{5,6},{6,5},{7,4},{8,11},{9,10},{10,... | collective-permute-start | bytes 1572872 | tf_op jit(solution)/shard_map/ppermute | solution.py:486
  304.0 22.0 %copy-start.3 = (bf16[1,256,1024]{2,1,0:T(8,128)(2,1)S(1)}, bf16[1,256,1024]{2,1,0:T(8,128)(2,1)}, u32[]{:S(2)}) copy-start(bf16[1,256,1024]{2,1,0:T(8,128)(2,1)} %param.14) | copy-start | bytes 1572868
  304.0 22.0 %copy-start.33 = (f32[1,1024]{1,0:T(1,128)S(1)}, f32[1,1024]{1,0:T(1,128)}, u32[]{:S(2)}) copy-start(f32[1,1024]{1,0:T(1,128)} %get-tuple-element.80) | copy-start | bytes 12292
  305.5 21.1 %copy-start.7 = (bf16[1,256,1024]{2,1,0:T(8,128)(2,1)S(1)}, bf16[1,256,1024]{2,1,0:T(8,128)(2,1)}, u32[]{:S(2)}) copy-start(bf16[1,256,1024]{2,1,0:T(8,128)(2,1)} %param.15) | copy-start | bytes 1572868
  305.5 23.4 %collective-permute-start.20 = (bf16[176,512]{1,0:T(8,128)(2,1)S(1)}, bf16[176,512]{1,0:T(8,128)(2,1)S(1)}, u32[]{:S(2)}, u32[]{:S(2)}) collective-permute-start(bf16[176,512]{1,0:T(8,128)(2,1)S(1)} %get-tuple-element.144), channel_id=1, source_target_pairs={{0,8},{4,12},{8,0},{12,4},{16,24},{20,28},{24,16},{28,20},{1,9},{5... | collective-permute-start | bytes 540680 | tf_op jit(solution)/shard_map/ppermute | solution.py:486
  314.4 14.6 %collective-permute-start.21 = (bf16[176,512]{1,0:T(8,128)(2,1)S(1)}, bf16[176,512]{1,0:T(8,128)(2,1)S(1)}, u32[]{:S(2)}, u32[]{:S(2)}) collective-permute-start(bf16[176,512]{1,0:T(8,128)(2,1)S(1)} %get-tuple-element.145), channel_id=1, source_target_pairs={{0,16},{4,20},{8,24},{12,28},{16,0},{20,4},{24,8},{28,12},{1,17},{... | collective-permute-start | bytes 540680 | tf_op jit(solution)/shard_map/ppermute | solution.py:486
  316.8 24.7 %collective-permute-start.22 = (bf16[176,512]{1,0:T(8,128)(2,1)S(1)}, bf16[176,512]{1,0:T(8,128)(2,1)S(1)}, u32[]{:S(2)}, u32[]{:S(2)}) collective-permute-start(bf16[176,512]{1,0:T(8,128)(2,1)S(1)} %get-tuple-element.146), channel_id=1, source_target_pairs={{0,24},{4,28},{8,16},{12,20},{16,8},{20,12},{24,0},{28,4},{1,25},{... | collective-permute-start | bytes 540680 | tf_op jit(solution)/shard_map/ppermute | solution.py:486
  342.9 8.8 %all-to-all-start.1 = ((f32[4,32,512]{2,1,0:T(8,128)}), f32[4,32,512]{2,1,0:T(8,128)S(1)}, u32[]{:S(2)}, u32[]{:S(2)}) async-start(f32[4,32,512]{2,1,0:T(8,128)} %bitcast.71), calls=%async_computation.1 | async-start | bytes 524288 | tf_op jit(solution)/shard_map/all_to_all | solution.py:823
  351.7 8.8 %copy-start.14 = (f32[4,32,512]{2,1,0:T(8,128)}, f32[4,32,512]{2,1,0:T(8,128)S(1)}, u32[]{:S(2)}) copy-start(f32[4,32,512]{2,1,0:T(8,128)S(1)} %all-to-all-done.1.refs_0_) | copy-start | bytes 786436
  351.7 8.8 %all-to-all-start.2 = ((f32[4,32,512]{2,1,0:T(8,128)}), f32[4,32,512]{2,1,0:T(8,128)S(1)}, u32[]{:S(2)}, u32[]{:S(2)}) async-start(f32[4,32,512]{2,1,0:T(8,128)} %bitcast.73), calls=%async_computation.3 | async-start | bytes 524288 | tf_op jit(solution)/shard_map/all_to_all | solution.py:821
  (11 other events, 10.4 us)
Sparse Core Ops, SparseCore 0:
  26.4 39.5 all-gather.2
  205.5 43.9 reduce-scatter.2
  298.1 52.1 reduce-scatter.4

commit v2 on v1

--- a/solution.py
+++ b/solution.py
@@ -76,14 +76,12 @@
     return x * lax.rsqrt(jnp.mean(x * x, axis=-1, keepdims=True) + 1e-05)
 
 
-def start_kernel(
-    me_ref, x_ref, *refs,
-):
-    parts = refs[:-13]
+def start_kernel(me_ref, x_ref, *refs):
+    parts = refs[:-14]
     (
-        normed_ref, stream_ref, pre_ref, act_ref, proj_ref, w_ref, vec_ref, xproj_ref, gain_ref, marks_ref,
+        normed_ref, turned_ref, stream_ref, pre_ref, act_ref, proj_ref, w_ref, vec_ref, xproj_ref, gain_ref, marks_ref,
         wide_ref, ext_ref, cols_ref,
-    ) = refs[-13:]
+    ) = refs[-14:]
     rows, chans = stream_ref.shape
     taps = CONVB - CONV
 
@@ -115,6 +113,7 @@
 
     normed = (unit_of(x_ref[...].astype(f32)) * gain_ref[...]).astype(bf16)
     normed_ref[...] = normed
+    turned_ref[...] = normed.T
     stream = dot(normed, w_ref[...]).astype(bf16)
     stream_ref[...] = stream
     wide_ref[8:, :] = stream.astype(f32)
@@ -159,10 +158,12 @@
 
 
 def ahead_kernel(
-    me_ref, proj_ref, act_ref, normed_ref, g_ref, vec_ref, second_ref,
-    hp_ref, mixed_ref, gate_ref, gated_ref, branch_ref, wgate_ref, outw_ref,
-    carry_ref, u_ref, step_ref, col_ref, diag_ref, s_ref, y_ref,
+    local, me_ref, proj_ref, act_ref, normed_ref, g_ref, vec_ref, second_ref,
+    hp_ref, mixed_ref, gate_ref, gated_ref, wgate_ref, outw_ref,
+    *refs,
 ):
+    branch_refs = refs[:-7]
+    carry_ref, u_ref, step_ref, col_ref, diag_ref, s_ref, y_ref = refs[-7:]
     rows, c = act_ref.shape
     n = carry_ref.shape[0]
 
@@ -215,15 +216,15 @@
     gate = dot(normed_ref[...], wgate_ref[...])
     gate_ref[...] = gate
     gated = (mixed * (gate * sigmoid(gate))).astype(bf16)
-    gated_ref[...] = gated
-    branch_ref[...] = dot(gated, outw_ref[...]).astype(bf16)
+    gated_ref[...] = gated.T
+    write_slot(branch_refs, slot_of(me_ref, local), dot(gated, outw_ref[...]).astype(bf16))
 
 
 def piece_grad_kernel(
-    me_ref, proj_ref, act_ref, mixed_ref, gate_ref, db_ref, vec_ref, outw_ref,
-    q_ref, dm_ref, dg_ref, sgrad_ref,
-    carry_ref, stepm_ref, col_ref,
+    local, me_ref, proj_ref, act_ref, mixed_ref, gate_ref, vec_ref, outw_ref, *refs,
 ):
+    db_refs = refs[:-7]
+    q_ref, dm_ref, dg_ref, sgrad_ref, carry_ref, stepm_ref, col_ref = refs[-7:]
     rows, c = act_ref.shape
     n = carry_ref.shape[0]
 
@@ -236,8 +237,7 @@
     _, pre = dt_of(proj, vec_ref, INTO)
     stepm_ref[...] = jnp.where(proj[:, CARRY : CARRY + 1] > 0.5, softplus(pre), NEVER)
     columns(proj.T, OUT, n, col_ref)
-    db = db_ref[...]
-    dgated = dot_t(db, outw_ref[...])
+    dgated = dot_t(read_slot(db_refs, slot_of(me_ref, local)), outw_ref[...])
     gate = gate_ref[...]
     s = sigmoid(gate)
     dm = dgated * (gate * s)
@@ -260,7 +260,7 @@
 
 
 def state_grad_kernel(
-    me_ref, proj_ref, act_ref, dm_ref, g_ref, hp_ref, q_ref, vec_ref, sgrad_ref,
+    me_ref, proj_ref, act_ref, dm_ref, g_ref, hp_ref, q_ref, vec_ref, sgrad_ref, pieces_ref,
     dact_ref, dproj_ref, table_ref,
     carry_ref, u_ref, step_ref, col_ref, diag_ref, ig_ref, rr_ref, rs_ref, pair_ref, own_ref, x_ref, y_ref, dp_ref,
 ):
@@ -346,16 +346,18 @@
 
     @pl.when(pl.program_id(0) == pl.num_programs(0) - 1)
     def _():
+        dproj_ref[:BLOCK, CARRY:] = pieces_ref[:, CARRY:]
         table_ref[ALOG : ALOG + n, :] *= -jnp.exp(vec_ref[ALOG : ALOG + n, :])
 
 
-def end_kernel(own, me_ref, *refs):
-    parts = refs[:-17]
+def end_kernel(own, local, count, me_ref, *refs):
+    dn_refs, refs = refs[-count - 8 : -8], refs[: -count - 8] + refs[-8:]
+    parts = refs[:-18]
     (
         dact_ref, pre_ref, stream_ref, act_ref, dg_ref, vec_ref, xproj_ref, ws_ref, wg_ref, table_ref,
-        dn_ref, ds_ref, small_ref,
+        ds_ref, small_ref, pieces_ref, sum_ref,
         wide_ref, xgrad_ref, cgrad_ref, turned_ref,
-    ) = refs[-17:]
+    ) = refs[-18:]
     rows, c = act_ref.shape
     taps = CONVB - CONV
 
@@ -385,7 +387,8 @@
         dstream = dstream + vec_ref[CONV + tap : CONV + tap + 1, :] * moved
     wide_ref[rows:, :] = dconv[:8, :]
     dstream_low = dstream.astype(bf16)
-    dn_ref[...] = (dot_t(dstream_low, ws_ref[...]) + dot_t(dg_ref[...], wg_ref[...])).astype(bf16)
+    dn = (dot_t(dstream_low, ws_ref[...]) + dot_t(dg_ref[...], wg_ref[...])).astype(bf16)
+    write_slot(dn_refs, slot_of(me_ref, local, True), dn)
     ds_ref[...] = dstream_low
 
     @pl.when(pl.program_id(0) == pl.num_programs(0) - 1)
@@ -393,6 +396,17 @@
         for k in range(c // LANES):
             at = slice(k * LANES, (k + 1) * LANES)
             turned_ref[at, :] = cgrad_ref[:, at].T
+        sums = tree([row_sum(part[:BLOCK, :]) for part in parts])
+        sums = jnp.where(lax.broadcasted_iota(jnp.int32, sums.shape, 1) < CARRY, 0.0, sums)
+        sum_ref[...] = sums
+        pieces = [jnp.zeros((BLOCK, LANES), f32)]
+        row = lax.broadcasted_iota(jnp.int32, (BLOCK, LANES), 0)
+        for k in range(3):
+            term = sums.astype(bf16).astype(f32)
+            pieces = [jnp.where(row == k, term, pieces[0])]
+            sums = sums - term
+        for k in range(c // LANES):
+            pieces_ref[:, k * LANES : (k + 1) * LANES] = pieces[0].astype(bf16)
         lines = 2 * own * LANES // c
         for b in range(c // own):
             at = slice(b * own, (b + 1) * own)
@@ -401,14 +415,58 @@
                 small_ref[b * lines : (b + 1) * lines, k * LANES : (k + 1) * LANES] = both[k * lines : (k + 1) * lines]
 
 
+def slot_of(me_ref, local, reverse=False):
+    step = pl.program_id(0)
+    if reverse:
+        step = pl.num_programs(0) - 1 - step
+    return (step // (local // ROWS)) ^ me_ref[0]
+
+
+def read_slot(refs, slot):
+    value = refs[0][...]
+    for k in range(1, len(refs)):
+        value = jnp.where(slot == k, refs[k][...], value)
+    return value
+
+
+def write_slot(refs, slot, value):
+    if len(refs) == 1:
+        refs[0][...] = value
+        return
+    for k, ref in enumerate(refs):
+
+        @pl.when(slot == k)
+        def _(ref=ref):
+            ref[...] = value
+
+
 def call(kernel, me, ins, outs, scratch, total, local, reverse=False):
     steps = total // ROWS
     per = local // ROWS
     turn = (lambda i: steps - 1 - i) if reverse else (lambda i: i)
 
+    def slot_map(k):
+        def index(i, me_ref):
+            group = k ^ me_ref[0]
+            if reverse:
+                group = steps // per - 1 - group
+            first, last = (per - 1, 0) if reverse else (0, per - 1)
+            now = i // per
+            return (jnp.where(now < group, first, jnp.where(now > group, last, turn(i) % per)), 0)
+
+        return index
+
     def spec(shape, kind):
+        if isinstance(kind, int):
+            return pl.BlockSpec((ROWS, shape[1]), slot_map(kind))
         if kind == "f":
             return pl.BlockSpec(shape, lambda i, me_ref: (0,) * len(shape))
+        if kind == "c":
+            return pl.BlockSpec(
+                (shape[0], ROWS), lambda i, me_ref: (0, ((turn(i) // per) ^ me_ref[0]) * per + turn(i) % per)
+            )
+        if kind == "y":
+            return pl.BlockSpec((None, ROWS, shape[2]), lambda i, me_ref: (turn(i) // per, turn(i) % per, 0))
         if kind == "x":
             return pl.BlockSpec(
                 (None, ROWS, shape[2]), lambda i, me_ref: ((turn(i) // per) ^ me_ref[0], turn(i) % per, 0)
@@ -429,8 +487,112 @@
     )(me, *[a for a, _ in ins])
 
 
-def split_kernel(seqs, batches, own, w_ref, extra_ref, out_ref):
-    half, chans = w_ref.shape[1] // 2, batches * own
+def slots_in(parts):
+    if len(parts) == 1:
+        return [(parts[0], "x")]
+    return [(part, k) for k, part in enumerate(parts)]
+
+
+def slots_out(seqs, rows, width):
+    if seqs > 4:
+        return [((seqs, rows, width), bf16, "x")]
+    return [((rows, width), bf16, k) for k in range(seqs)]
+
+
+def early_grad_kernel(normed_ref, gated_ref, dg_ref, *refs):
+    parts, out_ref = refs[:-1], refs[-1]
+    group, _, c = out_ref.shape
+    lines, own = normed_ref.shape[0] // group, gated_ref.shape[0] // group
+    gate = dot(normed_ref[...], dg_ref[...])
+    out, first = 0.0, 0
+    for part in parts:
+        last = first + part.shape[0]
+        out = out + dot(gated_ref[:, first:last], part[...])
+        first = last
+    for b in range(group):
+        out_ref[b, :lines, :] = gate[b * lines : (b + 1) * lines]
+        for k in range(out.shape[1] // c):
+            out_ref[b, lines + k * own : lines + (k + 1) * own, :] = out[
+                b * own : (b + 1) * own, k * c : (k + 1) * c
+            ]
+
+
+def late_grad_kernel(normed_ref, small_ref, ds_ref, out_ref):
+    group, rows, c = out_ref.shape
+    lines = normed_ref.shape[0] // group
+    packed = rows - lines
+    stream = dot(normed_ref[...], ds_ref[...])
+    for b in range(group):
+        out_ref[b, :lines, :] = stream[b * lines : (b + 1) * lines]
+        out_ref[b, lines:, :] = small_ref[b * packed : (b + 1) * packed, :]
+
+
+def late_pair_kernel(me_ref, normed_ref, small_ref, ds_ref, pieces_ref, mine_ref, theirs_ref):
+    rows = mine_ref.shape[1]
+    lines = normed_ref.shape[0] // 2
+    packed = rows - lines
+    stream = dot(normed_ref[...], ds_ref[...])
+    small = small_ref[...]
+    first = me_ref[0] == 0
+    mine_ref[0, :lines, :] = jnp.where(first, stream[:lines], stream[lines:])
+    mine_ref[0, lines:, :] = jnp.where(first, small[:packed], small[packed:])
+    theirs_ref[0, :lines, :] = jnp.where(first, stream[lines:], stream[:lines]).astype(bf16)
+    theirs_ref[0, lines:rows, :] = jnp.where(first, small[packed:], small[:packed]).astype(bf16)
+    theirs_ref[0, rows:, :] = pieces_ref[...]
+
+
+def late_pairs(normed_t, small, ds, pieces, batches, rows, chans):
+    steps = batches // 2
+    whole = lambda a: pl.BlockSpec(a.shape, lambda i, me_ref: (0, 0))
+    cut = lambda a: pl.BlockSpec((a.shape[0] // steps, a.shape[1]), lambda i, me_ref: (i, 0))
+    block = lambda r: pl.BlockSpec((1, r, chans), lambda i, me_ref: (i, 0, 0))
+    return pl.pallas_call(
+        late_pair_kernel,
+        out_shape=[
+            jax.ShapeDtypeStruct((steps, rows, chans), f32),
+            jax.ShapeDtypeStruct((steps, rows + BLOCK, chans), bf16),
+        ],
+        grid_spec=pltpu.PrefetchScalarGridSpec(
+            num_scalar_prefetch=1,
+            grid=(steps,),
+            in_specs=[cut(normed_t), cut(small), whole(ds), whole(pieces)],
+            out_specs=[block(rows), block(rows + BLOCK)],
+        ),
+        compiler_params=pltpu.CompilerParams(dimension_semantics=("arbitrary",), vmem_limit_bytes=60 << 20),
+    )((lax.axis_index("batch") % 2).astype(jnp.int32).reshape(1), normed_t, small, ds, pieces)
+
+
+def by_blocks(kernel, batches, own, columns, whole, rows, chans):
+    group = LANES // own
+    steps = batches // group
+
+    def spec(array, cut):
+        if cut:
+            return pl.BlockSpec((array.shape[0] // steps, array.shape[1]), lambda i: (i, 0))
+        return pl.BlockSpec(array.shape, lambda i: (0,) * array.ndim)
+
+    return pl.pallas_call(
+        kernel,
+        out_shape=jax.ShapeDtypeStruct((batches, rows, chans), f32),
+        grid=(steps,),
+        in_specs=[spec(a, True) for a in columns] + [spec(a, False) for a in whole],
+        out_specs=pl.BlockSpec((group, rows, chans), lambda i: (i, 0, 0)),
+        compiler_params=pltpu.CompilerParams(dimension_semantics=("arbitrary",), vmem_limit_bytes=60 << 20),
+    )(*columns, *whole)
+
+
+def split_kernel(seqs, batches, own, w_ref, gain_ref, valid_ref, out_ref):
+    depth, half, chans = w_ref.shape[0], w_ref.shape[1] // 2, batches * own
+    count = jnp.sum(valid_ref[...].astype(f32), keepdims=True)
+    high = jnp.floor(count * (1.0 / 128.0))
+    iota = lambda shape, axis: lax.broadcasted_iota(jnp.int32, shape, axis)
+    gain = jnp.broadcast_to(gain_ref[...].astype(f32), (depth, depth))
+    gain = jnp.where(iota((depth, depth), 0) == iota((depth, depth), 1), gain, 0.0)
+    gain = jnp.sum(gain, axis=1, keepdims=True)
+    lane = iota((depth, LANES), 1)
+    extra = jnp.where(lane == LANES - 3, gain, 0.0)
+    extra = jnp.where(lane == LANES - 2, high, extra)
+    extra = jnp.where(lane == LANES - 1, count - high * 128.0, extra).astype(bf16)
     for s in range(seqs):
         for k in range(2):
             pieces = [
@@ -439,27 +601,30 @@
             ]
             first = k * (chans + LANES)
             out_ref[s, :, first : first + chans] = jnp.concatenate(pieces, axis=1).astype(bf16)
-        out_ref[s, :, chans : chans + LANES] = extra_ref[...]
-
-
-def split_columns(weight, extra, seqs, batches, own):
+        out_ref[s, :, chans : chans + LANES] = extra
+
+
+def split_columns(weight, gain, valid, seqs, batches, own):
     shape = jax.ShapeDtypeStruct((seqs, weight.shape[0], 2 * batches * own + LANES), bf16)
-    return pl.pallas_call(lambda *refs: split_kernel(seqs, batches, own, *refs), out_shape=shape)(weight, extra)
+    return pl.pallas_call(lambda *refs: split_kernel(seqs, batches, own, *refs), out_shape=shape)(weight, gain, valid)
 
 
 def join_kernel(
-    batches, stream_ref, gate_ref, small_ref, w_ref, gain_ref,
+    batches, both_ref, small_ref, w_ref, gain_ref,
     out_ref, gain_out_ref, xproj_ref, dt_ref, alog_ref, conv_ref, convb_ref, dtb_ref, skip_ref,
 ):
-    seqs, half = stream_ref.shape[0], w_ref.shape[1] // 2
+    seqs, half = both_ref.shape[0], w_ref.shape[1] // 2
     chans = half // seqs
     own = chans // batches
-    for k, part in enumerate((stream_ref, gate_ref)):
-        whole = [part[s] for s in range(seqs)]
+    for k in range(2):
+        whole = [both_ref[s, :, k * chans : (k + 1) * chans].astype(f32) for s in range(seqs)]
         pieces = [whole[s][:, b * own : (b + 1) * own] for b in range(batches) for s in range(seqs)]
         out_ref[:, k * half : (k + 1) * half] = jnp.concatenate(pieces, axis=1)
     products = out_ref[...] * w_ref[...].astype(f32)
-    gain_out_ref[...] = jnp.sum(products, axis=1, keepdims=True) / gain_ref[...]
+    depth = products.shape[0]
+    sums = jnp.broadcast_to(jnp.sum(products, axis=1, keepdims=True), (depth, depth))
+    eye = lax.broadcasted_iota(jnp.int32, (depth, depth), 0) == lax.broadcasted_iota(jnp.int32, (depth, depth), 1)
+    gain_out_ref[...] = jnp.sum(jnp.where(eye, sums, 0.0), axis=0, keepdims=True) / gain_ref[...].astype(f32)
     small = small_ref[...]
     both = jnp.concatenate([small[:, k : k + LANES] for k in range(0, chans, LANES)], axis=0)
     xproj_ref[...] = both[:own, :CARRY]
@@ -473,13 +638,13 @@
     skip_ref[...] = table[SKIP : SKIP + 1]
 
 
-def join_columns(stream, gate, small, weight, gain, batches, own):
+def join_columns(both, small, weight, gain, batches, own):
     depth = weight.shape[0]
-    shapes = [weight.shape, (depth, 1), (own, CARRY), (INTO, own), (own, CONV - ALOG), (CONVB - CONV, own)]
+    shapes = [weight.shape, (1, depth), (own, CARRY), (INTO, own), (own, CONV - ALOG), (CONVB - CONV, own)]
     shapes += [(1, own)] * 3
     return pl.pallas_call(
         lambda *refs: join_kernel(batches, *refs), out_shape=[jax.ShapeDtypeStruct(s, f32) for s in shapes]
-    )(stream, gate, small, weight, gain)
+    )(both, small, weight, gain)
 
 
 def partner(value, axis, k):
@@ -489,19 +654,19 @@
 def gather_parts(value, axis):
     n = lax.axis_size(axis)
     if n > 4:
-        return lax.all_gather(value, axis)
-    return jnp.stack([value] + [partner(value, axis, k) for k in range(1, n)])
-
-
-def gather_batch(value):
+        return [lax.all_gather(value, axis)]
+    return [value] + [partner(value, axis, k) for k in range(1, n)]
+
+
+def gather_batch(value, after):
     n = lax.axis_size("batch")
     if n > 8:
-        return [lax.all_gather(value, "batch")], [jnp.int32(k) for k in range(n)]
+        return [lax.all_gather(value, "batch")], [jnp.int32(k) for k in range(n)], after
     me = lax.axis_index("batch")
     chips = jnp.stack([value] + [partner(value, "batch", 2 * k) for k in range(1, n // 2)])
     other = partner(chips, "batch", 1)
     places = [me ^ (2 * k) for k in range(n // 2)] + [me ^ (2 * k + 1) for k in range(n // 2)]
-    return [chips, other], places
+    return [chips, other], places, after
 
 
 def exact(total, rows):
@@ -524,20 +689,15 @@
     return values[0]
 
 
-def scatter_batch(value, total):
+def scatter_batch(mine, theirs, total):
     n = lax.axis_size("batch")
-    if n > 8:
-        return lax.psum_scatter(value, "batch", scatter_dimension=0), sum_everywhere(total, ("batch",)), value
     me = lax.axis_index("batch")
-    rows, c = value.shape[1:]
-    block = lambda t: jnp.broadcast_to(exact(jnp.tile(t, (1, c // LANES)), BLOCK)[None], (n // 2, BLOCK, c))
-    pairs = value.reshape((n // 2, 2) + value.shape[1:])
-    mine = lax.dynamic_index_in_dim(pairs, me % 2, 1, False)
-    theirs = lax.dynamic_index_in_dim(pairs, 1 - me % 2, 1, False).astype(bf16)
-    got = partner(jnp.concatenate([theirs, block(total)], axis=1), "batch", 1)
+    rows, c = mine.shape[1:]
+    got = partner(theirs, "batch", 1)
     mine = mine + got[:, :rows].astype(f32)
     total = row_sum(exact(total, BLOCK)) + row_sum(got[0, rows:, :LANES])
-    low = jnp.concatenate([mine.astype(bf16), block(total)], axis=1)
+    pieces = exact(jnp.tile(total, (1, c // LANES)), BLOCK)
+    low = jnp.concatenate([mine.astype(bf16), jnp.broadcast_to(pieces[None], (n // 2, BLOCK, c))], axis=1)
     got = [
         partner(lax.dynamic_index_in_dim(low, (me // 2) ^ k, 0, False), "batch", 2 * k) for k in range(1, n // 2)
     ]
@@ -547,11 +707,11 @@
     return result, tree([row_sum(exact(total, BLOCK))] + [row_sum(part[rows:, :LANES]) for part in got]), low
 
 
-def scatter_parts(value, axis):
+def scatter_parts(values, axis):
     n = lax.axis_size(axis)
     if n > 4:
-        return [lax.psum_scatter(value.astype(f32), axis, scatter_dimension=0)]
-    return [value[0]] + [partner(value[k], axis, k) for k in range(1, n)]
+        return [lax.psum_scatter(values[0].astype(f32), axis, scatter_dimension=0)]
+    return [values[0]] + [partner(values[k], axis, k) for k in range(1, n)]
 
 
 def share_parts(value, axis):
@@ -608,17 +768,9 @@
     me = place.astype(jnp.int32).reshape(1)
     tok = tokens.reshape(rows, width)
 
-    counted = jnp.sum(valid_rows, axis=1, keepdims=True)
-    extra = jnp.concatenate(
-        [
-            jnp.zeros((depth, LANES - 3), bf16),
-            norm_gain[:, None],
-            jnp.broadcast_to((counted // 128).astype(bf16), (depth, 1)),
-            jnp.broadcast_to((counted % 128).astype(bf16), (depth, 1)),
-        ],
-        axis=1,
-    )
-    split = split_columns(in_weight, extra, seqs, batches, own)
+    flags = jnp.pad(piece_starts.astype(bf16), ((0, 15), (0, width - rows)))
+    everything = lax.all_gather(jnp.concatenate([tok, flags], axis=0), "seq")
+    split = split_columns(in_weight, norm_gain.reshape(1, depth), valid_rows, seqs, batches, own)
     split = lax.all_to_all(split, "seq", 0, 0).reshape(lines, 2 * chans + LANES)
     vectors = jnp.concatenate(
         [
@@ -634,26 +786,23 @@
     vectors = jnp.pad(vectors, ((0, 0), (0, LANES - vectors.shape[1])))
     columns_x = jnp.pad(xproj_weight, ((0, 0), (0, LANES - xproj_weight.shape[1])))
     local = jnp.pad(jnp.concatenate([vectors, columns_x], axis=0), ((0, lines - 2 * own), (chans, 0)))
-    blocks, places = gather_batch(split[:, : chans + LANES] + local)
     second = jnp.concatenate(
         [split[:, chans + LANES :]] + [out_weight[:, k : k + chans] for k in range(0, width, chans)], axis=0
     )
+    blocks, places, second = gather_batch(split[:, : chans + LANES] + local, second)
     second = lax.all_gather(second, "batch")
 
-    flags = jnp.pad(piece_starts.astype(bf16), ((0, 15), (0, width - rows)))
-    held = jnp.concatenate([tok, flags], axis=0)
-    held, split = lax.optimization_barrier((held, split))
-    everything = gather_parts(held, "seq")
 
     tile = ((total, chans), f32, "t")
     low_tile = ((total, chans), bf16, "t")
     state = ((total * states, chans), bf16, "t")
-    normed, stream, conv_pre, act, proj, w_stream, vec, xproj, gain, marks = call(
+    normed, normed_t, stream, conv_pre, act, proj, w_stream, vec, xproj, gain, marks = call(
         start_kernel,
         jnp.concatenate([me] + [p.astype(jnp.int32).reshape(1) for p in places]),
-        [(everything, "x")] + [(block, "f") for block in blocks],
+        [(everything, "y")] + [(block, "f") for block in blocks],
         [
             ((seqs, rows, width), bf16, "x"),
+            ((width, total), bf16, "c"),
             low_tile,
             tile,
             low_tile,
@@ -669,8 +818,7 @@
         rows,
     )
     total_valid = (marks[:, LANES - 2 : LANES - 1] * 128.0 + marks[:, LANES - 1 :]) / depth
-    slots = jnp.arange(seqs) ^ place
-    starts = jnp.take(everything[:, rows, :rows].astype(f32), slots, axis=0).reshape(total)
+    starts = everything[:, rows, :rows].astype(f32).reshape(total)
     running = jnp.cumsum(starts)
     lagged = jnp.concatenate([jnp.zeros((PIECE,), f32), running[: total - PIECE]])
     carry_on = jnp.where(running - lagged > 0.5, 1.0 - starts, 0.0)
@@ -692,19 +840,19 @@
         rows,
         reverse=True,
     )
-    hp, mixed, gate, gated, branch, w_gate, out_w = call(
-        ahead_kernel,
+    hp, mixed, gate, gated_t, w_gate, out_w, *branch = call(
+        lambda *refs: ahead_kernel(rows, *refs),
         me,
         [(proj, "t"), (act, "t"), (normed, "x"), (g, "t"), (vec, "f"), (second, "f")],
         [
             state,
             tile,
             tile,
-            ((seqs, rows, chans), bf16, "x"),
-            ((seqs, rows, width), bf16, "x"),
+            ((chans, total), bf16, "c"),
             ((width, chans), bf16, "f"),
             ((chans, width), bf16, "f"),
-        ],
+        ]
+        + slots_out(seqs, rows, width),
         [
             pltpu.VMEM((states, chans), f32),
             pltpu.VMEM((ROWS, chans), f32),
@@ -723,36 +871,49 @@
     output = result.astype(bf16)
     misfit = result - teacher.reshape(rows, width).astype(f32)
     squares = jnp.sum(valid_f * misfit * misfit, axis=0, keepdims=True)
-    square_sum = jnp.broadcast_to(jnp.sum(squares, axis=1, keepdims=True), (1, LANES))
+    part = LANES - CARRY
+    square_sum = squares[:, :LANES]
+    for k in range(LANES, width, LANES):
+        square_sum = square_sum + squares[:, k : k + LANES]
+    square_sum = sum(square_sum[:, k : k + part] for k in range(0, LANES, part))
+    square_sum = jnp.pad(square_sum, ((0, 0), (CARRY, 0)))
     d_result = 2.0 * (total * batches) / total_valid * valid_f * misfit
 
     d_branch = gather_parts(d_result.astype(bf16), "seq")
     q, d_mixed, d_gate, skip_grad = call(
-        piece_grad_kernel,
+        lambda *refs: piece_grad_kernel(rows, *refs),
         me,
         [
             (proj, "t"),
             (act, "t"),
             (mixed, "t"),
             (gate, "t"),
-            (d_branch, "x"),
             (vec, "f"),
             (out_w, "f"),
-        ],
+        ]
+        + slots_in(d_branch),
         [state, tile, ((seqs, rows, chans), bf16, "x"), ((1, chans), f32, "f")],
         [pltpu.VMEM((states, chans), f32), pltpu.VMEM((ROWS, chans), f32), pltpu.VMEM(groups, f32)],
         total,
         rows,
     )
     flat = lambda v: v.reshape(total, v.shape[2])
-    gate_grad = t_dot(flat(normed), flat(d_gate))
-    out_grad = t_dot(flat(gated), flat(d_branch))
-    gate_out = lax.psum_scatter(gate_grad, "batch", scatter_dimension=0, tiled=True)
-    out_out = lax.psum_scatter(out_grad, "batch", scatter_dimension=0, tiled=True)
+    branches = d_branch if seqs <= 4 else [flat(d_branch[0])]
+    early_sum = by_blocks(
+        early_grad_kernel,
+        batches,
+        own,
+        [normed_t, gated_t],
+        [flat(d_gate)] + branches,
+        lines + own * width // chans,
+        chans,
+    )
+    early = lax.psum_scatter(early_sum, "batch", scatter_dimension=0)
+    pieces = exact(square_sum, BLOCK)
     d_act, d_proj, table = call(
         state_grad_kernel,
         me,
-        [(proj, "t"), (act, "t"), (d_mixed, "t"), (g, "t"), (hp, "t"), (q, "t"), (vec, "f"), (skip_grad, "f")],
+        [(proj, "t"), (act, "t"), (d_mixed, "t"), (g, "t"), (hp, "t"), (q, "t"), (vec, "f"), (skip_grad, "f"), (pieces, "f")],
         [tile, ((total, LANES), bf16, "t"), ((LANES, chans), f32, "f")],
         [
             pltpu.VMEM((states, chans), f32),
@@ -772,15 +933,10 @@
         rows,
         reverse=True,
     )
-    if seqs <= 4:
-        d_proj = lax.dynamic_update_slice(d_proj, exact(square_sum[:, CARRY:], BLOCK), (0, CARRY))
-        d_proj = share_parts(d_proj, "seq")
-        square_sum = jnp.tile(tree([row_sum(part[:BLOCK, CARRY:]) for part in d_proj]), (1, LANES // (LANES - CARRY)))
-    else:
-        d_proj = share_parts(d_proj, "seq")
-        square_sum = sum_everywhere(square_sum, ("seq",))
-    d_normed, d_stream, small = call(
-        lambda *refs: end_kernel(own, *refs),
+    d_proj = share_parts(d_proj, "seq")
+    slots = slots_out(seqs, rows, width)
+    *d_normed, d_stream, small, sent, seq_sum = call(
+        lambda *refs: end_kernel(own, rows, len(slots), *refs),
         me,
         [(part, "t") for part in d_proj]
         + [
@@ -795,10 +951,12 @@
             (w_gate, "f"),
             (table, "f"),
         ],
-        [
-            ((seqs, rows, width), bf16, "x"),
+        slots
+        + [
             ((seqs, rows, chans), bf16, "x"),
             ((batches * packed, chans), f32, "f"),
+            ((BLOCK, chans), bf16, "f"),
+            ((1, LANES), f32, "f"),
         ],
         [
             pltpu.VMEM((ROWS + 8, chans), f32),
@@ -810,21 +968,25 @@
         rows,
         reverse=True,
     )
-    stream_grad = t_dot(flat(normed), flat(d_stream))
-    late = jnp.concatenate(
-        [stream_grad.reshape(batches, lines, chans), small.reshape(batches, packed, chans)], axis=1
-    )
-    d_normed, late = lax.optimization_barrier((d_normed, late))
-    late, square_sum, waiting = scatter_batch(late, square_sum)
-    loss = (square_sum / (total_valid * width))[0, 0]
+    if batches <= 8:
+        mine, theirs = late_pairs(normed_t, small, flat(d_stream), sent, batches, lines + packed, chans)
+        late, square_sum, waiting = scatter_batch(mine, theirs, seq_sum)
+    else:
+        late = by_blocks(
+            late_grad_kernel, batches, own, [normed_t, small], [flat(d_stream)], lines + packed, chans
+        )
+        waiting = late
+        late = lax.psum_scatter(late, "batch", scatter_dimension=0)
+        square_sum = sum_everywhere(square_sum, ("batch", "seq"))
+    loss = jnp.sum(square_sum) / (total_valid * width)[0, 0]
     nothing = waiting[0, :1].astype(f32) * 0.0
-    gate_out = lax.all_to_all((gate_out + nothing).reshape(seqs, depth, chans), "seq", 0, 0)
-    d_normed = [jnp.tile(nothing, (1, width // chans))] + scatter_parts(d_normed, "seq")
-    stream_out = lax.all_to_all(late[:lines].reshape(seqs, depth, chans), "seq", 0, 0)
+    d_normed = added([jnp.tile(nothing, (1, width // chans))] + scatter_parts(d_normed, "seq"))
+    in_out = jnp.concatenate([late[:lines], early[:lines]], axis=1).astype(bf16)
+    in_out = lax.all_to_all(in_out.reshape(seqs, depth, 2 * chans), "seq", 0, 0)
     in_out, gain_out, xproj_out, dt_out, alog_out, conv_out, convb_out, dtb_out, skip_out = join_columns(
-        stream_out, gate_out, late[lines:], in_weight, norm_gain.astype(f32)[:, None], batches, own
-    )
-    d_normed = added(d_normed)
+        in_out, late[lines:], in_weight, norm_gain.reshape(1, depth), batches, own
+    )
+    out_out = early[lines:].reshape(-1, own, chans).transpose(1, 0, 2).reshape(own, width)
     mean_sq = jnp.mean(tok_f * tok_f, axis=-1, keepdims=True)
     root_inv = lax.rsqrt(mean_sq + 1e-05)
     own_unit = tok_f * root_inv
@@ -834,7 +996,7 @@
         output[None],
         loss,
         input_grad[None],
-        gain_out[:, 0],
+        gain_out[0],
         in_out,
         conv_out,
         convb_out[0],

time: 377 us -> 334 us (0.89)
  starting transfers between devices: 57.4 us -> 35.9 us
  Pallas kernels: 133 us -> 147 us
  local copies, waits for them, and re-layouts: 22 us -> 8.65 us
  matrix products: 9.04 us -> 0 us
  other arithmetic: 23.2 us -> 15.6 us
  between operations: 23.9 us -> 17.4 us
    ppermute x26 -> x23, starting transfers between devices: 45.1 us -> 27.2 us  [partner(): lax.ppermute(value, axis, [(i, i ^ k) for i in range(lax.axis_size(axis))])]
    pallas_call x0 -> x2, Pallas kernels: none -> 11.8 us  [the longest x1 6.76 us: by_blocks(): pl.pallas_call(kernel, out_shape=jax.ShapeDtypeStruct((batches, rows, cha...]
    dot_general x3 -> x0, matrix products: 9.04 us -> none  [t_dot(): lax.dot_general(a, b, (((0,), (0,)), ((), ())), preferred_element_type=f32)]
    all_gather x0 -> x1, waiting for transfers between devices: none -> 6.87 us  [body(): everything = lax.all_gather(jnp.concatenate([tok, flags], axis=0), 'seq')]
    all_to_all x2 -> x1, waiting for transfers between devices: 7.78 us -> 3.18 us  [body(): in_out = lax.all_to_all(in_out.reshape(seqs, depth, 2 * chans), 'seq', 0, 0)]
    unnamed x94 -> x56, local copies, waits for them, and re-layouts: 8.12 us -> 4.3 us
    ppermute x26 -> x23, waiting for transfers between devices: 92 us -> 91.9 us  [partner(): lax.ppermute(value, axis, [(i, i ^ k) for i in range(lax.axis_size(axis))])]
  transfers between devices with their start and end apart: 32 -> 28, of which waited for: 17 -> 16; matrix products, arithmetic and copies ran while one was open for 9% -> 4% of each run, Pallas kernels for 23% -> 28%
where the time goes in v2:
time: 334 us; the launch traced here: 332 us
  Pallas kernels  147 us (44%)
  waiting for transfers between devices  108 us (32%)
  starting transfers between devices  35.9 us (11%)
  between operations  17.4 us (5%)
  other arithmetic  15.6 us (5%)
  local copies, waits for them, and re-layouts  8.65 us (3%)
    pallas_call x6, Pallas kernels, call(): pl.pallas_call(kernel, out_shape=[jax.ShapeDtypeStruct(s, d) for s, d, _...  132 us
    ppermute x23, waiting for transfers between devices, partner(): lax.ppermute(value, axis, [(i, i ^ k) for i in range(lax.axis_size(axis))])  91.9 us
    ppermute x23, starting transfers between devices, partner(): lax.ppermute(value, axis, [(i, i ^ k) for i in range(lax.axis_size(axis))])  27.2 us
    all_gather x1, waiting for transfers between devices, body(): everything = lax.all_gather(jnp.concatenate([tok, flags], axis=0), 'seq')  6.87 us
    pallas_call x1, Pallas kernels, by_blocks(): pl.pallas_call(kernel, out_shape=jax.ShapeDtypeStruct((batches, rows, cha...  6.76 us
  transfers between devices with their start and end apart: 28, of which 16 were waited for; matrix products, arithmetic and copies ran while one was open for 4% of the time, Pallas kernels for 28%

profile of v2, /device:TPU:0, one launch (start us, length us, event | category | flops | bytes accessed | tf_op | source)
XLA Modules:
  0.0 332.4 jit_solution(2740510961248730765)
XLA Ops:
  7.3 0.7 convert_element_type.144
  8.0 1.9 fusion.10
  9.9 1.8 shard_map.237
  11.8 5.2 %all-to-all-start = ((bf16[4,32,1152]{2,1,0:T(8,128)(2,1)}), bf16[4,32,1152]{2,1,0:T(8,128)(2,1)S(1)}, u32[]{:S(2)}, u32[]{:S(2)}) async-start(bf16[4,32,1152]{2,1,0:T(8,128)(2,1)} %shard_map.237), calls=%async_computation | async-start | bytes 589824 | tf_op jit(solution)/shard_map/all_to_all | solution.py:774
  17.0 5.6 %all-to-all-done = bf16[4,32,1152]{2,1,0:T(8,128)(2,1)S(1)} async-done(((bf16[4,32,1152]{2,1,0:T(8,128)(2,1)}), bf16[4,32,1152]{2,1,0:T(8,128)(2,1)S(1)}, u32[]{:S(2)}, u32[]{:S(2)}) %all-to-all-start) | async-done | bytes 294944 | tf_op jit(solution)/shard_map/all_to_all | solution.py:774
  22.6 0.7 pad_maximum_fusion.1
  24.2 3.7 %collective-permute-start.2 = (bf16[128,640]{1,0:T(8,128)(2,1)S(1)}, bf16[128,640]{1,0:T(8,128)(2,1)S(1)}, u32[]{:S(2)}, u32[]{:S(2)}) collective-permute-start(bf16[128,640]{1,0:T(8,128)(2,1)S(1)} %slice_add_fusion), channel_id=1, source_target_pairs={{0,24},{4,28},{8,16},{12,20},{16,8},{20,12},{24,0},{28,4},{1,25},{... | collective-permute-start | bytes 491528 | tf_op jit(solution)/shard_map/ppermute | solution.py:651
  27.9 0.8 collective-permute-start
  28.7 4.5 %collective-permute-done.2 = bf16[128,640]{1,0:T(8,128)(2,1)S(1)} collective-permute-done((bf16[128,640]{1,0:T(8,128)(2,1)S(1)}, bf16[128,640]{1,0:T(8,128)(2,1)S(1)}, u32[]{:S(2)}, u32[]{:S(2)}) %collective-permute-start.2) | collective-permute-done | bytes 163872 | tf_op jit(solution)/shard_map/ppermute | solution.py:651
  33.2 7.2 %collective-permute-done.1 = bf16[128,640]{1,0:T(8,128)(2,1)S(1)} collective-permute-done((bf16[128,640]{1,0:T(8,128)(2,1)S(1)}, bf16[128,640]{1,0:T(8,128)(2,1)S(1)}, u32[]{:S(2)}, u32[]{:S(2)}) %collective-permute-start.1) | collective-permute-done | bytes 163872 | tf_op jit(solution)/shard_map/ppermute | solution.py:651
  40.7 0.6 concatenate.54.me_ref
  41.3 1.4 collective-permute-done.3.refs_1_
  42.8 6.9 %all-gather.5.cloned.1.call-done = bf16[1088,1024]{1,0:T(8,128)(2,1)} async-done(((bf16[272,1024]{1,0:T(8,128)(2,1)}), bf16[1088,1024]{1,0:T(8,128)(2,1)}) %all-gather.5.cloned.1.call-update) | async-done | bytes 2228240 | tf_op jit(solution)/shard_map/all_gather | solution.py:772
  49.7 11.7 %shard_map.238 = (bf16[4,256,1024]{2,1,0:T(8,128)(2,1)}, bf16[1024,1024]{1,0:T(8,128)(2,1)}, bf16[1024,512]{1,0:T(8,128)(2,1)}, f32[1024,512]{1,0:T(8,128)}, bf1...) custom-call(s32[9]{0:T(128)} %concatenate.54.me_ref, ...), custom_call_target="tpu_custom_call" | custom-call | tf_op jit(solution)/shard_map/pallas_call | solution.py:476
  61.3 1.5 collective-permute-start.6
  62.8 1.5 collective-permute-start.5
  64.9 0.7 slice_convert_fusion.2
  66.2 0.7 broadcast_subtract_fusion
  67.0 4.7 %collective-permute-done.6 = bf16[1024,128]{1,0:T(8,128)(2,1)S(1)} collective-permute-done((bf16[1024,128]{1,0:T(8,128)(2,1)}, bf16[1024,128]{1,0:T(8,128)(2,1)S(1)}, u32[]{:S(2)}, u32[]{:S(2)}) %collective-permute-start.6) | collective-permute-done | bytes 262176 | tf_op jit(solution)/shard_map/ppermute | solution.py:651
  71.7 4.4 %collective-permute-done.5 = bf16[1024,128]{1,0:T(8,128)(2,1)S(1)} collective-permute-done((bf16[1024,128]{1,0:T(8,128)(2,1)}, bf16[1024,128]{1,0:T(8,128)(2,1)S(1)}, u32[]{:S(2)}, u32[]{:S(2)}) %collective-permute-start.5) | collective-permute-done | bytes 262176 | tf_op jit(solution)/shard_map/ppermute | solution.py:651
  76.2 1.9 add_select_fusion.proj_ref.refs_1_
  78.1 14.2 %shard_map.239.refs_4_.g_ref = bf16[16384,512]{1,0:T(8,128)(2,1)} custom-call(s32[1]{0:T(128)} %bitcast.1.me_ref.refs_0_, f32[1024,128]{1,0:T(8,128)} %add_select_fusion.proj_ref.refs_1_, bf16[1024,512]{1,0:T(8,128)(2,1)} %get-tuple-element.61.act_ref.refs_2_.refs_8_, f32[128,512]{1,0:T(8,128)} %get-tuple-element.63.vec_ref.refs_5_.refs_10_), custom_call_target="tpu_custom_call" | custom-call | tf_op jit(solution)/shard_map/pallas_call | solution.py:476
  92.4 27.1 %shard_map.240 = (bf16[16384,512]{1,0:T(8,128)(2,1)}, f32[1024,512]{1,0:T(8,128)}, f32[1024,512]{1,0:T(8,128)}, bf16[512,1024]{1,0:T(8,128)(2,1)}, bf16[1024,512...) custom-call(s32[1]{0:T(128)} %bitcast.1.me_ref.refs_0_, ...), custom_call_target="tpu_custom_call" | custom-call | tf_op jit(solution)/shard_map/pallas_call | solution.py:476
  119.5 1.5 collective-permute-start.9
  121.0 1.4 collective-permute-start.8
  122.4 0.6 collective-permute-start.7
  125.0 10.5 %collective-permute-done.9 = bf16[256,1024]{1,0:T(8,128)(2,1)S(1)} collective-permute-done((bf16[256,1024]{1,0:T(8,128)(2,1)}, bf16[256,1024]{1,0:T(8,128)(2,1)S(1)}, u32[]{:S(2)}, u32[]{:S(2)}) %collective-permute-start.9) | collective-permute-done | bytes 524320 | tf_op jit(solution)/shard_map/ppermute | solution.py:651
  135.5 10.3 %collective-permute-done.8 = bf16[256,1024]{1,0:T(8,128)(2,1)S(1)} collective-permute-done((bf16[256,1024]{1,0:T(8,128)(2,1)}, bf16[256,1024]{1,0:T(8,128)(2,1)S(1)}, u32[]{:S(2)}, u32[]{:S(2)}) %collective-permute-start.8) | collective-permute-done | bytes 524320 | tf_op jit(solution)/shard_map/ppermute | solution.py:651
  145.8 1.6 fusion.9
  147.6 1.5 collective-permute-start.10
  149.7 1.4 collective-permute-start.12
  151.2 11.3 %collective-permute-done.10.refs_8_.refs_1_ = bf16[256,1024]{1,0:T(8,128)(2,1)S(1)} collective-permute-done((bf16[256,1024]{1,0:T(8,128)(2,1)S(1)}, bf16[256,1024]{1,0:T(8,128)(2,1)S(1)}, u32[]{:S(2)}, u32[]{:S(2)}) %collective-permute-start.10) | collective-permute-done | bytes 524320 | tf_op jit(solution)/shard_map/ppermute | solution.py:651
  162.5 11.5 %collective-permute-done.11.refs_9_.refs_2_ = bf16[256,1024]{1,0:T(8,128)(2,1)S(1)} collective-permute-done((bf16[256,1024]{1,0:T(8,128)(2,1)S(1)}, bf16[256,1024]{1,0:T(8,128)(2,1)S(1)}, u32[]{:S(2)}, u32[]{:S(2)}) %collective-permute-start.11) | collective-permute-done | bytes 524320 | tf_op jit(solution)/shard_map/ppermute | solution.py:651
  174.0 0.8 copy-done.6
  174.9 18.7 %shard_map.241 = (bf16[16384,512]{1,0:T(8,128)(2,1)}, f32[1024,512]{1,0:T(8,128)}, bf16[4,256,512]{2,1,0:T(8,128)(2,1)}, f32[1,512]{1,0:T(1,128)}) custom-call(s32[1]{0:T(128)} %bitcast.1.me_ref.refs_0_, f32[1024,128]{1,0:T(8,128)} %add_select_fusion.proj_ref.refs_1_, bf16[1024,512]{1,0:T(8,128)(2,1)} %get-tuple-element.61.act_ref.refs_2_.refs_8_, ...), custom_call_target="tpu_custom_call" | custom-call | tf_op jit(solution)/shard_map/pallas_call | solution.py:476
  193.6 6.8 %shard_map.245 = f32[8,256,512]{2,1,0:T(8,128)} custom-call(bf16[1024,1024]{1,0:T(8,128)(2,1)} %get-tuple-element.86.normed_ref, bf16[512,1024]{1,0:T(8,128)(2,1)} %get-tuple-element.97.gated_ref, bf16[1024,512]{1,0:T(8,128)(2,1)} %bitcast.92, bf16[256,1024]{1,0:T(8,128)(2,1)} %copy-done.2, bf16[256,1024]{1,0:T(8,128)(2,1)} %copy-done.4, ...), custom_call_target="tpu_custom_call" | custom-call | tf_op jit(solution)/shard_map/pallas_call | solution.py:574
  200.6 0.7 maximum_maximum_fusion.1.pieces_ref
  201.3 47.4 %shard_map.242 = (f32[1024,512]{1,0:T(8,128)}, bf16[1024,128]{1,0:T(8,128)(2,1)}, f32[128,512]{1,0:T(8,128)}) custom-call(s32[1]{0:T(128)} %bitcast.1.me_ref.refs_0_, f32[1024,128]{1,0:T(8,128)} %add_select_fusion.proj_ref.refs_1_, bf16[1024,512]{1,0:T(8,128)(2,1)} %get-tuple-element.61.act_ref.refs_2_.refs_8_, f32[1024,512]{1,0:T(8,128)} %get-tuple-element.72.dm_ref, ...), custom_call_target="tpu_custom_call" | custom-call | tf_op jit(solution)/shard_map/pallas_call | solution.py:476
  248.7 0.7 collective-permute-start.13
  249.5 1.3 collective-permute-start.14
  250.8 1.5 collective-permute-start.15
  252.3 6.0 %collective-permute-done.13.refs_2_ = bf16[1024,128]{1,0:T(8,128)(2,1)S(1)} collective-permute-done((bf16[1024,128]{1,0:T(8,128)(2,1)}, bf16[1024,128]{1,0:T(8,128)(2,1)S(1)}, u32[]{:S(2)}, u32[]{:S(2)}) %collective-permute-start.13) | collective-permute-done | bytes 262176 | tf_op jit(solution)/shard_map/ppermute | solution.py:651
  258.3 3.6 %collective-permute-done.14.refs_3_ = bf16[1024,128]{1,0:T(8,128)(2,1)S(1)} collective-permute-done((bf16[1024,128]{1,0:T(8,128)(2,1)}, bf16[1024,128]{1,0:T(8,128)(2,1)S(1)}, u32[]{:S(2)}, u32[]{:S(2)}) %collective-permute-start.14) | collective-permute-done | bytes 262176 | tf_op jit(solution)/shard_map/ppermute | solution.py:651
  261.9 0.7 copy-done.11
  262.7 12.5 %shard_map.243 = (bf16[256,1024]{1,0:T(8,128)(2,1)}, bf16[256,1024]{1,0:T(8,128)(2,1)}, bf16[256,1024]{1,0:T(8,128)(2,1)}, bf16[256,1024]{1,0:T(8,128)(2,1)}, bf...) custom-call(s32[1]{0:T(128)} %bitcast.1.me_ref.refs_0_, ...), custom_call_target="tpu_custom_call" | custom-call | tf_op jit(solution)/shard_map/pallas_call | solution.py:476
  275.2 5.0 %shard_map.244 = (f32[4,160,512]{2,1,0:T(8,128)}, bf16[4,176,512]{2,1,0:T(8,128)(2,1)}) custom-call(s32[1]{0:T(128)} %bitcast.32.me_ref, bf16[1024,1024]{1,0:T(8,128)(2,1)} %get-tuple-element.86.normed_ref, f32[256,512]{1,0:T(8,128)} %get-tuple-element.87.small_ref, bf16[1024,512]{1,0:T(8,128)(2,1)} %bitcast.100, bf16[16,512]{1,0:T(8,128)(2,1)} %get-tuple-element.89.pieces_ref), custom_call_target="tpu_custom_call" | custom-call | tf_op jit(solution)/shard_map/pallas_call | solution.py:549
  280.3 1.5 collective-permute-start.22
  281.8 1.5 collective-permute-start.21
  283.9 1.6 fusion.33
  285.7 3.4 %collective-permute-start.19 = (bf16[176,512]{1,0:T(8,128)(2,1)S(1)}, bf16[176,512]{1,0:T(8,128)(2,1)S(1)}, u32[]{:S(2)}, u32[]{:S(2)}) collective-permute-start(bf16[176,512]{1,0:T(8,128)(2,1)S(1)} %get-tuple-element.143), channel_id=1, source_target_pairs={{0,24},{4,28},{8,16},{12,20},{16,8},{20,12},{24,0},{28,4},{1,25},{... | collective-permute-start | bytes 540680 | tf_op jit(solution)/shard_map/ppermute | solution.py:651
  289.2 7.1 %collective-permute-done.22 = bf16[256,1024]{1,0:T(8,128)(2,1)S(1)} collective-permute-done((bf16[256,1024]{1,0:T(8,128)(2,1)}, bf16[256,1024]{1,0:T(8,128)(2,1)S(1)}, u32[]{:S(2)}, u32[]{:S(2)}) %collective-permute-start.22) | collective-permute-done | bytes 524320 | tf_op jit(solution)/shard_map/ppermute | solution.py:651
  296.2 1.5 collective-permute-start.17
  297.7 9.2 %collective-permute-done.21 = bf16[256,1024]{1,0:T(8,128)(2,1)S(1)} collective-permute-done((bf16[256,1024]{1,0:T(8,128)(2,1)}, bf16[256,1024]{1,0:T(8,128)(2,1)S(1)}, u32[]{:S(2)}, u32[]{:S(2)}) %collective-permute-start.21) | collective-permute-done | bytes 524320 | tf_op jit(solution)/shard_map/ppermute | solution.py:651
  307.5 1.8 fusion.7
  309.6 1.0 slice.323
  310.6 0.7 pad_maximum_fusion.2
  311.3 3.4 %all-to-all-start.1 = ((bf16[4,32,1024]{2,1,0:T(8,128)(2,1)}), bf16[4,32,1024]{2,1,0:T(8,128)(2,1)S(1)}, u32[]{:S(2)}, u32[]{:S(2)}) async-start(bf16[4,32,1024]{2,1,0:T(8,128)(2,1)} %pad_maximum_fusion.2), calls=%async_computation.2 | async-start | bytes 524288 | tf_op jit(solution)/shard_map/all_to_all | solution.py:985
  314.7 0.6 slice.260.refs_1_
  315.4 0.6 add_reduce_fusion
  316.6 0.7 copy.43
  317.4 3.2 all-to-all-done.1.refs_0_
  320.5 0.7 copy-done.8
  321.2 2.1 shard_map.246
  323.3 1.4 copy.42
  (125 shorter events, 5.8 us)
Async XLA Ops:
  7.2 9.8 %copy-start.13 = (bf16[64,1024]{1,0:T(8,128)(2,1)S(1)}, bf16[64,1024]{1,0:T(8,128)(2,1)}, u32[]{:S(2)}) copy-start(bf16[64,1024]{1,0:T(8,128)(2,1)} %param.27) | copy-start | bytes 393220
  7.2 16.2 %copy-start.14 = (bf16[64,64]{1,0:T(8,128)(2,1)S(1)}, bf16[64,64]{1,0:T(8,128)(2,1)}, u32[]{:S(2)}) copy-start(bf16[64,64]{1,0:T(8,128)(2,1)} %param.23) | copy-start | bytes 24580
  7.2 16.3 %copy-start.18 = (bf16[64,16]{0,1:T(8,128)(2,1)S(1)}, bf16[64,16]{0,1:T(8,128)(2,1)}, u32[]{:S(2)}) copy-start(bf16[64,16]{0,1:T(8,128)(2,1)} %param.25) | copy-start | bytes 6148
  7.2 16.4 %copy-start.20 = (bf16[4,64]{1,0:T(4,128)(2,1)S(1)}, bf16[4,64]{1,0:T(4,128)(2,1)}, u32[]{:S(2)}) copy-start(bf16[4,64]{1,0:T(4,128)(2,1)} %param.20) | copy-start | bytes 1540
  7.2 16.5 %copy-start.21 = (bf16[64]{0:T(256)(128)(2,1)S(1)}, bf16[64]{0:T(256)(128)(2,1)}, u32[]{:S(2)}) copy-start(bf16[64]{0:T(256)(128)(2,1)} %param.21) | copy-start | bytes 388
  7.2 42.4 %all-gather.5.cloned.1.call-start = ((), (), s32[]{:S(2)}) async-start(), calls=%async_computation.4 | async-start | bytes 2785280 | tf_op jit(solution)/shard_map/all_gather | solution.py:772
  8.0 15.8 %copy-start.22 = (bf16[64]{0:T(256)(128)(2,1)S(1)}, bf16[64]{0:T(256)(128)(2,1)}, u32[]{:S(2)}) copy-start(bf16[64]{0:T(256)(128)(2,1)} %param.24) | copy-start | bytes 388
  8.0 16.0 %copy-start.23 = (bf16[64]{0:T(256)(128)(2,1)S(1)}, bf16[64]{0:T(256)(128)(2,1)}, u32[]{:S(2)}) copy-start(bf16[64]{0:T(256)(128)(2,1)} %param.26) | copy-start | bytes 388
  8.0 16.2 %copy-start.15 = (bf16[64,96]{1,0:T(8,128)(2,1)S(1)}, bf16[64,96]{1,0:T(8,128)(2,1)}, u32[]{:S(2)}) copy-start(bf16[64,96]{1,0:T(8,128)(2,1)} %param.22) | copy-start | bytes 36868
  11.8 10.8 %all-to-all-start = ((bf16[4,32,1152]{2,1,0:T(8,128)(2,1)}), bf16[4,32,1152]{2,1,0:T(8,128)(2,1)S(1)}, u32[]{:S(2)}, u32[]{:S(2)}) async-start(bf16[4,32,1152]{2,1,0:T(8,128)(2,1)} %shard_map.237), calls=%async_computation | async-start | bytes 589824 | tf_op jit(solution)/shard_map/all_to_all | solution.py:774
  17.0 75.4 %all-gather.7.cloned.1.call-start = ((), (), s32[]{:S(2)}) async-start(), calls=%async_computation.5 | async-start | bytes 2359296 | tf_op jit(solution)/shard_map/all_gather | solution.py:793
  23.3 286.2 %reduce-scatter.2.cloned.1.call-start = ((), (), s32[]{:S(2)}) async-start(), calls=%async_computation.3 | async-start | bytes 4718592 | tf_op jit(solution)/shard_map/reduce_scatter | solution.py:911
  24.2 9.0 %collective-permute-start.2 = (bf16[128,640]{1,0:T(8,128)(2,1)S(1)}, bf16[128,640]{1,0:T(8,128)(2,1)S(1)}, u32[]{:S(2)}, u32[]{:S(2)}) collective-permute-start(bf16[128,640]{1,0:T(8,128)(2,1)S(1)} %slice_add_fusion), channel_id=1, source_target_pairs={{0,24},{4,28},{8,16},{12,20},{16,8},{20,12},{24,0},{28,4},{1,25},{... | collective-permute-start | bytes 491528 | tf_op jit(solution)/shard_map/ppermute | solution.py:651
  27.9 12.6 %collective-permute-start.1 = (bf16[128,640]{1,0:T(8,128)(2,1)S(1)}, bf16[128,640]{1,0:T(8,128)(2,1)S(1)}, u32[]{:S(2)}, u32[]{:S(2)}) collective-permute-start(bf16[128,640]{1,0:T(8,128)(2,1)S(1)} %slice_add_fusion), channel_id=1, source_target_pairs={{0,16},{4,20},{8,24},{12,28},{16,0},{20,4},{24,8},{28,12},{1,17},{... | collective-permute-start | bytes 491528 | tf_op jit(solution)/shard_map/ppermute | solution.py:651
  27.9 12.6 %collective-permute-start = (bf16[128,640]{1,0:T(8,128)(2,1)S(1)}, bf16[128,640]{1,0:T(8,128)(2,1)S(1)}, u32[]{:S(2)}, u32[]{:S(2)}) collective-permute-start(bf16[128,640]{1,0:T(8,128)(2,1)S(1)} %slice_add_fusion), channel_id=1, source_target_pairs={{0,8},{4,12},{8,0},{12,4},{16,24},{20,28},{24,16},{28,20},{1,9},{5... | collective-permute-start | bytes 491528 | tf_op jit(solution)/shard_map/ppermute | solution.py:651
  40.6 9.1 %copy-start.3 = (bf16[4,128,640]{2,1,0:T(8,128)(2,1)}, bf16[4,128,640]{2,1,0:T(8,128)(2,1)S(1)}, u32[]{:S(2)}) copy-start(bf16[4,128,640]{2,1,0:T(8,128)(2,1)S(1)} %pad_maximum_fusion.refs_0_) | copy-start | bytes 1966084
  40.6 2.2 collective-permute-start.3
  42.8 6.9 %copy-start.9 = (bf16[4,128,640]{2,1,0:T(8,128)(2,1)}, bf16[4,128,640]{2,1,0:T(8,128)(2,1)S(1)}, u32[]{:S(2)}) copy-start(bf16[4,128,640]{2,1,0:T(8,128)(2,1)S(1)} %collective-permute-done.3.refs_1_) | copy-start | bytes 1966084
  61.3 10.4 %collective-permute-start.6 = (bf16[1024,128]{1,0:T(8,128)(2,1)}, bf16[1024,128]{1,0:T(8,128)(2,1)S(1)}, u32[]{:S(2)}, u32[]{:S(2)}) collective-permute-start(bf16[1024,128]{1,0:T(8,128)(2,1)} %get-tuple-element.60), channel_id=1, source_target_pairs={{0,3},{1,2},{2,1},{3,0},{4,7},{5,6},{6,5},{7,4},{8,11},{9,10},{10,... | collective-permute-start | bytes 786440 | tf_op jit(solution)/shard_map/ppermute | solution.py:651
  62.8 13.3 %collective-permute-start.5 = (bf16[1024,128]{1,0:T(8,128)(2,1)}, bf16[1024,128]{1,0:T(8,128)(2,1)S(1)}, u32[]{:S(2)}, u32[]{:S(2)}) collective-permute-start(bf16[1024,128]{1,0:T(8,128)(2,1)} %get-tuple-element.60), channel_id=1, source_target_pairs={{0,2},{1,3},{2,0},{3,1},{4,6},{5,7},{6,4},{7,5},{8,10},{9,11},{10,... | collective-permute-start | bytes 786440 | tf_op jit(solution)/shard_map/ppermute | solution.py:651
  64.3 11.9 %collective-permute-start.4 = (bf16[1024,128]{1,0:T(8,128)(2,1)}, bf16[1024,128]{1,0:T(8,128)(2,1)S(1)}, u32[]{:S(2)}, u32[]{:S(2)}) collective-permute-start(bf16[1024,128]{1,0:T(8,128)(2,1)} %get-tuple-element.60), channel_id=1, source_target_pairs={{0,1},{1,0},{2,3},{3,2},{4,5},{5,4},{6,7},{7,6},{8,9},{9,8},{10,11... | collective-permute-start | bytes 786440 | tf_op jit(solution)/shard_map/ppermute | solution.py:651
  92.3 30.7 %copy-start.17 = (s32[1,256]{1,0:T(1,128)S(1)}, s32[1,256]{1,0:T(1,128)}, u32[]{:S(2)}) copy-start(s32[1,256]{1,0:T(1,128)} %refs_2_.2) | copy-start | bytes 3076
  92.3 30.7 %copy-start.19 = (f32[1,128]{1,0:T(1,128)S(1)}, f32[1,128]{1,0:T(1,128)}, u32[]{:S(2)}) copy-start(f32[1,128]{1,0:T(1,128)} %get-tuple-element.71) | copy-start | bytes 1540
  92.3 53.5 %copy-start = (bf16[1,256,1024]{2,1,0:T(8,128)(2,1)S(1)}, bf16[1,256,1024]{2,1,0:T(8,128)(2,1)}, u32[]{:S(2)}) copy-start(bf16[1,256,1024]{2,1,0:T(8,128)(2,1)} %param.14) | copy-start | bytes 1572868
  92.3 53.5 %copy-start.1 = (bf16[1,256,1024]{2,1,0:T(8,128)(2,1)S(1)}, bf16[1,256,1024]{2,1,0:T(8,128)(2,1)}, u32[]{:S(2)}) copy-start(bf16[1,256,1024]{2,1,0:T(8,128)(2,1)} %param.15) | copy-start | bytes 1572868
  119.5 16.0 %collective-permute-start.9 = (bf16[256,1024]{1,0:T(8,128)(2,1)}, bf16[256,1024]{1,0:T(8,128)(2,1)S(1)}, u32[]{:S(2)}, u32[]{:S(2)}) collective-permute-start(bf16[256,1024]{1,0:T(8,128)(2,1)} %get-tuple-element.67), channel_id=1, source_target_pairs={{0,3},{1,2},{2,1},{3,0},{4,7},{5,6},{6,5},{7,4},{8,11},{9,10},{10,... | collective-permute-start | bytes 1572872 | tf_op jit(solution)/shard_map/ppermute | solution.py:651
  121.0 24.8 %collective-permute-start.8 = (bf16[256,1024]{1,0:T(8,128)(2,1)}, bf16[256,1024]{1,0:T(8,128)(2,1)S(1)}, u32[]{:S(2)}, u32[]{:S(2)}) collective-permute-start(bf16[256,1024]{1,0:T(8,128)(2,1)} %get-tuple-element.66), channel_id=1, source_target_pairs={{0,2},{1,3},{2,0},{3,1},{4,6},{5,7},{6,4},{7,5},{8,10},{9,11},{10,... | collective-permute-start | bytes 1572872 | tf_op jit(solution)/shard_map/ppermute | solution.py:651
  122.4 23.4 %collective-permute-start.7 = (bf16[256,1024]{1,0:T(8,128)(2,1)}, bf16[256,1024]{1,0:T(8,128)(2,1)S(1)}, u32[]{:S(2)}, u32[]{:S(2)}) collective-permute-start(bf16[256,1024]{1,0:T(8,128)(2,1)} %get-tuple-element.65), channel_id=1, source_target_pairs={{0,1},{1,0},{2,3},{3,2},{4,5},{5,4},{6,7},{7,6},{8,9},{9,8},{10,11... | collective-permute-start | bytes 1572872 | tf_op jit(solution)/shard_map/ppermute | solution.py:651
  147.6 27.2 %copy-start.2 = (bf16[256,1024]{1,0:T(8,128)(2,1)}, bf16[256,1024]{1,0:T(8,128)(2,1)S(1)}, u32[]{:S(2)}) copy-start(bf16[256,1024]{1,0:T(8,128)(2,1)S(1)} %multiply_convert_fusion.refs_7_.refs_0_) | copy-start | bytes 1572868
  147.6 14.9 %collective-permute-start.10 = (bf16[256,1024]{1,0:T(8,128)(2,1)S(1)}, bf16[256,1024]{1,0:T(8,128)(2,1)S(1)}, u32[]{:S(2)}, u32[]{:S(2)}) collective-permute-start(bf16[256,1024]{1,0:T(8,128)(2,1)S(1)} %multiply_convert_fusion.refs_7_.refs_0_), channel_id=1, source_target_pairs={{0,1},{1,0},{2,3},{3,2},{4,5},{5,4},{6,7},{7,6},{8,9},{9,8},{10,11... | collective-permute-start | bytes 1572872 | tf_op jit(solution)/shard_map/ppermute | solution.py:651
  149.1 24.8 %collective-permute-start.11 = (bf16[256,1024]{1,0:T(8,128)(2,1)S(1)}, bf16[256,1024]{1,0:T(8,128)(2,1)S(1)}, u32[]{:S(2)}, u32[]{:S(2)}) collective-permute-start(bf16[256,1024]{1,0:T(8,128)(2,1)S(1)} %multiply_convert_fusion.refs_7_.refs_0_), channel_id=1, source_target_pairs={{0,2},{1,3},{2,0},{3,1},{4,6},{5,7},{6,4},{7,5},{8,10},{9,11},{10,... | collective-permute-start | bytes 1572872 | tf_op jit(solution)/shard_map/ppermute | solution.py:651
  149.7 24.2 %collective-permute-start.12 = (bf16[256,1024]{1,0:T(8,128)(2,1)S(1)}, bf16[256,1024]{1,0:T(8,128)(2,1)S(1)}, u32[]{:S(2)}, u32[]{:S(2)}) collective-permute-start(bf16[256,1024]{1,0:T(8,128)(2,1)S(1)} %multiply_convert_fusion.refs_7_.refs_0_), channel_id=1, source_target_pairs={{0,3},{1,2},{2,1},{3,0},{4,7},{5,6},{6,5},{7,4},{8,11},{9,10},{10,... | collective-permute-start | bytes 1572872 | tf_op jit(solution)/shard_map/ppermute | solution.py:651
  162.5 12.3 %copy-start.4 = (bf16[256,1024]{1,0:T(8,128)(2,1)}, bf16[256,1024]{1,0:T(8,128)(2,1)S(1)}, u32[]{:S(2)}) copy-start(bf16[256,1024]{1,0:T(8,128)(2,1)S(1)} %collective-permute-done.10.refs_8_.refs_1_) | copy-start | bytes 1572868
  173.9 1.0 copy-start.5
  174.0 0.8 copy-start.6
  248.7 9.5 %collective-permute-start.13 = (bf16[1024,128]{1,0:T(8,128)(2,1)}, bf16[1024,128]{1,0:T(8,128)(2,1)S(1)}, u32[]{:S(2)}, u32[]{:S(2)}) collective-permute-start(bf16[1024,128]{1,0:T(8,128)(2,1)} %get-tuple-element.76.refs_1_), channel_id=1, source_target_pairs={{0,1},{1,0},{2,3},{3,2},{4,5},{5,4},{6,7},{7,6},{8,9},{9,8},{10,11... | collective-permute-start | bytes 786440 | tf_op jit(solution)/shard_map/ppermute | solution.py:651
  249.5 12.4 %collective-permute-start.14 = (bf16[1024,128]{1,0:T(8,128)(2,1)}, bf16[1024,128]{1,0:T(8,128)(2,1)S(1)}, u32[]{:S(2)}, u32[]{:S(2)}) collective-permute-start(bf16[1024,128]{1,0:T(8,128)(2,1)} %get-tuple-element.76.refs_1_), channel_id=1, source_target_pairs={{0,2},{1,3},{2,0},{3,1},{4,6},{5,7},{6,4},{7,5},{8,10},{9,11},{10,... | collective-permute-start | bytes 786440 | tf_op jit(solution)/shard_map/ppermute | solution.py:651
  250.8 11.1 %collective-permute-start.15 = (bf16[1024,128]{1,0:T(8,128)(2,1)}, bf16[1024,128]{1,0:T(8,128)(2,1)S(1)}, u32[]{:S(2)}, u32[]{:S(2)}) collective-permute-start(bf16[1024,128]{1,0:T(8,128)(2,1)} %get-tuple-element.76.refs_1_), channel_id=1, source_target_pairs={{0,3},{1,2},{2,1},{3,0},{4,7},{5,6},{6,5},{7,4},{8,11},{9,10},{10,... | collective-permute-start | bytes 786440 | tf_op jit(solution)/shard_map/ppermute | solution.py:651
  258.3 3.6 %copy-start.10 = (bf16[1024,128]{1,0:T(8,128)(2,1)}, bf16[1024,128]{1,0:T(8,128)(2,1)S(1)}, u32[]{:S(2)}) copy-start(bf16[1024,128]{1,0:T(8,128)(2,1)S(1)} %collective-permute-done.13.refs_2_) | copy-start | bytes 786436
  261.9 0.7 copy-start.11
  261.9 0.8 copy-start.12
  275.2 8.6 %copy-start.24 = (f32[1,128]{1,0:T(1,128)S(1)}, f32[1,128]{1,0:T(1,128)}, u32[]{:S(2)}) copy-start(f32[1,128]{1,0:T(1,128)} %get-tuple-element.85) | copy-start | bytes 1540
  280.2 3.6 %collective-permute-start.16 = (bf16[4,176,512]{2,1,0:T(8,128)(2,1)}, bf16[4,176,512]{2,1,0:T(8,128)(2,1)S(1)}, u32[]{:S(2)}, u32[]{:S(2)}) collective-permute-start(bf16[4,176,512]{2,1,0:T(8,128)(2,1)} %get-tuple-element.90), channel_id=1, source_target_pairs={{0,4},{4,0},{8,12},{12,8},{16,20},{20,16},{24,28},{28,24},{1,5},{5... | collective-permute-start | bytes 2162696 | tf_op jit(solution)/shard_map/ppermute | solution.py:651
  280.3 15.9 %collective-permute-start.22 = (bf16[256,1024]{1,0:T(8,128)(2,1)}, bf16[256,1024]{1,0:T(8,128)(2,1)S(1)}, u32[]{:S(2)}, u32[]{:S(2)}) collective-permute-start(bf16[256,1024]{1,0:T(8,128)(2,1)} %get-tuple-element.95), channel_id=1, source_target_pairs={{0,3},{1,2},{2,1},{3,0},{4,7},{5,6},{6,5},{7,4},{8,11},{9,10},{10,... | collective-permute-start | bytes 1572872 | tf_op jit(solution)/shard_map/ppermute | solution.py:651
  281.8 25.1 %collective-permute-start.21 = (bf16[256,1024]{1,0:T(8,128)(2,1)}, bf16[256,1024]{1,0:T(8,128)(2,1)S(1)}, u32[]{:S(2)}, u32[]{:S(2)}) collective-permute-start(bf16[256,1024]{1,0:T(8,128)(2,1)} %get-tuple-element.94), channel_id=1, source_target_pairs={{0,2},{1,3},{2,0},{3,1},{4,6},{5,7},{6,4},{7,5},{8,10},{9,11},{10,... | collective-permute-start | bytes 1572872 | tf_op jit(solution)/shard_map/ppermute | solution.py:651
  283.3 23.7 %collective-permute-start.20 = (bf16[256,1024]{1,0:T(8,128)(2,1)}, bf16[256,1024]{1,0:T(8,128)(2,1)S(1)}, u32[]{:S(2)}, u32[]{:S(2)}) collective-permute-start(bf16[256,1024]{1,0:T(8,128)(2,1)} %get-tuple-element.93), channel_id=1, source_target_pairs={{0,1},{1,0},{2,3},{3,2},{4,5},{5,4},{6,7},{7,6},{8,9},{9,8},{10,11... | collective-permute-start | bytes 1572872 | tf_op jit(solution)/shard_map/ppermute | solution.py:651
  283.9 23.1 %copy-start.7 = (bf16[256,1024]{1,0:T(8,128)(2,1)S(1)}, bf16[256,1024]{1,0:T(8,128)(2,1)}, u32[]{:S(2)}) copy-start(bf16[256,1024]{1,0:T(8,128)(2,1)} %get-tuple-element.92) | copy-start | bytes 1572868
  283.9 23.1 %copy-start.16 = (f32[1,1024]{1,0:T(1,128)S(1)}, f32[1,1024]{1,0:T(1,128)}, u32[]{:S(2)}) copy-start(f32[1,1024]{1,0:T(1,128)} %get-tuple-element.96) | copy-start | bytes 12292
  285.7 23.6 %collective-permute-start.19 = (bf16[176,512]{1,0:T(8,128)(2,1)S(1)}, bf16[176,512]{1,0:T(8,128)(2,1)S(1)}, u32[]{:S(2)}, u32[]{:S(2)}) collective-permute-start(bf16[176,512]{1,0:T(8,128)(2,1)S(1)} %get-tuple-element.143), channel_id=1, source_target_pairs={{0,24},{4,28},{8,16},{12,20},{16,8},{20,12},{24,0},{28,4},{1,25},{... | collective-permute-start | bytes 540680 | tf_op jit(solution)/shard_map/ppermute | solution.py:651
  289.2 20.2 %collective-permute-start.18 = (bf16[176,512]{1,0:T(8,128)(2,1)S(1)}, bf16[176,512]{1,0:T(8,128)(2,1)S(1)}, u32[]{:S(2)}, u32[]{:S(2)}) collective-permute-start(bf16[176,512]{1,0:T(8,128)(2,1)S(1)} %get-tuple-element.142), channel_id=1, source_target_pairs={{0,16},{4,20},{8,24},{12,28},{16,0},{20,4},{24,8},{28,12},{1,17},{... | collective-permute-start | bytes 540680 | tf_op jit(solution)/shard_map/ppermute | solution.py:651
  296.2 13.2 %collective-permute-start.17 = (bf16[176,512]{1,0:T(8,128)(2,1)S(1)}, bf16[176,512]{1,0:T(8,128)(2,1)S(1)}, u32[]{:S(2)}, u32[]{:S(2)}) collective-permute-start(bf16[176,512]{1,0:T(8,128)(2,1)S(1)} %get-tuple-element.141), channel_id=1, source_target_pairs={{0,8},{4,12},{8,0},{12,4},{16,24},{20,28},{24,16},{28,20},{1,9},{5... | collective-permute-start | bytes 540680 | tf_op jit(solution)/shard_map/ppermute | solution.py:651
  309.6 7.1 %slice-start = ((f32[1,256,512]{2,1,0:T(8,128)}), f32[1,128,512]{2,1,0:T(8,128)S(1)}, s32[]{:S(2)}) async-start(f32[1,256,512]{2,1,0:T(8,128)} %reduce-scatter.2.cloned.1.call-done), calls=%async_computation.6 | async-start | bytes 524288 | tf_op jit(solution)/shard_map/slice | solution.py:989
  311.3 9.2 %all-to-all-start.1 = ((bf16[4,32,1024]{2,1,0:T(8,128)(2,1)}), bf16[4,32,1024]{2,1,0:T(8,128)(2,1)S(1)}, u32[]{:S(2)}, u32[]{:S(2)}) async-start(bf16[4,32,1024]{2,1,0:T(8,128)(2,1)} %pad_maximum_fusion.2), calls=%async_computation.2 | async-start | bytes 524288 | tf_op jit(solution)/shard_map/all_to_all | solution.py:985
  320.5 0.7 copy-start.8
Sparse Core Ops, SparseCore 0:
  10.5 39.1 all-gather.4
  51.8 29.0 all-gather.6
  200.5 49.9 reduce-scatter.1

commit v3 on v2

--- a/solution.py
+++ b/solution.py
@@ -7,7 +7,8 @@
 
 PIECE = 256
 BLOCK = 16
-ROWS = 128
+ROWS = 256
+HALF = 128
 LOG2E = 1.4426950408889634
 LN2 = 0.6931471805599453
 NEVER = 1e9
@@ -158,18 +159,25 @@
 
 
 def ahead_kernel(
-    local, me_ref, proj_ref, act_ref, normed_ref, g_ref, vec_ref, second_ref,
-    hp_ref, mixed_ref, gate_ref, gated_ref, wgate_ref, outw_ref,
-    *refs,
+    first, places, per, local, me_ref, *refs,
 ):
-    branch_refs = refs[:-7]
-    carry_ref, u_ref, step_ref, col_ref, diag_ref, s_ref, y_ref = refs[-7:]
+    proj_ref, act_ref, normed_ref, g_ref, vec_ref, enter_ref = refs[:6]
+    if first:
+        wgate_ref, outw_ref = refs[6:8]
+        hp_ref, mixed_ref, gate_ref, gated_ref, leave_ref = refs[-8 - places - 5 : -8 - places]
+    else:
+        second_ref = refs[6]
+        hp_ref, mixed_ref, gate_ref, gated_ref, leave_ref, wgate_ref, outw_ref = refs[-8 - places - 7 : -8 - places]
+    branch_refs = refs[-8 - places : -8]
+    carry_ref, u_ref, step_ref, col_ref, diag_ref, s_ref, y_ref, out_ref = refs[-8:]
     rows, c = act_ref.shape
     n = carry_ref.shape[0]
 
     @pl.when(pl.program_id(0) == 0)
     def _():
-        carry_ref[...] = jnp.zeros_like(carry_ref)
+        carry_ref[...] = enter_ref[...]
+        if first:
+            return
         blocks = second_ref.shape[0]
         lines, own = wgate_ref.shape[0] // blocks, outw_ref.shape[0] // blocks
         for b in range(blocks):
@@ -217,27 +225,33 @@
     gate_ref[...] = gate
     gated = (mixed * (gate * sigmoid(gate))).astype(bf16)
     gated_ref[...] = gated.T
-    write_slot(branch_refs, slot_of(me_ref, local), dot(gated, outw_ref[...]).astype(bf16))
+    out_ref[...] = dot(gated, outw_ref[...]).astype(bf16)
+    write_rows(branch_refs, me_ref, places, per, local, out_ref)
+    leave_ref[...] = carry_ref[...]
 
 
 def piece_grad_kernel(
-    local, me_ref, proj_ref, act_ref, mixed_ref, gate_ref, vec_ref, outw_ref, *refs,
+    first, places, per, local, me_ref, *refs,
 ):
-    db_refs = refs[:-7]
-    q_ref, dm_ref, dg_ref, sgrad_ref, carry_ref, stepm_ref, col_ref = refs[-7:]
+    proj_ref, act_ref, mixed_ref, gate_ref, vec_ref, outw_ref, enter_ref, before_ref = refs[:8]
+    db_refs = refs[8 : 8 + places]
+    q_ref, dm_ref, dg_ref, db_ref, sgrad_ref, leave_ref = refs[-9:-3]
+    carry_ref, stepm_ref, col_ref = refs[-3:]
     rows, c = act_ref.shape
     n = carry_ref.shape[0]
 
     @pl.when(pl.program_id(0) == 0)
     def _():
-        carry_ref[...] = jnp.zeros_like(carry_ref)
-        sgrad_ref[...] = jnp.zeros_like(sgrad_ref)
+        carry_ref[...] = enter_ref[...]
+        sgrad_ref[...] = before_ref[...]
 
     proj = proj_ref[...]
     _, pre = dt_of(proj, vec_ref, INTO)
     stepm_ref[...] = jnp.where(proj[:, CARRY : CARRY + 1] > 0.5, softplus(pre), NEVER)
     columns(proj.T, OUT, n, col_ref)
-    dgated = dot_t(read_slot(db_refs, slot_of(me_ref, local)), outw_ref[...])
+    db = read_rows(db_refs, me_ref, places, per, local)
+    db_ref[...] = db
+    dgated = dot_t(db, outw_ref[...])
     gate = gate_ref[...]
     s = sigmoid(gate)
     dm = dgated * (gate * s)
@@ -247,7 +261,9 @@
     sgrad_ref[...] += jnp.sum(dm * act_ref[...].astype(f32), axis=0, keepdims=True)
     r2 = rates_of(vec_ref, n)
 
-    def block(j, w):
+    chunk = first + pl.program_id(0)
+
+    def scan(j, w):
         read = col_ref[j]
         for tt in range(BLOCK):
             t = j * BLOCK + tt
@@ -256,7 +272,16 @@
             w = q + row_of(dm_ref, t, n) * col_of(read, tt, c)
         return w
 
+    def fill(j, w):
+        at = pl.ds(pl.multiple_of(j * BLOCK * n, BLOCK * n), BLOCK * n)
+        q_ref[at, :] = jnp.zeros((BLOCK * n, c), bf16)
+        return row_of(dm_ref, j * BLOCK + BLOCK - 1, n) * col_of(col_ref[j], BLOCK - 1, c)
+
+    def block(j, w):
+        return lax.cond(me_ref[1 + chunk * (rows // BLOCK) + j] > 0, scan, fill, j, w)
+
     carry_ref[...] = lax.fori_loop(0, rows // BLOCK, block, carry_ref[...])
+    leave_ref[...] = carry_ref[...]
 
 
 def state_grad_kernel(
@@ -422,11 +447,38 @@
     return (step // (local // ROWS)) ^ me_ref[0]
 
 
-def read_slot(refs, slot):
-    value = refs[0][...]
-    for k in range(1, len(refs)):
-        value = jnp.where(slot == k, refs[k][...], value)
-    return value
+def read_rows(refs, me_ref, places, per, local):
+    step = pl.program_id(0)
+    each = ROWS // per
+    at = pl.ds(pl.multiple_of(step // (local // ROWS) * per, per), per)
+    pieces = []
+    for p in range(each):
+        j = step % (local // ROWS) * each + p
+        if len(refs) == 1:
+            pieces.append(refs[0][j, at, :])
+            continue
+        value = refs[0][at, :]
+        for k in range(1, places):
+            value = jnp.where(j ^ me_ref[0] == k, refs[k][at, :], value)
+        pieces.append(value)
+    return jnp.concatenate(pieces, axis=0)
+
+
+def write_rows(refs, me_ref, places, per, local, from_ref):
+    step = pl.program_id(0)
+    each = ROWS // per
+    at = pl.ds(pl.multiple_of(step // (local // ROWS) * per, per), per)
+    sub = step % (local // ROWS)
+    if len(refs) == 1:
+        for p in range(each):
+            refs[0][sub * each + p, at, :] = from_ref[p * per : (p + 1) * per, :]
+        return
+    for k, ref in enumerate(refs):
+        j = k ^ me_ref[0]
+
+        @pl.when(j // each == sub)
+        def _(ref=ref, j=j):
+            ref[at, :] = from_ref[pl.ds(pl.multiple_of(j % each * per, per), per), :]
 
 
 def write_slot(refs, slot, value):
@@ -440,10 +492,14 @@
             ref[...] = value
 
 
-def call(kernel, me, ins, outs, scratch, total, local, reverse=False):
-    steps = total // ROWS
-    per = local // ROWS
-    turn = (lambda i: steps - 1 - i) if reverse else (lambda i: i)
+def call(kernel, me, ins, outs, scratch, total, local, reverse=False, first=0, count=None, size=ROWS):
+    steps = total // size
+    per = local // size
+    turn = (lambda i: steps - 1 - i) if reverse else (lambda i: i + first)
+    aliases = {}
+    for index, (_, kind) in enumerate(ins):
+        if kind == "o":
+            aliases[index + 1] = len(aliases)
 
     def slot_map(k):
         def index(i, me_ref):
@@ -458,18 +514,20 @@
 
     def spec(shape, kind):
         if isinstance(kind, int):
-            return pl.BlockSpec((ROWS, shape[1]), slot_map(kind))
+            return pl.BlockSpec((size, shape[1]), slot_map(kind))
         if kind == "f":
             return pl.BlockSpec(shape, lambda i, me_ref: (0,) * len(shape))
+        if kind == "o":
+            return pl.BlockSpec(memory_space=pl.ANY)
         if kind == "c":
             return pl.BlockSpec(
-                (shape[0], ROWS), lambda i, me_ref: (0, ((turn(i) // per) ^ me_ref[0]) * per + turn(i) % per)
+                (shape[0], size), lambda i, me_ref: (0, turn(i))
             )
         if kind == "y":
-            return pl.BlockSpec((None, ROWS, shape[2]), lambda i, me_ref: (turn(i) // per, turn(i) % per, 0))
+            return pl.BlockSpec((None, size, shape[2]), lambda i, me_ref: (turn(i) // per, turn(i) % per, 0))
         if kind == "x":
             return pl.BlockSpec(
-                (None, ROWS, shape[2]), lambda i, me_ref: ((turn(i) // per) ^ me_ref[0], turn(i) % per, 0)
+                (None, size, shape[2]), lambda i, me_ref: ((turn(i) // per) ^ me_ref[0], turn(i) % per, 0)
             )
         return pl.BlockSpec((shape[0] // steps, shape[1]), lambda i, me_ref: (turn(i), 0))
 
@@ -478,11 +536,12 @@
         out_shape=[jax.ShapeDtypeStruct(s, d) for s, d, _ in outs],
         grid_spec=pltpu.PrefetchScalarGridSpec(
             num_scalar_prefetch=1,
-            grid=(steps,),
+            grid=(count or steps,),
             in_specs=[spec(a.shape, k) for a, k in ins],
             out_specs=[spec(s, k) for s, _, k in outs],
             scratch_shapes=scratch,
         ),
+        input_output_aliases=aliases,
         compiler_params=pltpu.CompilerParams(dimension_semantics=("arbitrary",), vmem_limit_bytes=60 << 20),
     )(me, *[a for a, _ in ins])
 
@@ -768,7 +827,8 @@
     me = place.astype(jnp.int32).reshape(1)
     tok = tokens.reshape(rows, width)
 
-    flags = jnp.pad(piece_starts.astype(bf16), ((0, 15), (0, width - rows)))
+    flags = jnp.concatenate([piece_starts, valid_rows], axis=0).astype(bf16)
+    flags = jnp.pad(flags, ((0, 14), (0, width - rows)))
     everything = lax.all_gather(jnp.concatenate([tok, flags], axis=0), "seq")
     split = split_columns(in_weight, norm_gain.reshape(1, depth), valid_rows, seqs, batches, own)
     split = lax.all_to_all(split, "seq", 0, 0).reshape(lines, 2 * chans + LANES)
@@ -801,7 +861,7 @@
         jnp.concatenate([me] + [p.astype(jnp.int32).reshape(1) for p in places]),
         [(everything, "y")] + [(block, "f") for block in blocks],
         [
-            ((seqs, rows, width), bf16, "x"),
+            ((total, width), bf16, "t"),
             ((width, total), bf16, "c"),
             low_tile,
             tile,
@@ -822,7 +882,9 @@
     running = jnp.cumsum(starts)
     lagged = jnp.concatenate([jnp.zeros((PIECE,), f32), running[: total - PIECE]])
     carry_on = jnp.where(running - lagged > 0.5, 1.0 - starts, 0.0)
+    flags = jnp.max(carry_on.reshape(total // BLOCK, BLOCK), axis=1).astype(jnp.int32)
     proj = added(share_parts(proj, "seq"))
+    me = jnp.concatenate([me, flags])
     proj = jnp.where(jnp.arange(LANES)[None, :] == CARRY, carry_on[:, None], proj)
     groups = (ROWS // BLOCK, states, BLOCK)
     (g,) = call(
@@ -840,71 +902,115 @@
         rows,
         reverse=True,
     )
-    hp, mixed, gate, gated_t, w_gate, out_w, *branch = call(
-        lambda *refs: ahead_kernel(rows, *refs),
-        me,
-        [(proj, "t"), (act, "t"), (normed, "x"), (g, "t"), (vec, "f"), (second, "f")],
-        [
-            state,
-            tile,
-            tile,
-            ((chans, total), bf16, "c"),
-            ((width, chans), bf16, "f"),
-            ((chans, width), bf16, "f"),
-        ]
-        + slots_out(seqs, rows, width),
-        [
-            pltpu.VMEM((states, chans), f32),
-            pltpu.VMEM((ROWS, chans), f32),
-            pltpu.VMEM((ROWS, chans), f32),
-            pltpu.VMEM(groups, f32),
-            pltpu.VMEM((2, ROWS + BLOCK, BLOCK * states), bf16),
-            pltpu.VMEM((BLOCK * states, chans), bf16),
-            pltpu.VMEM((ROWS + BLOCK, chans), f32),
-        ],
-        total,
-        rows,
-    )
-    tok_f = tok.astype(f32)
-    valid_f = valid_rows.reshape(rows, 1).astype(f32)
-    result = tok_f + added(scatter_parts(branch, "seq"))
-    output = result.astype(bf16)
-    misfit = result - teacher.reshape(rows, width).astype(f32)
-    squares = jnp.sum(valid_f * misfit * misfit, axis=0, keepdims=True)
+    halves = 2
+    per = rows // seqs
+    held = seqs // halves * per
+    count = total // ROWS // halves
+    places = seqs if seqs <= 4 else 1
+    if seqs <= 4:
+        messages = [((held, width), bf16, "f")] * seqs
+    else:
+        messages = [((seqs, held, width), bf16, "f")]
+    by_time = [state, tile, tile, ((chans, total), bf16, "c")]
+    weights = [((width, chans), bf16, "f"), ((chans, width), bf16, "f")]
+    mine = lambda v: lax.dynamic_slice_in_dim(v, lax.axis_index("seq") * per, per, axis=1)
+    tok_v = mine(everything[:, :rows]).astype(f32)
+    valid_v = mine(everything[:, rows + 1, :rows].reshape(seqs, rows, 1)).astype(f32)
+    teacher, g = lax.optimization_barrier((teacher, g))
+    teach_v = lax.all_to_all(teacher.reshape(seqs, per, width), "seq", 0, 0).astype(f32)
+    enter = jnp.zeros((states, chans), f32)
+    kept = []
+    branches = []
+    for half in range(halves):
+        out = call(
+            lambda *refs, half=half: ahead_kernel(half, places, per, rows, *refs),
+            me,
+            [(proj, "t"), (act, "t"), (normed, "t"), (g, "t"), (vec, "f"), (enter, "f")]
+            + ([(w_gate, "f"), (out_w, "f")] if half else [(second, "f")])
+            + [(array, "o") for array in kept],
+            by_time + [((states, chans), f32, "f")] + ([] if half else weights) + messages,
+            [
+                pltpu.VMEM((states, chans), f32),
+                pltpu.VMEM((ROWS, chans), f32),
+                pltpu.VMEM((ROWS, chans), f32),
+                pltpu.VMEM(groups, f32),
+                pltpu.VMEM((2, ROWS + BLOCK, BLOCK * states), bf16),
+                pltpu.VMEM((BLOCK * states, chans), bf16),
+                pltpu.VMEM((ROWS + BLOCK, chans), f32),
+                pltpu.VMEM((ROWS, width), bf16),
+            ],
+            total,
+            rows,
+            first=half * count,
+            count=count,
+        )
+        kept, enter = out[:4], out[4]
+        if not half:
+            w_gate, out_w = out[5:7]
+        branches.append(out[-places:])
+    hp, mixed, gate, gated_t = kept
+
+    factor = 2.0 * (total * batches) / total_valid
+    squares = jnp.zeros((1, width), f32)
+    results, d_branches = [], []
+    for half in range(halves):
+        at = slice(half * (seqs // halves), (half + 1) * (seqs // halves))
+        flat_half = lambda v: v[at].reshape(held, v.shape[2])
+        result = flat_half(tok_v) + added(scatter_parts(branches[half], "seq"))
+        results.append(result.astype(bf16).reshape(seqs // halves, per, width))
+        misfit = result - flat_half(teach_v)
+        valid_f = flat_half(valid_v)
+        squares = squares + jnp.sum(valid_f * misfit * misfit, axis=0, keepdims=True)
+        d_branches.append(gather_parts((factor * valid_f * misfit).astype(bf16), "seq"))
     part = LANES - CARRY
     square_sum = squares[:, :LANES]
     for k in range(LANES, width, LANES):
         square_sum = square_sum + squares[:, k : k + LANES]
     square_sum = sum(square_sum[:, k : k + part] for k in range(0, LANES, part))
     square_sum = jnp.pad(square_sum, ((0, 0), (CARRY, 0)))
-    d_result = 2.0 * (total * batches) / total_valid * valid_f * misfit
-
-    d_branch = gather_parts(d_result.astype(bf16), "seq")
-    q, d_mixed, d_gate, skip_grad = call(
-        lambda *refs: piece_grad_kernel(rows, *refs),
-        me,
-        [
-            (proj, "t"),
-            (act, "t"),
-            (mixed, "t"),
-            (gate, "t"),
-            (vec, "f"),
-            (out_w, "f"),
-        ]
-        + slots_in(d_branch),
-        [state, tile, ((seqs, rows, chans), bf16, "x"), ((1, chans), f32, "f")],
-        [pltpu.VMEM((states, chans), f32), pltpu.VMEM((ROWS, chans), f32), pltpu.VMEM(groups, f32)],
-        total,
-        rows,
-    )
-    flat = lambda v: v.reshape(total, v.shape[2])
-    branches = d_branch if seqs <= 4 else [flat(d_branch[0])]
+
+    kept = []
+    enter = jnp.zeros((states, chans), f32)
+    skip_grad = jnp.zeros((1, chans), f32)
+    for half in range(halves):
+        *kept, skip_grad, enter = call(
+            lambda *refs, half=half: piece_grad_kernel(half * count, places, per, rows, *refs),
+            me,
+            [
+                (proj, "t"),
+                (act, "t"),
+                (mixed, "t"),
+                (gate, "t"),
+                (vec, "f"),
+                (out_w, "f"),
+                (enter, "f"),
+                (skip_grad, "f"),
+            ]
+            + [(part, "f") for part in d_branches[half]]
+            + [(array, "o") for array in kept],
+            [
+                state,
+                tile,
+                low_tile,
+                ((total, width), bf16, "t"),
+                ((1, chans), f32, "f"),
+                ((states, chans), f32, "f"),
+            ],
+            [pltpu.VMEM((states, chans), f32), pltpu.VMEM((ROWS, chans), f32), pltpu.VMEM(groups, f32)],
+            total,
+            rows,
+            first=half * count,
+            count=count,
+        )
+    q, d_mixed, d_gate, d_branch = kept
+    output = lax.all_to_all(jnp.concatenate(results, axis=0), "seq", 0, 0).reshape(rows, width)
+    d_result = lax.dynamic_slice_in_dim(d_branch, lax.axis_index("seq") * rows, rows, axis=0).astype(f32)
     early_sum = by_blocks(
         early_grad_kernel,
         batches,
         own,
         [normed_t, gated_t],
-        [flat(d_gate)] + branches,
+        [d_gate, d_branch],
         lines + own * width // chans,
         chans,
     )
@@ -917,20 +1023,21 @@
         [tile, ((total, LANES), bf16, "t"), ((LANES, chans), f32, "f")],
         [
             pltpu.VMEM((states, chans), f32),
-            pltpu.VMEM((ROWS, chans), f32),
-            pltpu.VMEM((ROWS, chans), f32),
-            pltpu.VMEM(groups, f32),
-            pltpu.VMEM((ROWS + BLOCK, BLOCK * states), bf16),
+            pltpu.VMEM((HALF, chans), f32),
+            pltpu.VMEM((HALF, chans), f32),
+            pltpu.VMEM((HALF // BLOCK, states, BLOCK), f32),
+            pltpu.VMEM((HALF + BLOCK, BLOCK * states), bf16),
         ]
         + [pltpu.VMEM((BLOCK * states, chans), bf16)] * 3
         + [
             pltpu.VMEM((BLOCK * states, 2 * min(chans, 2 * LANES)), bf16),
             pltpu.VMEM((BLOCK * states, LANES), bf16),
         ]
-        + [pltpu.VMEM((ROWS + 2 * BLOCK, chans), f32)] * 2
-        + [pltpu.VMEM((ROWS + 2 * BLOCK, LANES), f32)],
+        + [pltpu.VMEM((HALF + 2 * BLOCK, chans), f32)] * 2
+        + [pltpu.VMEM((HALF + 2 * BLOCK, LANES), f32)],
         total,
         rows,
+        size=HALF,
         reverse=True,
     )
     d_proj = share_parts(d_proj, "seq")
@@ -944,7 +1051,7 @@
             (conv_pre, "t"),
             (stream, "t"),
             (act, "t"),
-            (d_gate, "x"),
+            (d_gate, "t"),
             (vec, "f"),
             (xproj, "f"),
             (w_stream, "f"),
@@ -953,7 +1060,7 @@
         ],
         slots
         + [
-            ((seqs, rows, chans), bf16, "x"),
+            low_tile,
             ((batches * packed, chans), f32, "f"),
             ((BLOCK, chans), bf16, "f"),
             ((1, LANES), f32, "f"),
@@ -969,11 +1076,11 @@
         reverse=True,
     )
     if batches <= 8:
-        mine, theirs = late_pairs(normed_t, small, flat(d_stream), sent, batches, lines + packed, chans)
+        mine, theirs = late_pairs(normed_t, small, d_stream, sent, batches, lines + packed, chans)
         late, square_sum, waiting = scatter_batch(mine, theirs, seq_sum)
     else:
         late = by_blocks(
-            late_grad_kernel, batches, own, [normed_t, small], [flat(d_stream)], lines + packed, chans
+            late_grad_kernel, batches, own, [normed_t, small], [d_stream], lines + packed, chans
         )
         waiting = late
         late = lax.psum_scatter(late, "batch", scatter_dimension=0)
@@ -987,6 +1094,7 @@
         in_out, late[lines:], in_weight, norm_gain.reshape(1, depth), batches, own
     )
     out_out = early[lines:].reshape(-1, own, chans).transpose(1, 0, 2).reshape(own, width)
+    tok_f = tok.astype(f32)
     mean_sq = jnp.mean(tok_f * tok_f, axis=-1, keepdims=True)
     root_inv = lax.rsqrt(mean_sq + 1e-05)
     own_unit = tok_f * root_inv

time: 334 us -> 322 us (0.964)
  waiting for transfers between devices: 108 us -> 62.6 us
  starting transfers between devices: 35.9 us -> 55.5 us
  Pallas kernels: 147 us -> 154 us
  local copies, waits for them, and re-layouts: 8.65 us -> 13.4 us
    ppermute x23 -> x29, waiting for transfers between devices: 91.9 us -> 47.2 us  [partner(): lax.ppermute(value, axis, [(i, i ^ k) for i in range(lax.axis_size(axis))])]
    ppermute x23 -> x29, starting transfers between devices: 27.2 us -> 39.5 us  [partner(): lax.ppermute(value, axis, [(i, i ^ k) for i in range(lax.axis_size(axis))])]
    all_to_all x0 -> x2, starting transfers between devices: none -> 7.16 us  [the longest x1 3.69 us: body(): lax.all_to_all(jnp.concatenate(results, axis=0), 'seq', 0, 0)]
    pallas_call x6 -> x8, Pallas kernels: 132 us -> 138 us  [call(): pl.pallas_call(kernel, out_shape=[jax.ShapeDtypeStruct(s, d) for s, d, _...]
  transfers between devices with their start and end apart: 28 -> 36, of which waited for: 16 -> 14; matrix products, arithmetic and copies ran while one was open for 4% -> 6% of each run, Pallas kernels for 28% -> 42%
where the time goes in v3:
time: 322 us; the launch traced here: 321 us
  Pallas kernels  154 us (48%)
  waiting for transfers between devices  62.6 us (19%)
  starting transfers between devices  55.5 us (17%)
  other arithmetic  17.7 us (5%)
  between operations  17.7 us (5%)
  local copies, waits for them, and re-layouts  13.4 us (4%)
    pallas_call x8, Pallas kernels, call(): pl.pallas_call(kernel, out_shape=[jax.ShapeDtypeStruct(s, d) for s, d, _...  138 us
    ppermute x29, waiting for transfers between devices, partner(): lax.ppermute(value, axis, [(i, i ^ k) for i in range(lax.axis_size(axis))])  47.2 us
    ppermute x29, starting transfers between devices, partner(): lax.ppermute(value, axis, [(i, i ^ k) for i in range(lax.axis_size(axis))])  39.5 us
    all_gather x1, waiting for transfers between devices, body(): everything = lax.all_gather(jnp.concatenate([tok, flags], axis=0), 'seq')  7.87 us
    pallas_call x1, Pallas kernels, by_blocks(): pl.pallas_call(kernel, out_shape=jax.ShapeDtypeStruct((batches, rows, cha...  6.8 us
  transfers between devices with their start and end apart: 36, of which 14 were waited for; matrix products, arithmetic and copies ran while one was open for 6% of the time, Pallas kernels for 42%

profile of v3, /device:TPU:0, one launch (start us, length us, event | category | flops | bytes accessed | tf_op | source)
XLA Modules:
  0.0 320.8 jit_solution(10673359234170608742)
XLA Ops:
  8.7 1.9 pad_maximum_fusion.1
  10.6 1.8 shard_map.237
  12.5 5.2 %all-to-all-start = ((bf16[4,32,1152]{2,1,0:T(8,128)(2,1)}), bf16[4,32,1152]{2,1,0:T(8,128)(2,1)S(1)}, u32[]{:S(2)}, u32[]{:S(2)}) async-start(bf16[4,32,1152]{2,1,0:T(8,128)(2,1)} %shard_map.237), calls=%async_computation | async-start | bytes 589824 | tf_op jit(solution)/shard_map/all_to_all | solution.py:834
  18.5 4.8 %all-to-all-done = bf16[4,32,1152]{2,1,0:T(8,128)(2,1)S(1)} async-done(((bf16[4,32,1152]{2,1,0:T(8,128)(2,1)}), bf16[4,32,1152]{2,1,0:T(8,128)(2,1)S(1)}, u32[]{:S(2)}, u32[]{:S(2)}) %all-to-all-start) | async-done | bytes 294944 | tf_op jit(solution)/shard_map/all_to_all | solution.py:834
  24.1 1.6 collective-permute-start
  25.7 2.6 collective-permute-start.1
  28.5 2.7 collective-permute-done
  31.2 8.6 %collective-permute-done.1 = bf16[128,640]{1,0:T(8,128)(2,1)S(1)} collective-permute-done((bf16[128,640]{1,0:T(8,128)(2,1)S(1)}, bf16[128,640]{1,0:T(8,128)(2,1)S(1)}, u32[]{:S(2)}, u32[]{:S(2)}) %collective-permute-start.1) | collective-permute-done | bytes 163872 | tf_op jit(solution)/shard_map/ppermute | solution.py:710
  40.6 1.4 collective-permute-done.3.refs_1_
  42.0 7.9 %all-gather.5.cloned.1.call-done = bf16[1088,1024]{1,0:T(8,128)(2,1)} async-done(((bf16[272,1024]{1,0:T(8,128)(2,1)}), bf16[1088,1024]{1,0:T(8,128)(2,1)}) %all-gather.5.cloned.1.call-update) | async-done | bytes 2228240 | tf_op jit(solution)/shard_map/all_gather | solution.py:832
  49.9 9.5 %shard_map.238 = (bf16[1024,1024]{1,0:T(8,128)(2,1)}, bf16[1024,1024]{1,0:T(8,128)(2,1)}, bf16[1024,512]{1,0:T(8,128)(2,1)}, f32[1024,512]{1,0:T(8,128)}, bf16[1...) custom-call(s32[9]{0:T(128)} %concatenate.66.me_ref, ...), custom_call_target="tpu_custom_call" | custom-call | tf_op jit(solution)/shard_map/pallas_call | solution.py:534
  59.5 1.5 collective-permute-start.4
  61.6 1.5 collective-permute-start.6
  63.0 1.5 slice.271
  68.2 1.2 dynamic-slice_convert_fusion
  69.4 5.2 %collective-permute-done.5 = bf16[1024,128]{1,0:T(8,128)(2,1)} collective-permute-done((bf16[1024,128]{1,0:T(8,128)(2,1)}, bf16[1024,128]{1,0:T(8,128)(2,1)}, u32[]{:S(2)}, u32[]{:S(2)}) %collective-permute-start.5) | collective-permute-done | bytes 262176 | tf_op jit(solution)/shard_map/ppermute | solution.py:710
  74.7 2.0 add_select_fusion.proj_ref.refs_1_
  76.7 14.8 %shard_map.239.refs_4_.g_ref = bf16[16384,512]{1,0:T(8,128)(2,1)} custom-call(s32[65]{0:T(128)} %pad_add_fusion.me_ref.refs_0_, f32[1024,128]{1,0:T(8,128)} %add_select_fusion.proj_ref.refs_1_, bf16[1024,512]{1,0:T(8,128)(2,1)} %get-tuple-element.79.act_ref.refs_2_.refs_8_, f32[128,512]{1,0:T(8,128)} %get-tuple-element.81.vec_ref.refs_5_.refs_10_), custom_call_target="tpu_custom_call" | custom-call | tf_op jit(solution)/shard_map/pallas_call | solution.py:534
  91.5 3.5 %all-to-all-start.2 = ((bf16[4,64,1024]{2,1,0:T(8,128)(2,1)}), bf16[4,64,1024]{2,1,0:T(8,128)(2,1)S(1)}, u32[]{:S(2)}, u32[]{:S(2)}) async-start(bf16[4,64,1024]{2,1,0:T(8,128)(2,1)} %bitcast.33), calls=%async_computation.2 | async-start | bytes 1048576 | tf_op jit(solution)/shard_map/all_to_all | solution.py:920
  95.9 16.8 %shard_map.240 = (bf16[16384,512]{1,0:T(8,128)(2,1)}, f32[1024,512]{1,0:T(8,128)}, f32[1024,512]{1,0:T(8,128)}, bf16[512,1024]{1,0:T(8,128)(2,1)}, f32[16,512]{1...) custom-call(s32[65]{0:T(128)} %pad_add_fusion.me_ref.refs_0_, ...), custom_call_target="tpu_custom_call" | custom-call | tf_op jit(solution)/shard_map/pallas_call | solution.py:534
  112.7 1.8 collective-permute-start.7
  114.5 1.5 collective-permute-start.8
  116.3 15.9 %shard_map.241 = (bf16[16384,512]{1,0:T(8,128)(2,1)}, f32[1024,512]{1,0:T(8,128)}, f32[1024,512]{1,0:T(8,128)}, bf16[512,1024]{1,0:T(8,128)(2,1)}, f32[16,512]{1...) custom-call(s32[65]{0:T(128)} %pad_add_fusion.me_ref.refs_0_, ...), custom_call_target="tpu_custom_call", output_to_operand_aliasing={{0}: (9, {}), {1}: (10, {}), {2}: (11, {}), {3}: (12, {})} | custom-call | tf_op jit(solution)/shard_map/pallas_call | solution.py:534
  132.2 1.8 collective-permute-start.10
  134.0 1.5 collective-permute-start.11
  135.6 0.8 copy-done.34
  137.2 1.8 collective-permute-start.13
  139.0 1.5 collective-permute-start.14
  140.5 1.2 collective-permute-done.10
  141.7 2.7 collective-permute-start.15
  144.4 4.4 %collective-permute-done.11 = bf16[128,1024]{1,0:T(8,128)(2,1)S(1)} collective-permute-done((bf16[128,1024]{1,0:T(8,128)(2,1)}, bf16[128,1024]{1,0:T(8,128)(2,1)S(1)}, u32[]{:S(2)}, u32[]{:S(2)}) %collective-permute-start.11) | collective-permute-done | bytes 262176 | tf_op jit(solution)/shard_map/ppermute | solution.py:710
  149.2 1.4 collective-permute-start.16
  150.6 0.8 collective-permute-start.17
  151.4 1.5 collective-permute-done.13.refs_10_
  152.9 2.8 collective-permute-start.18
  155.7 4.3 %collective-permute-done.14.refs_11_ = bf16[128,1024]{1,0:T(8,128)(2,1)S(1)} collective-permute-done((bf16[128,1024]{1,0:T(8,128)(2,1)S(1)}, bf16[128,1024]{1,0:T(8,128)(2,1)S(1)}, u32[]{:S(2)}, u32[]{:S(2)}) %collective-permute-start.14) | collective-permute-done | bytes 262176 | tf_op jit(solution)/shard_map/ppermute | solution.py:710
  160.8 11.0 %shard_map.242 = (bf16[16384,512]{1,0:T(8,128)(2,1)}, f32[1024,512]{1,0:T(8,128)}, bf16[1024,512]{1,0:T(8,128)(2,1)}, bf16[1024,1024]{1,0:T(8,128)(2,1)}, f32[1,512]{1,0:T(1,128)}, /*index=5*/f32[16,512]{1,0:T(8,128)}) custom-call(s32[65]{0:T(128)} %pad_add_fusion.me_ref.refs_0_, f32[1024,128]{1,0:T(8,128)} %add_select_fusion.proj_ref.refs_1_, ...), custom_call_target="tpu_custom_call" | custom-call | tf_op jit(solution)/shard_map/pallas_call | solution.py:534
  172.7 11.0 %shard_map.243 = (bf16[16384,512]{1,0:T(8,128)(2,1)}, f32[1024,512]{1,0:T(8,128)}, bf16[1024,512]{1,0:T(8,128)(2,1)}, bf16[1024,1024]{1,0:T(8,128)(2,1)}, f32[1,512]{1,0:T(1,128)}, /*index=5*/f32[16,512]{1,0:T(8,128)}) custom-call(s32[65]{0:T(128)} %pad_add_fusion.me_ref.refs_0_, ...), custom_call_target="tpu_custom_call", output_to_operand_aliasing={{0}: (13, {}), {1}: (14, {}), {2}: (15, {}), {3}: (16, {})} | custom-call | tf_op jit(solution)/shard_map/pallas_call | solution.py:534
  183.7 6.8 %shard_map.247 = f32[8,256,512]{2,1,0:T(8,128)} custom-call(bf16[1024,1024]{1,0:T(8,128)(2,1)} %get-tuple-element.121.normed_ref, bf16[512,1024]{1,0:T(8,128)(2,1)} %get-tuple-element.133.gated_ref, bf16[1024,512]{1,0:T(8,128)(2,1)} %get-tuple-element.116.refs_9_.dg_ref, bf16[1024,1024]{1,0:T(8,128)(2,1)} %get-tuple-element.127.refs_0_), custom_call_target="tpu_custom_call" | custom-call | tf_op jit(solution)/shard_map/pallas_call | solution.py:633
  191.5 48.1 %shard_map.244 = (f32[1024,512]{1,0:T(8,128)}, bf16[1024,128]{1,0:T(8,128)(2,1)}, f32[128,512]{1,0:T(8,128)}) custom-call(s32[65]{0:T(128)} %pad_add_fusion.me_ref.refs_0_, f32[1024,128]{1,0:T(8,128)} %add_select_fusion.proj_ref.refs_1_, bf16[1024,512]{1,0:T(8,128)(2,1)} %get-tuple-element.79.act_ref.refs_2_.refs_8_, f32[1024,512]{1,0:T(8,128)} %get-tuple-element.108.dm_ref, ...), custom_call_target="tpu_custom_call" | custom-call | tf_op jit(solution)/shard_map/pallas_call | solution.py:534
  239.5 1.3 collective-permute-start.19
  240.9 0.8 collective-permute-start.20
  241.7 1.4 collective-permute-start.21
  243.1 0.8 pad_maximum_fusion.2
  243.9 3.7 %all-to-all-start.1 = ((bf16[4,64,1024]{2,1,0:T(8,128)(2,1)}), bf16[4,64,1024]{2,1,0:T(8,128)(2,1)S(1)}, u32[]{:S(2)}, u32[]{:S(2)}) async-start(bf16[4,64,1024]{2,1,0:T(8,128)(2,1)} %pad_maximum_fusion.2), calls=%async_computation.1 | async-start | bytes 1048576 | tf_op jit(solution)/shard_map/all_to_all | solution.py:1006
  247.7 3.3 %collective-permute-done.21.refs_4_ = bf16[1024,128]{1,0:T(8,128)(2,1)S(1)} collective-permute-done((bf16[1024,128]{1,0:T(8,128)(2,1)}, bf16[1024,128]{1,0:T(8,128)(2,1)S(1)}, u32[]{:S(2)}, u32[]{:S(2)}) %collective-permute-start.21) | collective-permute-done | bytes 262176 | tf_op jit(solution)/shard_map/ppermute | solution.py:710
  251.7 10.9 %shard_map.245 = (bf16[256,1024]{1,0:T(8,128)(2,1)}, bf16[256,1024]{1,0:T(8,128)(2,1)}, bf16[256,1024]{1,0:T(8,128)(2,1)}, bf16[256,1024]{1,0:T(8,128)(2,1)}, bf...) custom-call(s32[65]{0:T(128)} %pad_add_fusion.me_ref.refs_0_, ...), custom_call_target="tpu_custom_call" | custom-call | tf_op jit(solution)/shard_map/pallas_call | solution.py:534
  262.7 5.1 %shard_map.246 = (f32[4,160,512]{2,1,0:T(8,128)}, bf16[4,176,512]{2,1,0:T(8,128)(2,1)}) custom-call(s32[1]{0:T(128)} %bitcast.37.me_ref, bf16[1024,1024]{1,0:T(8,128)(2,1)} %get-tuple-element.121.normed_ref, f32[256,512]{1,0:T(8,128)} %get-tuple-element.122.small_ref, bf16[1024,512]{1,0:T(8,128)(2,1)} %get-tuple-element.123.ds_ref, ...), custom_call_target="tpu_custom_call" | custom-call | tf_op jit(solution)/shard_map/pallas_call | solution.py:608
  268.0 0.9 collective-permute-start.26
  268.9 0.8 collective-permute-start.27
  269.8 1.8 collective-permute-start.28
  271.8 1.6 fusion.39
  273.5 1.1 collective-permute-start.23
  274.6 2.4 collective-permute-start.24
  276.9 5.9 %collective-permute-done.26 = bf16[256,1024]{1,0:T(8,128)(2,1)S(1)} collective-permute-done((bf16[256,1024]{1,0:T(8,128)(2,1)S(1)}, bf16[256,1024]{1,0:T(8,128)(2,1)S(1)}, u32[]{:S(2)}, u32[]{:S(2)}) %collective-permute-start.26) | collective-permute-done | bytes 524320 | tf_op jit(solution)/shard_map/ppermute | solution.py:710
  282.8 2.8 collective-permute-start.25
  285.7 8.5 %collective-permute-done.27 = bf16[256,1024]{1,0:T(8,128)(2,1)S(1)} collective-permute-done((bf16[256,1024]{1,0:T(8,128)(2,1)S(1)}, bf16[256,1024]{1,0:T(8,128)(2,1)S(1)}, u32[]{:S(2)}, u32[]{:S(2)}) %collective-permute-start.27) | collective-permute-done | bytes 524320 | tf_op jit(solution)/shard_map/ppermute | solution.py:710
  294.8 2.6 fusion.6
  297.6 1.0 slice.367
  299.4 3.4 %all-to-all-start.3 = ((bf16[4,32,1024]{2,1,0:T(8,128)(2,1)}), bf16[4,32,1024]{2,1,0:T(8,128)(2,1)S(1)}, u32[]{:S(2)}, u32[]{:S(2)}) async-start(bf16[4,32,1024]{2,1,0:T(8,128)(2,1)} %pad_maximum_fusion.4), calls=%async_computation.4 | async-start | bytes 524288 | tf_op jit(solution)/shard_map/all_to_all | solution.py:1092
  305.4 2.7 all-to-all-done.3.refs_0_
  308.8 2.1 shard_map.248
  310.9 1.4 copy.50
  312.3 0.8 copy.62
  (185 shorter events, 17.3 us)
Async XLA Ops:
  7.2 10.5 %copy-start.21 = (bf16[64,64]{1,0:T(8,128)(2,1)S(1)}, bf16[64,64]{1,0:T(8,128)(2,1)}, u32[]{:S(2)}) copy-start(bf16[64,64]{1,0:T(8,128)(2,1)} %param.23) | copy-start | bytes 24580
  7.2 10.6 %copy-start.26 = (bf16[4,64]{1,0:T(4,128)(2,1)S(1)}, bf16[4,64]{1,0:T(4,128)(2,1)}, u32[]{:S(2)}) copy-start(bf16[4,64]{1,0:T(4,128)(2,1)} %param.20) | copy-start | bytes 1540
  7.2 10.7 %copy-start.24 = (bf16[64,16]{0,1:T(8,128)(2,1)S(1)}, bf16[64,16]{0,1:T(8,128)(2,1)}, u32[]{:S(2)}) copy-start(bf16[64,16]{0,1:T(8,128)(2,1)} %param.25) | copy-start | bytes 6148
  7.2 10.8 %copy-start.27 = (bf16[64]{0:T(256)(128)(2,1)S(1)}, bf16[64]{0:T(256)(128)(2,1)}, u32[]{:S(2)}) copy-start(bf16[64]{0:T(256)(128)(2,1)} %param.21) | copy-start | bytes 388
  7.2 10.9 %copy-start.28 = (bf16[64]{0:T(256)(128)(2,1)S(1)}, bf16[64]{0:T(256)(128)(2,1)}, u32[]{:S(2)}) copy-start(bf16[64]{0:T(256)(128)(2,1)} %param.24) | copy-start | bytes 388
  7.2 11.0 %copy-start.29 = (bf16[64]{0:T(256)(128)(2,1)S(1)}, bf16[64]{0:T(256)(128)(2,1)}, u32[]{:S(2)}) copy-start(bf16[64]{0:T(256)(128)(2,1)} %param.26) | copy-start | bytes 388
  7.2 11.2 %copy-start.22 = (bf16[64,96]{1,0:T(8,128)(2,1)S(1)}, bf16[64,96]{1,0:T(8,128)(2,1)}, u32[]{:S(2)}) copy-start(bf16[64,96]{1,0:T(8,128)(2,1)} %param.22) | copy-start | bytes 36868
  7.3 11.2 %copy-start.20 = (bf16[64,1024]{1,0:T(8,128)(2,1)S(1)}, bf16[64,1024]{1,0:T(8,128)(2,1)}, u32[]{:S(2)}) copy-start(bf16[64,1024]{1,0:T(8,128)(2,1)} %param.27) | copy-start | bytes 393220
  7.3 42.6 %all-gather.5.cloned.1.call-start = ((), (), s32[]{:S(2)}) async-start(), calls=%async_computation.6 | async-start | bytes 2785280 | tf_op jit(solution)/shard_map/all_gather | solution.py:832
  12.5 10.8 %all-to-all-start = ((bf16[4,32,1152]{2,1,0:T(8,128)(2,1)}), bf16[4,32,1152]{2,1,0:T(8,128)(2,1)S(1)}, u32[]{:S(2)}, u32[]{:S(2)}) async-start(bf16[4,32,1152]{2,1,0:T(8,128)(2,1)} %shard_map.237), calls=%async_computation | async-start | bytes 589824 | tf_op jit(solution)/shard_map/all_to_all | solution.py:834
  17.6 77.6 %all-gather.7.cloned.1.call-start = ((), (), s32[]{:S(2)}) async-start(), calls=%async_computation.7 | async-start | bytes 2359296 | tf_op jit(solution)/shard_map/all_gather | solution.py:853
  24.1 7.1 %collective-permute-start = (bf16[128,640]{1,0:T(8,128)(2,1)S(1)}, bf16[128,640]{1,0:T(8,128)(2,1)S(1)}, u32[]{:S(2)}, u32[]{:S(2)}) collective-permute-start(bf16[128,640]{1,0:T(8,128)(2,1)S(1)} %slice_add_fusion), channel_id=1, source_target_pairs={{0,8},{4,12},{8,0},{12,4},{16,24},{20,28},{24,16},{28,20},{1,9},{5... | collective-permute-start | bytes 491528 | tf_op jit(solution)/shard_map/ppermute | solution.py:710
  25.7 14.0 %collective-permute-start.1 = (bf16[128,640]{1,0:T(8,128)(2,1)S(1)}, bf16[128,640]{1,0:T(8,128)(2,1)S(1)}, u32[]{:S(2)}, u32[]{:S(2)}) collective-permute-start(bf16[128,640]{1,0:T(8,128)(2,1)S(1)} %slice_add_fusion), channel_id=1, source_target_pairs={{0,16},{4,20},{8,24},{12,28},{16,0},{20,4},{24,8},{28,12},{1,17},{... | collective-permute-start | bytes 491528 | tf_op jit(solution)/shard_map/ppermute | solution.py:710
  28.3 11.4 %collective-permute-start.2 = (bf16[128,640]{1,0:T(8,128)(2,1)S(1)}, bf16[128,640]{1,0:T(8,128)(2,1)S(1)}, u32[]{:S(2)}, u32[]{:S(2)}) collective-permute-start(bf16[128,640]{1,0:T(8,128)(2,1)S(1)} %slice_add_fusion), channel_id=1, source_target_pairs={{0,24},{4,28},{8,16},{12,20},{16,8},{20,12},{24,0},{28,4},{1,25},{... | collective-permute-start | bytes 491528 | tf_op jit(solution)/shard_map/ppermute | solution.py:710
  39.8 10.0 %copy-start.2 = (bf16[4,128,640]{2,1,0:T(8,128)(2,1)}, bf16[4,128,640]{2,1,0:T(8,128)(2,1)S(1)}, u32[]{:S(2)}) copy-start(bf16[4,128,640]{2,1,0:T(8,128)(2,1)S(1)} %pad_maximum_fusion.refs_0_) | copy-start | bytes 1966084
  39.9 2.2 collective-permute-start.3
  42.0 7.9 %copy-start.7 = (bf16[4,128,640]{2,1,0:T(8,128)(2,1)}, bf16[4,128,640]{2,1,0:T(8,128)(2,1)S(1)}, u32[]{:S(2)}) copy-start(bf16[4,128,640]{2,1,0:T(8,128)(2,1)S(1)} %collective-permute-done.3.refs_1_) | copy-start | bytes 1966084
  49.9 13.1 %copy-start = (bf16[1088,1024]{1,0:T(8,128)(2,1)S(1)}, bf16[1088,1024]{1,0:T(8,128)(2,1)}, u32[]{:S(2)}) copy-start(bf16[1088,1024]{1,0:T(8,128)(2,1)} %all-gather.5.cloned.1.call-done) | copy-start | bytes 6684676
  59.5 6.2 %copy-start.25 = (f32[1,128]{1,0:T(1,128)S(1)}, f32[1,128]{1,0:T(1,128)}, u32[]{:S(2)}) copy-start(f32[1,128]{1,0:T(1,128)} %get-tuple-element.100) | copy-start | bytes 1540
  59.5 10.0 %collective-permute-start.4 = (bf16[1024,128]{1,0:T(8,128)(2,1)}, bf16[1024,128]{1,0:T(8,128)(2,1)S(1)}, u32[]{:S(2)}, u32[]{:S(2)}) collective-permute-start(bf16[1024,128]{1,0:T(8,128)(2,1)} %get-tuple-element.78), channel_id=1, source_target_pairs={{0,1},{1,0},{2,3},{3,2},{4,5},{5,4},{6,7},{7,6},{8,9},{9,8},{10,11... | collective-permute-start | bytes 786440 | tf_op jit(solution)/shard_map/ppermute | solution.py:710
  61.0 13.7 %collective-permute-start.5 = (bf16[1024,128]{1,0:T(8,128)(2,1)}, bf16[1024,128]{1,0:T(8,128)(2,1)}, u32[]{:S(2)}, u32[]{:S(2)}) collective-permute-start(bf16[1024,128]{1,0:T(8,128)(2,1)} %get-tuple-element.78), channel_id=1, source_target_pairs={{0,2},{1,3},{2,0},{3,1},{4,6},{5,7},{6,4},{7,5},{8,10},{9,11},{10,... | collective-permute-start | bytes 786440 | tf_op jit(solution)/shard_map/ppermute | solution.py:710
  61.6 13.1 %collective-permute-start.6 = (bf16[1024,128]{1,0:T(8,128)(2,1)}, bf16[1024,128]{1,0:T(8,128)(2,1)}, u32[]{:S(2)}, u32[]{:S(2)}) collective-permute-start(bf16[1024,128]{1,0:T(8,128)(2,1)} %get-tuple-element.78), channel_id=1, source_target_pairs={{0,3},{1,2},{2,1},{3,0},{4,7},{5,6},{6,5},{7,4},{8,11},{9,10},{10,... | collective-permute-start | bytes 786440 | tf_op jit(solution)/shard_map/ppermute | solution.py:710
  64.5 10.2 %copy-start.19 = (bf16[1024,128]{1,0:T(8,128)(2,1)S(1)}, bf16[1024,128]{1,0:T(8,128)(2,1)}, u32[]{:S(2)}) copy-start(bf16[1024,128]{1,0:T(8,128)(2,1)} %get-tuple-element.78) | copy-start | bytes 786436
  91.5 44.0 %all-to-all-start.2 = ((bf16[4,64,1024]{2,1,0:T(8,128)(2,1)}), bf16[4,64,1024]{2,1,0:T(8,128)(2,1)S(1)}, u32[]{:S(2)}, u32[]{:S(2)}) async-start(bf16[4,64,1024]{2,1,0:T(8,128)(2,1)} %bitcast.33), calls=%async_computation.2 | async-start | bytes 1048576 | tf_op jit(solution)/shard_map/all_to_all | solution.py:920
  95.0 202.6 %reduce-scatter.2.cloned.1.call-start = ((), (), s32[]{:S(2)}) async-start(), calls=%async_computation.5 | async-start | bytes 4718592 | tf_op jit(solution)/shard_map/reduce_scatter | solution.py:1017
  112.7 22.9 %collective-permute-start.7 = (bf16[128,1024]{1,0:T(8,128)(2,1)}, bf16[128,1024]{1,0:T(8,128)(2,1)S(1)}, u32[]{:S(2)}, u32[]{:S(2)}) collective-permute-start(bf16[128,1024]{1,0:T(8,128)(2,1)} %get-tuple-element.84), channel_id=1, source_target_pairs={{0,1},{1,0},{2,3},{3,2},{4,5},{5,4},{6,7},{7,6},{8,9},{9,8},{10,11... | collective-permute-start | bytes 786440 | tf_op jit(solution)/shard_map/ppermute | solution.py:710
  114.5 22.2 %collective-permute-start.8 = (bf16[128,1024]{1,0:T(8,128)(2,1)}, bf16[128,1024]{1,0:T(8,128)(2,1)S(1)}, u32[]{:S(2)}, u32[]{:S(2)}) collective-permute-start(bf16[128,1024]{1,0:T(8,128)(2,1)} %get-tuple-element.85), channel_id=1, source_target_pairs={{0,2},{1,3},{2,0},{3,1},{4,6},{5,7},{6,4},{7,5},{8,10},{9,11},{10,... | collective-permute-start | bytes 786440 | tf_op jit(solution)/shard_map/ppermute | solution.py:710
  116.0 20.7 %collective-permute-start.9 = (bf16[128,1024]{1,0:T(8,128)(2,1)}, bf16[128,1024]{1,0:T(8,128)(2,1)S(1)}, u32[]{:S(2)}, u32[]{:S(2)}) collective-permute-start(bf16[128,1024]{1,0:T(8,128)(2,1)} %get-tuple-element.86), channel_id=1, source_target_pairs={{0,3},{1,2},{2,1},{3,0},{4,7},{5,6},{6,5},{7,4},{8,11},{9,10},{10,... | collective-permute-start | bytes 786440 | tf_op jit(solution)/shard_map/ppermute | solution.py:710
  132.2 4.5 %copy-start.12 = (bf16[128,1024]{1,0:T(8,128)(2,1)S(1)}, bf16[128,1024]{1,0:T(8,128)(2,1)}, u32[]{:S(2)}) copy-start(bf16[128,1024]{1,0:T(8,128)(2,1)} %get-tuple-element.83) | copy-start | bytes 786436
  132.2 9.4 %collective-permute-start.10 = (bf16[128,1024]{1,0:T(8,128)(2,1)}, bf16[128,1024]{1,0:T(8,128)(2,1)S(1)}, u32[]{:S(2)}, u32[]{:S(2)}) collective-permute-start(bf16[128,1024]{1,0:T(8,128)(2,1)} %get-tuple-element.95), channel_id=1, source_target_pairs={{0,1},{1,0},{2,3},{3,2},{4,5},{5,4},{6,7},{7,6},{8,9},{9,8},{10,11... | collective-permute-start | bytes 786440 | tf_op jit(solution)/shard_map/ppermute | solution.py:710
  134.0 14.7 %collective-permute-start.11 = (bf16[128,1024]{1,0:T(8,128)(2,1)}, bf16[128,1024]{1,0:T(8,128)(2,1)S(1)}, u32[]{:S(2)}, u32[]{:S(2)}) collective-permute-start(bf16[128,1024]{1,0:T(8,128)(2,1)} %get-tuple-element.96), channel_id=1, source_target_pairs={{0,2},{1,3},{2,0},{3,1},{4,6},{5,7},{6,4},{7,5},{8,10},{9,11},{10,... | collective-permute-start | bytes 786440 | tf_op jit(solution)/shard_map/ppermute | solution.py:710
  136.4 12.3 %collective-permute-start.12 = (bf16[128,1024]{1,0:T(8,128)(2,1)S(1)}, bf16[128,1024]{1,0:T(8,128)(2,1)S(1)}, u32[]{:S(2)}, u32[]{:S(2)}) collective-permute-start(bf16[128,1024]{1,0:T(8,128)(2,1)S(1)} %copy-done.34), channel_id=1, source_target_pairs={{0,3},{1,2},{2,1},{3,0},{4,7},{5,6},{6,5},{7,4},{8,11},{9,10},{10,... | collective-permute-start | bytes 786440 | tf_op jit(solution)/shard_map/ppermute | solution.py:710
  136.7 12.0 %copy-start.11 = (bf16[128,1024]{1,0:T(8,128)(2,1)S(1)}, bf16[128,1024]{1,0:T(8,128)(2,1)}, u32[]{:S(2)}) copy-start(bf16[128,1024]{1,0:T(8,128)(2,1)} %get-tuple-element.94) | copy-start | bytes 786436
  137.2 12.0 %copy-start.5 = (bf16[128,1024]{1,0:T(8,128)(2,1)}, bf16[128,1024]{1,0:T(8,128)(2,1)S(1)}, u32[]{:S(2)}) copy-start(bf16[128,1024]{1,0:T(8,128)(2,1)S(1)} %get-tuple-element.188.refs_9_) | copy-start | bytes 786436
  137.2 15.7 %collective-permute-start.13 = (bf16[128,1024]{1,0:T(8,128)(2,1)S(1)}, bf16[128,1024]{1,0:T(8,128)(2,1)S(1)}, u32[]{:S(2)}, u32[]{:S(2)}) collective-permute-start(bf16[128,1024]{1,0:T(8,128)(2,1)S(1)} %get-tuple-element.188.refs_9_), channel_id=1, source_target_pairs={{0,1},{1,0},{2,3},{3,2},{4,5},{5,4},{6,7},{7,6},{8,9},{9,8},{10,11... | collective-permute-start | bytes 786440 | tf_op jit(solution)/shard_map/ppermute | solution.py:710
  139.0 21.0 %collective-permute-start.14 = (bf16[128,1024]{1,0:T(8,128)(2,1)S(1)}, bf16[128,1024]{1,0:T(8,128)(2,1)S(1)}, u32[]{:S(2)}, u32[]{:S(2)}) collective-permute-start(bf16[128,1024]{1,0:T(8,128)(2,1)S(1)} %get-tuple-element.188.refs_9_), channel_id=1, source_target_pairs={{0,2},{1,3},{2,0},{3,1},{4,6},{5,7},{6,4},{7,5},{8,10},{9,11},{10,... | collective-permute-start | bytes 786440 | tf_op jit(solution)/shard_map/ppermute | solution.py:710
  141.7 18.3 %collective-permute-start.15 = (bf16[128,1024]{1,0:T(8,128)(2,1)S(1)}, bf16[128,1024]{1,0:T(8,128)(2,1)S(1)}, u32[]{:S(2)}, u32[]{:S(2)}) collective-permute-start(bf16[128,1024]{1,0:T(8,128)(2,1)S(1)} %get-tuple-element.188.refs_9_), channel_id=1, source_target_pairs={{0,3},{1,2},{2,1},{3,0},{4,7},{5,6},{6,5},{7,4},{8,11},{9,10},{10,... | collective-permute-start | bytes 786440 | tf_op jit(solution)/shard_map/ppermute | solution.py:710
  149.2 22.6 %copy-start.4 = (bf16[128,1024]{1,0:T(8,128)(2,1)}, bf16[128,1024]{1,0:T(8,128)(2,1)S(1)}, u32[]{:S(2)}) copy-start(bf16[128,1024]{1,0:T(8,128)(2,1)S(1)} %get-tuple-element.186.refs_9_) | copy-start | bytes 786436
  149.2 22.6 %collective-permute-start.16 = (bf16[128,1024]{1,0:T(8,128)(2,1)S(1)}, bf16[128,1024]{1,0:T(8,128)(2,1)S(1)}, u32[]{:S(2)}, u32[]{:S(2)}) collective-permute-start(bf16[128,1024]{1,0:T(8,128)(2,1)S(1)} %get-tuple-element.186.refs_9_), channel_id=1, source_target_pairs={{0,1},{1,0},{2,3},{3,2},{4,5},{5,4},{6,7},{7,6},{8,9},{9,8},{10,11... | collective-permute-start | bytes 786440 | tf_op jit(solution)/shard_map/ppermute | solution.py:710
  150.6 21.2 %collective-permute-start.17 = (bf16[128,1024]{1,0:T(8,128)(2,1)S(1)}, bf16[128,1024]{1,0:T(8,128)(2,1)S(1)}, u32[]{:S(2)}, u32[]{:S(2)}) collective-permute-start(bf16[128,1024]{1,0:T(8,128)(2,1)S(1)} %get-tuple-element.186.refs_9_), channel_id=1, source_target_pairs={{0,2},{1,3},{2,0},{3,1},{4,6},{5,7},{6,4},{7,5},{8,10},{9,11},{10,... | collective-permute-start | bytes 786440 | tf_op jit(solution)/shard_map/ppermute | solution.py:710
  152.9 7.7 %copy-start.13 = (bf16[128,1024]{1,0:T(8,128)(2,1)}, bf16[128,1024]{1,0:T(8,128)(2,1)S(1)}, u32[]{:S(2)}) copy-start(bf16[128,1024]{1,0:T(8,128)(2,1)S(1)} %collective-permute-done.13.refs_10_) | copy-start | bytes 786436
  152.9 19.0 %collective-permute-start.18 = (bf16[128,1024]{1,0:T(8,128)(2,1)S(1)}, bf16[128,1024]{1,0:T(8,128)(2,1)S(1)}, u32[]{:S(2)}, u32[]{:S(2)}) collective-permute-start(bf16[128,1024]{1,0:T(8,128)(2,1)S(1)} %get-tuple-element.186.refs_9_), channel_id=1, source_target_pairs={{0,3},{1,2},{2,1},{3,0},{4,7},{5,6},{6,5},{7,4},{8,11},{9,10},{10,... | collective-permute-start | bytes 786440 | tf_op jit(solution)/shard_map/ppermute | solution.py:710
  239.5 8.1 %collective-permute-start.19 = (bf16[1024,128]{1,0:T(8,128)(2,1)}, bf16[1024,128]{1,0:T(8,128)(2,1)S(1)}, u32[]{:S(2)}, u32[]{:S(2)}) collective-permute-start(bf16[1024,128]{1,0:T(8,128)(2,1)} %get-tuple-element.112.refs_1_), channel_id=1, source_target_pairs={{0,1},{1,0},{2,3},{3,2},{4,5},{5,4},{6,7},{7,6},{8,9},{9,8},{10,11... | collective-permute-start | bytes 786440 | tf_op jit(solution)/shard_map/ppermute | solution.py:710
  240.9 6.8 %collective-permute-start.20 = (bf16[1024,128]{1,0:T(8,128)(2,1)}, bf16[1024,128]{1,0:T(8,128)(2,1)S(1)}, u32[]{:S(2)}, u32[]{:S(2)}) collective-permute-start(bf16[1024,128]{1,0:T(8,128)(2,1)} %get-tuple-element.112.refs_1_), channel_id=1, source_target_pairs={{0,2},{1,3},{2,0},{3,1},{4,6},{5,7},{6,4},{7,5},{8,10},{9,11},{10,... | collective-permute-start | bytes 786440 | tf_op jit(solution)/shard_map/ppermute | solution.py:710
  241.7 9.4 %collective-permute-start.21 = (bf16[1024,128]{1,0:T(8,128)(2,1)}, bf16[1024,128]{1,0:T(8,128)(2,1)S(1)}, u32[]{:S(2)}, u32[]{:S(2)}) collective-permute-start(bf16[1024,128]{1,0:T(8,128)(2,1)} %get-tuple-element.112.refs_1_), channel_id=1, source_target_pairs={{0,3},{1,2},{2,1},{3,0},{4,7},{5,6},{6,5},{7,4},{8,11},{9,10},{10,... | collective-permute-start | bytes 786440 | tf_op jit(solution)/shard_map/ppermute | solution.py:710
  243.9 24.1 %all-to-all-start.1 = ((bf16[4,64,1024]{2,1,0:T(8,128)(2,1)}), bf16[4,64,1024]{2,1,0:T(8,128)(2,1)S(1)}, u32[]{:S(2)}, u32[]{:S(2)}) async-start(bf16[4,64,1024]{2,1,0:T(8,128)(2,1)} %pad_maximum_fusion.2), calls=%async_computation.1 | async-start | bytes 1048576 | tf_op jit(solution)/shard_map/all_to_all | solution.py:1006
  247.7 3.4 %copy-start.14 = (bf16[1024,128]{1,0:T(8,128)(2,1)}, bf16[1024,128]{1,0:T(8,128)(2,1)S(1)}, u32[]{:S(2)}) copy-start(bf16[1024,128]{1,0:T(8,128)(2,1)S(1)} %collective-permute-done.19.refs_2_) | copy-start | bytes 786436
  247.7 3.4 %copy-start.16 = (bf16[1024,128]{1,0:T(8,128)(2,1)}, bf16[1024,128]{1,0:T(8,128)(2,1)S(1)}, u32[]{:S(2)}) copy-start(bf16[1024,128]{1,0:T(8,128)(2,1)S(1)} %collective-permute-done.20.refs_3_) | copy-start | bytes 786436
  262.6 5.2 %copy-start.1 = (bf16[1,256,1024]{2,1,0:T(8,128)(2,1)S(1)}, bf16[1,256,1024]{2,1,0:T(8,128)(2,1)}, u32[]{:S(2)}) copy-start(bf16[1,256,1024]{2,1,0:T(8,128)(2,1)} %param.14) | copy-start | bytes 1572868
  262.6 5.4 %copy-start.33 = (bf16[256,1024]{1,0:T(8,128)(2,1)S(1)}, bf16[256,1024]{1,0:T(8,128)(2,1)}, u32[]{:S(2)}) copy-start(bf16[256,1024]{1,0:T(8,128)(2,1)} %get-tuple-element.129) | copy-start | bytes 1572868
  262.6 6.3 %copy-start.32 = (bf16[256,1024]{1,0:T(8,128)(2,1)S(1)}, bf16[256,1024]{1,0:T(8,128)(2,1)}, u32[]{:S(2)}) copy-start(bf16[256,1024]{1,0:T(8,128)(2,1)} %get-tuple-element.130) | copy-start | bytes 1572868
  262.6 7.1 %copy-start.31 = (bf16[256,1024]{1,0:T(8,128)(2,1)S(1)}, bf16[256,1024]{1,0:T(8,128)(2,1)}, u32[]{:S(2)}) copy-start(bf16[256,1024]{1,0:T(8,128)(2,1)} %get-tuple-element.131) | copy-start | bytes 1572868
  262.6 9.0 %copy-start.30 = (f32[1,128]{1,0:T(1,128)S(1)}, f32[1,128]{1,0:T(1,128)}, u32[]{:S(2)}) copy-start(f32[1,128]{1,0:T(1,128)} %get-tuple-element.120) | copy-start | bytes 1540
  267.8 3.8 %collective-permute-start.22 = (bf16[4,176,512]{2,1,0:T(8,128)(2,1)}, bf16[4,176,512]{2,1,0:T(8,128)(2,1)S(1)}, u32[]{:S(2)}, u32[]{:S(2)}) collective-permute-start(bf16[4,176,512]{2,1,0:T(8,128)(2,1)} %get-tuple-element.125), channel_id=1, source_target_pairs={{0,4},{4,0},{8,12},{12,8},{16,20},{20,16},{24,28},{28,24},{1,5},{5... | collective-permute-start | bytes 2162696 | tf_op jit(solution)/shard_map/ppermute | solution.py:710
  268.0 14.8 %collective-permute-start.26 = (bf16[256,1024]{1,0:T(8,128)(2,1)S(1)}, bf16[256,1024]{1,0:T(8,128)(2,1)S(1)}, u32[]{:S(2)}, u32[]{:S(2)}) collective-permute-start(bf16[256,1024]{1,0:T(8,128)(2,1)S(1)} %copy-done.33), channel_id=1, source_target_pairs={{0,1},{1,0},{2,3},{3,2},{4,5},{5,4},{6,7},{7,6},{8,9},{9,8},{10,11... | collective-permute-start | bytes 1572872 | tf_op jit(solution)/shard_map/ppermute | solution.py:710
  268.9 25.3 %collective-permute-start.27 = (bf16[256,1024]{1,0:T(8,128)(2,1)S(1)}, bf16[256,1024]{1,0:T(8,128)(2,1)S(1)}, u32[]{:S(2)}, u32[]{:S(2)}) collective-permute-start(bf16[256,1024]{1,0:T(8,128)(2,1)S(1)} %copy-done.32), channel_id=1, source_target_pairs={{0,2},{1,3},{2,0},{3,1},{4,6},{5,7},{6,4},{7,5},{8,10},{9,11},{10,... | collective-permute-start | bytes 1572872 | tf_op jit(solution)/shard_map/ppermute | solution.py:710
  269.8 24.4 %collective-permute-start.28 = (bf16[256,1024]{1,0:T(8,128)(2,1)S(1)}, bf16[256,1024]{1,0:T(8,128)(2,1)S(1)}, u32[]{:S(2)}, u32[]{:S(2)}) collective-permute-start(bf16[256,1024]{1,0:T(8,128)(2,1)S(1)} %copy-done.31), channel_id=1, source_target_pairs={{0,3},{1,2},{2,1},{3,0},{4,7},{5,6},{6,5},{7,4},{8,11},{9,10},{10,... | collective-permute-start | bytes 1572872 | tf_op jit(solution)/shard_map/ppermute | solution.py:710
  271.8 22.4 %copy-start.3 = (bf16[256,1024]{1,0:T(8,128)(2,1)S(1)}, bf16[256,1024]{1,0:T(8,128)(2,1)}, u32[]{:S(2)}) copy-start(bf16[256,1024]{1,0:T(8,128)(2,1)} %get-tuple-element.128) | copy-start | bytes 1572868
  271.8 22.4 %copy-start.23 = (f32[1,1024]{1,0:T(1,128)S(1)}, f32[1,1024]{1,0:T(1,128)}, u32[]{:S(2)}) copy-start(f32[1,1024]{1,0:T(1,128)} %get-tuple-element.132) | copy-start | bytes 12292
  273.5 23.9 %collective-permute-start.23 = (bf16[176,512]{1,0:T(8,128)(2,1)S(1)}, bf16[176,512]{1,0:T(8,128)(2,1)S(1)}, u32[]{:S(2)}, u32[]{:S(2)}) collective-permute-start(bf16[176,512]{1,0:T(8,128)(2,1)S(1)} %get-tuple-element.183), channel_id=1, source_target_pairs={{0,8},{4,12},{8,0},{12,4},{16,24},{20,28},{24,16},{28,20},{1,9},{5... | collective-permute-start | bytes 540680 | tf_op jit(solution)/shard_map/ppermute | solution.py:710
  274.6 22.9 %collective-permute-start.24 = (bf16[176,512]{1,0:T(8,128)(2,1)S(1)}, bf16[176,512]{1,0:T(8,128)(2,1)S(1)}, u32[]{:S(2)}, u32[]{:S(2)}) collective-permute-start(bf16[176,512]{1,0:T(8,128)(2,1)S(1)} %get-tuple-element.184), channel_id=1, source_target_pairs={{0,16},{4,20},{8,24},{12,28},{16,0},{20,4},{24,8},{28,12},{1,17},{... | collective-permute-start | bytes 540680 | tf_op jit(solution)/shard_map/ppermute | solution.py:710
  282.8 14.6 %collective-permute-start.25 = (bf16[176,512]{1,0:T(8,128)(2,1)S(1)}, bf16[176,512]{1,0:T(8,128)(2,1)S(1)}, u32[]{:S(2)}, u32[]{:S(2)}) collective-permute-start(bf16[176,512]{1,0:T(8,128)(2,1)S(1)} %get-tuple-element.185), channel_id=1, source_target_pairs={{0,24},{4,28},{8,16},{12,20},{16,8},{20,12},{24,0},{28,4},{1,25},{... | collective-permute-start | bytes 540680 | tf_op jit(solution)/shard_map/ppermute | solution.py:710
  297.6 7.1 %slice-start = ((f32[1,256,512]{2,1,0:T(8,128)}), f32[1,128,512]{2,1,0:T(8,128)S(1)}, s32[]{:S(2)}) async-start(f32[1,256,512]{2,1,0:T(8,128)} %reduce-scatter.2.cloned.1.call-done), calls=%async_computation.8 | async-start | bytes 524288 | tf_op jit(solution)/shard_map/slice | solution.py:1096
  299.4 8.8 %all-to-all-start.3 = ((bf16[4,32,1024]{2,1,0:T(8,128)(2,1)}), bf16[4,32,1024]{2,1,0:T(8,128)(2,1)S(1)}, u32[]{:S(2)}, u32[]{:S(2)}) async-start(bf16[4,32,1024]{2,1,0:T(8,128)(2,1)} %pad_maximum_fusion.4), calls=%async_computation.4 | async-start | bytes 524288 | tf_op jit(solution)/shard_map/all_to_all | solution.py:1092
  (8 other events, 6.1 us)
Sparse Core Ops, SparseCore 0:
  10.8 39.0 all-gather.4
  52.1 29.0 all-gather.6
  190.7 50.1 reduce-scatter.1

commit v4 on v3

--- a/solution.py
+++ b/solution.py
@@ -7,6 +7,7 @@
 
 PIECE = 256
 BLOCK = 16
+UNROLL = 4
 ROWS = 256
 HALF = 128
 LOG2E = 1.4426950408889634
@@ -129,6 +130,15 @@
     proj_ref[...] = dot(act, xproj_ref[...]).astype(bf16)
 
 
+def several(block):
+    def blocks(i, carry):
+        for k in range(UNROLL):
+            carry = block(UNROLL * i + k, carry)
+        return carry
+
+    return blocks
+
+
 def piece_kernel(me_ref, proj_ref, act_ref, vec_ref, g_ref, carry_ref, u_ref, stepm_ref, col_ref):
     rows, c = act_ref.shape
     n = carry_ref.shape[0]
@@ -155,7 +165,7 @@
             carry = jnp.exp2(row_of(stepm_ref, t, n) * r2) * g
         return carry
 
-    carry_ref[...] = lax.fori_loop(0, rows // BLOCK, block, carry_ref[...])
+    carry_ref[...] = lax.fori_loop(0, rows // BLOCK // UNROLL, several(block), carry_ref[...])
 
 
 def ahead_kernel(
@@ -217,7 +227,7 @@
             s_ref[tt * n : (tt + 1) * n, :] = (hp + g_ref[at, :].astype(f32)).astype(bf16)
         return h
 
-    carry_ref[...] = lax.fori_loop(0, rows // BLOCK, block, carry_ref[...])
+    carry_ref[...] = lax.fori_loop(0, rows // BLOCK // UNROLL, several(block), carry_ref[...])
     read_out(rows // BLOCK)
     mixed = y_ref[BLOCK:] + vec_ref[SKIP : SKIP + 1, :] * act
     mixed_ref[...] = mixed
@@ -263,31 +273,36 @@
 
     chunk = first + pl.program_id(0)
 
-    def scan(j, w):
-        read = col_ref[j]
-        for tt in range(BLOCK):
-            t = j * BLOCK + tt
-            q = jnp.exp2(row_of(stepm_ref, t, n) * r2) * w
-            q_ref[pl.ds(pl.multiple_of(t * n, n), n), :] = q.astype(bf16)
-            w = q + row_of(dm_ref, t, n) * col_of(read, tt, c)
+    size = UNROLL * BLOCK
+
+    def scan(i, w):
+        for k in range(UNROLL):
+            j = UNROLL * i + k
+            read = col_ref[j]
+            for tt in range(BLOCK):
+                t = j * BLOCK + tt
+                q = jnp.exp2(row_of(stepm_ref, t, n) * r2) * w
+                q_ref[pl.ds(pl.multiple_of(t * n, n), n), :] = q.astype(bf16)
+                w = q + row_of(dm_ref, t, n) * col_of(read, tt, c)
         return w
 
-    def fill(j, w):
-        at = pl.ds(pl.multiple_of(j * BLOCK * n, BLOCK * n), BLOCK * n)
-        q_ref[at, :] = jnp.zeros((BLOCK * n, c), bf16)
-        return row_of(dm_ref, j * BLOCK + BLOCK - 1, n) * col_of(col_ref[j], BLOCK - 1, c)
-
-    def block(j, w):
-        return lax.cond(me_ref[1 + chunk * (rows // BLOCK) + j] > 0, scan, fill, j, w)
-
-    carry_ref[...] = lax.fori_loop(0, rows // BLOCK, block, carry_ref[...])
+    def fill(i, w):
+        for k in range(UNROLL):
+            at = pl.ds(pl.multiple_of((UNROLL * i + k) * BLOCK * n, BLOCK * n), BLOCK * n)
+            q_ref[at, :] = jnp.zeros((BLOCK * n, c), bf16)
+        return row_of(dm_ref, (i + 1) * size - 1, n) * col_of(col_ref[(i + 1) * UNROLL - 1], BLOCK - 1, c)
+
+    def group(i, w):
+        return lax.cond(me_ref[1 + chunk * (rows // size) + i] > 0, scan, fill, i, w)
+
+    carry_ref[...] = lax.fori_loop(0, rows // size, group, carry_ref[...])
     leave_ref[...] = carry_ref[...]
 
 
 def state_grad_kernel(
     me_ref, proj_ref, act_ref, dm_ref, g_ref, hp_ref, q_ref, vec_ref, sgrad_ref, pieces_ref,
     dact_ref, dproj_ref, table_ref,
-    carry_ref, u_ref, step_ref, col_ref, diag_ref, ig_ref, rr_ref, rs_ref, pair_ref, own_ref, x_ref, y_ref, dp_ref,
+    carry_ref, u_ref, step_ref, col_ref, diag_ref, ig_ref, rr_ref, pair_ref, own_ref, x_ref, y_ref, dp_ref,
 ):
     rows, c = act_ref.shape
     n = carry_ref.shape[0]
@@ -298,7 +313,6 @@
         carry_ref[...] = jnp.zeros_like(carry_ref)
         table_ref[...] = jnp.zeros_like(table_ref)
         table_ref[SKIP : SKIP + 1, :] = sgrad_ref[...]
-        rs_ref[...] = jnp.zeros_like(rs_ref)
 
     proj = proj_ref[...]
     act = act_ref[...].astype(f32)
@@ -312,7 +326,6 @@
     iota = lambda shape, axis: lax.broadcasted_iota(jnp.int32, shape, axis)
     mask = lambda v: v.astype(f32).astype(bf16)
     by_row = mask(iota((BLOCK, wide), 1) // n == iota((BLOCK, wide), 0))
-    by_state = mask(iota((n, wide), 1) % n == iota((n, wide), 0))
     part = min(c, 2 * LANES)
     which = mask(iota((2 * part, LANES), 0) // part == iota((2 * part, LANES), 1) // n % 2)
     own_lane = iota((wide, LANES), 1) % n == iota((wide, LANES), 0) % n
@@ -321,11 +334,11 @@
         r16 = pl.ds(pl.multiple_of(j * BLOCK, BLOCK), BLOCK)
         x_ref[r16, :] = dot(diag_ref[r16, :], ig_ref[...])
         y_ref[r16, :] = dot(by_row, rr_ref[...])
-        table_ref[ALOG : ALOG + n, :] += dot(by_state, rs_ref[...])
         dp_ref[pl.ds(pl.multiple_of((j + 1) * BLOCK, BLOCK), BLOCK), :] = dot(by_row, own_ref[...])
         own_ref[...] = jnp.where(own_lane, dot(pair_ref[...], which), 0.0).astype(bf16)
 
-    def block(i, m):
+    def block(i, both):
+        m, al = both
         j = rows // BLOCK - 1 - i
         sums(j + 1)
         read = col_ref[j]
@@ -344,8 +357,9 @@
             rg = low_mu * hp + q * g
             ig = low_mu + q
             ig_ref[loc, :] = ig
-            rr_ref[loc, :] = (rg.astype(f32) * r2).astype(bf16)
-            rs_ref[loc, :] = rg * srow.astype(bf16)
+            rg = rg.astype(f32)
+            al = al + rg * srow
+            rr_ref[loc, :] = (rg * r2).astype(bf16)
             pb = ig * row_of(u_ref, t, n).astype(bf16)
             pc = (hp + g) * drow.astype(bf16)
             sb, sc = pb[:, :part], pc[:, :part]
@@ -354,12 +368,13 @@
                 sc = sc + pc[:, k * part : (k + 1) * part]
             pair_ref[loc, :part] = sb
             pair_ref[loc, part:] = sc
-        return m
-
-    carry_ref[...] = lax.fori_loop(0, rows // BLOCK, block, carry_ref[...])
+        return m, al
+
+    m, al = lax.fori_loop(0, rows // BLOCK, block, (carry_ref[...], table_ref[ALOG : ALOG + n, :]))
+    carry_ref[...] = m
+    table_ref[ALOG : ALOG + n, :] = al
     sums(0)
     dp_ref[:BLOCK, :] = dot(by_row, own_ref[...])
-    rs_ref[...] = jnp.zeros_like(rs_ref)
     xs = x_ref[:rows]
     dact_ref[...] = step_ref[...] * xs + vec_ref[SKIP : SKIP + 1, :] * dm_ref[...]
     dpre = (y_ref[:rows] * LN2 + act * xs) * sigmoid(pre)
@@ -882,7 +897,10 @@
     running = jnp.cumsum(starts)
     lagged = jnp.concatenate([jnp.zeros((PIECE,), f32), running[: total - PIECE]])
     carry_on = jnp.where(running - lagged > 0.5, 1.0 - starts, 0.0)
-    flags = jnp.max(carry_on.reshape(total // BLOCK, BLOCK), axis=1).astype(jnp.int32)
+    flags = jnp.max(carry_on.reshape(-1, UNROLL * BLOCK), axis=1).astype(jnp.int32)
+    teacher, proj = lax.optimization_barrier((teacher, proj))
+    per = rows // seqs
+    teach_v = lax.all_to_all(teacher.reshape(seqs, per, width), "seq", 0, 0).astype(f32)
     proj = added(share_parts(proj, "seq"))
     me = jnp.concatenate([me, flags])
     proj = jnp.where(jnp.arange(LANES)[None, :] == CARRY, carry_on[:, None], proj)
@@ -903,7 +921,6 @@
         reverse=True,
     )
     halves = 2
-    per = rows // seqs
     held = seqs // halves * per
     count = total // ROWS // halves
     places = seqs if seqs <= 4 else 1
@@ -916,8 +933,6 @@
     mine = lambda v: lax.dynamic_slice_in_dim(v, lax.axis_index("seq") * per, per, axis=1)
     tok_v = mine(everything[:, :rows]).astype(f32)
     valid_v = mine(everything[:, rows + 1, :rows].reshape(seqs, rows, 1)).astype(f32)
-    teacher, g = lax.optimization_barrier((teacher, g))
-    teach_v = lax.all_to_all(teacher.reshape(seqs, per, width), "seq", 0, 0).astype(f32)
     enter = jnp.zeros((states, chans), f32)
     kept = []
     branches = []
@@ -1028,7 +1043,7 @@
             pltpu.VMEM((HALF // BLOCK, states, BLOCK), f32),
             pltpu.VMEM((HALF + BLOCK, BLOCK * states), bf16),
         ]
-        + [pltpu.VMEM((BLOCK * states, chans), bf16)] * 3
+        + [pltpu.VMEM((BLOCK * states, chans), bf16)] * 2
         + [
             pltpu.VMEM((BLOCK * states, 2 * min(chans, 2 * LANES)), bf16),
             pltpu.VMEM((BLOCK * states, LANES), bf16),

time: 322 us -> 309 us (0.960)
  Pallas kernels: 154 us -> 144 us
  starting transfers between devices: 55.5 us -> 49.5 us
    pallas_call x8, Pallas kernels: 138 us -> 129 us  [call(): pl.pallas_call(kernel, out_shape=[jax.ShapeDtypeStruct(s, d) for s, d, _...]
    ppermute x29, starting transfers between devices: 39.5 us -> 33.7 us  [partner(): lax.ppermute(value, axis, [(i, i ^ k) for i in range(lax.axis_size(axis))])]
  transfers between devices with their start and end apart: 36 -> 36, of which waited for: 14 -> 16; matrix products, arithmetic and copies ran while one was open for 6% -> 7% of each run, Pallas kernels for 42% -> 41%
where the time goes in v4:
time: 309 us; the launch traced here: 308 us
  Pallas kernels  144 us (47%)
  waiting for transfers between devices  65.8 us (21%)
  starting transfers between devices  49.5 us (16%)
  other arithmetic  17.6 us (6%)
  between operations  17.6 us (6%)
  local copies, waits for them, and re-layouts  12.5 us (4%)
    pallas_call x8, Pallas kernels, call(): pl.pallas_call(kernel, out_shape=[jax.ShapeDtypeStruct(s, d) for s, d, _...  129 us
    ppermute x29, waiting for transfers between devices, partner(): lax.ppermute(value, axis, [(i, i ^ k) for i in range(lax.axis_size(axis))])  50.4 us
    ppermute x29, starting transfers between devices, partner(): lax.ppermute(value, axis, [(i, i ^ k) for i in range(lax.axis_size(axis))])  33.7 us
    all_gather x1, waiting for transfers between devices, body(): everything = lax.all_gather(jnp.concatenate([tok, flags], axis=0), 'seq')  7.87 us
    pallas_call x1, Pallas kernels, by_blocks(): pl.pallas_call(kernel, out_shape=jax.ShapeDtypeStruct((batches, rows, cha...  6.79 us
  transfers between devices with their start and end apart: 36, of which 16 were waited for; matrix products, arithmetic and copies ran while one was open for 7% of the time, Pallas kernels for 41%

profile of v4, /device:TPU:0, one launch (start us, length us, event | category | flops | bytes accessed | tf_op | source)
XLA Modules:
  0.0 307.5 jit_solution(12170548902760535162)
XLA Ops:
  7.3 0.7 convert.61
  8.7 1.9 pad_maximum_fusion.1
  10.6 1.8 shard_map.237
  12.5 5.2 %all-to-all-start = ((bf16[4,32,1152]{2,1,0:T(8,128)(2,1)}), bf16[4,32,1152]{2,1,0:T(8,128)(2,1)S(1)}, u32[]{:S(2)}, u32[]{:S(2)}) async-start(bf16[4,32,1152]{2,1,0:T(8,128)(2,1)} %shard_map.237), calls=%async_computation | async-start | bytes 589824 | tf_op jit(solution)/shard_map/all_to_all | solution.py:849
  18.5 4.8 %all-to-all-done = bf16[4,32,1152]{2,1,0:T(8,128)(2,1)S(1)} async-done(((bf16[4,32,1152]{2,1,0:T(8,128)(2,1)}), bf16[4,32,1152]{2,1,0:T(8,128)(2,1)S(1)}, u32[]{:S(2)}, u32[]{:S(2)}) %all-to-all-start) | async-done | bytes 294944 | tf_op jit(solution)/shard_map/all_to_all | solution.py:849
  23.3 0.7 pad_maximum_fusion.3
  24.1 1.6 collective-permute-start
  25.7 2.6 collective-permute-start.1
  28.5 2.7 collective-permute-done
  31.2 8.6 %collective-permute-done.1 = bf16[128,640]{1,0:T(8,128)(2,1)S(1)} collective-permute-done((bf16[128,640]{1,0:T(8,128)(2,1)S(1)}, bf16[128,640]{1,0:T(8,128)(2,1)S(1)}, u32[]{:S(2)}, u32[]{:S(2)}) %collective-permute-start.1) | collective-permute-done | bytes 163872 | tf_op jit(solution)/shard_map/ppermute | solution.py:725
  40.6 1.4 collective-permute-done.3.refs_1_
  42.0 7.9 %all-gather.5.cloned.1.call-done = bf16[1088,1024]{1,0:T(8,128)(2,1)} async-done(((bf16[272,1024]{1,0:T(8,128)(2,1)}), bf16[1088,1024]{1,0:T(8,128)(2,1)}) %all-gather.5.cloned.1.call-update) | async-done | bytes 2228240 | tf_op jit(solution)/shard_map/all_gather | solution.py:847
  49.9 9.5 %shard_map.238 = (bf16[1024,1024]{1,0:T(8,128)(2,1)}, bf16[1024,1024]{1,0:T(8,128)(2,1)}, bf16[1024,512]{1,0:T(8,128)(2,1)}, f32[1024,512]{1,0:T(8,128)}, bf16[1...) custom-call(s32[9]{0:T(128)} %concatenate.66.me_ref, ...), custom_call_target="tpu_custom_call" | custom-call | tf_op jit(solution)/shard_map/pallas_call | solution.py:549
  59.5 1.5 collective-permute-start.4
  61.6 1.5 collective-permute-start.6
  63.0 1.5 slice.271
  65.4 3.5 %all-to-all-start.2 = ((bf16[4,64,1024]{2,1,0:T(8,128)(2,1)}), bf16[4,64,1024]{2,1,0:T(8,128)(2,1)S(1)}, u32[]{:S(2)}, u32[]{:S(2)}) async-start(bf16[4,64,1024]{2,1,0:T(8,128)(2,1)} %bitcast.33), calls=%async_computation.2 | async-start | bytes 1048576 | tf_op jit(solution)/shard_map/all_to_all | solution.py:903
  71.9 1.1 dynamic-slice_convert_fusion
  73.2 3.6 %collective-permute-done.5 = bf16[1024,128]{1,0:T(8,128)(2,1)S(1)} collective-permute-done((bf16[1024,128]{1,0:T(8,128)(2,1)}, bf16[1024,128]{1,0:T(8,128)(2,1)S(1)}, u32[]{:S(2)}, u32[]{:S(2)}) %collective-permute-start.5) | collective-permute-done | bytes 262176 | tf_op jit(solution)/shard_map/ppermute | solution.py:725
  76.7 1.9 add_select_fusion.proj_ref.refs_1_
  78.7 12.8 %shard_map.239.refs_4_.g_ref = bf16[16384,512]{1,0:T(8,128)(2,1)} custom-call(s32[17]{0:T(128)} %pad_add_fusion.me_ref.refs_0_, f32[1024,128]{1,0:T(8,128)} %add_select_fusion.proj_ref.refs_1_, bf16[1024,512]{1,0:T(8,128)(2,1)} %get-tuple-element.80.act_ref.refs_2_.refs_8_, f32[128,512]{1,0:T(8,128)} %get-tuple-element.82.vec_ref.refs_5_.refs_10_), custom_call_target="tpu_custom_call" | custom-call | tf_op jit(solution)/shard_map/pallas_call | solution.py:549
  92.1 15.7 %shard_map.240 = (bf16[16384,512]{1,0:T(8,128)(2,1)}, f32[1024,512]{1,0:T(8,128)}, f32[1024,512]{1,0:T(8,128)}, bf16[512,1024]{1,0:T(8,128)(2,1)}, f32[16,512]{1...) custom-call(s32[17]{0:T(128)} %pad_add_fusion.me_ref.refs_0_, ...), custom_call_target="tpu_custom_call" | custom-call | tf_op jit(solution)/shard_map/pallas_call | solution.py:549
  107.9 0.9 collective-permute-start.8
  108.8 2.6 collective-permute-start.9
  111.6 15.0 %shard_map.241 = (bf16[16384,512]{1,0:T(8,128)(2,1)}, f32[1024,512]{1,0:T(8,128)}, f32[1024,512]{1,0:T(8,128)}, bf16[512,1024]{1,0:T(8,128)(2,1)}, f32[16,512]{1...) custom-call(s32[17]{0:T(128)} %pad_add_fusion.me_ref.refs_0_, ...), custom_call_target="tpu_custom_call", output_to_operand_aliasing={{0}: (9, {}), {1}: (10, {}), {2}: (11, {}), {3}: (12, {})} | custom-call | tf_op jit(solution)/shard_map/pallas_call | solution.py:549
  126.7 0.8 collective-permute-start.11
  127.5 2.6 collective-permute-start.12
  130.7 0.8 collective-permute-start.14
  131.5 4.5 %collective-permute-done.10 = bf16[128,1024]{1,0:T(8,128)(2,1)S(1)} collective-permute-done((bf16[128,1024]{1,0:T(8,128)(2,1)}, bf16[128,1024]{1,0:T(8,128)(2,1)S(1)}, u32[]{:S(2)}, u32[]{:S(2)}) %collective-permute-start.10) | collective-permute-done | bytes 262176 | tf_op jit(solution)/shard_map/ppermute | solution.py:725
  136.4 5.5 %collective-permute-done.11 = bf16[128,1024]{1,0:T(8,128)(2,1)S(1)} collective-permute-done((bf16[128,1024]{1,0:T(8,128)(2,1)}, bf16[128,1024]{1,0:T(8,128)(2,1)S(1)}, u32[]{:S(2)}, u32[]{:S(2)}) %collective-permute-start.11) | collective-permute-done | bytes 262176 | tf_op jit(solution)/shard_map/ppermute | solution.py:725
  142.3 2.0 collective-permute-start.16
  144.8 2.6 collective-permute-done.13.refs_10_
  148.4 4.6 %collective-permute-done.15.refs_12_ = bf16[128,1024]{1,0:T(8,128)(2,1)S(1)} collective-permute-done((bf16[128,1024]{1,0:T(8,128)(2,1)S(1)}, bf16[128,1024]{1,0:T(8,128)(2,1)S(1)}, u32[]{:S(2)}, u32[]{:S(2)}) %collective-permute-start.15) | collective-permute-done | bytes 262176 | tf_op jit(solution)/shard_map/ppermute | solution.py:725
  153.7 9.9 %shard_map.242 = (bf16[16384,512]{1,0:T(8,128)(2,1)}, f32[1024,512]{1,0:T(8,128)}, bf16[1024,512]{1,0:T(8,128)(2,1)}, bf16[1024,1024]{1,0:T(8,128)(2,1)}, f32[1,512]{1,0:T(1,128)}, /*index=5*/f32[16,512]{1,0:T(8,128)}) custom-call(s32[17]{0:T(128)} %pad_add_fusion.me_ref.refs_0_, f32[1024,128]{1,0:T(8,128)} %add_select_fusion.proj_ref.refs_1_, ...), custom_call_target="tpu_custom_call" | custom-call | tf_op jit(solution)/shard_map/pallas_call | solution.py:549
  164.5 9.9 %shard_map.243 = (bf16[16384,512]{1,0:T(8,128)(2,1)}, f32[1024,512]{1,0:T(8,128)}, bf16[1024,512]{1,0:T(8,128)(2,1)}, bf16[1024,1024]{1,0:T(8,128)(2,1)}, f32[1,512]{1,0:T(1,128)}, /*index=5*/f32[16,512]{1,0:T(8,128)}) custom-call(s32[17]{0:T(128)} %pad_add_fusion.me_ref.refs_0_, ...), custom_call_target="tpu_custom_call", output_to_operand_aliasing={{0}: (13, {}), {1}: (14, {}), {2}: (15, {}), {3}: (16, {})} | custom-call | tf_op jit(solution)/shard_map/pallas_call | solution.py:549
  174.4 6.8 %shard_map.247 = f32[8,256,512]{2,1,0:T(8,128)} custom-call(bf16[1024,1024]{1,0:T(8,128)(2,1)} %get-tuple-element.121.normed_ref, bf16[512,1024]{1,0:T(8,128)(2,1)} %get-tuple-element.133.gated_ref, bf16[1024,512]{1,0:T(8,128)(2,1)} %get-tuple-element.116.refs_9_.dg_ref, bf16[1024,1024]{1,0:T(8,128)(2,1)} %get-tuple-element.127.refs_0_), custom_call_target="tpu_custom_call" | custom-call | tf_op jit(solution)/shard_map/pallas_call | solution.py:648
  182.1 44.9 %shard_map.244 = (f32[1024,512]{1,0:T(8,128)}, bf16[1024,128]{1,0:T(8,128)(2,1)}, f32[128,512]{1,0:T(8,128)}) custom-call(s32[17]{0:T(128)} %pad_add_fusion.me_ref.refs_0_, f32[1024,128]{1,0:T(8,128)} %add_select_fusion.proj_ref.refs_1_, bf16[1024,512]{1,0:T(8,128)(2,1)} %get-tuple-element.80.act_ref.refs_2_.refs_8_, f32[1024,512]{1,0:T(8,128)} %get-tuple-element.108.dm_ref, ...), custom_call_target="tpu_custom_call" | custom-call | tf_op jit(solution)/shard_map/pallas_call | solution.py:549
  227.0 0.8 collective-permute-start.19
  227.8 1.2 collective-permute-start.20
  229.0 1.6 collective-permute-start.21
  230.6 0.8 pad_maximum_fusion.2
  231.4 3.5 %all-to-all-start.1 = ((bf16[4,64,1024]{2,1,0:T(8,128)(2,1)}), bf16[4,64,1024]{2,1,0:T(8,128)(2,1)S(1)}, u32[]{:S(2)}, u32[]{:S(2)}) async-start(bf16[4,64,1024]{2,1,0:T(8,128)(2,1)} %pad_maximum_fusion.2), calls=%async_computation.1 | async-start | bytes 1048576 | tf_op jit(solution)/shard_map/all_to_all | solution.py:1021
  234.9 1.1 collective-permute-done.20.refs_3_
  236.1 1.4 collective-permute-done.21.refs_4_
  238.1 10.9 %shard_map.245 = (bf16[256,1024]{1,0:T(8,128)(2,1)}, bf16[256,1024]{1,0:T(8,128)(2,1)}, bf16[256,1024]{1,0:T(8,128)(2,1)}, bf16[256,1024]{1,0:T(8,128)(2,1)}, bf...) custom-call(s32[17]{0:T(128)} %pad_add_fusion.me_ref.refs_0_, ...), custom_call_target="tpu_custom_call" | custom-call | tf_op jit(solution)/shard_map/pallas_call | solution.py:549
  249.0 5.1 %shard_map.246 = (f32[4,160,512]{2,1,0:T(8,128)}, bf16[4,176,512]{2,1,0:T(8,128)(2,1)}) custom-call(s32[1]{0:T(128)} %bitcast.37.me_ref, bf16[1024,1024]{1,0:T(8,128)(2,1)} %get-tuple-element.121.normed_ref, f32[256,512]{1,0:T(8,128)} %get-tuple-element.122.small_ref, bf16[1024,512]{1,0:T(8,128)(2,1)} %get-tuple-element.123.ds_ref, ...), custom_call_target="tpu_custom_call" | custom-call | tf_op jit(solution)/shard_map/pallas_call | solution.py:623
  254.4 1.2 collective-permute-start.26
  255.7 1.5 collective-permute-start.27
  257.2 0.8 collective-permute-start.28
  258.2 1.6 fusion.39
  259.9 1.5 collective-permute-start.23
  261.4 2.5 collective-permute-start.24
  263.9 5.4 %collective-permute-done.26 = bf16[256,1024]{1,0:T(8,128)(2,1)S(1)} collective-permute-done((bf16[256,1024]{1,0:T(8,128)(2,1)S(1)}, bf16[256,1024]{1,0:T(8,128)(2,1)S(1)}, u32[]{:S(2)}, u32[]{:S(2)}) %collective-permute-start.26) | collective-permute-done | bytes 524320 | tf_op jit(solution)/shard_map/ppermute | solution.py:725
  269.2 3.4 %collective-permute-start.25 = (bf16[176,512]{1,0:T(8,128)(2,1)S(1)}, bf16[176,512]{1,0:T(8,128)(2,1)S(1)}, u32[]{:S(2)}, u32[]{:S(2)}) collective-permute-start(bf16[176,512]{1,0:T(8,128)(2,1)S(1)} %get-tuple-element.198), channel_id=1, source_target_pairs={{0,24},{4,28},{8,16},{12,20},{16,8},{20,12},{24,0},{28,4},{1,25},{... | collective-permute-start | bytes 540680 | tf_op jit(solution)/shard_map/ppermute | solution.py:725
  272.6 8.3 %collective-permute-done.27 = bf16[256,1024]{1,0:T(8,128)(2,1)S(1)} collective-permute-done((bf16[256,1024]{1,0:T(8,128)(2,1)S(1)}, bf16[256,1024]{1,0:T(8,128)(2,1)S(1)}, u32[]{:S(2)}, u32[]{:S(2)}) %collective-permute-start.27) | collective-permute-done | bytes 524320 | tf_op jit(solution)/shard_map/ppermute | solution.py:725
  281.5 2.6 fusion.6
  284.4 1.0 slice.367
  285.4 0.7 pad_maximum_fusion.4
  286.1 3.4 %all-to-all-start.3 = ((bf16[4,32,1024]{2,1,0:T(8,128)(2,1)}), bf16[4,32,1024]{2,1,0:T(8,128)(2,1)S(1)}, u32[]{:S(2)}, u32[]{:S(2)}) async-start(bf16[4,32,1024]{2,1,0:T(8,128)(2,1)} %pad_maximum_fusion.4), calls=%async_computation.4 | async-start | bytes 524288 | tf_op jit(solution)/shard_map/all_to_all | solution.py:1107
  291.4 0.7 copy.59
  292.2 2.7 all-to-all-done.3.refs_0_
  295.6 2.1 shard_map.248
  297.6 1.4 copy.58
  299.0 0.8 copy.70
  (183 shorter events, 15.9 us)
Async XLA Ops:
  7.2 10.5 %copy-start.21 = (bf16[64,64]{1,0:T(8,128)(2,1)S(1)}, bf16[64,64]{1,0:T(8,128)(2,1)}, u32[]{:S(2)}) copy-start(bf16[64,64]{1,0:T(8,128)(2,1)} %param.23) | copy-start | bytes 24580
  7.2 10.6 %copy-start.26 = (bf16[4,64]{1,0:T(4,128)(2,1)S(1)}, bf16[4,64]{1,0:T(4,128)(2,1)}, u32[]{:S(2)}) copy-start(bf16[4,64]{1,0:T(4,128)(2,1)} %param.20) | copy-start | bytes 1540
  7.2 10.7 %copy-start.24 = (bf16[64,16]{0,1:T(8,128)(2,1)S(1)}, bf16[64,16]{0,1:T(8,128)(2,1)}, u32[]{:S(2)}) copy-start(bf16[64,16]{0,1:T(8,128)(2,1)} %param.25) | copy-start | bytes 6148
  7.2 10.8 %copy-start.27 = (bf16[64]{0:T(256)(128)(2,1)S(1)}, bf16[64]{0:T(256)(128)(2,1)}, u32[]{:S(2)}) copy-start(bf16[64]{0:T(256)(128)(2,1)} %param.21) | copy-start | bytes 388
  7.2 10.9 %copy-start.28 = (bf16[64]{0:T(256)(128)(2,1)S(1)}, bf16[64]{0:T(256)(128)(2,1)}, u32[]{:S(2)}) copy-start(bf16[64]{0:T(256)(128)(2,1)} %param.24) | copy-start | bytes 388
  7.2 11.0 %copy-start.29 = (bf16[64]{0:T(256)(128)(2,1)S(1)}, bf16[64]{0:T(256)(128)(2,1)}, u32[]{:S(2)}) copy-start(bf16[64]{0:T(256)(128)(2,1)} %param.26) | copy-start | bytes 388
  7.2 11.2 %copy-start.22 = (bf16[64,96]{1,0:T(8,128)(2,1)S(1)}, bf16[64,96]{1,0:T(8,128)(2,1)}, u32[]{:S(2)}) copy-start(bf16[64,96]{1,0:T(8,128)(2,1)} %param.22) | copy-start | bytes 36868
  7.3 11.2 %copy-start.20 = (bf16[64,1024]{1,0:T(8,128)(2,1)S(1)}, bf16[64,1024]{1,0:T(8,128)(2,1)}, u32[]{:S(2)}) copy-start(bf16[64,1024]{1,0:T(8,128)(2,1)} %param.27) | copy-start | bytes 393220
  7.3 42.6 %all-gather.5.cloned.1.call-start = ((), (), s32[]{:S(2)}) async-start(), calls=%async_computation.6 | async-start | bytes 2785280 | tf_op jit(solution)/shard_map/all_gather | solution.py:847
  12.5 10.8 %all-to-all-start = ((bf16[4,32,1152]{2,1,0:T(8,128)(2,1)}), bf16[4,32,1152]{2,1,0:T(8,128)(2,1)S(1)}, u32[]{:S(2)}, u32[]{:S(2)}) async-start(bf16[4,32,1152]{2,1,0:T(8,128)(2,1)} %shard_map.237), calls=%async_computation | async-start | bytes 589824 | tf_op jit(solution)/shard_map/all_to_all | solution.py:849
  17.6 73.9 %all-gather.7.cloned.1.call-start = ((), (), s32[]{:S(2)}) async-start(), calls=%async_computation.7 | async-start | bytes 2359296 | tf_op jit(solution)/shard_map/all_gather | solution.py:868
  24.1 7.1 %collective-permute-start = (bf16[128,640]{1,0:T(8,128)(2,1)S(1)}, bf16[128,640]{1,0:T(8,128)(2,1)S(1)}, u32[]{:S(2)}, u32[]{:S(2)}) collective-permute-start(bf16[128,640]{1,0:T(8,128)(2,1)S(1)} %slice_add_fusion), channel_id=1, source_target_pairs={{0,8},{4,12},{8,0},{12,4},{16,24},{20,28},{24,16},{28,20},{1,9},{5... | collective-permute-start | bytes 491528 | tf_op jit(solution)/shard_map/ppermute | solution.py:725
  25.7 14.0 %collective-permute-start.1 = (bf16[128,640]{1,0:T(8,128)(2,1)S(1)}, bf16[128,640]{1,0:T(8,128)(2,1)S(1)}, u32[]{:S(2)}, u32[]{:S(2)}) collective-permute-start(bf16[128,640]{1,0:T(8,128)(2,1)S(1)} %slice_add_fusion), channel_id=1, source_target_pairs={{0,16},{4,20},{8,24},{12,28},{16,0},{20,4},{24,8},{28,12},{1,17},{... | collective-permute-start | bytes 491528 | tf_op jit(solution)/shard_map/ppermute | solution.py:725
  28.3 11.4 %collective-permute-start.2 = (bf16[128,640]{1,0:T(8,128)(2,1)S(1)}, bf16[128,640]{1,0:T(8,128)(2,1)S(1)}, u32[]{:S(2)}, u32[]{:S(2)}) collective-permute-start(bf16[128,640]{1,0:T(8,128)(2,1)S(1)} %slice_add_fusion), channel_id=1, source_target_pairs={{0,24},{4,28},{8,16},{12,20},{16,8},{20,12},{24,0},{28,4},{1,25},{... | collective-permute-start | bytes 491528 | tf_op jit(solution)/shard_map/ppermute | solution.py:725
  39.8 10.0 %copy-start.2 = (bf16[4,128,640]{2,1,0:T(8,128)(2,1)}, bf16[4,128,640]{2,1,0:T(8,128)(2,1)S(1)}, u32[]{:S(2)}) copy-start(bf16[4,128,640]{2,1,0:T(8,128)(2,1)S(1)} %pad_maximum_fusion.refs_0_) | copy-start | bytes 1966084
  39.9 2.2 collective-permute-start.3
  42.0 7.9 %copy-start.7 = (bf16[4,128,640]{2,1,0:T(8,128)(2,1)}, bf16[4,128,640]{2,1,0:T(8,128)(2,1)S(1)}, u32[]{:S(2)}) copy-start(bf16[4,128,640]{2,1,0:T(8,128)(2,1)S(1)} %collective-permute-done.3.refs_1_) | copy-start | bytes 1966084
  49.9 13.1 %copy-start = (bf16[1088,1024]{1,0:T(8,128)(2,1)S(1)}, bf16[1088,1024]{1,0:T(8,128)(2,1)}, u32[]{:S(2)}) copy-start(bf16[1088,1024]{1,0:T(8,128)(2,1)} %all-gather.5.cloned.1.call-done) | copy-start | bytes 6684676
  59.5 9.9 %copy-start.25 = (f32[1,128]{1,0:T(1,128)S(1)}, f32[1,128]{1,0:T(1,128)}, u32[]{:S(2)}) copy-start(f32[1,128]{1,0:T(1,128)} %get-tuple-element.100) | copy-start | bytes 1540
  59.5 13.7 %collective-permute-start.4 = (bf16[1024,128]{1,0:T(8,128)(2,1)}, bf16[1024,128]{1,0:T(8,128)(2,1)S(1)}, u32[]{:S(2)}, u32[]{:S(2)}) collective-permute-start(bf16[1024,128]{1,0:T(8,128)(2,1)} %get-tuple-element.79), channel_id=1, source_target_pairs={{0,1},{1,0},{2,3},{3,2},{4,5},{5,4},{6,7},{7,6},{8,9},{9,8},{10,11... | collective-permute-start | bytes 786440 | tf_op jit(solution)/shard_map/ppermute | solution.py:725
  61.0 15.7 %collective-permute-start.5 = (bf16[1024,128]{1,0:T(8,128)(2,1)}, bf16[1024,128]{1,0:T(8,128)(2,1)S(1)}, u32[]{:S(2)}, u32[]{:S(2)}) collective-permute-start(bf16[1024,128]{1,0:T(8,128)(2,1)} %get-tuple-element.79), channel_id=1, source_target_pairs={{0,2},{1,3},{2,0},{3,1},{4,6},{5,7},{6,4},{7,5},{8,10},{9,11},{10,... | collective-permute-start | bytes 786440 | tf_op jit(solution)/shard_map/ppermute | solution.py:725
  61.6 15.2 %collective-permute-start.6 = (bf16[1024,128]{1,0:T(8,128)(2,1)}, bf16[1024,128]{1,0:T(8,128)(2,1)}, u32[]{:S(2)}, u32[]{:S(2)}) collective-permute-start(bf16[1024,128]{1,0:T(8,128)(2,1)} %get-tuple-element.79), channel_id=1, source_target_pairs={{0,3},{1,2},{2,1},{3,0},{4,7},{5,6},{6,5},{7,4},{8,11},{9,10},{10,... | collective-permute-start | bytes 786440 | tf_op jit(solution)/shard_map/ppermute | solution.py:725
  65.4 46.0 %all-to-all-start.2 = ((bf16[4,64,1024]{2,1,0:T(8,128)(2,1)}), bf16[4,64,1024]{2,1,0:T(8,128)(2,1)S(1)}, u32[]{:S(2)}, u32[]{:S(2)}) async-start(bf16[4,64,1024]{2,1,0:T(8,128)(2,1)} %bitcast.33), calls=%async_computation.2 | async-start | bytes 1048576 | tf_op jit(solution)/shard_map/all_to_all | solution.py:903
  68.9 7.9 %copy-start.19 = (bf16[1024,128]{1,0:T(8,128)(2,1)S(1)}, bf16[1024,128]{1,0:T(8,128)(2,1)}, u32[]{:S(2)}) copy-start(bf16[1024,128]{1,0:T(8,128)(2,1)} %get-tuple-element.79) | copy-start | bytes 786436
  68.9 215.5 %reduce-scatter.2.cloned.1.call-start = ((), (), s32[]{:S(2)}) async-start(), calls=%async_computation.5 | async-start | bytes 4718592 | tf_op jit(solution)/shard_map/reduce_scatter | solution.py:1032
  107.9 19.6 %collective-permute-start.7 = (bf16[128,1024]{1,0:T(8,128)(2,1)}, bf16[128,1024]{1,0:T(8,128)(2,1)S(1)}, u32[]{:S(2)}, u32[]{:S(2)}) collective-permute-start(bf16[128,1024]{1,0:T(8,128)(2,1)} %get-tuple-element.84), channel_id=1, source_target_pairs={{0,1},{1,0},{2,3},{3,2},{4,5},{5,4},{6,7},{7,6},{8,9},{9,8},{10,11... | collective-permute-start | bytes 786440 | tf_op jit(solution)/shard_map/ppermute | solution.py:725
  107.9 22.2 %collective-permute-start.8 = (bf16[128,1024]{1,0:T(8,128)(2,1)}, bf16[128,1024]{1,0:T(8,128)(2,1)S(1)}, u32[]{:S(2)}, u32[]{:S(2)}) collective-permute-start(bf16[128,1024]{1,0:T(8,128)(2,1)} %get-tuple-element.85), channel_id=1, source_target_pairs={{0,2},{1,3},{2,0},{3,1},{4,6},{5,7},{6,4},{7,5},{8,10},{9,11},{10,... | collective-permute-start | bytes 786440 | tf_op jit(solution)/shard_map/ppermute | solution.py:725
  108.8 21.3 %collective-permute-start.9 = (bf16[128,1024]{1,0:T(8,128)(2,1)}, bf16[128,1024]{1,0:T(8,128)(2,1)S(1)}, u32[]{:S(2)}, u32[]{:S(2)}) collective-permute-start(bf16[128,1024]{1,0:T(8,128)(2,1)} %get-tuple-element.86), channel_id=1, source_target_pairs={{0,3},{1,2},{2,1},{3,0},{4,7},{5,6},{6,5},{7,4},{8,11},{9,10},{10,... | collective-permute-start | bytes 786440 | tf_op jit(solution)/shard_map/ppermute | solution.py:725
  111.5 18.6 %copy-start.12 = (bf16[128,1024]{1,0:T(8,128)(2,1)S(1)}, bf16[128,1024]{1,0:T(8,128)(2,1)}, u32[]{:S(2)}) copy-start(bf16[128,1024]{1,0:T(8,128)(2,1)} %get-tuple-element.83) | copy-start | bytes 786436
  126.5 9.5 %collective-permute-start.10 = (bf16[128,1024]{1,0:T(8,128)(2,1)}, bf16[128,1024]{1,0:T(8,128)(2,1)S(1)}, u32[]{:S(2)}, u32[]{:S(2)}) collective-permute-start(bf16[128,1024]{1,0:T(8,128)(2,1)} %get-tuple-element.95), channel_id=1, source_target_pairs={{0,1},{1,0},{2,3},{3,2},{4,5},{5,4},{6,7},{7,6},{8,9},{9,8},{10,11... | collective-permute-start | bytes 786440 | tf_op jit(solution)/shard_map/ppermute | solution.py:725
  126.7 15.2 %collective-permute-start.11 = (bf16[128,1024]{1,0:T(8,128)(2,1)}, bf16[128,1024]{1,0:T(8,128)(2,1)S(1)}, u32[]{:S(2)}, u32[]{:S(2)}) collective-permute-start(bf16[128,1024]{1,0:T(8,128)(2,1)} %get-tuple-element.96), channel_id=1, source_target_pairs={{0,2},{1,3},{2,0},{3,1},{4,6},{5,7},{6,4},{7,5},{8,10},{9,11},{10,... | collective-permute-start | bytes 786440 | tf_op jit(solution)/shard_map/ppermute | solution.py:725
  127.5 14.3 %collective-permute-start.12 = (bf16[128,1024]{1,0:T(8,128)(2,1)}, bf16[128,1024]{1,0:T(8,128)(2,1)S(1)}, u32[]{:S(2)}, u32[]{:S(2)}) collective-permute-start(bf16[128,1024]{1,0:T(8,128)(2,1)} %get-tuple-element.97), channel_id=1, source_target_pairs={{0,3},{1,2},{2,1},{3,0},{4,7},{5,6},{6,5},{7,4},{8,11},{9,10},{10,... | collective-permute-start | bytes 786440 | tf_op jit(solution)/shard_map/ppermute | solution.py:725
  130.1 11.7 %copy-start.11 = (bf16[128,1024]{1,0:T(8,128)(2,1)S(1)}, bf16[128,1024]{1,0:T(8,128)(2,1)}, u32[]{:S(2)}) copy-start(bf16[128,1024]{1,0:T(8,128)(2,1)} %get-tuple-element.94) | copy-start | bytes 786436
  130.5 11.7 %copy-start.5 = (bf16[128,1024]{1,0:T(8,128)(2,1)}, bf16[128,1024]{1,0:T(8,128)(2,1)S(1)}, u32[]{:S(2)}) copy-start(bf16[128,1024]{1,0:T(8,128)(2,1)S(1)} %get-tuple-element.201.refs_9_) | copy-start | bytes 786436
  130.6 16.8 %collective-permute-start.13 = (bf16[128,1024]{1,0:T(8,128)(2,1)S(1)}, bf16[128,1024]{1,0:T(8,128)(2,1)S(1)}, u32[]{:S(2)}, u32[]{:S(2)}) collective-permute-start(bf16[128,1024]{1,0:T(8,128)(2,1)S(1)} %get-tuple-element.201.refs_9_), channel_id=1, source_target_pairs={{0,1},{1,0},{2,3},{3,2},{4,5},{5,4},{6,7},{7,6},{8,9},{9,8},{10,11... | collective-permute-start | bytes 786440 | tf_op jit(solution)/shard_map/ppermute | solution.py:725
  130.7 17.7 %collective-permute-start.14 = (bf16[128,1024]{1,0:T(8,128)(2,1)S(1)}, bf16[128,1024]{1,0:T(8,128)(2,1)S(1)}, u32[]{:S(2)}, u32[]{:S(2)}) collective-permute-start(bf16[128,1024]{1,0:T(8,128)(2,1)S(1)} %get-tuple-element.201.refs_9_), channel_id=1, source_target_pairs={{0,2},{1,3},{2,0},{3,1},{4,6},{5,7},{6,4},{7,5},{8,10},{9,11},{10,... | collective-permute-start | bytes 786440 | tf_op jit(solution)/shard_map/ppermute | solution.py:725
  136.1 17.0 %collective-permute-start.15 = (bf16[128,1024]{1,0:T(8,128)(2,1)S(1)}, bf16[128,1024]{1,0:T(8,128)(2,1)S(1)}, u32[]{:S(2)}, u32[]{:S(2)}) collective-permute-start(bf16[128,1024]{1,0:T(8,128)(2,1)S(1)} %get-tuple-element.201.refs_9_), channel_id=1, source_target_pairs={{0,3},{1,2},{2,1},{3,0},{4,7},{5,6},{6,5},{7,4},{8,11},{9,10},{10,... | collective-permute-start | bytes 786440 | tf_op jit(solution)/shard_map/ppermute | solution.py:725
  142.3 21.3 %copy-start.4 = (bf16[128,1024]{1,0:T(8,128)(2,1)}, bf16[128,1024]{1,0:T(8,128)(2,1)S(1)}, u32[]{:S(2)}) copy-start(bf16[128,1024]{1,0:T(8,128)(2,1)S(1)} %get-tuple-element.199.refs_9_) | copy-start | bytes 786436
  142.3 21.3 %collective-permute-start.16 = (bf16[128,1024]{1,0:T(8,128)(2,1)S(1)}, bf16[128,1024]{1,0:T(8,128)(2,1)S(1)}, u32[]{:S(2)}, u32[]{:S(2)}) collective-permute-start(bf16[128,1024]{1,0:T(8,128)(2,1)S(1)} %get-tuple-element.199.refs_9_), channel_id=1, source_target_pairs={{0,1},{1,0},{2,3},{3,2},{4,5},{5,4},{6,7},{7,6},{8,9},{9,8},{10,11... | collective-permute-start | bytes 786440 | tf_op jit(solution)/shard_map/ppermute | solution.py:725
  144.2 19.4 %collective-permute-start.17 = (bf16[128,1024]{1,0:T(8,128)(2,1)S(1)}, bf16[128,1024]{1,0:T(8,128)(2,1)S(1)}, u32[]{:S(2)}, u32[]{:S(2)}) collective-permute-start(bf16[128,1024]{1,0:T(8,128)(2,1)S(1)} %get-tuple-element.199.refs_9_), channel_id=1, source_target_pairs={{0,2},{1,3},{2,0},{3,1},{4,6},{5,7},{6,4},{7,5},{8,10},{9,11},{10,... | collective-permute-start | bytes 786440 | tf_op jit(solution)/shard_map/ppermute | solution.py:725
  147.3 6.3 %copy-start.13 = (bf16[128,1024]{1,0:T(8,128)(2,1)}, bf16[128,1024]{1,0:T(8,128)(2,1)S(1)}, u32[]{:S(2)}) copy-start(bf16[128,1024]{1,0:T(8,128)(2,1)S(1)} %collective-permute-done.13.refs_10_) | copy-start | bytes 786436
  147.3 16.3 %collective-permute-start.18 = (bf16[128,1024]{1,0:T(8,128)(2,1)S(1)}, bf16[128,1024]{1,0:T(8,128)(2,1)S(1)}, u32[]{:S(2)}, u32[]{:S(2)}) collective-permute-start(bf16[128,1024]{1,0:T(8,128)(2,1)S(1)} %get-tuple-element.199.refs_9_), channel_id=1, source_target_pairs={{0,3},{1,2},{2,1},{3,0},{4,7},{5,6},{6,5},{7,4},{8,11},{9,10},{10,... | collective-permute-start | bytes 786440 | tf_op jit(solution)/shard_map/ppermute | solution.py:725
  148.4 5.3 %copy-start.15 = (bf16[128,1024]{1,0:T(8,128)(2,1)}, bf16[128,1024]{1,0:T(8,128)(2,1)S(1)}, u32[]{:S(2)}) copy-start(bf16[128,1024]{1,0:T(8,128)(2,1)S(1)} %collective-permute-done.14.refs_11_) | copy-start | bytes 786436
  227.0 7.9 %collective-permute-start.19 = (bf16[1024,128]{1,0:T(8,128)(2,1)}, bf16[1024,128]{1,0:T(8,128)(2,1)S(1)}, u32[]{:S(2)}, u32[]{:S(2)}) collective-permute-start(bf16[1024,128]{1,0:T(8,128)(2,1)} %get-tuple-element.112.refs_1_), channel_id=1, source_target_pairs={{0,1},{1,0},{2,3},{3,2},{4,5},{5,4},{6,7},{7,6},{8,9},{9,8},{10,11... | collective-permute-start | bytes 786440 | tf_op jit(solution)/shard_map/ppermute | solution.py:725
  227.8 8.3 %collective-permute-start.20 = (bf16[1024,128]{1,0:T(8,128)(2,1)}, bf16[1024,128]{1,0:T(8,128)(2,1)S(1)}, u32[]{:S(2)}, u32[]{:S(2)}) collective-permute-start(bf16[1024,128]{1,0:T(8,128)(2,1)} %get-tuple-element.112.refs_1_), channel_id=1, source_target_pairs={{0,2},{1,3},{2,0},{3,1},{4,6},{5,7},{6,4},{7,5},{8,10},{9,11},{10,... | collective-permute-start | bytes 786440 | tf_op jit(solution)/shard_map/ppermute | solution.py:725
  229.0 8.4 %collective-permute-start.21 = (bf16[1024,128]{1,0:T(8,128)(2,1)}, bf16[1024,128]{1,0:T(8,128)(2,1)S(1)}, u32[]{:S(2)}, u32[]{:S(2)}) collective-permute-start(bf16[1024,128]{1,0:T(8,128)(2,1)} %get-tuple-element.112.refs_1_), channel_id=1, source_target_pairs={{0,3},{1,2},{2,1},{3,0},{4,7},{5,6},{6,5},{7,4},{8,11},{9,10},{10,... | collective-permute-start | bytes 786440 | tf_op jit(solution)/shard_map/ppermute | solution.py:725
  231.4 23.0 %all-to-all-start.1 = ((bf16[4,64,1024]{2,1,0:T(8,128)(2,1)}), bf16[4,64,1024]{2,1,0:T(8,128)(2,1)S(1)}, u32[]{:S(2)}, u32[]{:S(2)}) async-start(bf16[4,64,1024]{2,1,0:T(8,128)(2,1)} %pad_maximum_fusion.2), calls=%async_computation.1 | async-start | bytes 1048576 | tf_op jit(solution)/shard_map/all_to_all | solution.py:1021
  234.9 2.5 copy-start.14
  249.0 5.2 %copy-start.1 = (bf16[1,256,1024]{2,1,0:T(8,128)(2,1)S(1)}, bf16[1,256,1024]{2,1,0:T(8,128)(2,1)}, u32[]{:S(2)}) copy-start(bf16[1,256,1024]{2,1,0:T(8,128)(2,1)} %param.14) | copy-start | bytes 1572868
  249.0 5.4 %copy-start.33 = (bf16[256,1024]{1,0:T(8,128)(2,1)S(1)}, bf16[256,1024]{1,0:T(8,128)(2,1)}, u32[]{:S(2)}) copy-start(bf16[256,1024]{1,0:T(8,128)(2,1)} %get-tuple-element.129) | copy-start | bytes 1572868
  249.0 6.7 %copy-start.32 = (bf16[256,1024]{1,0:T(8,128)(2,1)S(1)}, bf16[256,1024]{1,0:T(8,128)(2,1)}, u32[]{:S(2)}) copy-start(bf16[256,1024]{1,0:T(8,128)(2,1)} %get-tuple-element.130) | copy-start | bytes 1572868
  249.0 8.2 %copy-start.31 = (bf16[256,1024]{1,0:T(8,128)(2,1)S(1)}, bf16[256,1024]{1,0:T(8,128)(2,1)}, u32[]{:S(2)}) copy-start(bf16[256,1024]{1,0:T(8,128)(2,1)} %get-tuple-element.131) | copy-start | bytes 1572868
  249.0 9.0 %copy-start.30 = (f32[1,128]{1,0:T(1,128)S(1)}, f32[1,128]{1,0:T(1,128)}, u32[]{:S(2)}) copy-start(f32[1,128]{1,0:T(1,128)} %get-tuple-element.120) | copy-start | bytes 1540
  254.2 3.8 %collective-permute-start.22 = (bf16[4,176,512]{2,1,0:T(8,128)(2,1)}, bf16[4,176,512]{2,1,0:T(8,128)(2,1)S(1)}, u32[]{:S(2)}, u32[]{:S(2)}) collective-permute-start(bf16[4,176,512]{2,1,0:T(8,128)(2,1)} %get-tuple-element.125), channel_id=1, source_target_pairs={{0,4},{4,0},{8,12},{12,8},{16,20},{20,16},{24,28},{28,24},{1,5},{5... | collective-permute-start | bytes 2162696 | tf_op jit(solution)/shard_map/ppermute | solution.py:725
  254.4 14.8 %collective-permute-start.26 = (bf16[256,1024]{1,0:T(8,128)(2,1)S(1)}, bf16[256,1024]{1,0:T(8,128)(2,1)S(1)}, u32[]{:S(2)}, u32[]{:S(2)}) collective-permute-start(bf16[256,1024]{1,0:T(8,128)(2,1)S(1)} %copy-done.33), channel_id=1, source_target_pairs={{0,1},{1,0},{2,3},{3,2},{4,5},{5,4},{6,7},{7,6},{8,9},{9,8},{10,11... | collective-permute-start | bytes 1572872 | tf_op jit(solution)/shard_map/ppermute | solution.py:725
  255.7 25.3 %collective-permute-start.27 = (bf16[256,1024]{1,0:T(8,128)(2,1)S(1)}, bf16[256,1024]{1,0:T(8,128)(2,1)S(1)}, u32[]{:S(2)}, u32[]{:S(2)}) collective-permute-start(bf16[256,1024]{1,0:T(8,128)(2,1)S(1)} %copy-done.32), channel_id=1, source_target_pairs={{0,2},{1,3},{2,0},{3,1},{4,6},{5,7},{6,4},{7,5},{8,10},{9,11},{10,... | collective-permute-start | bytes 1572872 | tf_op jit(solution)/shard_map/ppermute | solution.py:725
  257.2 23.8 %collective-permute-start.28 = (bf16[256,1024]{1,0:T(8,128)(2,1)S(1)}, bf16[256,1024]{1,0:T(8,128)(2,1)S(1)}, u32[]{:S(2)}, u32[]{:S(2)}) collective-permute-start(bf16[256,1024]{1,0:T(8,128)(2,1)S(1)} %copy-done.31), channel_id=1, source_target_pairs={{0,3},{1,2},{2,1},{3,0},{4,7},{5,6},{6,5},{7,4},{8,11},{9,10},{10,... | collective-permute-start | bytes 1572872 | tf_op jit(solution)/shard_map/ppermute | solution.py:725
  258.2 22.8 %copy-start.3 = (bf16[256,1024]{1,0:T(8,128)(2,1)S(1)}, bf16[256,1024]{1,0:T(8,128)(2,1)}, u32[]{:S(2)}) copy-start(bf16[256,1024]{1,0:T(8,128)(2,1)} %get-tuple-element.128) | copy-start | bytes 1572868
  258.2 22.8 %copy-start.23 = (f32[1,1024]{1,0:T(1,128)S(1)}, f32[1,1024]{1,0:T(1,128)}, u32[]{:S(2)}) copy-start(f32[1,1024]{1,0:T(1,128)} %get-tuple-element.132) | copy-start | bytes 12292
  259.9 24.3 %collective-permute-start.23 = (bf16[176,512]{1,0:T(8,128)(2,1)S(1)}, bf16[176,512]{1,0:T(8,128)(2,1)S(1)}, u32[]{:S(2)}, u32[]{:S(2)}) collective-permute-start(bf16[176,512]{1,0:T(8,128)(2,1)S(1)} %get-tuple-element.196), channel_id=1, source_target_pairs={{0,8},{4,12},{8,0},{12,4},{16,24},{20,28},{24,16},{28,20},{1,9},{5... | collective-permute-start | bytes 540680 | tf_op jit(solution)/shard_map/ppermute | solution.py:725
  261.4 22.8 %collective-permute-start.24 = (bf16[176,512]{1,0:T(8,128)(2,1)S(1)}, bf16[176,512]{1,0:T(8,128)(2,1)S(1)}, u32[]{:S(2)}, u32[]{:S(2)}) collective-permute-start(bf16[176,512]{1,0:T(8,128)(2,1)S(1)} %get-tuple-element.197), channel_id=1, source_target_pairs={{0,16},{4,20},{8,24},{12,28},{16,0},{20,4},{24,8},{28,12},{1,17},{... | collective-permute-start | bytes 540680 | tf_op jit(solution)/shard_map/ppermute | solution.py:725
  269.2 14.9 %collective-permute-start.25 = (bf16[176,512]{1,0:T(8,128)(2,1)S(1)}, bf16[176,512]{1,0:T(8,128)(2,1)S(1)}, u32[]{:S(2)}, u32[]{:S(2)}) collective-permute-start(bf16[176,512]{1,0:T(8,128)(2,1)S(1)} %get-tuple-element.198), channel_id=1, source_target_pairs={{0,24},{4,28},{8,16},{12,20},{16,8},{20,12},{24,0},{28,4},{1,25},{... | collective-permute-start | bytes 540680 | tf_op jit(solution)/shard_map/ppermute | solution.py:725
  284.3 7.1 %slice-start = ((f32[1,256,512]{2,1,0:T(8,128)}), f32[1,128,512]{2,1,0:T(8,128)S(1)}, s32[]{:S(2)}) async-start(f32[1,256,512]{2,1,0:T(8,128)} %reduce-scatter.2.cloned.1.call-done), calls=%async_computation.8 | async-start | bytes 524288 | tf_op jit(solution)/shard_map/slice | solution.py:1111
  286.1 8.8 %all-to-all-start.3 = ((bf16[4,32,1024]{2,1,0:T(8,128)(2,1)}), bf16[4,32,1024]{2,1,0:T(8,128)(2,1)S(1)}, u32[]{:S(2)}, u32[]{:S(2)}) async-start(bf16[4,32,1024]{2,1,0:T(8,128)(2,1)} %pad_maximum_fusion.4), calls=%async_computation.4 | async-start | bytes 524288 | tf_op jit(solution)/shard_map/all_to_all | solution.py:1107
  (7 other events, 5.8 us)
Sparse Core Ops, SparseCore 0:
  10.8 39.0 all-gather.4
  52.1 29.0 all-gather.6
  181.3 50.0 reduce-scatter.1

commit v5 on v4

--- a/solution.py
+++ b/solution.py
@@ -58,6 +58,11 @@
     return jnp.maximum(v, 0.0) + jnp.log1p(jnp.exp(-jnp.abs(v)))
 
 
+def slope_of(step):
+    small = step * (1.0 - step * (0.5 - step * (1.0 / 6.0 - step * (1.0 / 24.0))))
+    return jnp.where(step < 0.02, small, 1.0 - jnp.exp(-step))
+
+
 def columns(proj_t, first, n, into_ref):
     for j in range(into_ref.shape[0]):
         into_ref[j] = proj_t[first : first + n, j * BLOCK : (j + 1) * BLOCK]
@@ -78,8 +83,8 @@
     return x * lax.rsqrt(jnp.mean(x * x, axis=-1, keepdims=True) + 1e-05)
 
 
-def start_kernel(me_ref, x_ref, *refs):
-    parts = refs[:-14]
+def start_kernel(count, me_ref, x_ref, *refs):
+    bottom, parts = refs[:count], refs[count:-14]
     (
         normed_ref, turned_ref, stream_ref, pre_ref, act_ref, proj_ref, w_ref, vec_ref, xproj_ref, gain_ref, marks_ref,
         wide_ref, ext_ref, cols_ref,
@@ -113,7 +118,10 @@
             vec_ref[:, at] = cols_ref[at, :].T
         marks_ref[...] = jnp.sum(ext_ref[...], axis=0, keepdims=True)
 
-    normed = (unit_of(x_ref[...].astype(f32)) * gain_ref[...]).astype(bf16)
+    x = x_ref[...]
+    if count:
+        x = jnp.concatenate([x, read_slot(bottom, pl.program_id(0) ^ me_ref[0])], axis=0)
+    normed = (unit_of(x.astype(f32)) * gain_ref[...]).astype(bf16)
     normed_ref[...] = normed
     turned_ref[...] = normed.T
     stream = dot(normed, w_ref[...]).astype(bf16)
@@ -139,7 +147,7 @@
     return blocks
 
 
-def piece_kernel(me_ref, proj_ref, act_ref, vec_ref, g_ref, carry_ref, u_ref, stepm_ref, col_ref):
+def piece_kernel(me_ref, proj_ref, act_ref, vec_ref, g_ref, step_ref, carry_ref, u_ref, stepm_ref, col_ref):
     rows, c = act_ref.shape
     n = carry_ref.shape[0]
 
@@ -150,6 +158,7 @@
     proj = proj_ref[...]
     _, pre = dt_of(proj, vec_ref, INTO)
     step = softplus(pre)
+    step_ref[...] = step
     u_ref[...] = step * act_ref[...].astype(f32)
     stepm_ref[...] = jnp.where(proj[:, CARRY : CARRY + 1] > 0.5, step, NEVER)
     columns(proj.T, INTO, n, col_ref)
@@ -171,15 +180,15 @@
 def ahead_kernel(
     first, places, per, local, me_ref, *refs,
 ):
-    proj_ref, act_ref, normed_ref, g_ref, vec_ref, enter_ref = refs[:6]
+    proj_ref, act_ref, normed_ref, g_ref, step_ref, vec_ref, enter_ref = refs[:7]
     if first:
-        wgate_ref, outw_ref = refs[6:8]
-        hp_ref, mixed_ref, gate_ref, gated_ref, leave_ref = refs[-8 - places - 5 : -8 - places]
+        wgate_ref, outw_ref = refs[7:9]
+        hp_ref, mixed_ref, gate_ref, gated_ref, leave_ref = refs[-7 - places - 5 : -7 - places]
     else:
-        second_ref = refs[6]
-        hp_ref, mixed_ref, gate_ref, gated_ref, leave_ref, wgate_ref, outw_ref = refs[-8 - places - 7 : -8 - places]
-    branch_refs = refs[-8 - places : -8]
-    carry_ref, u_ref, step_ref, col_ref, diag_ref, s_ref, y_ref, out_ref = refs[-8:]
+        second_ref = refs[7]
+        hp_ref, mixed_ref, gate_ref, gated_ref, leave_ref, wgate_ref, outw_ref = refs[-7 - places - 7 : -7 - places]
+    branch_refs = refs[-7 - places : -7]
+    carry_ref, u_ref, col_ref, diag_ref, s_ref, y_ref, out_ref = refs[-7:]
     rows, c = act_ref.shape
     n = carry_ref.shape[0]
 
@@ -199,10 +208,7 @@
 
     proj = proj_ref[...]
     act = act_ref[...].astype(f32)
-    _, pre = dt_of(proj, vec_ref, INTO)
-    step = softplus(pre)
-    step_ref[...] = step
-    u_ref[...] = step * act
+    u_ref[...] = step_ref[...] * act
     columns(proj.T, INTO, n, col_ref)
     read = proj[:, OUT : OUT + n]
     high = read.astype(bf16)
@@ -236,15 +242,15 @@
     gated = (mixed * (gate * sigmoid(gate))).astype(bf16)
     gated_ref[...] = gated.T
     out_ref[...] = dot(gated, outw_ref[...]).astype(bf16)
-    write_rows(branch_refs, me_ref, places, per, local, out_ref)
+    write_rows(branch_refs, me_ref, places, per, local, rows, out_ref)
     leave_ref[...] = carry_ref[...]
 
 
 def piece_grad_kernel(
     first, places, per, local, me_ref, *refs,
 ):
-    proj_ref, act_ref, mixed_ref, gate_ref, vec_ref, outw_ref, enter_ref, before_ref = refs[:8]
-    db_refs = refs[8 : 8 + places]
+    proj_ref, act_ref, mixed_ref, gate_ref, step_ref, vec_ref, outw_ref, enter_ref, before_ref = refs[:9]
+    db_refs = refs[9 : 9 + places]
     q_ref, dm_ref, dg_ref, db_ref, sgrad_ref, leave_ref = refs[-9:-3]
     carry_ref, stepm_ref, col_ref = refs[-3:]
     rows, c = act_ref.shape
@@ -256,10 +262,9 @@
         sgrad_ref[...] = before_ref[...]
 
     proj = proj_ref[...]
-    _, pre = dt_of(proj, vec_ref, INTO)
-    stepm_ref[...] = jnp.where(proj[:, CARRY : CARRY + 1] > 0.5, softplus(pre), NEVER)
+    stepm_ref[...] = jnp.where(proj[:, CARRY : CARRY + 1] > 0.5, step_ref[...], NEVER)
     columns(proj.T, OUT, n, col_ref)
-    db = read_rows(db_refs, me_ref, places, per, local)
+    db = read_rows(db_refs, me_ref, places, per, local, rows)
     db_ref[...] = db
     dgated = dot_t(db, outw_ref[...])
     gate = gate_ref[...]
@@ -300,9 +305,9 @@
 
 
 def state_grad_kernel(
-    me_ref, proj_ref, act_ref, dm_ref, g_ref, hp_ref, q_ref, vec_ref, sgrad_ref, pieces_ref,
+    me_ref, proj_ref, act_ref, dm_ref, g_ref, hp_ref, q_ref, step_ref, vec_ref, sgrad_ref, pieces_ref,
     dact_ref, dproj_ref, table_ref,
-    carry_ref, u_ref, step_ref, col_ref, diag_ref, ig_ref, rr_ref, pair_ref, own_ref, x_ref, y_ref, dp_ref,
+    carry_ref, u_ref, col_ref, diag_ref, ig_ref, rr_ref, pair_ref, own_ref, x_ref, y_ref, dp_ref,
 ):
     rows, c = act_ref.shape
     n = carry_ref.shape[0]
@@ -316,10 +321,8 @@
 
     proj = proj_ref[...]
     act = act_ref[...].astype(f32)
-    low, pre = dt_of(proj, vec_ref, INTO)
-    step = softplus(pre)
-    step_ref[...] = step
-    u_ref[...] = step * act
+    low = proj[:, :INTO].astype(bf16)
+    u_ref[...] = step_ref[...] * act
     columns(proj.T, OUT, n, col_ref)
     diag_ref[:rows] = block_diag(proj[:, INTO : INTO + n].astype(bf16), n)
     r2 = rates_of(vec_ref, n)
@@ -377,7 +380,7 @@
     dp_ref[:BLOCK, :] = dot(by_row, own_ref[...])
     xs = x_ref[:rows]
     dact_ref[...] = step_ref[...] * xs + vec_ref[SKIP : SKIP + 1, :] * dm_ref[...]
-    dpre = (y_ref[:rows] * LN2 + act * xs) * sigmoid(pre)
+    dpre = (y_ref[:rows] * LN2 + act * xs) * slope_of(step_ref[...])
     table_ref[DTB : DTB + 1, :] += jnp.sum(dpre, axis=0, keepdims=True)
     dpre_low = dpre.astype(bf16)
     table_ref[:INTO, :] += t_dot(low, dpre_low)
@@ -390,14 +393,16 @@
         table_ref[ALOG : ALOG + n, :] *= -jnp.exp(vec_ref[ALOG : ALOG + n, :])
 
 
-def end_kernel(own, local, count, me_ref, *refs):
-    dn_refs, refs = refs[-count - 8 : -8], refs[: -count - 8] + refs[-8:]
-    parts = refs[:-18]
+def end_kernel(own, local, count, paired, me_ref, *refs):
+    sent = 2 if paired else 1
+    dn_refs, refs = refs[-count - sent - 6 : -sent - 6], refs[: -count - sent - 6] + refs[-sent - 6 :]
+    late_refs, refs = refs[-sent - 6 : -6], refs[: -sent - 6] + refs[-6:]
+    parts = refs[:-17]
     (
-        dact_ref, pre_ref, stream_ref, act_ref, dg_ref, vec_ref, xproj_ref, ws_ref, wg_ref, table_ref,
-        ds_ref, small_ref, pieces_ref, sum_ref,
-        wide_ref, xgrad_ref, cgrad_ref, turned_ref,
-    ) = refs[-18:]
+        dact_ref, pre_ref, stream_ref, act_ref, dg_ref, vec_ref, xproj_ref, ws_ref, wg_ref, table_ref, normed_ref,
+        sum_ref,
+        wide_ref, xgrad_ref, cgrad_ref, turned_ref, grad_ref,
+    ) = refs[-17:]
     rows, c = act_ref.shape
     taps = CONVB - CONV
 
@@ -406,6 +411,7 @@
         wide_ref[rows:, :] = jnp.zeros((8, c), f32)
         xgrad_ref[...] = jnp.zeros_like(xgrad_ref)
         cgrad_ref[...] = table_ref[...]
+        grad_ref[...] = jnp.zeros_like(grad_ref)
 
     dproj = parts[0][...].astype(f32)
     for part in parts[1:]:
@@ -429,7 +435,7 @@
     dstream_low = dstream.astype(bf16)
     dn = (dot_t(dstream_low, ws_ref[...]) + dot_t(dg_ref[...], wg_ref[...])).astype(bf16)
     write_slot(dn_refs, slot_of(me_ref, local, True), dn)
-    ds_ref[...] = dstream_low
+    grad_ref[...] += dot(normed_ref[...], dstream_low)
 
     @pl.when(pl.program_id(0) == pl.num_programs(0) - 1)
     def _():
@@ -445,14 +451,26 @@
             term = sums.astype(bf16).astype(f32)
             pieces = [jnp.where(row == k, term, pieces[0])]
             sums = sums - term
-        for k in range(c // LANES):
-            pieces_ref[:, k * LANES : (k + 1) * LANES] = pieces[0].astype(bf16)
-        lines = 2 * own * LANES // c
-        for b in range(c // own):
+        pieces = jnp.concatenate([pieces[0].astype(bf16)] * (c // LANES), axis=1)
+        packed, lines = 2 * own * LANES // c, grad_ref.shape[0] * own // c
+
+        def block(b):
             at = slice(b * own, (b + 1) * own)
             both = jnp.concatenate([xgrad_ref[at, :], turned_ref[at, :]], axis=0)
-            for k in range(c // LANES):
-                small_ref[b * lines : (b + 1) * lines, k * LANES : (k + 1) * LANES] = both[k * lines : (k + 1) * lines]
+            small = [both[k * packed : (k + 1) * packed] for k in range(c // LANES)]
+            return grad_ref[b * lines : (b + 1) * lines, :], jnp.concatenate(small, axis=1)
+
+        if not paired:
+            for b in range(c // own):
+                late_refs[0][b, :lines, :], late_refs[0][b, lines:, :] = block(b)
+            return
+        mine_ref, theirs_ref = late_refs
+        first = me_ref[me_ref.shape[0] - 1] == 0
+        for z in range(c // own // 2):
+            for part, at, end in zip(zip(block(2 * z), block(2 * z + 1)), (0, lines), (lines, lines + packed)):
+                mine_ref[z, at:end, :] = jnp.where(first, part[0], part[1])
+                theirs_ref[z, at:end, :] = jnp.where(first, part[1], part[0]).astype(bf16)
+            theirs_ref[z, lines + packed :, :] = pieces
 
 
 def slot_of(me_ref, local, reverse=False):
@@ -462,13 +480,13 @@
     return (step // (local // ROWS)) ^ me_ref[0]
 
 
-def read_rows(refs, me_ref, places, per, local):
+def read_rows(refs, me_ref, places, per, local, size):
     step = pl.program_id(0)
-    each = ROWS // per
-    at = pl.ds(pl.multiple_of(step // (local // ROWS) * per, per), per)
+    each = size // per
+    at = pl.ds(pl.multiple_of(step // (local // size) * per, per), per)
     pieces = []
     for p in range(each):
-        j = step % (local // ROWS) * each + p
+        j = step % (local // size) * each + p
         if len(refs) == 1:
             pieces.append(refs[0][j, at, :])
             continue
@@ -479,11 +497,18 @@
     return jnp.concatenate(pieces, axis=0)
 
 
-def write_rows(refs, me_ref, places, per, local, from_ref):
+def read_slot(refs, slot):
+    value = refs[0][...]
+    for k in range(1, len(refs)):
+        value = jnp.where(slot == k, refs[k][...], value)
+    return value
+
+
+def write_rows(refs, me_ref, places, per, local, size, from_ref):
     step = pl.program_id(0)
-    each = ROWS // per
-    at = pl.ds(pl.multiple_of(step // (local // ROWS) * per, per), per)
-    sub = step % (local // ROWS)
+    each = size // per
+    at = pl.ds(pl.multiple_of(step // (local // size) * per, per), per)
+    sub = step % (local // size)
     if len(refs) == 1:
         for p in range(each):
             refs[0][sub * each + p, at, :] = from_ref[p * per : (p + 1) * per, :]
@@ -538,8 +563,10 @@
             return pl.BlockSpec(
                 (shape[0], size), lambda i, me_ref: (0, turn(i))
             )
-        if kind == "y":
-            return pl.BlockSpec((None, size, shape[2]), lambda i, me_ref: (turn(i) // per, turn(i) % per, 0))
+        if isinstance(kind, tuple):
+            return pl.BlockSpec(
+                (None, min(size, kind[1]), shape[2]), lambda i, me_ref: (turn(i) // per, turn(i) % per, 0)
+            )
         if kind == "x":
             return pl.BlockSpec(
                 (None, size, shape[2]), lambda i, me_ref: ((turn(i) // per) ^ me_ref[0], turn(i) % per, 0)
@@ -589,51 +616,6 @@
             out_ref[b, lines + k * own : lines + (k + 1) * own, :] = out[
                 b * own : (b + 1) * own, k * c : (k + 1) * c
             ]
-
-
-def late_grad_kernel(normed_ref, small_ref, ds_ref, out_ref):
-    group, rows, c = out_ref.shape
-    lines = normed_ref.shape[0] // group
-    packed = rows - lines
-    stream = dot(normed_ref[...], ds_ref[...])
-    for b in range(group):
-        out_ref[b, :lines, :] = stream[b * lines : (b + 1) * lines]
-        out_ref[b, lines:, :] = small_ref[b * packed : (b + 1) * packed, :]
-
-
-def late_pair_kernel(me_ref, normed_ref, small_ref, ds_ref, pieces_ref, mine_ref, theirs_ref):
-    rows = mine_ref.shape[1]
-    lines = normed_ref.shape[0] // 2
-    packed = rows - lines
-    stream = dot(normed_ref[...], ds_ref[...])
-    small = small_ref[...]
-    first = me_ref[0] == 0
-    mine_ref[0, :lines, :] = jnp.where(first, stream[:lines], stream[lines:])
-    mine_ref[0, lines:, :] = jnp.where(first, small[:packed], small[packed:])
-    theirs_ref[0, :lines, :] = jnp.where(first, stream[lines:], stream[:lines]).astype(bf16)
-    theirs_ref[0, lines:rows, :] = jnp.where(first, small[packed:], small[:packed]).astype(bf16)
-    theirs_ref[0, rows:, :] = pieces_ref[...]
-
-
-def late_pairs(normed_t, small, ds, pieces, batches, rows, chans):
-    steps = batches // 2
-    whole = lambda a: pl.BlockSpec(a.shape, lambda i, me_ref: (0, 0))
-    cut = lambda a: pl.BlockSpec((a.shape[0] // steps, a.shape[1]), lambda i, me_ref: (i, 0))
-    block = lambda r: pl.BlockSpec((1, r, chans), lambda i, me_ref: (i, 0, 0))
-    return pl.pallas_call(
-        late_pair_kernel,
-        out_shape=[
-            jax.ShapeDtypeStruct((steps, rows, chans), f32),
-            jax.ShapeDtypeStruct((steps, rows + BLOCK, chans), bf16),
-        ],
-        grid_spec=pltpu.PrefetchScalarGridSpec(
-            num_scalar_prefetch=1,
-            grid=(steps,),
-            in_specs=[cut(normed_t), cut(small), whole(ds), whole(pieces)],
-            out_specs=[block(rows), block(rows + BLOCK)],
-        ),
-        compiler_params=pltpu.CompilerParams(dimension_semantics=("arbitrary",), vmem_limit_bytes=60 << 20),
-    )((lax.axis_index("batch") % 2).astype(jnp.int32).reshape(1), normed_t, small, ds, pieces)
 
 
 def by_blocks(kernel, batches, own, columns, whole, rows, chans):
@@ -844,7 +826,9 @@
 
     flags = jnp.concatenate([piece_starts, valid_rows], axis=0).astype(bf16)
     flags = jnp.pad(flags, ((0, 14), (0, width - rows)))
-    everything = lax.all_gather(jnp.concatenate([tok, flags], axis=0), "seq")
+    top = rows // 2 if seqs <= 4 else rows
+    bottom = gather_parts(tok[top:], "seq") if top < rows else []
+    everything = lax.all_gather(jnp.concatenate([tok[:top], flags], axis=0), "seq")
     split = split_columns(in_weight, norm_gain.reshape(1, depth), valid_rows, seqs, batches, own)
     split = lax.all_to_all(split, "seq", 0, 0).reshape(lines, 2 * chans + LANES)
     vectors = jnp.concatenate(
@@ -872,9 +856,9 @@
     low_tile = ((total, chans), bf16, "t")
     state = ((total * states, chans), bf16, "t")
     normed, normed_t, stream, conv_pre, act, proj, w_stream, vec, xproj, gain, marks = call(
-        start_kernel,
+        lambda *refs: start_kernel(len(bottom), *refs),
         jnp.concatenate([me] + [p.astype(jnp.int32).reshape(1) for p in places]),
-        [(everything, "y")] + [(block, "f") for block in blocks],
+        [(everything, ("y", top))] + [(part, "f") for part in bottom] + [(block, "f") for block in blocks],
         [
             ((total, width), bf16, "t"),
             ((width, total), bf16, "c"),
@@ -893,7 +877,7 @@
         rows,
     )
     total_valid = (marks[:, LANES - 2 : LANES - 1] * 128.0 + marks[:, LANES - 1 :]) / depth
-    starts = everything[:, rows, :rows].astype(f32).reshape(total)
+    starts = everything[:, top, :rows].astype(f32).reshape(total)
     running = jnp.cumsum(starts)
     lagged = jnp.concatenate([jnp.zeros((PIECE,), f32), running[: total - PIECE]])
     carry_on = jnp.where(running - lagged > 0.5, 1.0 - starts, 0.0)
@@ -905,11 +889,11 @@
     me = jnp.concatenate([me, flags])
     proj = jnp.where(jnp.arange(LANES)[None, :] == CARRY, carry_on[:, None], proj)
     groups = (ROWS // BLOCK, states, BLOCK)
-    (g,) = call(
+    g, step = call(
         piece_kernel,
         me,
         [(proj, "t"), (act, "t"), (vec, "f")],
-        [state],
+        [state, tile],
         [
             pltpu.VMEM((states, chans), f32),
             pltpu.VMEM((ROWS, chans), f32),
@@ -931,8 +915,15 @@
     by_time = [state, tile, tile, ((chans, total), bf16, "c")]
     weights = [((width, chans), bf16, "f"), ((chans, width), bf16, "f")]
     mine = lambda v: lax.dynamic_slice_in_dim(v, lax.axis_index("seq") * per, per, axis=1)
-    tok_v = mine(everything[:, :rows]).astype(f32)
-    valid_v = mine(everything[:, rows + 1, :rows].reshape(seqs, rows, 1)).astype(f32)
+    if bottom:
+        above = top // per
+        tok_v = jnp.stack([lax.dynamic_slice_in_dim(b, jnp.maximum(place - above, 0) * per, per, axis=0) for b in bottom])
+        tok_v = jnp.take(tok_v, jnp.arange(seqs) ^ place, axis=0)
+        tops = lax.dynamic_slice_in_dim(everything, jnp.minimum(place, above - 1) * per, per, axis=1)
+        tok_v = jnp.where(place < above, tops, tok_v).astype(f32)
+    else:
+        tok_v = mine(everything[:, :rows]).astype(f32)
+    valid_v = mine(everything[:, top + 1, :rows].reshape(seqs, rows, 1)).astype(f32)
     enter = jnp.zeros((states, chans), f32)
     kept = []
     branches = []
@@ -940,24 +931,24 @@
         out = call(
             lambda *refs, half=half: ahead_kernel(half, places, per, rows, *refs),
             me,
-            [(proj, "t"), (act, "t"), (normed, "t"), (g, "t"), (vec, "f"), (enter, "f")]
+            [(proj, "t"), (act, "t"), (normed, "t"), (g, "t"), (step, "t"), (vec, "f"), (enter, "f")]
             + ([(w_gate, "f"), (out_w, "f")] if half else [(second, "f")])
             + [(array, "o") for array in kept],
             by_time + [((states, chans), f32, "f")] + ([] if half else weights) + messages,
             [
                 pltpu.VMEM((states, chans), f32),
-                pltpu.VMEM((ROWS, chans), f32),
-                pltpu.VMEM((ROWS, chans), f32),
-                pltpu.VMEM(groups, f32),
-                pltpu.VMEM((2, ROWS + BLOCK, BLOCK * states), bf16),
+                pltpu.VMEM((HALF, chans), f32),
+                pltpu.VMEM((HALF // BLOCK, states, BLOCK), f32),
+                pltpu.VMEM((2, HALF + BLOCK, BLOCK * states), bf16),
                 pltpu.VMEM((BLOCK * states, chans), bf16),
-                pltpu.VMEM((ROWS + BLOCK, chans), f32),
-                pltpu.VMEM((ROWS, width), bf16),
+                pltpu.VMEM((HALF + BLOCK, chans), f32),
+                pltpu.VMEM((HALF, width), bf16),
             ],
             total,
             rows,
-            first=half * count,
-            count=count,
+            first=half * count * ROWS // HALF,
+            count=count * ROWS // HALF,
+            size=HALF,
         )
         kept, enter = out[:4], out[4]
         if not half:
@@ -996,6 +987,7 @@
                 (act, "t"),
                 (mixed, "t"),
                 (gate, "t"),
+                (step, "t"),
                 (vec, "f"),
                 (out_w, "f"),
                 (enter, "f"),
@@ -1034,11 +1026,10 @@
     d_act, d_proj, table = call(
         state_grad_kernel,
         me,
-        [(proj, "t"), (act, "t"), (d_mixed, "t"), (g, "t"), (hp, "t"), (q, "t"), (vec, "f"), (skip_grad, "f"), (pieces, "f")],
+        [(proj, "t"), (act, "t"), (d_mixed, "t"), (g, "t"), (hp, "t"), (q, "t"), (step, "t"), (vec, "f"), (skip_grad, "f"), (pieces, "f")],
         [tile, ((total, LANES), bf16, "t"), ((LANES, chans), f32, "f")],
         [
             pltpu.VMEM((states, chans), f32),
-            pltpu.VMEM((HALF, chans), f32),
             pltpu.VMEM((HALF, chans), f32),
             pltpu.VMEM((HALF // BLOCK, states, BLOCK), f32),
             pltpu.VMEM((HALF + BLOCK, BLOCK * states), bf16),
@@ -1057,9 +1048,16 @@
     )
     d_proj = share_parts(d_proj, "seq")
     slots = slots_out(seqs, rows, width)
-    *d_normed, d_stream, small, sent, seq_sum = call(
-        lambda *refs: end_kernel(own, rows, len(slots), *refs),
-        me,
+    paired = batches <= 8
+    size = lines + packed
+    if paired:
+        lates = [((batches // 2, size, chans), f32, "f"), ((batches // 2, size + BLOCK, chans), bf16, "f")]
+    else:
+        lates = [((batches, size, chans), f32, "f")]
+    core = (lax.axis_index("batch") % 2).astype(jnp.int32).reshape(1)
+    out = call(
+        lambda *refs: end_kernel(own, rows, len(slots), paired, *refs),
+        jnp.concatenate([me, core]),
         [(part, "t") for part in d_proj]
         + [
             (d_act, "t"),
@@ -1072,38 +1070,35 @@
             (w_stream, "f"),
             (w_gate, "f"),
             (table, "f"),
+            (normed_t, "c"),
         ],
-        slots
-        + [
-            low_tile,
-            ((batches * packed, chans), f32, "f"),
-            ((BLOCK, chans), bf16, "f"),
-            ((1, LANES), f32, "f"),
-        ],
+        slots + lates + [((1, LANES), f32, "f")],
         [
             pltpu.VMEM((ROWS + 8, chans), f32),
             pltpu.VMEM((chans, LANES), f32),
             pltpu.VMEM((LANES, chans), f32),
             pltpu.VMEM((chans, LANES), f32),
+            pltpu.VMEM((width, chans), f32),
         ],
         total,
         rows,
         reverse=True,
     )
-    if batches <= 8:
-        mine, theirs = late_pairs(normed_t, small, d_stream, sent, batches, lines + packed, chans)
-        late, square_sum, waiting = scatter_batch(mine, theirs, seq_sum)
+    d_normed, seq_sum = out[: len(slots)], out[-1]
+    if paired:
+        late, square_sum, waiting = scatter_batch(out[-3], out[-2], seq_sum)
     else:
-        late = by_blocks(
-            late_grad_kernel, batches, own, [normed_t, small], [d_stream], lines + packed, chans
-        )
-        waiting = late
-        late = lax.psum_scatter(late, "batch", scatter_dimension=0)
+        waiting = out[-2]
+        late = lax.psum_scatter(out[-2], "batch", scatter_dimension=0)
         square_sum = sum_everywhere(square_sum, ("batch", "seq"))
     loss = jnp.sum(square_sum) / (total_valid * width)[0, 0]
-    nothing = waiting[0, :1].astype(f32) * 0.0
-    d_normed = added([jnp.tile(nothing, (1, width // chans))] + scatter_parts(d_normed, "seq"))
     in_out = jnp.concatenate([late[:lines], early[:lines]], axis=1).astype(bf16)
+    if False:
+        row = (waiting[0, :1] * 0).astype(bf16)
+        d_normed = list(d_normed)
+        d_normed[-1] = d_normed[-1] + jnp.tile(row, (1, width // chans))
+    row = in_out[:1].astype(f32) * 0.0
+    d_normed = added([jnp.tile(row, (1, width // (2 * chans)))] + scatter_parts(d_normed, "seq"))
     in_out = lax.all_to_all(in_out.reshape(seqs, depth, 2 * chans), "seq", 0, 0)
     in_out, gain_out, xproj_out, dt_out, alog_out, conv_out, convb_out, dtb_out, skip_out = join_columns(
         in_out, late[lines:], in_weight, norm_gain.reshape(1, depth), batches, own

time: 309 us -> 298 us (0.964)
  waiting for transfers between devices: 65.8 us -> 46.6 us
  starting transfers between devices: 49.5 us -> 57.9 us
    ppermute x29 -> x32, waiting for transfers between devices: 50.4 us -> 38.6 us  [partner(): lax.ppermute(value, axis, [(i, i ^ k) for i in range(lax.axis_size(axis))])]
    ppermute x29 -> x32, starting transfers between devices: 33.7 us -> 42.8 us  [partner(): lax.ppermute(value, axis, [(i, i ^ k) for i in range(lax.axis_size(axis))])]
    all_gather x1, waiting for transfers between devices: 7.87 us -> 0.02 us  [body(): lax.all_gather(jnp.concatenate([tok[:top], flags], axis=0), 'seq')]
    pallas_call x1 -> x0, Pallas kernels: 5.14 us -> none  [late_pairs(): pl.pallas_call(late_pair_kernel, out_shape=[jax.ShapeDtypeStruct((steps,...]
  transfers between devices with their start and end apart: 36 -> 39, of which waited for: 16 -> 14; matrix products, arithmetic and copies ran while one was open for 7% -> 8% of each run, Pallas kernels for 41% -> 41%
where the time goes in v5:
time: 298 us; the launch traced here: 297 us
  Pallas kernels  141 us (47%)
  starting transfers between devices  57.9 us (19%)
  waiting for transfers between devices  46.6 us (16%)
  other arithmetic  18.5 us (6%)
  between operations  17.8 us (6%)
  local copies, waits for them, and re-layouts  14.6 us (5%)
    pallas_call x8, Pallas kernels, call(): pl.pallas_call(kernel, out_shape=[jax.ShapeDtypeStruct(s, d) for s, d, _...  131 us
    ppermute x32, starting transfers between devices, partner(): lax.ppermute(value, axis, [(i, i ^ k) for i in range(lax.axis_size(axis))])  42.8 us
    ppermute x32, waiting for transfers between devices, partner(): lax.ppermute(value, axis, [(i, i ^ k) for i in range(lax.axis_size(axis))])  38.6 us
    all_to_all x1, waiting for transfers between devices, body(): split = lax.all_to_all(split, 'seq', 0, 0).reshape(lines, 2 * chans + LANES)  7.43 us
    pallas_call x1, Pallas kernels, by_blocks(): pl.pallas_call(kernel, out_shape=jax.ShapeDtypeStruct((batches, rows, cha...  6.8 us
  transfers between devices with their start and end apart: 39, of which 14 were waited for; matrix products, arithmetic and copies ran while one was open for 8% of the time, Pallas kernels for 41%

profile of v5, /device:TPU:0, one launch (start us, length us, event | category | flops | bytes accessed | tf_op | source)
XLA Modules:
  0.0 296.7 jit_solution(10814157213990759231)
XLA Ops:
  7.3 1.1 fusion.44
  10.6 3.0 %collective-permute-start = (bf16[128,1024]{1,0:T(8,128)(2,1)S(1)}, bf16[128,1024]{1,0:T(8,128)(2,1)S(1)}, u32[]{:S(2)}, u32[]{:S(2)}) collective-permute-start(bf16[128,1024]{1,0:T(8,128)(2,1)S(1)} %get-tuple-element.204.refs_2_), channel_id=1, source_target_pairs={{0,1},{1,0},{2,3},{3,2},{4,5},{5,4},{6,7},{7,6},{8,9},{9,8},{10,11... | collective-permute-start | bytes 786440 | tf_op jit(solution)/shard_map/ppermute | solution.py:707
  13.6 1.5 collective-permute-start.1
  15.2 1.8 shard_map.237
  17.0 3.5 %all-to-all-start = ((bf16[4,32,1152]{2,1,0:T(8,128)(2,1)}), bf16[4,32,1152]{2,1,0:T(8,128)(2,1)S(1)}, u32[]{:S(2)}, u32[]{:S(2)}) async-start(bf16[4,32,1152]{2,1,0:T(8,128)(2,1)} %shard_map.237), calls=%async_computation | async-start | bytes 589824 | tf_op jit(solution)/shard_map/all_to_all | solution.py:833
  21.4 7.4 %all-to-all-done = bf16[4,32,1152]{2,1,0:T(8,128)(2,1)S(1)} async-done(((bf16[4,32,1152]{2,1,0:T(8,128)(2,1)}), bf16[4,32,1152]{2,1,0:T(8,128)(2,1)S(1)}, u32[]{:S(2)}, u32[]{:S(2)}) %all-to-all-start) | async-done | bytes 294944 | tf_op jit(solution)/shard_map/all_to_all | solution.py:833
  28.8 1.6 collective-permute-start.3
  30.5 2.6 collective-permute-start.4
  34.1 1.0 collective-permute-done.3
  35.1 2.4 collective-permute-start.2
  37.5 6.1 %collective-permute-done.4 = bf16[128,640]{1,0:T(8,128)(2,1)S(1)} collective-permute-done((bf16[128,640]{1,0:T(8,128)(2,1)S(1)}, bf16[128,640]{1,0:T(8,128)(2,1)S(1)}, u32[]{:S(2)}, u32[]{:S(2)}) %collective-permute-start.4) | collective-permute-done | bytes 163872 | tf_op jit(solution)/shard_map/ppermute | solution.py:707
  44.5 2.3 collective-permute-done.2.refs_5_
  47.7 0.8 copy-done.6
  48.5 9.8 %shard_map.238 = (bf16[1024,1024]{1,0:T(8,128)(2,1)}, bf16[1024,1024]{1,0:T(8,128)(2,1)}, bf16[1024,512]{1,0:T(8,128)(2,1)}, f32[1024,512]{1,0:T(8,128)}, bf16[1...) custom-call(s32[9]{0:T(128)} %concatenate.73.refs_0_, ...), custom_call_target="tpu_custom_call" | custom-call | tf_op jit(solution)/shard_map/pallas_call | solution.py:576
  58.3 0.9 collective-permute-start.7
  59.6 2.3 collective-permute-start.9
  61.8 0.8 slice_convert_fusion.2
  64.2 3.5 %all-to-all-start.2 = ((bf16[4,64,1024]{2,1,0:T(8,128)(2,1)}), bf16[4,64,1024]{2,1,0:T(8,128)(2,1)S(1)}, u32[]{:S(2)}, u32[]{:S(2)}) async-start(bf16[4,64,1024]{2,1,0:T(8,128)(2,1)} %bitcast.39), calls=%async_computation.2 | async-start | bytes 1048576 | tf_op jit(solution)/shard_map/all_to_all | solution.py:887
  68.2 1.3 fusion.46
  71.5 1.4 select_convert_fusion
  72.9 1.1 collective-permute-done.9
  74.0 1.0 add_select_fusion.proj_ref.refs_1_
  75.0 13.0 %shard_map.239 = (bf16[16384,512]{1,0:T(8,128)(2,1)}, f32[1024,512]{1,0:T(8,128)}) custom-call(s32[17]{0:T(128)} %pad_add_fusion.me_ref.refs_0_, f32[1024,128]{1,0:T(8,128)} %add_select_fusion.proj_ref.refs_1_, bf16[1024,512]{1,0:T(8,128)(2,1)} %get-tuple-element.79.act_ref.refs_2_.refs_8_, f32[128,512]{1,0:T(8,128)} %get-tuple-element.81.vec_ref.refs_6_.refs_10_), custom_call_target="tpu_custom_call" | custom-call | tf_op jit(solution)/shard_map/pallas_call | solution.py:576
  88.6 16.1 %shard_map.240 = (bf16[16384,512]{1,0:T(8,128)(2,1)}, f32[1024,512]{1,0:T(8,128)}, f32[1024,512]{1,0:T(8,128)}, bf16[512,1024]{1,0:T(8,128)(2,1)}, f32[16,512]{1...) custom-call(s32[17]{0:T(128)} %pad_add_fusion.me_ref.refs_0_, ...), custom_call_target="tpu_custom_call" | custom-call | tf_op jit(solution)/shard_map/pallas_call | solution.py:576
  105.4 1.5 collective-permute-start.11
  106.9 1.4 collective-permute-start.12
  108.4 15.4 %shard_map.241 = (bf16[16384,512]{1,0:T(8,128)(2,1)}, f32[1024,512]{1,0:T(8,128)}, f32[1024,512]{1,0:T(8,128)}, bf16[512,1024]{1,0:T(8,128)(2,1)}, f32[16,512]{1...) custom-call(s32[17]{0:T(128)} %pad_add_fusion.me_ref.refs_0_, ...), custom_call_target="tpu_custom_call", output_to_operand_aliasing={{0}: (10, {}), {1}: (11, {}), {2}: (12, {}), {3}: (13, {})} | custom-call | tf_op jit(solution)/shard_map/pallas_call | solution.py:576
  124.6 1.5 collective-permute-start.14
  126.1 1.4 collective-permute-start.15
  128.6 1.5 collective-permute-start.17
  130.1 3.3 %collective-permute-done.13 = bf16[128,1024]{1,0:T(8,128)(2,1)S(1)} collective-permute-done((bf16[128,1024]{1,0:T(8,128)(2,1)}, bf16[128,1024]{1,0:T(8,128)(2,1)S(1)}, u32[]{:S(2)}, u32[]{:S(2)}) %collective-permute-start.13) | collective-permute-done | bytes 262176 | tf_op jit(solution)/shard_map/ppermute | solution.py:707
  133.4 1.6 collective-permute-start.18
  134.9 4.7 %collective-permute-done.14 = bf16[128,1024]{1,0:T(8,128)(2,1)S(1)} collective-permute-done((bf16[128,1024]{1,0:T(8,128)(2,1)}, bf16[128,1024]{1,0:T(8,128)(2,1)S(1)}, u32[]{:S(2)}, u32[]{:S(2)}) %collective-permute-start.14) | collective-permute-done | bytes 262176 | tf_op jit(solution)/shard_map/ppermute | solution.py:707
  140.1 1.4 collective-permute-start.19
  141.6 0.9 collective-permute-start.20
  142.5 2.2 collective-permute-done.16.refs_11_
  144.7 1.6 collective-permute-start.21
  146.2 4.6 %collective-permute-done.17.refs_12_ = bf16[128,1024]{1,0:T(8,128)(2,1)S(1)} collective-permute-done((bf16[128,1024]{1,0:T(8,128)(2,1)S(1)}, bf16[128,1024]{1,0:T(8,128)(2,1)S(1)}, u32[]{:S(2)}, u32[]{:S(2)}) %collective-permute-start.17) | collective-permute-done | bytes 262176 | tf_op jit(solution)/shard_map/ppermute | solution.py:707
  151.6 9.6 %shard_map.242 = (bf16[16384,512]{1,0:T(8,128)(2,1)}, f32[1024,512]{1,0:T(8,128)}, bf16[1024,512]{1,0:T(8,128)(2,1)}, bf16[1024,1024]{1,0:T(8,128)(2,1)}, f32[1,512]{1,0:T(1,128)}, /*index=5*/f32[16,512]{1,0:T(8,128)}) custom-call(s32[17]{0:T(128)} %pad_add_fusion.me_ref.refs_0_, f32[1024,128]{1,0:T(8,128)} %add_select_fusion.proj_ref.refs_1_, ...), custom_call_target="tpu_custom_call" | custom-call | tf_op jit(solution)/shard_map/pallas_call | solution.py:576
  162.1 9.5 %shard_map.243 = (bf16[16384,512]{1,0:T(8,128)(2,1)}, f32[1024,512]{1,0:T(8,128)}, bf16[1024,512]{1,0:T(8,128)(2,1)}, bf16[1024,1024]{1,0:T(8,128)(2,1)}, f32[1,512]{1,0:T(1,128)}, /*index=5*/f32[16,512]{1,0:T(8,128)}) custom-call(s32[17]{0:T(128)} %pad_add_fusion.me_ref.refs_0_, ...), custom_call_target="tpu_custom_call", output_to_operand_aliasing={{0}: (14, {}), {1}: (15, {}), {2}: (16, {}), {3}: (17, {})} | custom-call | tf_op jit(solution)/shard_map/pallas_call | solution.py:576
  171.6 6.8 %shard_map.246 = f32[8,256,512]{2,1,0:T(8,128)} custom-call(bf16[1024,1024]{1,0:T(8,128)(2,1)} %get-tuple-element.121.refs_15_.normed_ref, bf16[512,1024]{1,0:T(8,128)(2,1)} %get-tuple-element.126.gated_ref, bf16[1024,512]{1,0:T(8,128)(2,1)} %get-tuple-element.117.refs_9_.dg_ref, bf16[1024,1024]{1,0:T(8,128)(2,1)} %get-tuple-element.125.refs_0_), custom_call_target="tpu_custom_call" | custom-call | tf_op jit(solution)/shard_map/pallas_call | solution.py:630
  179.4 44.1 %shard_map.244 = (f32[1024,512]{1,0:T(8,128)}, bf16[1024,128]{1,0:T(8,128)(2,1)}, f32[128,512]{1,0:T(8,128)}) custom-call(s32[17]{0:T(128)} %pad_add_fusion.me_ref.refs_0_, f32[1024,128]{1,0:T(8,128)} %add_select_fusion.proj_ref.refs_1_, bf16[1024,512]{1,0:T(8,128)(2,1)} %get-tuple-element.79.act_ref.refs_2_.refs_8_, f32[1024,512]{1,0:T(8,128)} %get-tuple-element.109.dm_ref, ...), custom_call_target="tpu_custom_call" | custom-call | tf_op jit(solution)/shard_map/pallas_call | solution.py:576
  223.5 1.1 collective-permute-start.22
  224.6 0.9 collective-permute-start.23
  225.5 1.6 collective-permute-start.24
  227.0 0.8 pad_maximum_fusion.2
  227.9 3.7 %all-to-all-start.1 = ((bf16[4,64,1024]{2,1,0:T(8,128)(2,1)}), bf16[4,64,1024]{2,1,0:T(8,128)(2,1)S(1)}, u32[]{:S(2)}, u32[]{:S(2)}) async-start(bf16[4,64,1024]{2,1,0:T(8,128)(2,1)} %pad_maximum_fusion.2), calls=%async_computation.1 | async-start | bytes 1048576 | tf_op jit(solution)/shard_map/all_to_all | solution.py:1013
  232.5 1.4 collective-permute-done.24.refs_4_
  234.7 13.1 %shard_map.245 = (bf16[256,1024]{1,0:T(8,128)(2,1)}, bf16[256,1024]{1,0:T(8,128)(2,1)}, bf16[256,1024]{1,0:T(8,128)(2,1)}, bf16[256,1024]{1,0:T(8,128)(2,1)}, f3...) custom-call(s32[18]{0:T(128)} %pad_add_fusion.1.refs_0_, ...), custom_call_target="tpu_custom_call" | custom-call | tf_op jit(solution)/shard_map/pallas_call | solution.py:576
  248.1 1.2 collective-permute-start.29
  249.3 1.5 collective-permute-start.30
  251.6 1.6 fusion.41
  253.3 1.5 collective-permute-start.26
  254.8 3.5 %collective-permute-start.27 = (bf16[176,512]{1,0:T(8,128)(2,1)S(1)}, bf16[176,512]{1,0:T(8,128)(2,1)S(1)}, u32[]{:S(2)}, u32[]{:S(2)}) collective-permute-start(bf16[176,512]{1,0:T(8,128)(2,1)S(1)} %get-tuple-element.195), channel_id=1, source_target_pairs={{0,16},{4,20},{8,24},{12,28},{16,0},{20,4},{24,8},{28,12},{1,17},{... | collective-permute-start | bytes 540680 | tf_op jit(solution)/shard_map/ppermute | solution.py:707
  258.3 4.5 %collective-permute-done.26 = bf16[176,512]{1,0:T(8,128)(2,1)S(1)} collective-permute-done((bf16[176,512]{1,0:T(8,128)(2,1)S(1)}, bf16[176,512]{1,0:T(8,128)(2,1)S(1)}, u32[]{:S(2)}, u32[]{:S(2)}) %collective-permute-start.26) | collective-permute-done | bytes 180256 | tf_op jit(solution)/shard_map/ppermute | solution.py:707
  262.8 1.7 collective-permute-start.31
  264.5 6.9 %collective-permute-done.27 = bf16[176,512]{1,0:T(8,128)(2,1)S(1)} collective-permute-done((bf16[176,512]{1,0:T(8,128)(2,1)S(1)}, bf16[176,512]{1,0:T(8,128)(2,1)S(1)}, u32[]{:S(2)}, u32[]{:S(2)}) %collective-permute-start.27) | collective-permute-done | bytes 180256 | tf_op jit(solution)/shard_map/ppermute | solution.py:707
  273.4 1.0 slice.379
  275.2 4.2 %all-to-all-start.3 = ((bf16[4,32,1024]{2,1,0:T(8,128)(2,1)}), bf16[4,32,1024]{2,1,0:T(8,128)(2,1)}, u32[]{:S(2)}, u32[]{:S(2)}) async-start(bf16[4,32,1024]{2,1,0:T(8,128)(2,1)} %pad_maximum_fusion.5), calls=%async_computation.4 | async-start | bytes 524288 | tf_op jit(solution)/shard_map/all_to_all | solution.py:1102
  279.3 1.0 slice_bitcast_fusion.3
  281.6 2.6 fusion.6
  284.8 2.1 shard_map.247
  286.8 1.4 copy.58
  288.3 0.8 copy.69
  (191 shorter events, 21.8 us)
Async XLA Ops:
  7.2 13.3 %copy-start.23 = (bf16[64,64]{1,0:T(8,128)(2,1)S(1)}, bf16[64,64]{1,0:T(8,128)(2,1)}, u32[]{:S(2)}) copy-start(bf16[64,64]{1,0:T(8,128)(2,1)} %param.23) | copy-start | bytes 24580
  7.2 13.4 %copy-start.27 = (bf16[4,64]{1,0:T(4,128)(2,1)S(1)}, bf16[4,64]{1,0:T(4,128)(2,1)}, u32[]{:S(2)}) copy-start(bf16[4,64]{1,0:T(4,128)(2,1)} %param.20) | copy-start | bytes 1540
  7.2 13.5 %copy-start.26 = (bf16[64,16]{0,1:T(8,128)(2,1)S(1)}, bf16[64,16]{0,1:T(8,128)(2,1)}, u32[]{:S(2)}) copy-start(bf16[64,16]{0,1:T(8,128)(2,1)} %param.25) | copy-start | bytes 6148
  7.2 13.6 %copy-start.28 = (bf16[64]{0:T(256)(128)(2,1)S(1)}, bf16[64]{0:T(256)(128)(2,1)}, u32[]{:S(2)}) copy-start(bf16[64]{0:T(256)(128)(2,1)} %param.21) | copy-start | bytes 388
  7.2 13.7 %copy-start.29 = (bf16[64]{0:T(256)(128)(2,1)S(1)}, bf16[64]{0:T(256)(128)(2,1)}, u32[]{:S(2)}) copy-start(bf16[64]{0:T(256)(128)(2,1)} %param.24) | copy-start | bytes 388
  7.2 13.8 %copy-start.30 = (bf16[64]{0:T(256)(128)(2,1)S(1)}, bf16[64]{0:T(256)(128)(2,1)}, u32[]{:S(2)}) copy-start(bf16[64]{0:T(256)(128)(2,1)} %param.26) | copy-start | bytes 388
  7.2 14.1 %copy-start.24 = (bf16[64,96]{1,0:T(8,128)(2,1)S(1)}, bf16[64,96]{1,0:T(8,128)(2,1)}, u32[]{:S(2)}) copy-start(bf16[64,96]{1,0:T(8,128)(2,1)} %param.22) | copy-start | bytes 36868
  7.3 14.1 %copy-start.22 = (bf16[64,1024]{1,0:T(8,128)(2,1)S(1)}, bf16[64,1024]{1,0:T(8,128)(2,1)}, u32[]{:S(2)}) copy-start(bf16[64,1024]{1,0:T(8,128)(2,1)} %param.27) | copy-start | bytes 393220
  7.3 40.4 %all-gather.5.cloned.1.call-start = ((), (), s32[]{:S(2)}) async-start(), calls=%async_computation.6 | async-start | bytes 1474560 | tf_op jit(solution)/shard_map/all_gather | solution.py:831
  8.5 26.6 %copy-start.5 = (bf16[128,1024]{1,0:T(8,128)(2,1)}, bf16[128,1024]{1,0:T(8,128)(2,1)S(1)}, u32[]{:S(2)}) copy-start(bf16[128,1024]{1,0:T(8,128)(2,1)S(1)} %get-tuple-element.204.refs_2_) | copy-start | bytes 786436
  10.6 36.2 %collective-permute-start = (bf16[128,1024]{1,0:T(8,128)(2,1)S(1)}, bf16[128,1024]{1,0:T(8,128)(2,1)S(1)}, u32[]{:S(2)}, u32[]{:S(2)}) collective-permute-start(bf16[128,1024]{1,0:T(8,128)(2,1)S(1)} %get-tuple-element.204.refs_2_), channel_id=1, source_target_pairs={{0,1},{1,0},{2,3},{3,2},{4,5},{5,4},{6,7},{7,6},{8,9},{9,8},{10,11... | collective-permute-start | bytes 786440 | tf_op jit(solution)/shard_map/ppermute | solution.py:707
  13.6 33.2 %collective-permute-start.1 = (bf16[128,1024]{1,0:T(8,128)(2,1)S(1)}, bf16[128,1024]{1,0:T(8,128)(2,1)S(1)}, u32[]{:S(2)}, u32[]{:S(2)}) collective-permute-start(bf16[128,1024]{1,0:T(8,128)(2,1)S(1)} %get-tuple-element.204.refs_2_), channel_id=1, source_target_pairs={{0,2},{1,3},{2,0},{3,1},{4,6},{5,7},{6,4},{7,5},{8,10},{9,11},{10,... | collective-permute-start | bytes 786440 | tf_op jit(solution)/shard_map/ppermute | solution.py:707
  17.0 11.8 %all-to-all-start = ((bf16[4,32,1152]{2,1,0:T(8,128)(2,1)}), bf16[4,32,1152]{2,1,0:T(8,128)(2,1)S(1)}, u32[]{:S(2)}, u32[]{:S(2)}) async-start(bf16[4,32,1152]{2,1,0:T(8,128)(2,1)} %shard_map.237), calls=%async_computation | async-start | bytes 589824 | tf_op jit(solution)/shard_map/all_to_all | solution.py:833
  20.5 67.6 %all-gather.7.cloned.1.call-start = ((), (), s32[]{:S(2)}) async-start(), calls=%async_computation.7 | async-start | bytes 2359296 | tf_op jit(solution)/shard_map/all_gather | solution.py:852
  28.8 6.2 %collective-permute-start.3 = (bf16[128,640]{1,0:T(8,128)(2,1)S(1)}, bf16[128,640]{1,0:T(8,128)(2,1)S(1)}, u32[]{:S(2)}, u32[]{:S(2)}) collective-permute-start(bf16[128,640]{1,0:T(8,128)(2,1)S(1)} %slice_add_fusion), channel_id=1, source_target_pairs={{0,8},{4,12},{8,0},{12,4},{16,24},{20,28},{24,16},{28,20},{1,9},{5... | collective-permute-start | bytes 491528 | tf_op jit(solution)/shard_map/ppermute | solution.py:707
  30.5 13.1 %collective-permute-start.4 = (bf16[128,640]{1,0:T(8,128)(2,1)S(1)}, bf16[128,640]{1,0:T(8,128)(2,1)S(1)}, u32[]{:S(2)}, u32[]{:S(2)}) collective-permute-start(bf16[128,640]{1,0:T(8,128)(2,1)S(1)} %slice_add_fusion), channel_id=1, source_target_pairs={{0,16},{4,20},{8,24},{12,28},{16,0},{20,4},{24,8},{28,12},{1,17},{... | collective-permute-start | bytes 491528 | tf_op jit(solution)/shard_map/ppermute | solution.py:707
  33.1 10.5 %collective-permute-start.5 = (bf16[128,640]{1,0:T(8,128)(2,1)S(1)}, bf16[128,640]{1,0:T(8,128)(2,1)S(1)}, u32[]{:S(2)}, u32[]{:S(2)}) collective-permute-start(bf16[128,640]{1,0:T(8,128)(2,1)S(1)} %slice_add_fusion), channel_id=1, source_target_pairs={{0,24},{4,28},{8,16},{12,20},{16,8},{20,12},{24,0},{28,4},{1,25},{... | collective-permute-start | bytes 491528 | tf_op jit(solution)/shard_map/ppermute | solution.py:707
  35.1 11.7 %collective-permute-start.2 = (bf16[128,1024]{1,0:T(8,128)(2,1)S(1)}, bf16[128,1024]{1,0:T(8,128)(2,1)S(1)}, u32[]{:S(2)}, u32[]{:S(2)}) collective-permute-start(bf16[128,1024]{1,0:T(8,128)(2,1)S(1)} %get-tuple-element.204.refs_2_), channel_id=1, source_target_pairs={{0,3},{1,2},{2,1},{3,0},{4,7},{5,6},{6,5},{7,4},{8,11},{9,10},{10,... | collective-permute-start | bytes 786440 | tf_op jit(solution)/shard_map/ppermute | solution.py:707
  43.7 3.9 %copy-start.1 = (bf16[4,128,640]{2,1,0:T(8,128)(2,1)}, bf16[4,128,640]{2,1,0:T(8,128)(2,1)S(1)}, u32[]{:S(2)}) copy-start(bf16[4,128,640]{2,1,0:T(8,128)(2,1)S(1)} %pad_maximum_fusion.refs_6_) | copy-start | bytes 1966084
  43.7 3.9 %collective-permute-start.6 = (bf16[4,128,640]{2,1,0:T(8,128)(2,1)S(1)}, bf16[4,128,640]{2,1,0:T(8,128)(2,1)S(1)}, u32[]{:S(2)}, u32[]{:S(2)}) collective-permute-start(bf16[4,128,640]{2,1,0:T(8,128)(2,1)S(1)} %pad_maximum_fusion.refs_6_), channel_id=1, source_target_pairs={{0,4},{4,0},{8,12},{12,8},{16,20},{20,16},{24,28},{28,24},{1,5},{5... | collective-permute-start | bytes 1966088 | tf_op jit(solution)/shard_map/ppermute | solution.py:707
  46.8 0.8 copy-start.9
  47.6 0.9 copy-start.6
  58.3 14.6 %collective-permute-start.7 = (bf16[1024,128]{1,0:T(8,128)(2,1)}, bf16[1024,128]{1,0:T(8,128)(2,1)S(1)}, u32[]{:S(2)}, u32[]{:S(2)}) collective-permute-start(bf16[1024,128]{1,0:T(8,128)(2,1)} %get-tuple-element.78), channel_id=1, source_target_pairs={{0,1},{1,0},{2,3},{3,2},{4,5},{5,4},{6,7},{7,6},{8,9},{9,8},{10,11... | collective-permute-start | bytes 786440 | tf_op jit(solution)/shard_map/ppermute | solution.py:707
  59.1 13.8 %collective-permute-start.8 = (bf16[1024,128]{1,0:T(8,128)(2,1)}, bf16[1024,128]{1,0:T(8,128)(2,1)S(1)}, u32[]{:S(2)}, u32[]{:S(2)}) collective-permute-start(bf16[1024,128]{1,0:T(8,128)(2,1)} %get-tuple-element.78), channel_id=1, source_target_pairs={{0,2},{1,3},{2,0},{3,1},{4,6},{5,7},{6,4},{7,5},{8,10},{9,11},{10,... | collective-permute-start | bytes 786440 | tf_op jit(solution)/shard_map/ppermute | solution.py:707
  59.6 14.5 %collective-permute-start.9 = (bf16[1024,128]{1,0:T(8,128)(2,1)}, bf16[1024,128]{1,0:T(8,128)(2,1)S(1)}, u32[]{:S(2)}, u32[]{:S(2)}) collective-permute-start(bf16[1024,128]{1,0:T(8,128)(2,1)} %get-tuple-element.78), channel_id=1, source_target_pairs={{0,3},{1,2},{2,1},{3,0},{4,7},{5,6},{6,5},{7,4},{8,11},{9,10},{10,... | collective-permute-start | bytes 786440 | tf_op jit(solution)/shard_map/ppermute | solution.py:707
  64.2 44.1 %all-to-all-start.2 = ((bf16[4,64,1024]{2,1,0:T(8,128)(2,1)}), bf16[4,64,1024]{2,1,0:T(8,128)(2,1)S(1)}, u32[]{:S(2)}, u32[]{:S(2)}) async-start(bf16[4,64,1024]{2,1,0:T(8,128)(2,1)} %bitcast.39), calls=%async_computation.2 | async-start | bytes 1048576 | tf_op jit(solution)/shard_map/all_to_all | solution.py:887
  67.7 205.7 %reduce-scatter.2.cloned.1.call-start = ((), (), s32[]{:S(2)}) async-start(), calls=%async_computation.5 | async-start | bytes 4718592 | tf_op jit(solution)/shard_map/reduce_scatter | solution.py:1024
  71.5 2.6 copy-start.21
  104.7 21.3 %collective-permute-start.10 = (bf16[128,1024]{1,0:T(8,128)(2,1)}, bf16[128,1024]{1,0:T(8,128)(2,1)S(1)}, u32[]{:S(2)}, u32[]{:S(2)}) collective-permute-start(bf16[128,1024]{1,0:T(8,128)(2,1)} %get-tuple-element.85), channel_id=1, source_target_pairs={{0,1},{1,0},{2,3},{3,2},{4,5},{5,4},{6,7},{7,6},{8,9},{9,8},{10,11... | collective-permute-start | bytes 786440 | tf_op jit(solution)/shard_map/ppermute | solution.py:707
  105.4 22.0 %collective-permute-start.11 = (bf16[128,1024]{1,0:T(8,128)(2,1)}, bf16[128,1024]{1,0:T(8,128)(2,1)S(1)}, u32[]{:S(2)}, u32[]{:S(2)}) collective-permute-start(bf16[128,1024]{1,0:T(8,128)(2,1)} %get-tuple-element.86), channel_id=1, source_target_pairs={{0,2},{1,3},{2,0},{3,1},{4,6},{5,7},{6,4},{7,5},{8,10},{9,11},{10,... | collective-permute-start | bytes 786440 | tf_op jit(solution)/shard_map/ppermute | solution.py:707
  106.9 20.5 %collective-permute-start.12 = (bf16[128,1024]{1,0:T(8,128)(2,1)}, bf16[128,1024]{1,0:T(8,128)(2,1)S(1)}, u32[]{:S(2)}, u32[]{:S(2)}) collective-permute-start(bf16[128,1024]{1,0:T(8,128)(2,1)} %get-tuple-element.87), channel_id=1, source_target_pairs={{0,3},{1,2},{2,1},{3,0},{4,7},{5,6},{6,5},{7,4},{8,11},{9,10},{10,... | collective-permute-start | bytes 786440 | tf_op jit(solution)/shard_map/ppermute | solution.py:707
  108.4 19.0 %copy-start.14 = (bf16[128,1024]{1,0:T(8,128)(2,1)S(1)}, bf16[128,1024]{1,0:T(8,128)(2,1)}, u32[]{:S(2)}) copy-start(bf16[128,1024]{1,0:T(8,128)(2,1)} %get-tuple-element.84) | copy-start | bytes 786436
  123.9 9.5 %collective-permute-start.13 = (bf16[128,1024]{1,0:T(8,128)(2,1)}, bf16[128,1024]{1,0:T(8,128)(2,1)S(1)}, u32[]{:S(2)}, u32[]{:S(2)}) collective-permute-start(bf16[128,1024]{1,0:T(8,128)(2,1)} %get-tuple-element.96), channel_id=1, source_target_pairs={{0,1},{1,0},{2,3},{3,2},{4,5},{5,4},{6,7},{7,6},{8,9},{9,8},{10,11... | collective-permute-start | bytes 786440 | tf_op jit(solution)/shard_map/ppermute | solution.py:707
  124.6 15.1 %collective-permute-start.14 = (bf16[128,1024]{1,0:T(8,128)(2,1)}, bf16[128,1024]{1,0:T(8,128)(2,1)S(1)}, u32[]{:S(2)}, u32[]{:S(2)}) collective-permute-start(bf16[128,1024]{1,0:T(8,128)(2,1)} %get-tuple-element.97), channel_id=1, source_target_pairs={{0,2},{1,3},{2,0},{3,1},{4,6},{5,7},{6,4},{7,5},{8,10},{9,11},{10,... | collective-permute-start | bytes 786440 | tf_op jit(solution)/shard_map/ppermute | solution.py:707
  126.1 13.6 %collective-permute-start.15 = (bf16[128,1024]{1,0:T(8,128)(2,1)}, bf16[128,1024]{1,0:T(8,128)(2,1)S(1)}, u32[]{:S(2)}, u32[]{:S(2)}) collective-permute-start(bf16[128,1024]{1,0:T(8,128)(2,1)} %get-tuple-element.98), channel_id=1, source_target_pairs={{0,3},{1,2},{2,1},{3,0},{4,7},{5,6},{6,5},{7,4},{8,11},{9,10},{10,... | collective-permute-start | bytes 786440 | tf_op jit(solution)/shard_map/ppermute | solution.py:707
  127.4 12.2 %copy-start.13 = (bf16[128,1024]{1,0:T(8,128)(2,1)S(1)}, bf16[128,1024]{1,0:T(8,128)(2,1)}, u32[]{:S(2)}) copy-start(bf16[128,1024]{1,0:T(8,128)(2,1)} %get-tuple-element.95) | copy-start | bytes 786436
  127.9 12.2 %copy-start.4 = (bf16[128,1024]{1,0:T(8,128)(2,1)}, bf16[128,1024]{1,0:T(8,128)(2,1)S(1)}, u32[]{:S(2)}) copy-start(bf16[128,1024]{1,0:T(8,128)(2,1)S(1)} %get-tuple-element.199.refs_10_) | copy-start | bytes 786436
  127.9 16.8 %collective-permute-start.16 = (bf16[128,1024]{1,0:T(8,128)(2,1)S(1)}, bf16[128,1024]{1,0:T(8,128)(2,1)S(1)}, u32[]{:S(2)}, u32[]{:S(2)}) collective-permute-start(bf16[128,1024]{1,0:T(8,128)(2,1)S(1)} %get-tuple-element.199.refs_10_), channel_id=1, source_target_pairs={{0,1},{1,0},{2,3},{3,2},{4,5},{5,4},{6,7},{7,6},{8,9},{9,8},{10,11... | collective-permute-start | bytes 786440 | tf_op jit(solution)/shard_map/ppermute | solution.py:707
  128.6 22.3 %collective-permute-start.17 = (bf16[128,1024]{1,0:T(8,128)(2,1)S(1)}, bf16[128,1024]{1,0:T(8,128)(2,1)S(1)}, u32[]{:S(2)}, u32[]{:S(2)}) collective-permute-start(bf16[128,1024]{1,0:T(8,128)(2,1)S(1)} %get-tuple-element.199.refs_10_), channel_id=1, source_target_pairs={{0,2},{1,3},{2,0},{3,1},{4,6},{5,7},{6,4},{7,5},{8,10},{9,11},{10,... | collective-permute-start | bytes 786440 | tf_op jit(solution)/shard_map/ppermute | solution.py:707
  133.4 17.5 %collective-permute-start.18 = (bf16[128,1024]{1,0:T(8,128)(2,1)S(1)}, bf16[128,1024]{1,0:T(8,128)(2,1)S(1)}, u32[]{:S(2)}, u32[]{:S(2)}) collective-permute-start(bf16[128,1024]{1,0:T(8,128)(2,1)S(1)} %get-tuple-element.199.refs_10_), channel_id=1, source_target_pairs={{0,3},{1,2},{2,1},{3,0},{4,7},{5,6},{6,5},{7,4},{8,11},{9,10},{10,... | collective-permute-start | bytes 786440 | tf_op jit(solution)/shard_map/ppermute | solution.py:707
  140.1 21.1 %copy-start.3 = (bf16[128,1024]{1,0:T(8,128)(2,1)}, bf16[128,1024]{1,0:T(8,128)(2,1)S(1)}, u32[]{:S(2)}) copy-start(bf16[128,1024]{1,0:T(8,128)(2,1)S(1)} %get-tuple-element.197.refs_10_) | copy-start | bytes 786436
  140.1 21.1 %collective-permute-start.19 = (bf16[128,1024]{1,0:T(8,128)(2,1)S(1)}, bf16[128,1024]{1,0:T(8,128)(2,1)S(1)}, u32[]{:S(2)}, u32[]{:S(2)}) collective-permute-start(bf16[128,1024]{1,0:T(8,128)(2,1)S(1)} %get-tuple-element.197.refs_10_), channel_id=1, source_target_pairs={{0,1},{1,0},{2,3},{3,2},{4,5},{5,4},{6,7},{7,6},{8,9},{9,8},{10,11... | collective-permute-start | bytes 786440 | tf_op jit(solution)/shard_map/ppermute | solution.py:707
  141.6 19.7 %collective-permute-start.20 = (bf16[128,1024]{1,0:T(8,128)(2,1)S(1)}, bf16[128,1024]{1,0:T(8,128)(2,1)S(1)}, u32[]{:S(2)}, u32[]{:S(2)}) collective-permute-start(bf16[128,1024]{1,0:T(8,128)(2,1)S(1)} %get-tuple-element.197.refs_10_), channel_id=1, source_target_pairs={{0,2},{1,3},{2,0},{3,1},{4,6},{5,7},{6,4},{7,5},{8,10},{9,11},{10,... | collective-permute-start | bytes 786440 | tf_op jit(solution)/shard_map/ppermute | solution.py:707
  144.7 6.8 %copy-start.15 = (bf16[128,1024]{1,0:T(8,128)(2,1)}, bf16[128,1024]{1,0:T(8,128)(2,1)S(1)}, u32[]{:S(2)}) copy-start(bf16[128,1024]{1,0:T(8,128)(2,1)S(1)} %collective-permute-done.16.refs_11_) | copy-start | bytes 786436
  144.7 16.6 %collective-permute-start.21 = (bf16[128,1024]{1,0:T(8,128)(2,1)S(1)}, bf16[128,1024]{1,0:T(8,128)(2,1)S(1)}, u32[]{:S(2)}, u32[]{:S(2)}) collective-permute-start(bf16[128,1024]{1,0:T(8,128)(2,1)S(1)} %get-tuple-element.197.refs_10_), channel_id=1, source_target_pairs={{0,3},{1,2},{2,1},{3,0},{4,7},{5,6},{6,5},{7,4},{8,11},{9,10},{10,... | collective-permute-start | bytes 786440 | tf_op jit(solution)/shard_map/ppermute | solution.py:707
  161.3 0.8 copy-start.12
  223.5 8.7 %collective-permute-start.22 = (bf16[1024,128]{1,0:T(8,128)(2,1)}, bf16[1024,128]{1,0:T(8,128)(2,1)S(1)}, u32[]{:S(2)}, u32[]{:S(2)}) collective-permute-start(bf16[1024,128]{1,0:T(8,128)(2,1)} %get-tuple-element.113.refs_1_), channel_id=1, source_target_pairs={{0,1},{1,0},{2,3},{3,2},{4,5},{5,4},{6,7},{7,6},{8,9},{9,8},{10,11... | collective-permute-start | bytes 786440 | tf_op jit(solution)/shard_map/ppermute | solution.py:707
  224.6 8.0 %collective-permute-start.23 = (bf16[1024,128]{1,0:T(8,128)(2,1)}, bf16[1024,128]{1,0:T(8,128)(2,1)S(1)}, u32[]{:S(2)}, u32[]{:S(2)}) collective-permute-start(bf16[1024,128]{1,0:T(8,128)(2,1)} %get-tuple-element.113.refs_1_), channel_id=1, source_target_pairs={{0,2},{1,3},{2,0},{3,1},{4,6},{5,7},{6,4},{7,5},{8,10},{9,11},{10,... | collective-permute-start | bytes 786440 | tf_op jit(solution)/shard_map/ppermute | solution.py:707
  225.5 8.5 %collective-permute-start.24 = (bf16[1024,128]{1,0:T(8,128)(2,1)}, bf16[1024,128]{1,0:T(8,128)(2,1)S(1)}, u32[]{:S(2)}, u32[]{:S(2)}) collective-permute-start(bf16[1024,128]{1,0:T(8,128)(2,1)} %get-tuple-element.113.refs_1_), channel_id=1, source_target_pairs={{0,3},{1,2},{2,1},{3,0},{4,7},{5,6},{6,5},{7,4},{8,11},{9,10},{10,... | collective-permute-start | bytes 786440 | tf_op jit(solution)/shard_map/ppermute | solution.py:707
  227.9 20.2 %all-to-all-start.1 = ((bf16[4,64,1024]{2,1,0:T(8,128)(2,1)}), bf16[4,64,1024]{2,1,0:T(8,128)(2,1)S(1)}, u32[]{:S(2)}, u32[]{:S(2)}) async-start(bf16[4,64,1024]{2,1,0:T(8,128)(2,1)} %pad_maximum_fusion.2), calls=%async_computation.1 | async-start | bytes 1048576 | tf_op jit(solution)/shard_map/all_to_all | solution.py:1013
  232.2 1.8 copy-start.16
  232.5 1.4 copy-start.18
  234.7 13.2 %copy-start = (bf16[1,256,1024]{2,1,0:T(8,128)(2,1)S(1)}, bf16[1,256,1024]{2,1,0:T(8,128)(2,1)}, u32[]{:S(2)}) copy-start(bf16[1,256,1024]{2,1,0:T(8,128)(2,1)} %param.14) | copy-start | bytes 1572868
  247.8 3.7 %collective-permute-start.25 = (bf16[4,176,512]{2,1,0:T(8,128)(2,1)}, bf16[4,176,512]{2,1,0:T(8,128)(2,1)S(1)}, u32[]{:S(2)}, u32[]{:S(2)}) collective-permute-start(bf16[4,176,512]{2,1,0:T(8,128)(2,1)} %get-tuple-element.123), channel_id=1, source_target_pairs={{0,4},{4,0},{8,12},{12,8},{16,20},{20,16},{24,28},{28,24},{1,5},{5... | collective-permute-start | bytes 2162696 | tf_op jit(solution)/shard_map/ppermute | solution.py:707
  248.1 32.2 %collective-permute-start.29 = (bf16[256,1024]{1,0:T(8,128)(2,1)}, bf16[256,1024]{1,0:T(8,128)(2,1)S(1)}, u32[]{:S(2)}, u32[]{:S(2)}) collective-permute-start(bf16[256,1024]{1,0:T(8,128)(2,1)} %get-tuple-element.128), channel_id=1, source_target_pairs={{0,1},{1,0},{2,3},{3,2},{4,5},{5,4},{6,7},{7,6},{8,9},{9,8},{10,11... | collective-permute-start | bytes 1572872 | tf_op jit(solution)/shard_map/ppermute | solution.py:707
  249.3 31.1 %collective-permute-start.30 = (bf16[256,1024]{1,0:T(8,128)(2,1)}, bf16[256,1024]{1,0:T(8,128)(2,1)S(1)}, u32[]{:S(2)}, u32[]{:S(2)}) collective-permute-start(bf16[256,1024]{1,0:T(8,128)(2,1)} %get-tuple-element.129), channel_id=1, source_target_pairs={{0,2},{1,3},{2,0},{3,1},{4,6},{5,7},{6,4},{7,5},{8,10},{9,11},{10,... | collective-permute-start | bytes 1572872 | tf_op jit(solution)/shard_map/ppermute | solution.py:707
  253.2 27.2 %copy-start.2 = (bf16[256,1024]{1,0:T(8,128)(2,1)S(1)}, bf16[256,1024]{1,0:T(8,128)(2,1)}, u32[]{:S(2)}) copy-start(bf16[256,1024]{1,0:T(8,128)(2,1)} %get-tuple-element.127) | copy-start | bytes 1572868
  253.2 27.2 %copy-start.25 = (f32[1,1024]{1,0:T(1,128)S(1)}, f32[1,1024]{1,0:T(1,128)}, u32[]{:S(2)}) copy-start(f32[1,1024]{1,0:T(1,128)} %get-tuple-element.131) | copy-start | bytes 12292
  253.3 9.5 %collective-permute-start.26 = (bf16[176,512]{1,0:T(8,128)(2,1)S(1)}, bf16[176,512]{1,0:T(8,128)(2,1)S(1)}, u32[]{:S(2)}, u32[]{:S(2)}) collective-permute-start(bf16[176,512]{1,0:T(8,128)(2,1)S(1)} %get-tuple-element.194), channel_id=1, source_target_pairs={{0,8},{4,12},{8,0},{12,4},{16,24},{20,28},{24,16},{28,20},{1,9},{5... | collective-permute-start | bytes 540680 | tf_op jit(solution)/shard_map/ppermute | solution.py:707
  254.8 16.7 %collective-permute-start.27 = (bf16[176,512]{1,0:T(8,128)(2,1)S(1)}, bf16[176,512]{1,0:T(8,128)(2,1)S(1)}, u32[]{:S(2)}, u32[]{:S(2)}) collective-permute-start(bf16[176,512]{1,0:T(8,128)(2,1)S(1)} %get-tuple-element.195), channel_id=1, source_target_pairs={{0,16},{4,20},{8,24},{12,28},{16,0},{20,4},{24,8},{28,12},{1,17},{... | collective-permute-start | bytes 540680 | tf_op jit(solution)/shard_map/ppermute | solution.py:707
  258.3 13.1 %collective-permute-start.28 = (bf16[176,512]{1,0:T(8,128)(2,1)S(1)}, bf16[176,512]{1,0:T(8,128)(2,1)S(1)}, u32[]{:S(2)}, u32[]{:S(2)}) collective-permute-start(bf16[176,512]{1,0:T(8,128)(2,1)S(1)} %get-tuple-element.196), channel_id=1, source_target_pairs={{0,24},{4,28},{8,16},{12,20},{16,8},{20,12},{24,0},{28,4},{1,25},{... | collective-permute-start | bytes 540680 | tf_op jit(solution)/shard_map/ppermute | solution.py:707
  262.8 17.6 %collective-permute-start.31 = (bf16[256,1024]{1,0:T(8,128)(2,1)}, bf16[256,1024]{1,0:T(8,128)(2,1)S(1)}, u32[]{:S(2)}, u32[]{:S(2)}) collective-permute-start(bf16[256,1024]{1,0:T(8,128)(2,1)} %get-tuple-element.130), channel_id=1, source_target_pairs={{0,3},{1,2},{2,1},{3,0},{4,7},{5,6},{6,5},{7,4},{8,11},{9,10},{10,... | collective-permute-start | bytes 1572872 | tf_op jit(solution)/shard_map/ppermute | solution.py:707
  275.2 5.8 %slice-start = ((f32[1,256,512]{2,1,0:T(8,128)}), f32[1,128,512]{2,1,0:T(8,128)S(1)}, s32[]{:S(2)}) async-start(f32[1,256,512]{2,1,0:T(8,128)} %reduce-scatter.2.cloned.1.call-done), calls=%async_computation.8 | async-start | bytes 524288 | tf_op jit(solution)/shard_map/slice | solution.py:1106
  275.2 9.6 %all-to-all-start.3 = ((bf16[4,32,1024]{2,1,0:T(8,128)(2,1)}), bf16[4,32,1024]{2,1,0:T(8,128)(2,1)}, u32[]{:S(2)}, u32[]{:S(2)}) async-start(bf16[4,32,1024]{2,1,0:T(8,128)(2,1)} %pad_maximum_fusion.5), calls=%async_computation.4 | async-start | bytes 524288 | tf_op jit(solution)/shard_map/all_to_all | solution.py:1102
  (7 other events, 5.3 us)
Sparse Core Ops, SparseCore 0:
  10.7 35.3 all-gather.4
  47.7 29.7 all-gather.6
  178.6 51.0 reduce-scatter.1

commit v6 on v5

--- a/solution.py
+++ b/solution.py
@@ -135,7 +135,7 @@
     pre_ref[...] = pre
     act = (pre * sigmoid(pre)).astype(bf16)
     act_ref[...] = act
-    proj_ref[...] = dot(act, xproj_ref[...]).astype(bf16)
+    proj_ref[...] = dot(act, xproj_ref[...]).T[:CARRY, :].astype(bf16)
 
 
 def several(block):
@@ -155,13 +155,13 @@
     def _():
         carry_ref[...] = jnp.zeros_like(carry_ref)
 
-    proj = proj_ref[...]
+    proj = proj_ref[...].T
     _, pre = dt_of(proj, vec_ref, INTO)
     step = softplus(pre)
     step_ref[...] = step
     u_ref[...] = step * act_ref[...].astype(f32)
     stepm_ref[...] = jnp.where(proj[:, CARRY : CARRY + 1] > 0.5, step, NEVER)
-    columns(proj.T, INTO, n, col_ref)
+    columns(proj_ref[...], INTO, n, col_ref)
     r2 = rates_of(vec_ref, n)
 
     def block(i, carry):
@@ -180,12 +180,12 @@
 def ahead_kernel(
     first, places, per, local, me_ref, *refs,
 ):
-    proj_ref, act_ref, normed_ref, g_ref, step_ref, vec_ref, enter_ref = refs[:7]
+    proj_ref, act_ref, normed_ref, g_ref, step_ref, vec_ref = refs[:6]
     if first:
-        wgate_ref, outw_ref = refs[7:9]
+        enter_ref, wgate_ref, outw_ref = refs[6:9]
         hp_ref, mixed_ref, gate_ref, gated_ref, leave_ref = refs[-7 - places - 5 : -7 - places]
     else:
-        second_ref = refs[7]
+        second_ref = refs[6]
         hp_ref, mixed_ref, gate_ref, gated_ref, leave_ref, wgate_ref, outw_ref = refs[-7 - places - 7 : -7 - places]
     branch_refs = refs[-7 - places : -7]
     carry_ref, u_ref, col_ref, diag_ref, s_ref, y_ref, out_ref = refs[-7:]
@@ -194,9 +194,10 @@
 
     @pl.when(pl.program_id(0) == 0)
     def _():
-        carry_ref[...] = enter_ref[...]
         if first:
+            carry_ref[...] = enter_ref[...]
             return
+        carry_ref[...] = jnp.zeros_like(carry_ref)
         blocks = second_ref.shape[0]
         lines, own = wgate_ref.shape[0] // blocks, outw_ref.shape[0] // blocks
         for b in range(blocks):
@@ -206,11 +207,10 @@
                     b, lines + k * own : lines + (k + 1) * own, :
                 ]
 
-    proj = proj_ref[...]
     act = act_ref[...].astype(f32)
     u_ref[...] = step_ref[...] * act
-    columns(proj.T, INTO, n, col_ref)
-    read = proj[:, OUT : OUT + n]
+    columns(proj_ref[...], INTO, n, col_ref)
+    read = proj_ref[OUT : OUT + n, :].T
     high = read.astype(bf16)
     diag_ref[0, BLOCK:] = block_diag(high, n)
     diag_ref[1, BLOCK:] = block_diag((read - high.astype(f32)).astype(bf16), n)
@@ -249,8 +249,10 @@
 def piece_grad_kernel(
     first, places, per, local, me_ref, *refs,
 ):
-    proj_ref, act_ref, mixed_ref, gate_ref, step_ref, vec_ref, outw_ref, enter_ref, before_ref = refs[:9]
-    db_refs = refs[9 : 9 + places]
+    proj_ref, act_ref, mixed_ref, gate_ref, step_ref, vec_ref, outw_ref = refs[:7]
+    db_refs = refs[7 : 7 + places]
+    if first:
+        enter_ref, before_ref = refs[7 + places : 9 + places]
     q_ref, dm_ref, dg_ref, db_ref, sgrad_ref, leave_ref = refs[-9:-3]
     carry_ref, stepm_ref, col_ref = refs[-3:]
     rows, c = act_ref.shape
@@ -258,12 +260,15 @@
 
     @pl.when(pl.program_id(0) == 0)
     def _():
-        carry_ref[...] = enter_ref[...]
-        sgrad_ref[...] = before_ref[...]
-
-    proj = proj_ref[...]
-    stepm_ref[...] = jnp.where(proj[:, CARRY : CARRY + 1] > 0.5, step_ref[...], NEVER)
-    columns(proj.T, OUT, n, col_ref)
+        if first:
+            carry_ref[...] = enter_ref[...]
+            sgrad_ref[...] = before_ref[...]
+        else:
+            carry_ref[...] = jnp.zeros_like(carry_ref)
+            sgrad_ref[...] = jnp.zeros_like(sgrad_ref)
+
+    stepm_ref[...] = jnp.where(proj_ref[CARRY : CARRY + 8, :].T[:, :1] > 0.5, step_ref[...], NEVER)
+    columns(proj_ref[...], OUT, n, col_ref)
     db = read_rows(db_refs, me_ref, places, per, local, rows)
     db_ref[...] = db
     dgated = dot_t(db, outw_ref[...])
@@ -319,12 +324,10 @@
         table_ref[...] = jnp.zeros_like(table_ref)
         table_ref[SKIP : SKIP + 1, :] = sgrad_ref[...]
 
-    proj = proj_ref[...]
     act = act_ref[...].astype(f32)
-    low = proj[:, :INTO].astype(bf16)
     u_ref[...] = step_ref[...] * act
-    columns(proj.T, OUT, n, col_ref)
-    diag_ref[:rows] = block_diag(proj[:, INTO : INTO + n].astype(bf16), n)
+    columns(proj_ref[...], OUT, n, col_ref)
+    diag_ref[:rows] = block_diag(proj_ref[INTO : INTO + n, :].T.astype(bf16), n)
     r2 = rates_of(vec_ref, n)
     iota = lambda shape, axis: lax.broadcasted_iota(jnp.int32, shape, axis)
     mask = lambda v: v.astype(f32).astype(bf16)
@@ -383,7 +386,7 @@
     dpre = (y_ref[:rows] * LN2 + act * xs) * slope_of(step_ref[...])
     table_ref[DTB : DTB + 1, :] += jnp.sum(dpre, axis=0, keepdims=True)
     dpre_low = dpre.astype(bf16)
-    table_ref[:INTO, :] += t_dot(low, dpre_low)
+    table_ref[:INTO, :] += dot(proj_ref[:INTO, :].astype(bf16), dpre_low)
     dproj_ref[...] = dp_ref[:rows].astype(bf16)
     dproj_ref[:, :INTO] = dot_t(dpre_low, vec_ref[:INTO, :].astype(bf16)).astype(bf16)
 
@@ -619,7 +622,7 @@
 
 
 def by_blocks(kernel, batches, own, columns, whole, rows, chans):
-    group = LANES // own
+    group = min(2 * LANES // own, batches)
     steps = batches // group
 
     def spec(array, cut):
@@ -865,7 +868,7 @@
             low_tile,
             tile,
             low_tile,
-            ((total, LANES), bf16, "t"),
+            ((CARRY, total), bf16, "c"),
             ((width, chans), bf16, "f"),
             ((LANES, chans), f32, "f"),
             ((chans, LANES), bf16, "f"),
@@ -876,7 +879,6 @@
         total,
         rows,
     )
-    total_valid = (marks[:, LANES - 2 : LANES - 1] * 128.0 + marks[:, LANES - 1 :]) / depth
     starts = everything[:, top, :rows].astype(f32).reshape(total)
     running = jnp.cumsum(starts)
     lagged = jnp.concatenate([jnp.zeros((PIECE,), f32), running[: total - PIECE]])
@@ -887,12 +889,12 @@
     teach_v = lax.all_to_all(teacher.reshape(seqs, per, width), "seq", 0, 0).astype(f32)
     proj = added(share_parts(proj, "seq"))
     me = jnp.concatenate([me, flags])
-    proj = jnp.where(jnp.arange(LANES)[None, :] == CARRY, carry_on[:, None], proj)
+    proj = jnp.concatenate([proj, jnp.broadcast_to(carry_on[None], (8, total))], axis=0)
     groups = (ROWS // BLOCK, states, BLOCK)
     g, step = call(
         piece_kernel,
         me,
-        [(proj, "t"), (act, "t"), (vec, "f")],
+        [(proj, "c"), (act, "t"), (vec, "f")],
         [state, tile],
         [
             pltpu.VMEM((states, chans), f32),
@@ -924,15 +926,16 @@
     else:
         tok_v = mine(everything[:, :rows]).astype(f32)
     valid_v = mine(everything[:, top + 1, :rows].reshape(seqs, rows, 1)).astype(f32)
-    enter = jnp.zeros((states, chans), f32)
+    marks, step = lax.optimization_barrier((marks, step))
+    total_valid = (marks[:, LANES - 2 : LANES - 1] * 128.0 + marks[:, LANES - 1 :]) / depth
     kept = []
     branches = []
     for half in range(halves):
         out = call(
             lambda *refs, half=half: ahead_kernel(half, places, per, rows, *refs),
             me,
-            [(proj, "t"), (act, "t"), (normed, "t"), (g, "t"), (step, "t"), (vec, "f"), (enter, "f")]
-            + ([(w_gate, "f"), (out_w, "f")] if half else [(second, "f")])
+            [(proj, "c"), (act, "t"), (normed, "t"), (g, "t"), (step, "t"), (vec, "f")]
+            + ([(enter, "f"), (w_gate, "f"), (out_w, "f")] if half else [(second, "f")])
             + [(array, "o") for array in kept],
             by_time + [((states, chans), f32, "f")] + ([] if half else weights) + messages,
             [
@@ -976,24 +979,21 @@
     square_sum = jnp.pad(square_sum, ((0, 0), (CARRY, 0)))
 
     kept = []
-    enter = jnp.zeros((states, chans), f32)
-    skip_grad = jnp.zeros((1, chans), f32)
     for half in range(halves):
         *kept, skip_grad, enter = call(
             lambda *refs, half=half: piece_grad_kernel(half * count, places, per, rows, *refs),
             me,
             [
-                (proj, "t"),
+                (proj, "c"),
                 (act, "t"),
                 (mixed, "t"),
                 (gate, "t"),
                 (step, "t"),
                 (vec, "f"),
                 (out_w, "f"),
-                (enter, "f"),
-                (skip_grad, "f"),
             ]
             + [(part, "f") for part in d_branches[half]]
+            + ([(enter, "f"), (skip_grad, "f")] if half else [])
             + [(array, "o") for array in kept],
             [
                 state,
@@ -1026,7 +1026,7 @@
     d_act, d_proj, table = call(
         state_grad_kernel,
         me,
-        [(proj, "t"), (act, "t"), (d_mixed, "t"), (g, "t"), (hp, "t"), (q, "t"), (step, "t"), (vec, "f"), (skip_grad, "f"), (pieces, "f")],
+        [(proj, "c"), (act, "t"), (d_mixed, "t"), (g, "t"), (hp, "t"), (q, "t"), (step, "t"), (vec, "f"), (skip_grad, "f"), (pieces, "f")],
         [tile, ((total, LANES), bf16, "t"), ((LANES, chans), f32, "f")],
         [
             pltpu.VMEM((states, chans), f32),

time: 298 us -> 296 us (level)
  transfers between devices with their start and end apart: 39 -> 39, of which waited for: 14 -> 13; matrix products, arithmetic and copies ran while one was open for 8% -> 8% of each run, Pallas kernels for 41% -> 41%
where the time goes in v6:
time: 296 us; the launch traced here: 294 us
  Pallas kernels  140 us (47%)
  starting transfers between devices  60.7 us (21%)
  waiting for transfers between devices  43.9 us (15%)
  other arithmetic  18.3 us (6%)
  between operations  17.8 us (6%)
  local copies, waits for them, and re-layouts  13.2 us (4%)
    pallas_call x8, Pallas kernels, call(): pl.pallas_call(kernel, out_shape=[jax.ShapeDtypeStruct(s, d) for s, d, _...  130 us
    ppermute x32, starting transfers between devices, partner(): lax.ppermute(value, axis, [(i, i ^ k) for i in range(lax.axis_size(axis))])  45.6 us
    ppermute x32, waiting for transfers between devices, partner(): lax.ppermute(value, axis, [(i, i ^ k) for i in range(lax.axis_size(axis))])  35.8 us
    all_to_all x1, waiting for transfers between devices, body(): split = lax.all_to_all(split, 'seq', 0, 0).reshape(lines, 2 * chans + LANES)  7.41 us
    pallas_call x1, Pallas kernels, by_blocks(): pl.pallas_call(kernel, out_shape=jax.ShapeDtypeStruct((batches, rows, cha...  6.25 us
  transfers between devices with their start and end apart: 39, of which 13 were waited for; matrix products, arithmetic and copies ran while one was open for 8% of the time, Pallas kernels for 41%

profile of v6, /device:TPU:0, one launch (start us, length us, event | category | flops | bytes accessed | tf_op | source)
XLA Modules:
  0.0 293.9 jit_solution(1446215110265451007)
XLA Ops:
  7.3 1.1 fusion.44
  9.9 0.7 pad_maximum_fusion.4
  10.6 3.0 %collective-permute-start = (bf16[128,1024]{1,0:T(8,128)(2,1)S(1)}, bf16[128,1024]{1,0:T(8,128)(2,1)S(1)}, u32[]{:S(2)}, u32[]{:S(2)}) collective-permute-start(bf16[128,1024]{1,0:T(8,128)(2,1)S(1)} %get-tuple-element.208.refs_2_), channel_id=1, source_target_pairs={{0,1},{1,0},{2,3},{3,2},{4,5},{5,4},{6,7},{7,6},{8,9},{9,8},{10,11... | collective-permute-start | bytes 786440 | tf_op jit(solution)/shard_map/ppermute | solution.py:710
  13.6 1.5 collective-permute-start.1
  15.2 1.8 shard_map.237
  17.0 3.5 %all-to-all-start = ((bf16[4,32,1152]{2,1,0:T(8,128)(2,1)}), bf16[4,32,1152]{2,1,0:T(8,128)(2,1)S(1)}, u32[]{:S(2)}, u32[]{:S(2)}) async-start(bf16[4,32,1152]{2,1,0:T(8,128)(2,1)} %shard_map.237), calls=%async_computation | async-start | bytes 589824 | tf_op jit(solution)/shard_map/all_to_all | solution.py:836
  21.4 7.4 %all-to-all-done = bf16[4,32,1152]{2,1,0:T(8,128)(2,1)S(1)} async-done(((bf16[4,32,1152]{2,1,0:T(8,128)(2,1)}), bf16[4,32,1152]{2,1,0:T(8,128)(2,1)S(1)}, u32[]{:S(2)}, u32[]{:S(2)}) %all-to-all-start) | async-done | bytes 294944 | tf_op jit(solution)/shard_map/all_to_all | solution.py:836
  28.8 1.6 collective-permute-start.3
  30.5 2.6 collective-permute-start.4
  34.0 1.0 collective-permute-done.3
  35.1 2.4 collective-permute-start.2
  37.5 6.1 %collective-permute-done.4 = bf16[128,640]{1,0:T(8,128)(2,1)S(1)} collective-permute-done((bf16[128,640]{1,0:T(8,128)(2,1)S(1)}, bf16[128,640]{1,0:T(8,128)(2,1)S(1)}, u32[]{:S(2)}, u32[]{:S(2)}) %collective-permute-start.4) | collective-permute-done | bytes 163872 | tf_op jit(solution)/shard_map/ppermute | solution.py:710
  44.4 2.4 collective-permute-done.2.refs_5_
  47.7 0.8 copy-done.6
  48.4 10.0 %shard_map.238 = (bf16[1024,1024]{1,0:T(8,128)(2,1)}, bf16[1024,1024]{1,0:T(8,128)(2,1)}, bf16[1024,512]{1,0:T(8,128)(2,1)}, f32[1024,512]{1,0:T(8,128)}, bf16[1...) custom-call(s32[9]{0:T(128)} %concatenate.76.refs_0_, ...), custom_call_target="tpu_custom_call" | custom-call | tf_op jit(solution)/shard_map/pallas_call | solution.py:579
  58.4 0.8 collective-permute-start.7
  59.7 2.3 collective-permute-start.9
  62.0 0.8 slice_convert_fusion.2
  64.3 3.5 %all-to-all-start.2 = ((bf16[4,64,1024]{2,1,0:T(8,128)(2,1)}), bf16[4,64,1024]{2,1,0:T(8,128)(2,1)S(1)}, u32[]{:S(2)}, u32[]{:S(2)}) async-start(bf16[4,64,1024]{2,1,0:T(8,128)(2,1)} %bitcast.122), calls=%async_computation.2 | async-start | bytes 1048576 | tf_op jit(solution)/shard_map/all_to_all | solution.py:889
  68.9 1.3 select_convert_fusion
  70.5 0.8 pad_maximum_fusion.3.proj_ref.refs_1_
  71.3 13.2 %shard_map.239 = (bf16[16384,512]{1,0:T(8,128)(2,1)}, f32[1024,512]{1,0:T(8,128)}) custom-call(s32[17]{0:T(128)} %pad_add_fusion.me_ref.refs_0_, f32[104,1024]{1,0:T(8,128)} %pad_maximum_fusion.3.proj_ref.refs_1_, bf16[1024,512]{1,0:T(8,128)(2,1)} %get-tuple-element.81.act_ref.refs_2_.refs_8_, f32[128,512]{1,0:T(8,128)} %get-tuple-element.83.vec_ref.refs_6_.refs_10_), custom_call_target="tpu_custom_call" | custom-call | tf_op jit(solution)/shard_map/pallas_call | solution.py:579
  86.5 16.2 %shard_map.240 = (bf16[16384,512]{1,0:T(8,128)(2,1)}, f32[1024,512]{1,0:T(8,128)}, f32[1024,512]{1,0:T(8,128)}, bf16[512,1024]{1,0:T(8,128)(2,1)}, f32[16,512]{1...) custom-call(s32[17]{0:T(128)} %pad_add_fusion.me_ref.refs_0_, ...), custom_call_target="tpu_custom_call" | custom-call | tf_op jit(solution)/shard_map/pallas_call | solution.py:579
  102.7 1.8 collective-permute-start.10
  104.5 1.5 collective-permute-start.11
  106.4 15.5 %shard_map.241 = (bf16[16384,512]{1,0:T(8,128)(2,1)}, f32[1024,512]{1,0:T(8,128)}, f32[1024,512]{1,0:T(8,128)}, bf16[512,1024]{1,0:T(8,128)(2,1)}, f32[16,512]{1...) custom-call(s32[17]{0:T(128)} %pad_add_fusion.me_ref.refs_0_, ...), custom_call_target="tpu_custom_call", output_to_operand_aliasing={{0}: (10, {}), {1}: (11, {}), {2}: (12, {}), {3}: (13, {})} | custom-call | tf_op jit(solution)/shard_map/pallas_call | solution.py:579
  121.8 1.8 collective-permute-start.13
  123.7 1.5 collective-permute-start.14
  125.8 1.8 collective-permute-start.19
  127.7 1.5 collective-permute-start.20
  129.1 2.2 collective-permute-done.13
  131.3 2.7 collective-permute-start.21
  134.0 4.7 %collective-permute-done.14 = bf16[128,1024]{1,0:T(8,128)(2,1)S(1)} collective-permute-done((bf16[128,1024]{1,0:T(8,128)(2,1)}, bf16[128,1024]{1,0:T(8,128)(2,1)S(1)}, u32[]{:S(2)}, u32[]{:S(2)}) %collective-permute-start.14) | collective-permute-done | bytes 262176 | tf_op jit(solution)/shard_map/ppermute | solution.py:710
  139.2 1.1 collective-permute-start.16
  140.3 1.0 collective-permute-start.17
  141.3 1.3 collective-permute-done.19.refs_9_
  142.6 2.7 collective-permute-start.18
  145.3 4.5 %collective-permute-done.20.refs_10_ = bf16[128,1024]{1,0:T(8,128)(2,1)S(1)} collective-permute-done((bf16[128,1024]{1,0:T(8,128)(2,1)S(1)}, bf16[128,1024]{1,0:T(8,128)(2,1)S(1)}, u32[]{:S(2)}, u32[]{:S(2)}) %collective-permute-start.20) | collective-permute-done | bytes 262176 | tf_op jit(solution)/shard_map/ppermute | solution.py:710
  150.6 9.6 %shard_map.242 = (bf16[16384,512]{1,0:T(8,128)(2,1)}, f32[1024,512]{1,0:T(8,128)}, bf16[1024,512]{1,0:T(8,128)(2,1)}, bf16[1024,1024]{1,0:T(8,128)(2,1)}, f32[1,512]{1,0:T(1,128)}, /*index=5*/f32[16,512]{1,0:T(8,128)}) custom-call(s32[17]{0:T(128)} %pad_add_fusion.me_ref.refs_0_, f32[104,1024]{1,0:T(8,128)} %pad_maximum_fusion.3.proj_ref.refs_1_, ...), custom_call_target="tpu_custom_call" | custom-call | tf_op jit(solution)/shard_map/pallas_call | solution.py:579
  161.1 9.7 %shard_map.243 = (bf16[16384,512]{1,0:T(8,128)(2,1)}, f32[1024,512]{1,0:T(8,128)}, bf16[1024,512]{1,0:T(8,128)(2,1)}, bf16[1024,1024]{1,0:T(8,128)(2,1)}, f32[1,512]{1,0:T(1,128)}, /*index=5*/f32[16,512]{1,0:T(8,128)}) custom-call(s32[17]{0:T(128)} %pad_add_fusion.me_ref.refs_0_, ...), custom_call_target="tpu_custom_call", output_to_operand_aliasing={{0}: (14, {}), {1}: (15, {}), {2}: (16, {}), {3}: (17, {})} | custom-call | tf_op jit(solution)/shard_map/pallas_call | solution.py:579
  170.8 6.2 %shard_map.246 = f32[8,256,512]{2,1,0:T(8,128)} custom-call(bf16[1024,1024]{1,0:T(8,128)(2,1)} %get-tuple-element.125.refs_15_.normed_ref, bf16[512,1024]{1,0:T(8,128)(2,1)} %get-tuple-element.130.gated_ref, bf16[1024,512]{1,0:T(8,128)(2,1)} %get-tuple-element.121.refs_9_.dg_ref, bf16[1024,1024]{1,0:T(8,128)(2,1)} %get-tuple-element.129.refs_0_), custom_call_target="tpu_custom_call" | custom-call | tf_op jit(solution)/shard_map/pallas_call | solution.py:633
  178.0 42.6 %shard_map.244 = (f32[1024,512]{1,0:T(8,128)}, bf16[1024,128]{1,0:T(8,128)(2,1)}, f32[128,512]{1,0:T(8,128)}) custom-call(s32[17]{0:T(128)} %pad_add_fusion.me_ref.refs_0_, f32[104,1024]{1,0:T(8,128)} %pad_maximum_fusion.3.proj_ref.refs_1_, bf16[1024,512]{1,0:T(8,128)(2,1)} %get-tuple-element.81.act_ref.refs_2_.refs_8_, ...), custom_call_target="tpu_custom_call" | custom-call | tf_op jit(solution)/shard_map/pallas_call | solution.py:579
  220.7 1.2 collective-permute-start.22
  221.9 0.9 collective-permute-start.23
  222.7 1.5 collective-permute-start.24
  224.2 0.8 pad_maximum_fusion.2
  225.1 3.7 %all-to-all-start.1 = ((bf16[4,64,1024]{2,1,0:T(8,128)(2,1)}), bf16[4,64,1024]{2,1,0:T(8,128)(2,1)S(1)}, u32[]{:S(2)}, u32[]{:S(2)}) async-start(bf16[4,64,1024]{2,1,0:T(8,128)(2,1)} %pad_maximum_fusion.2), calls=%async_computation.1 | async-start | bytes 1048576 | tf_op jit(solution)/shard_map/all_to_all | solution.py:1013
  229.8 1.5 collective-permute-done.24.refs_4_
  232.0 13.1 %shard_map.245 = (bf16[256,1024]{1,0:T(8,128)(2,1)}, bf16[256,1024]{1,0:T(8,128)(2,1)}, bf16[256,1024]{1,0:T(8,128)(2,1)}, bf16[256,1024]{1,0:T(8,128)(2,1)}, f3...) custom-call(s32[18]{0:T(128)} %pad_add_fusion.1.refs_0_, ...), custom_call_target="tpu_custom_call" | custom-call | tf_op jit(solution)/shard_map/pallas_call | solution.py:579
  245.4 1.1 collective-permute-start.29
  246.5 1.6 collective-permute-start.30
  248.9 1.6 fusion.41
  250.5 1.5 collective-permute-start.26
  252.0 3.5 %collective-permute-start.27 = (bf16[176,512]{1,0:T(8,128)(2,1)S(1)}, bf16[176,512]{1,0:T(8,128)(2,1)S(1)}, u32[]{:S(2)}, u32[]{:S(2)}) collective-permute-start(bf16[176,512]{1,0:T(8,128)(2,1)S(1)} %get-tuple-element.199), channel_id=1, source_target_pairs={{0,16},{4,20},{8,24},{12,28},{16,0},{20,4},{24,8},{28,12},{1,17},{... | collective-permute-start | bytes 540680 | tf_op jit(solution)/shard_map/ppermute | solution.py:710
  255.5 4.6 %collective-permute-done.26 = bf16[176,512]{1,0:T(8,128)(2,1)S(1)} collective-permute-done((bf16[176,512]{1,0:T(8,128)(2,1)S(1)}, bf16[176,512]{1,0:T(8,128)(2,1)S(1)}, u32[]{:S(2)}, u32[]{:S(2)}) %collective-permute-start.26) | collective-permute-done | bytes 180256 | tf_op jit(solution)/shard_map/ppermute | solution.py:710
  260.1 1.5 collective-permute-start.31
  261.6 7.0 %collective-permute-done.27 = bf16[176,512]{1,0:T(8,128)(2,1)S(1)} collective-permute-done((bf16[176,512]{1,0:T(8,128)(2,1)S(1)}, bf16[176,512]{1,0:T(8,128)(2,1)S(1)}, u32[]{:S(2)}, u32[]{:S(2)}) %collective-permute-start.27) | collective-permute-done | bytes 180256 | tf_op jit(solution)/shard_map/ppermute | solution.py:710
  270.7 1.0 slice.379
  272.4 4.2 %all-to-all-start.3 = ((bf16[4,32,1024]{2,1,0:T(8,128)(2,1)}), bf16[4,32,1024]{2,1,0:T(8,128)(2,1)}, u32[]{:S(2)}, u32[]{:S(2)}) async-start(bf16[4,32,1024]{2,1,0:T(8,128)(2,1)} %pad_maximum_fusion.6), calls=%async_computation.4 | async-start | bytes 524288 | tf_op jit(solution)/shard_map/all_to_all | solution.py:1102
  276.6 1.0 slice_bitcast_fusion.3
  278.9 2.6 fusion.6
  282.0 2.1 shard_map.247
  284.0 1.4 copy.58
  285.5 0.8 copy.69
  (192 shorter events, 19.6 us)
Async XLA Ops:
  7.2 13.3 %copy-start.23 = (bf16[64,64]{1,0:T(8,128)(2,1)S(1)}, bf16[64,64]{1,0:T(8,128)(2,1)}, u32[]{:S(2)}) copy-start(bf16[64,64]{1,0:T(8,128)(2,1)} %param.23) | copy-start | bytes 24580
  7.2 13.4 %copy-start.28 = (bf16[4,64]{1,0:T(4,128)(2,1)S(1)}, bf16[4,64]{1,0:T(4,128)(2,1)}, u32[]{:S(2)}) copy-start(bf16[4,64]{1,0:T(4,128)(2,1)} %param.20) | copy-start | bytes 1540
  7.2 13.5 %copy-start.26 = (bf16[64,16]{0,1:T(8,128)(2,1)S(1)}, bf16[64,16]{0,1:T(8,128)(2,1)}, u32[]{:S(2)}) copy-start(bf16[64,16]{0,1:T(8,128)(2,1)} %param.25) | copy-start | bytes 6148
  7.2 13.6 %copy-start.29 = (bf16[64]{0:T(256)(128)(2,1)S(1)}, bf16[64]{0:T(256)(128)(2,1)}, u32[]{:S(2)}) copy-start(bf16[64]{0:T(256)(128)(2,1)} %param.21) | copy-start | bytes 388
  7.2 13.7 %copy-start.30 = (bf16[64]{0:T(256)(128)(2,1)S(1)}, bf16[64]{0:T(256)(128)(2,1)}, u32[]{:S(2)}) copy-start(bf16[64]{0:T(256)(128)(2,1)} %param.24) | copy-start | bytes 388
  7.2 13.8 %copy-start.31 = (bf16[64]{0:T(256)(128)(2,1)S(1)}, bf16[64]{0:T(256)(128)(2,1)}, u32[]{:S(2)}) copy-start(bf16[64]{0:T(256)(128)(2,1)} %param.26) | copy-start | bytes 388
  7.2 14.1 %copy-start.24 = (bf16[64,96]{1,0:T(8,128)(2,1)S(1)}, bf16[64,96]{1,0:T(8,128)(2,1)}, u32[]{:S(2)}) copy-start(bf16[64,96]{1,0:T(8,128)(2,1)} %param.22) | copy-start | bytes 36868
  7.3 14.1 %copy-start.22 = (bf16[64,1024]{1,0:T(8,128)(2,1)S(1)}, bf16[64,1024]{1,0:T(8,128)(2,1)}, u32[]{:S(2)}) copy-start(bf16[64,1024]{1,0:T(8,128)(2,1)} %param.27) | copy-start | bytes 393220
  7.3 40.4 %all-gather.5.cloned.1.call-start = ((), (), s32[]{:S(2)}) async-start(), calls=%async_computation.6 | async-start | bytes 1474560 | tf_op jit(solution)/shard_map/all_gather | solution.py:834
  8.5 26.6 %copy-start.5 = (bf16[128,1024]{1,0:T(8,128)(2,1)}, bf16[128,1024]{1,0:T(8,128)(2,1)S(1)}, u32[]{:S(2)}) copy-start(bf16[128,1024]{1,0:T(8,128)(2,1)S(1)} %get-tuple-element.208.refs_2_) | copy-start | bytes 786436
  10.6 36.2 %collective-permute-start = (bf16[128,1024]{1,0:T(8,128)(2,1)S(1)}, bf16[128,1024]{1,0:T(8,128)(2,1)S(1)}, u32[]{:S(2)}, u32[]{:S(2)}) collective-permute-start(bf16[128,1024]{1,0:T(8,128)(2,1)S(1)} %get-tuple-element.208.refs_2_), channel_id=1, source_target_pairs={{0,1},{1,0},{2,3},{3,2},{4,5},{5,4},{6,7},{7,6},{8,9},{9,8},{10,11... | collective-permute-start | bytes 786440 | tf_op jit(solution)/shard_map/ppermute | solution.py:710
  13.6 33.2 %collective-permute-start.1 = (bf16[128,1024]{1,0:T(8,128)(2,1)S(1)}, bf16[128,1024]{1,0:T(8,128)(2,1)S(1)}, u32[]{:S(2)}, u32[]{:S(2)}) collective-permute-start(bf16[128,1024]{1,0:T(8,128)(2,1)S(1)} %get-tuple-element.208.refs_2_), channel_id=1, source_target_pairs={{0,2},{1,3},{2,0},{3,1},{4,6},{5,7},{6,4},{7,5},{8,10},{9,11},{10,... | collective-permute-start | bytes 786440 | tf_op jit(solution)/shard_map/ppermute | solution.py:710
  17.0 11.8 %all-to-all-start = ((bf16[4,32,1152]{2,1,0:T(8,128)(2,1)}), bf16[4,32,1152]{2,1,0:T(8,128)(2,1)S(1)}, u32[]{:S(2)}, u32[]{:S(2)}) async-start(bf16[4,32,1152]{2,1,0:T(8,128)(2,1)} %shard_map.237), calls=%async_computation | async-start | bytes 589824 | tf_op jit(solution)/shard_map/all_to_all | solution.py:836
  20.5 66.0 %all-gather.7.cloned.1.call-start = ((), (), s32[]{:S(2)}) async-start(), calls=%async_computation.7 | async-start | bytes 2359296 | tf_op jit(solution)/shard_map/all_gather | solution.py:855
  28.8 6.2 %collective-permute-start.3 = (bf16[128,640]{1,0:T(8,128)(2,1)S(1)}, bf16[128,640]{1,0:T(8,128)(2,1)S(1)}, u32[]{:S(2)}, u32[]{:S(2)}) collective-permute-start(bf16[128,640]{1,0:T(8,128)(2,1)S(1)} %slice_add_fusion), channel_id=1, source_target_pairs={{0,8},{4,12},{8,0},{12,4},{16,24},{20,28},{24,16},{28,20},{1,9},{5... | collective-permute-start | bytes 491528 | tf_op jit(solution)/shard_map/ppermute | solution.py:710
  30.5 13.1 %collective-permute-start.4 = (bf16[128,640]{1,0:T(8,128)(2,1)S(1)}, bf16[128,640]{1,0:T(8,128)(2,1)S(1)}, u32[]{:S(2)}, u32[]{:S(2)}) collective-permute-start(bf16[128,640]{1,0:T(8,128)(2,1)S(1)} %slice_add_fusion), channel_id=1, source_target_pairs={{0,16},{4,20},{8,24},{12,28},{16,0},{20,4},{24,8},{28,12},{1,17},{... | collective-permute-start | bytes 491528 | tf_op jit(solution)/shard_map/ppermute | solution.py:710
  33.1 10.5 %collective-permute-start.5 = (bf16[128,640]{1,0:T(8,128)(2,1)S(1)}, bf16[128,640]{1,0:T(8,128)(2,1)S(1)}, u32[]{:S(2)}, u32[]{:S(2)}) collective-permute-start(bf16[128,640]{1,0:T(8,128)(2,1)S(1)} %slice_add_fusion), channel_id=1, source_target_pairs={{0,24},{4,28},{8,16},{12,20},{16,8},{20,12},{24,0},{28,4},{1,25},{... | collective-permute-start | bytes 491528 | tf_op jit(solution)/shard_map/ppermute | solution.py:710
  35.1 11.7 %collective-permute-start.2 = (bf16[128,1024]{1,0:T(8,128)(2,1)S(1)}, bf16[128,1024]{1,0:T(8,128)(2,1)S(1)}, u32[]{:S(2)}, u32[]{:S(2)}) collective-permute-start(bf16[128,1024]{1,0:T(8,128)(2,1)S(1)} %get-tuple-element.208.refs_2_), channel_id=1, source_target_pairs={{0,3},{1,2},{2,1},{3,0},{4,7},{5,6},{6,5},{7,4},{8,11},{9,10},{10,... | collective-permute-start | bytes 786440 | tf_op jit(solution)/shard_map/ppermute | solution.py:710
  43.7 3.9 %copy-start.1 = (bf16[4,128,640]{2,1,0:T(8,128)(2,1)}, bf16[4,128,640]{2,1,0:T(8,128)(2,1)S(1)}, u32[]{:S(2)}) copy-start(bf16[4,128,640]{2,1,0:T(8,128)(2,1)S(1)} %pad_maximum_fusion.refs_6_) | copy-start | bytes 1966084
  43.7 3.9 %collective-permute-start.6 = (bf16[4,128,640]{2,1,0:T(8,128)(2,1)S(1)}, bf16[4,128,640]{2,1,0:T(8,128)(2,1)S(1)}, u32[]{:S(2)}, u32[]{:S(2)}) collective-permute-start(bf16[4,128,640]{2,1,0:T(8,128)(2,1)S(1)} %pad_maximum_fusion.refs_6_), channel_id=1, source_target_pairs={{0,4},{4,0},{8,12},{12,8},{16,20},{20,16},{24,28},{28,24},{1,5},{5... | collective-permute-start | bytes 1966088 | tf_op jit(solution)/shard_map/ppermute | solution.py:710
  47.6 0.8 copy-start.6
  58.4 12.0 %collective-permute-start.7 = (bf16[96,1024]{1,0:T(8,128)(2,1)}, bf16[96,1024]{1,0:T(8,128)(2,1)S(1)}, u32[]{:S(2)}, u32[]{:S(2)}) collective-permute-start(bf16[96,1024]{1,0:T(8,128)(2,1)} %get-tuple-element.80), channel_id=1, source_target_pairs={{0,1},{1,0},{2,3},{3,2},{4,5},{5,4},{6,7},{7,6},{8,9},{9,8},{10,11... | collective-permute-start | bytes 589832 | tf_op jit(solution)/shard_map/ppermute | solution.py:710
  59.2 11.1 %collective-permute-start.8 = (bf16[96,1024]{1,0:T(8,128)(2,1)}, bf16[96,1024]{1,0:T(8,128)(2,1)S(1)}, u32[]{:S(2)}, u32[]{:S(2)}) collective-permute-start(bf16[96,1024]{1,0:T(8,128)(2,1)} %get-tuple-element.80), channel_id=1, source_target_pairs={{0,2},{1,3},{2,0},{3,1},{4,6},{5,7},{6,4},{7,5},{8,10},{9,11},{10,... | collective-permute-start | bytes 589832 | tf_op jit(solution)/shard_map/ppermute | solution.py:710
  59.7 10.7 %collective-permute-start.9 = (bf16[96,1024]{1,0:T(8,128)(2,1)}, bf16[96,1024]{1,0:T(8,128)(2,1)S(1)}, u32[]{:S(2)}, u32[]{:S(2)}) collective-permute-start(bf16[96,1024]{1,0:T(8,128)(2,1)} %get-tuple-element.80), channel_id=1, source_target_pairs={{0,3},{1,2},{2,1},{3,0},{4,7},{5,6},{6,5},{7,4},{8,11},{9,10},{10,... | collective-permute-start | bytes 589832 | tf_op jit(solution)/shard_map/ppermute | solution.py:710
  64.3 41.9 %all-to-all-start.2 = ((bf16[4,64,1024]{2,1,0:T(8,128)(2,1)}), bf16[4,64,1024]{2,1,0:T(8,128)(2,1)S(1)}, u32[]{:S(2)}, u32[]{:S(2)}) async-start(bf16[4,64,1024]{2,1,0:T(8,128)(2,1)} %bitcast.122), calls=%async_computation.2 | async-start | bytes 1048576 | tf_op jit(solution)/shard_map/all_to_all | solution.py:889
  67.8 202.8 %reduce-scatter.2.cloned.1.call-start = ((), (), s32[]{:S(2)}) async-start(), calls=%async_computation.5 | async-start | bytes 4718592 | tf_op jit(solution)/shard_map/reduce_scatter | solution.py:1024
  68.9 1.5 copy-start.21
  70.3 14.2 %copy-start.27 = (f32[1,128]{1,0:T(1,128)S(1)}, f32[1,128]{1,0:T(1,128)}, u32[]{:S(2)}) copy-start(f32[1,128]{1,0:T(1,128)} %get-tuple-element.105) | copy-start | bytes 1540
  102.7 22.5 %collective-permute-start.10 = (bf16[128,1024]{1,0:T(8,128)(2,1)}, bf16[128,1024]{1,0:T(8,128)(2,1)S(1)}, u32[]{:S(2)}, u32[]{:S(2)}) collective-permute-start(bf16[128,1024]{1,0:T(8,128)(2,1)} %get-tuple-element.89), channel_id=1, source_target_pairs={{0,1},{1,0},{2,3},{3,2},{4,5},{5,4},{6,7},{7,6},{8,9},{9,8},{10,11... | collective-permute-start | bytes 786440 | tf_op jit(solution)/shard_map/ppermute | solution.py:710
  104.5 20.9 %collective-permute-start.11 = (bf16[128,1024]{1,0:T(8,128)(2,1)}, bf16[128,1024]{1,0:T(8,128)(2,1)S(1)}, u32[]{:S(2)}, u32[]{:S(2)}) collective-permute-start(bf16[128,1024]{1,0:T(8,128)(2,1)} %get-tuple-element.90), channel_id=1, source_target_pairs={{0,2},{1,3},{2,0},{3,1},{4,6},{5,7},{6,4},{7,5},{8,10},{9,11},{10,... | collective-permute-start | bytes 786440 | tf_op jit(solution)/shard_map/ppermute | solution.py:710
  106.0 19.4 %collective-permute-start.12 = (bf16[128,1024]{1,0:T(8,128)(2,1)}, bf16[128,1024]{1,0:T(8,128)(2,1)S(1)}, u32[]{:S(2)}, u32[]{:S(2)}) collective-permute-start(bf16[128,1024]{1,0:T(8,128)(2,1)} %get-tuple-element.91), channel_id=1, source_target_pairs={{0,3},{1,2},{2,1},{3,0},{4,7},{5,6},{6,5},{7,4},{8,11},{9,10},{10,... | collective-permute-start | bytes 786440 | tf_op jit(solution)/shard_map/ppermute | solution.py:710
  106.3 19.1 %copy-start.14 = (bf16[128,1024]{1,0:T(8,128)(2,1)S(1)}, bf16[128,1024]{1,0:T(8,128)(2,1)}, u32[]{:S(2)}) copy-start(bf16[128,1024]{1,0:T(8,128)(2,1)} %get-tuple-element.88) | copy-start | bytes 786436
  121.8 9.5 %collective-permute-start.13 = (bf16[128,1024]{1,0:T(8,128)(2,1)}, bf16[128,1024]{1,0:T(8,128)(2,1)S(1)}, u32[]{:S(2)}, u32[]{:S(2)}) collective-permute-start(bf16[128,1024]{1,0:T(8,128)(2,1)} %get-tuple-element.100), channel_id=1, source_target_pairs={{0,1},{1,0},{2,3},{3,2},{4,5},{5,4},{6,7},{7,6},{8,9},{9,8},{10,11... | collective-permute-start | bytes 786440 | tf_op jit(solution)/shard_map/ppermute | solution.py:710
  123.7 15.1 %collective-permute-start.14 = (bf16[128,1024]{1,0:T(8,128)(2,1)}, bf16[128,1024]{1,0:T(8,128)(2,1)S(1)}, u32[]{:S(2)}, u32[]{:S(2)}) collective-permute-start(bf16[128,1024]{1,0:T(8,128)(2,1)} %get-tuple-element.101), channel_id=1, source_target_pairs={{0,2},{1,3},{2,0},{3,1},{4,6},{5,7},{6,4},{7,5},{8,10},{9,11},{10,... | collective-permute-start | bytes 786440 | tf_op jit(solution)/shard_map/ppermute | solution.py:710
  125.1 13.6 %collective-permute-start.15 = (bf16[128,1024]{1,0:T(8,128)(2,1)}, bf16[128,1024]{1,0:T(8,128)(2,1)S(1)}, u32[]{:S(2)}, u32[]{:S(2)}) collective-permute-start(bf16[128,1024]{1,0:T(8,128)(2,1)} %get-tuple-element.102), channel_id=1, source_target_pairs={{0,3},{1,2},{2,1},{3,0},{4,7},{5,6},{6,5},{7,4},{8,11},{9,10},{10,... | collective-permute-start | bytes 786440 | tf_op jit(solution)/shard_map/ppermute | solution.py:710
  125.4 13.3 %copy-start.13 = (bf16[128,1024]{1,0:T(8,128)(2,1)S(1)}, bf16[128,1024]{1,0:T(8,128)(2,1)}, u32[]{:S(2)}) copy-start(bf16[128,1024]{1,0:T(8,128)(2,1)} %get-tuple-element.99) | copy-start | bytes 786436
  125.8 13.3 %copy-start.4 = (bf16[128,1024]{1,0:T(8,128)(2,1)}, bf16[128,1024]{1,0:T(8,128)(2,1)S(1)}, u32[]{:S(2)}) copy-start(bf16[128,1024]{1,0:T(8,128)(2,1)S(1)} %get-tuple-element.201.refs_8_) | copy-start | bytes 786436
  125.8 16.8 %collective-permute-start.19 = (bf16[128,1024]{1,0:T(8,128)(2,1)S(1)}, bf16[128,1024]{1,0:T(8,128)(2,1)S(1)}, u32[]{:S(2)}, u32[]{:S(2)}) collective-permute-start(bf16[128,1024]{1,0:T(8,128)(2,1)S(1)} %get-tuple-element.201.refs_8_), channel_id=1, source_target_pairs={{0,1},{1,0},{2,3},{3,2},{4,5},{5,4},{6,7},{7,6},{8,9},{9,8},{10,11... | collective-permute-start | bytes 786440 | tf_op jit(solution)/shard_map/ppermute | solution.py:710
  127.7 22.1 %collective-permute-start.20 = (bf16[128,1024]{1,0:T(8,128)(2,1)S(1)}, bf16[128,1024]{1,0:T(8,128)(2,1)S(1)}, u32[]{:S(2)}, u32[]{:S(2)}) collective-permute-start(bf16[128,1024]{1,0:T(8,128)(2,1)S(1)} %get-tuple-element.201.refs_8_), channel_id=1, source_target_pairs={{0,2},{1,3},{2,0},{3,1},{4,6},{5,7},{6,4},{7,5},{8,10},{9,11},{10,... | collective-permute-start | bytes 786440 | tf_op jit(solution)/shard_map/ppermute | solution.py:710
  131.3 18.5 %collective-permute-start.21 = (bf16[128,1024]{1,0:T(8,128)(2,1)S(1)}, bf16[128,1024]{1,0:T(8,128)(2,1)S(1)}, u32[]{:S(2)}, u32[]{:S(2)}) collective-permute-start(bf16[128,1024]{1,0:T(8,128)(2,1)S(1)} %get-tuple-element.201.refs_8_), channel_id=1, source_target_pairs={{0,3},{1,2},{2,1},{3,0},{4,7},{5,6},{6,5},{7,4},{8,11},{9,10},{10,... | collective-permute-start | bytes 786440 | tf_op jit(solution)/shard_map/ppermute | solution.py:710
  139.2 21.0 %copy-start.3 = (bf16[128,1024]{1,0:T(8,128)(2,1)}, bf16[128,1024]{1,0:T(8,128)(2,1)S(1)}, u32[]{:S(2)}) copy-start(bf16[128,1024]{1,0:T(8,128)(2,1)S(1)} %get-tuple-element.203.refs_8_) | copy-start | bytes 786436
  139.2 21.0 %collective-permute-start.16 = (bf16[128,1024]{1,0:T(8,128)(2,1)S(1)}, bf16[128,1024]{1,0:T(8,128)(2,1)S(1)}, u32[]{:S(2)}, u32[]{:S(2)}) collective-permute-start(bf16[128,1024]{1,0:T(8,128)(2,1)S(1)} %get-tuple-element.203.refs_8_), channel_id=1, source_target_pairs={{0,1},{1,0},{2,3},{3,2},{4,5},{5,4},{6,7},{7,6},{8,9},{9,8},{10,11... | collective-permute-start | bytes 786440 | tf_op jit(solution)/shard_map/ppermute | solution.py:710
  140.3 19.9 %collective-permute-start.17 = (bf16[128,1024]{1,0:T(8,128)(2,1)S(1)}, bf16[128,1024]{1,0:T(8,128)(2,1)S(1)}, u32[]{:S(2)}, u32[]{:S(2)}) collective-permute-start(bf16[128,1024]{1,0:T(8,128)(2,1)S(1)} %get-tuple-element.203.refs_8_), channel_id=1, source_target_pairs={{0,2},{1,3},{2,0},{3,1},{4,6},{5,7},{6,4},{7,5},{8,10},{9,11},{10,... | collective-permute-start | bytes 786440 | tf_op jit(solution)/shard_map/ppermute | solution.py:710
  142.6 7.2 %copy-start.16 = (bf16[128,1024]{1,0:T(8,128)(2,1)}, bf16[128,1024]{1,0:T(8,128)(2,1)S(1)}, u32[]{:S(2)}) copy-start(bf16[128,1024]{1,0:T(8,128)(2,1)S(1)} %collective-permute-done.19.refs_9_) | copy-start | bytes 786436
  142.6 17.6 %collective-permute-start.18 = (bf16[128,1024]{1,0:T(8,128)(2,1)S(1)}, bf16[128,1024]{1,0:T(8,128)(2,1)S(1)}, u32[]{:S(2)}, u32[]{:S(2)}) collective-permute-start(bf16[128,1024]{1,0:T(8,128)(2,1)S(1)} %get-tuple-element.203.refs_8_), channel_id=1, source_target_pairs={{0,3},{1,2},{2,1},{3,0},{4,7},{5,6},{6,5},{7,4},{8,11},{9,10},{10,... | collective-permute-start | bytes 786440 | tf_op jit(solution)/shard_map/ppermute | solution.py:710
  160.2 0.8 copy-start.12
  220.7 8.7 %collective-permute-start.22 = (bf16[1024,128]{1,0:T(8,128)(2,1)}, bf16[1024,128]{1,0:T(8,128)(2,1)S(1)}, u32[]{:S(2)}, u32[]{:S(2)}) collective-permute-start(bf16[1024,128]{1,0:T(8,128)(2,1)} %get-tuple-element.117.refs_1_), channel_id=1, source_target_pairs={{0,1},{1,0},{2,3},{3,2},{4,5},{5,4},{6,7},{7,6},{8,9},{9,8},{10,11... | collective-permute-start | bytes 786440 | tf_op jit(solution)/shard_map/ppermute | solution.py:710
  221.9 7.9 %collective-permute-start.23 = (bf16[1024,128]{1,0:T(8,128)(2,1)}, bf16[1024,128]{1,0:T(8,128)(2,1)S(1)}, u32[]{:S(2)}, u32[]{:S(2)}) collective-permute-start(bf16[1024,128]{1,0:T(8,128)(2,1)} %get-tuple-element.117.refs_1_), channel_id=1, source_target_pairs={{0,2},{1,3},{2,0},{3,1},{4,6},{5,7},{6,4},{7,5},{8,10},{9,11},{10,... | collective-permute-start | bytes 786440 | tf_op jit(solution)/shard_map/ppermute | solution.py:710
  222.7 8.5 %collective-permute-start.24 = (bf16[1024,128]{1,0:T(8,128)(2,1)}, bf16[1024,128]{1,0:T(8,128)(2,1)S(1)}, u32[]{:S(2)}, u32[]{:S(2)}) collective-permute-start(bf16[1024,128]{1,0:T(8,128)(2,1)} %get-tuple-element.117.refs_1_), channel_id=1, source_target_pairs={{0,3},{1,2},{2,1},{3,0},{4,7},{5,6},{6,5},{7,4},{8,11},{9,10},{10,... | collective-permute-start | bytes 786440 | tf_op jit(solution)/shard_map/ppermute | solution.py:710
  225.1 20.3 %all-to-all-start.1 = ((bf16[4,64,1024]{2,1,0:T(8,128)(2,1)}), bf16[4,64,1024]{2,1,0:T(8,128)(2,1)S(1)}, u32[]{:S(2)}, u32[]{:S(2)}) async-start(bf16[4,64,1024]{2,1,0:T(8,128)(2,1)} %pad_maximum_fusion.2), calls=%async_computation.1 | async-start | bytes 1048576 | tf_op jit(solution)/shard_map/all_to_all | solution.py:1013
  229.4 1.9 copy-start.15
  229.8 1.5 copy-start.17
  232.0 13.2 %copy-start = (bf16[1,256,1024]{2,1,0:T(8,128)(2,1)S(1)}, bf16[1,256,1024]{2,1,0:T(8,128)(2,1)}, u32[]{:S(2)}) copy-start(bf16[1,256,1024]{2,1,0:T(8,128)(2,1)} %param.14) | copy-start | bytes 1572868
  245.1 3.7 %collective-permute-start.25 = (bf16[4,176,512]{2,1,0:T(8,128)(2,1)}, bf16[4,176,512]{2,1,0:T(8,128)(2,1)S(1)}, u32[]{:S(2)}, u32[]{:S(2)}) collective-permute-start(bf16[4,176,512]{2,1,0:T(8,128)(2,1)} %get-tuple-element.127), channel_id=1, source_target_pairs={{0,4},{4,0},{8,12},{12,8},{16,20},{20,16},{24,28},{28,24},{1,5},{5... | collective-permute-start | bytes 2162696 | tf_op jit(solution)/shard_map/ppermute | solution.py:710
  245.4 32.2 %collective-permute-start.29 = (bf16[256,1024]{1,0:T(8,128)(2,1)}, bf16[256,1024]{1,0:T(8,128)(2,1)S(1)}, u32[]{:S(2)}, u32[]{:S(2)}) collective-permute-start(bf16[256,1024]{1,0:T(8,128)(2,1)} %get-tuple-element.132), channel_id=1, source_target_pairs={{0,1},{1,0},{2,3},{3,2},{4,5},{5,4},{6,7},{7,6},{8,9},{9,8},{10,11... | collective-permute-start | bytes 1572872 | tf_op jit(solution)/shard_map/ppermute | solution.py:710
  246.5 31.1 %collective-permute-start.30 = (bf16[256,1024]{1,0:T(8,128)(2,1)}, bf16[256,1024]{1,0:T(8,128)(2,1)S(1)}, u32[]{:S(2)}, u32[]{:S(2)}) collective-permute-start(bf16[256,1024]{1,0:T(8,128)(2,1)} %get-tuple-element.133), channel_id=1, source_target_pairs={{0,2},{1,3},{2,0},{3,1},{4,6},{5,7},{6,4},{7,5},{8,10},{9,11},{10,... | collective-permute-start | bytes 1572872 | tf_op jit(solution)/shard_map/ppermute | solution.py:710
  250.5 27.1 %copy-start.2 = (bf16[256,1024]{1,0:T(8,128)(2,1)S(1)}, bf16[256,1024]{1,0:T(8,128)(2,1)}, u32[]{:S(2)}) copy-start(bf16[256,1024]{1,0:T(8,128)(2,1)} %get-tuple-element.131) | copy-start | bytes 1572868
  250.5 27.1 %copy-start.25 = (f32[1,1024]{1,0:T(1,128)S(1)}, f32[1,1024]{1,0:T(1,128)}, u32[]{:S(2)}) copy-start(f32[1,1024]{1,0:T(1,128)} %get-tuple-element.135) | copy-start | bytes 12292
  250.5 9.5 %collective-permute-start.26 = (bf16[176,512]{1,0:T(8,128)(2,1)S(1)}, bf16[176,512]{1,0:T(8,128)(2,1)S(1)}, u32[]{:S(2)}, u32[]{:S(2)}) collective-permute-start(bf16[176,512]{1,0:T(8,128)(2,1)S(1)} %get-tuple-element.198), channel_id=1, source_target_pairs={{0,8},{4,12},{8,0},{12,4},{16,24},{20,28},{24,16},{28,20},{1,9},{5... | collective-permute-start | bytes 540680 | tf_op jit(solution)/shard_map/ppermute | solution.py:710
  252.0 16.6 %collective-permute-start.27 = (bf16[176,512]{1,0:T(8,128)(2,1)S(1)}, bf16[176,512]{1,0:T(8,128)(2,1)S(1)}, u32[]{:S(2)}, u32[]{:S(2)}) collective-permute-start(bf16[176,512]{1,0:T(8,128)(2,1)S(1)} %get-tuple-element.199), channel_id=1, source_target_pairs={{0,16},{4,20},{8,24},{12,28},{16,0},{20,4},{24,8},{28,12},{1,17},{... | collective-permute-start | bytes 540680 | tf_op jit(solution)/shard_map/ppermute | solution.py:710
  255.5 13.1 %collective-permute-start.28 = (bf16[176,512]{1,0:T(8,128)(2,1)S(1)}, bf16[176,512]{1,0:T(8,128)(2,1)S(1)}, u32[]{:S(2)}, u32[]{:S(2)}) collective-permute-start(bf16[176,512]{1,0:T(8,128)(2,1)S(1)} %get-tuple-element.200), channel_id=1, source_target_pairs={{0,24},{4,28},{8,16},{12,20},{16,8},{20,12},{24,0},{28,4},{1,25},{... | collective-permute-start | bytes 540680 | tf_op jit(solution)/shard_map/ppermute | solution.py:710
  260.1 17.5 %collective-permute-start.31 = (bf16[256,1024]{1,0:T(8,128)(2,1)}, bf16[256,1024]{1,0:T(8,128)(2,1)S(1)}, u32[]{:S(2)}, u32[]{:S(2)}) collective-permute-start(bf16[256,1024]{1,0:T(8,128)(2,1)} %get-tuple-element.134), channel_id=1, source_target_pairs={{0,3},{1,2},{2,1},{3,0},{4,7},{5,6},{6,5},{7,4},{8,11},{9,10},{10,... | collective-permute-start | bytes 1572872 | tf_op jit(solution)/shard_map/ppermute | solution.py:710
  272.4 5.8 %slice-start = ((f32[1,256,512]{2,1,0:T(8,128)}), f32[1,128,512]{2,1,0:T(8,128)S(1)}, s32[]{:S(2)}) async-start(f32[1,256,512]{2,1,0:T(8,128)} %reduce-scatter.2.cloned.1.call-done), calls=%async_computation.8 | async-start | bytes 524288 | tf_op jit(solution)/shard_map/slice | solution.py:1106
  272.4 9.6 %all-to-all-start.3 = ((bf16[4,32,1024]{2,1,0:T(8,128)(2,1)}), bf16[4,32,1024]{2,1,0:T(8,128)(2,1)}, u32[]{:S(2)}, u32[]{:S(2)}) async-start(bf16[4,32,1024]{2,1,0:T(8,128)(2,1)} %pad_maximum_fusion.6), calls=%async_computation.4 | async-start | bytes 524288 | tf_op jit(solution)/shard_map/all_to_all | solution.py:1102
  (8 other events, 6.2 us)
Sparse Core Ops, SparseCore 0:
  10.7 35.2 all-gather.4
  47.7 29.8 all-gather.6
  177.2 51.1 reduce-scatter.1

commit v7 on v6

--- a/solution.py
+++ b/solution.py
@@ -8,6 +8,7 @@
 PIECE = 256
 BLOCK = 16
 UNROLL = 4
+STEPS = 8
 ROWS = 256
 HALF = 128
 LOG2E = 1.4426950408889634
@@ -140,8 +141,8 @@
 
 def several(block):
     def blocks(i, carry):
-        for k in range(UNROLL):
-            carry = block(UNROLL * i + k, carry)
+        for k in range(STEPS):
+            carry = block(STEPS * i + k, carry)
         return carry
 
     return blocks
@@ -174,7 +175,7 @@
             carry = jnp.exp2(row_of(stepm_ref, t, n) * r2) * g
         return carry
 
-    carry_ref[...] = lax.fori_loop(0, rows // BLOCK // UNROLL, several(block), carry_ref[...])
+    carry_ref[...] = lax.fori_loop(0, rows // BLOCK // STEPS, several(block), carry_ref[...])
 
 
 def ahead_kernel(
@@ -233,7 +234,7 @@
             s_ref[tt * n : (tt + 1) * n, :] = (hp + g_ref[at, :].astype(f32)).astype(bf16)
         return h
 
-    carry_ref[...] = lax.fori_loop(0, rows // BLOCK // UNROLL, several(block), carry_ref[...])
+    carry_ref[...] = lax.fori_loop(0, rows // BLOCK // STEPS, several(block), carry_ref[...])
     read_out(rows // BLOCK)
     mixed = y_ref[BLOCK:] + vec_ref[SKIP : SKIP + 1, :] * act
     mixed_ref[...] = mixed

time: 296 us -> 294 us (level)
  transfers between devices with their start and end apart: 39 -> 39, of which waited for: 13 -> 12; matrix products, arithmetic and copies ran while one was open for 8% -> 8% of each run, Pallas kernels for 41% -> 41%
where the time goes in v7:
time: 294 us; the launch traced here: 293 us
  Pallas kernels  139 us (47%)
  starting transfers between devices  60 us (20%)
  waiting for transfers between devices  44.3 us (15%)
  other arithmetic  18.3 us (6%)
  between operations  17.8 us (6%)
  local copies, waits for them, and re-layouts  13.3 us (5%)
    pallas_call x8, Pallas kernels, call(): pl.pallas_call(kernel, out_shape=[jax.ShapeDtypeStruct(s, d) for s, d, _...  129 us
    ppermute x32, starting transfers between devices, partner(): lax.ppermute(value, axis, [(i, i ^ k) for i in range(lax.axis_size(axis))])  45.1 us
    ppermute x32, waiting for transfers between devices, partner(): lax.ppermute(value, axis, [(i, i ^ k) for i in range(lax.axis_size(axis))])  36.3 us
    all_to_all x1, waiting for transfers between devices, body(): split = lax.all_to_all(split, 'seq', 0, 0).reshape(lines, 2 * chans + LANES)  7.41 us
    pallas_call x1, Pallas kernels, by_blocks(): pl.pallas_call(kernel, out_shape=jax.ShapeDtypeStruct((batches, rows, cha...  6.25 us
  transfers between devices with their start and end apart: 39, of which 12 were waited for; matrix products, arithmetic and copies ran while one was open for 8% of the time, Pallas kernels for 41%

profile of v7, /device:TPU:0, one launch (start us, length us, event | category | flops | bytes accessed | tf_op | source)
XLA Modules:
  0.0 292.7 jit_solution(5798935178697177820)
XLA Ops:
  7.3 1.1 fusion.44
  9.9 0.7 pad_maximum_fusion.4
  10.6 3.0 %collective-permute-start = (bf16[128,1024]{1,0:T(8,128)(2,1)S(1)}, bf16[128,1024]{1,0:T(8,128)(2,1)S(1)}, u32[]{:S(2)}, u32[]{:S(2)}) collective-permute-start(bf16[128,1024]{1,0:T(8,128)(2,1)S(1)} %get-tuple-element.208.refs_2_), channel_id=1, source_target_pairs={{0,1},{1,0},{2,3},{3,2},{4,5},{5,4},{6,7},{7,6},{8,9},{9,8},{10,11... | collective-permute-start | bytes 786440 | tf_op jit(solution)/shard_map/ppermute | solution.py:711
  13.6 1.5 collective-permute-start.1
  15.2 1.8 shard_map.237
  17.0 3.5 %all-to-all-start = ((bf16[4,32,1152]{2,1,0:T(8,128)(2,1)}), bf16[4,32,1152]{2,1,0:T(8,128)(2,1)S(1)}, u32[]{:S(2)}, u32[]{:S(2)}) async-start(bf16[4,32,1152]{2,1,0:T(8,128)(2,1)} %shard_map.237), calls=%async_computation | async-start | bytes 589824 | tf_op jit(solution)/shard_map/all_to_all | solution.py:837
  21.4 7.4 %all-to-all-done = bf16[4,32,1152]{2,1,0:T(8,128)(2,1)S(1)} async-done(((bf16[4,32,1152]{2,1,0:T(8,128)(2,1)}), bf16[4,32,1152]{2,1,0:T(8,128)(2,1)S(1)}, u32[]{:S(2)}, u32[]{:S(2)}) %all-to-all-start) | async-done | bytes 294944 | tf_op jit(solution)/shard_map/all_to_all | solution.py:837
  28.8 1.6 collective-permute-start.3
  30.5 2.6 collective-permute-start.4
  34.0 1.0 collective-permute-done.3
  35.1 2.4 collective-permute-start.2
  37.5 6.1 %collective-permute-done.4 = bf16[128,640]{1,0:T(8,128)(2,1)S(1)} collective-permute-done((bf16[128,640]{1,0:T(8,128)(2,1)S(1)}, bf16[128,640]{1,0:T(8,128)(2,1)S(1)}, u32[]{:S(2)}, u32[]{:S(2)}) %collective-permute-start.4) | collective-permute-done | bytes 163872 | tf_op jit(solution)/shard_map/ppermute | solution.py:711
  44.4 2.4 collective-permute-done.2.refs_5_
  47.7 0.8 copy-done.6
  48.4 10.0 %shard_map.238 = (bf16[1024,1024]{1,0:T(8,128)(2,1)}, bf16[1024,1024]{1,0:T(8,128)(2,1)}, bf16[1024,512]{1,0:T(8,128)(2,1)}, f32[1024,512]{1,0:T(8,128)}, bf16[1...) custom-call(s32[9]{0:T(128)} %concatenate.76.refs_0_, ...), custom_call_target="tpu_custom_call" | custom-call | tf_op jit(solution)/shard_map/pallas_call | solution.py:580
  58.4 0.8 collective-permute-start.7
  59.7 2.3 collective-permute-start.9
  62.0 0.8 slice_convert_fusion.2
  64.3 3.5 %all-to-all-start.2 = ((bf16[4,64,1024]{2,1,0:T(8,128)(2,1)}), bf16[4,64,1024]{2,1,0:T(8,128)(2,1)S(1)}, u32[]{:S(2)}, u32[]{:S(2)}) async-start(bf16[4,64,1024]{2,1,0:T(8,128)(2,1)} %bitcast.122), calls=%async_computation.2 | async-start | bytes 1048576 | tf_op jit(solution)/shard_map/all_to_all | solution.py:890
  68.9 1.3 select_convert_fusion
  70.5 0.8 pad_maximum_fusion.3.proj_ref.refs_1_
  71.3 12.8 %shard_map.239 = (bf16[16384,512]{1,0:T(8,128)(2,1)}, f32[1024,512]{1,0:T(8,128)}) custom-call(s32[17]{0:T(128)} %pad_add_fusion.me_ref.refs_0_, f32[104,1024]{1,0:T(8,128)} %pad_maximum_fusion.3.proj_ref.refs_1_, bf16[1024,512]{1,0:T(8,128)(2,1)} %get-tuple-element.81.act_ref.refs_2_.refs_8_, f32[128,512]{1,0:T(8,128)} %get-tuple-element.83.vec_ref.refs_6_.refs_10_), custom_call_target="tpu_custom_call" | custom-call | tf_op jit(solution)/shard_map/pallas_call | solution.py:580
  86.1 15.8 %shard_map.240 = (bf16[16384,512]{1,0:T(8,128)(2,1)}, f32[1024,512]{1,0:T(8,128)}, f32[1024,512]{1,0:T(8,128)}, bf16[512,1024]{1,0:T(8,128)(2,1)}, f32[16,512]{1...) custom-call(s32[17]{0:T(128)} %pad_add_fusion.me_ref.refs_0_, ...), custom_call_target="tpu_custom_call" | custom-call | tf_op jit(solution)/shard_map/pallas_call | solution.py:580
  101.9 1.8 collective-permute-start.10
  103.7 1.5 collective-permute-start.11
  105.6 15.2 %shard_map.241 = (bf16[16384,512]{1,0:T(8,128)(2,1)}, f32[1024,512]{1,0:T(8,128)}, f32[1024,512]{1,0:T(8,128)}, bf16[512,1024]{1,0:T(8,128)(2,1)}, f32[16,512]{1...) custom-call(s32[17]{0:T(128)} %pad_add_fusion.me_ref.refs_0_, ...), custom_call_target="tpu_custom_call", output_to_operand_aliasing={{0}: (10, {}), {1}: (11, {}), {2}: (12, {}), {3}: (13, {})} | custom-call | tf_op jit(solution)/shard_map/pallas_call | solution.py:580
  120.8 1.8 collective-permute-start.13
  122.6 1.5 collective-permute-start.14
  124.8 1.8 collective-permute-start.19
  126.6 1.5 collective-permute-start.20
  128.1 2.2 collective-permute-done.13
  130.3 2.7 collective-permute-start.21
  133.0 4.7 %collective-permute-done.14 = bf16[128,1024]{1,0:T(8,128)(2,1)S(1)} collective-permute-done((bf16[128,1024]{1,0:T(8,128)(2,1)}, bf16[128,1024]{1,0:T(8,128)(2,1)S(1)}, u32[]{:S(2)}, u32[]{:S(2)}) %collective-permute-start.14) | collective-permute-done | bytes 262176 | tf_op jit(solution)/shard_map/ppermute | solution.py:711
  138.1 1.2 collective-permute-start.16
  139.3 0.9 collective-permute-start.17
  140.2 1.4 collective-permute-done.19.refs_9_
  141.6 2.7 collective-permute-start.18
  144.2 4.5 %collective-permute-done.20.refs_10_ = bf16[128,1024]{1,0:T(8,128)(2,1)S(1)} collective-permute-done((bf16[128,1024]{1,0:T(8,128)(2,1)S(1)}, bf16[128,1024]{1,0:T(8,128)(2,1)S(1)}, u32[]{:S(2)}, u32[]{:S(2)}) %collective-permute-start.20) | collective-permute-done | bytes 262176 | tf_op jit(solution)/shard_map/ppermute | solution.py:711
  149.5 9.6 %shard_map.242 = (bf16[16384,512]{1,0:T(8,128)(2,1)}, f32[1024,512]{1,0:T(8,128)}, bf16[1024,512]{1,0:T(8,128)(2,1)}, bf16[1024,1024]{1,0:T(8,128)(2,1)}, f32[1,512]{1,0:T(1,128)}, /*index=5*/f32[16,512]{1,0:T(8,128)}) custom-call(s32[17]{0:T(128)} %pad_add_fusion.me_ref.refs_0_, f32[104,1024]{1,0:T(8,128)} %pad_maximum_fusion.3.proj_ref.refs_1_, ...), custom_call_target="tpu_custom_call" | custom-call | tf_op jit(solution)/shard_map/pallas_call | solution.py:580
  160.0 9.5 %shard_map.243 = (bf16[16384,512]{1,0:T(8,128)(2,1)}, f32[1024,512]{1,0:T(8,128)}, bf16[1024,512]{1,0:T(8,128)(2,1)}, bf16[1024,1024]{1,0:T(8,128)(2,1)}, f32[1,512]{1,0:T(1,128)}, /*index=5*/f32[16,512]{1,0:T(8,128)}) custom-call(s32[17]{0:T(128)} %pad_add_fusion.me_ref.refs_0_, ...), custom_call_target="tpu_custom_call", output_to_operand_aliasing={{0}: (14, {}), {1}: (15, {}), {2}: (16, {}), {3}: (17, {})} | custom-call | tf_op jit(solution)/shard_map/pallas_call | solution.py:580
  169.5 6.2 %shard_map.246 = f32[8,256,512]{2,1,0:T(8,128)} custom-call(bf16[1024,1024]{1,0:T(8,128)(2,1)} %get-tuple-element.125.refs_15_.normed_ref, bf16[512,1024]{1,0:T(8,128)(2,1)} %get-tuple-element.130.gated_ref, bf16[1024,512]{1,0:T(8,128)(2,1)} %get-tuple-element.121.refs_9_.dg_ref, bf16[1024,1024]{1,0:T(8,128)(2,1)} %get-tuple-element.129.refs_0_), custom_call_target="tpu_custom_call" | custom-call | tf_op jit(solution)/shard_map/pallas_call | solution.py:634
  176.7 42.9 %shard_map.244 = (f32[1024,512]{1,0:T(8,128)}, bf16[1024,128]{1,0:T(8,128)(2,1)}, f32[128,512]{1,0:T(8,128)}) custom-call(s32[17]{0:T(128)} %pad_add_fusion.me_ref.refs_0_, f32[104,1024]{1,0:T(8,128)} %pad_maximum_fusion.3.proj_ref.refs_1_, bf16[1024,512]{1,0:T(8,128)(2,1)} %get-tuple-element.81.act_ref.refs_2_.refs_8_, ...), custom_call_target="tpu_custom_call" | custom-call | tf_op jit(solution)/shard_map/pallas_call | solution.py:580
  219.5 1.3 collective-permute-start.22
  220.8 0.9 collective-permute-start.23
  221.7 1.4 collective-permute-start.24
  223.1 0.8 pad_maximum_fusion.2
  223.9 3.5 %all-to-all-start.1 = ((bf16[4,64,1024]{2,1,0:T(8,128)(2,1)}), bf16[4,64,1024]{2,1,0:T(8,128)(2,1)S(1)}, u32[]{:S(2)}, u32[]{:S(2)}) async-start(bf16[4,64,1024]{2,1,0:T(8,128)(2,1)} %pad_maximum_fusion.2), calls=%async_computation.1 | async-start | bytes 1048576 | tf_op jit(solution)/shard_map/all_to_all | solution.py:1014
  228.0 2.2 collective-permute-done.23.refs_3_
  231.0 13.1 %shard_map.245 = (bf16[256,1024]{1,0:T(8,128)(2,1)}, bf16[256,1024]{1,0:T(8,128)(2,1)}, bf16[256,1024]{1,0:T(8,128)(2,1)}, bf16[256,1024]{1,0:T(8,128)(2,1)}, f3...) custom-call(s32[18]{0:T(128)} %pad_add_fusion.1.refs_0_, ...), custom_call_target="tpu_custom_call" | custom-call | tf_op jit(solution)/shard_map/pallas_call | solution.py:580
  244.4 0.9 collective-permute-start.29
  245.3 1.6 collective-permute-start.30
  247.8 1.6 fusion.41
  249.5 1.3 collective-permute-start.26
  250.7 3.5 %collective-permute-start.27 = (bf16[176,512]{1,0:T(8,128)(2,1)S(1)}, bf16[176,512]{1,0:T(8,128)(2,1)S(1)}, u32[]{:S(2)}, u32[]{:S(2)}) collective-permute-start(bf16[176,512]{1,0:T(8,128)(2,1)S(1)} %get-tuple-element.199), channel_id=1, source_target_pairs={{0,16},{4,20},{8,24},{12,28},{16,0},{20,4},{24,8},{28,12},{1,17},{... | collective-permute-start | bytes 540680 | tf_op jit(solution)/shard_map/ppermute | solution.py:711
  254.2 4.8 %collective-permute-done.26 = bf16[176,512]{1,0:T(8,128)(2,1)S(1)} collective-permute-done((bf16[176,512]{1,0:T(8,128)(2,1)S(1)}, bf16[176,512]{1,0:T(8,128)(2,1)S(1)}, u32[]{:S(2)}, u32[]{:S(2)}) %collective-permute-start.26) | collective-permute-done | bytes 180256 | tf_op jit(solution)/shard_map/ppermute | solution.py:711
  259.1 1.3 collective-permute-start.31
  260.4 7.0 %collective-permute-done.27 = bf16[176,512]{1,0:T(8,128)(2,1)S(1)} collective-permute-done((bf16[176,512]{1,0:T(8,128)(2,1)S(1)}, bf16[176,512]{1,0:T(8,128)(2,1)S(1)}, u32[]{:S(2)}, u32[]{:S(2)}) %collective-permute-start.27) | collective-permute-done | bytes 180256 | tf_op jit(solution)/shard_map/ppermute | solution.py:711
  269.4 1.0 slice.379
  271.1 4.2 %all-to-all-start.3 = ((bf16[4,32,1024]{2,1,0:T(8,128)(2,1)}), bf16[4,32,1024]{2,1,0:T(8,128)(2,1)}, u32[]{:S(2)}, u32[]{:S(2)}) async-start(bf16[4,32,1024]{2,1,0:T(8,128)(2,1)} %pad_maximum_fusion.6), calls=%async_computation.4 | async-start | bytes 524288 | tf_op jit(solution)/shard_map/all_to_all | solution.py:1103
  275.3 1.0 slice_bitcast_fusion.3
  277.6 2.6 fusion.6
  280.7 2.1 shard_map.247
  282.8 1.4 copy.58
  284.2 0.8 copy.69
  (192 shorter events, 19.3 us)
Async XLA Ops:
  7.2 13.3 %copy-start.23 = (bf16[64,64]{1,0:T(8,128)(2,1)S(1)}, bf16[64,64]{1,0:T(8,128)(2,1)}, u32[]{:S(2)}) copy-start(bf16[64,64]{1,0:T(8,128)(2,1)} %param.23) | copy-start | bytes 24580
  7.2 13.4 %copy-start.28 = (bf16[4,64]{1,0:T(4,128)(2,1)S(1)}, bf16[4,64]{1,0:T(4,128)(2,1)}, u32[]{:S(2)}) copy-start(bf16[4,64]{1,0:T(4,128)(2,1)} %param.20) | copy-start | bytes 1540
  7.2 13.5 %copy-start.26 = (bf16[64,16]{0,1:T(8,128)(2,1)S(1)}, bf16[64,16]{0,1:T(8,128)(2,1)}, u32[]{:S(2)}) copy-start(bf16[64,16]{0,1:T(8,128)(2,1)} %param.25) | copy-start | bytes 6148
  7.2 13.6 %copy-start.29 = (bf16[64]{0:T(256)(128)(2,1)S(1)}, bf16[64]{0:T(256)(128)(2,1)}, u32[]{:S(2)}) copy-start(bf16[64]{0:T(256)(128)(2,1)} %param.21) | copy-start | bytes 388
  7.2 13.7 %copy-start.30 = (bf16[64]{0:T(256)(128)(2,1)S(1)}, bf16[64]{0:T(256)(128)(2,1)}, u32[]{:S(2)}) copy-start(bf16[64]{0:T(256)(128)(2,1)} %param.24) | copy-start | bytes 388
  7.2 13.8 %copy-start.31 = (bf16[64]{0:T(256)(128)(2,1)S(1)}, bf16[64]{0:T(256)(128)(2,1)}, u32[]{:S(2)}) copy-start(bf16[64]{0:T(256)(128)(2,1)} %param.26) | copy-start | bytes 388
  7.2 14.1 %copy-start.24 = (bf16[64,96]{1,0:T(8,128)(2,1)S(1)}, bf16[64,96]{1,0:T(8,128)(2,1)}, u32[]{:S(2)}) copy-start(bf16[64,96]{1,0:T(8,128)(2,1)} %param.22) | copy-start | bytes 36868
  7.3 14.1 %copy-start.22 = (bf16[64,1024]{1,0:T(8,128)(2,1)S(1)}, bf16[64,1024]{1,0:T(8,128)(2,1)}, u32[]{:S(2)}) copy-start(bf16[64,1024]{1,0:T(8,128)(2,1)} %param.27) | copy-start | bytes 393220
  7.3 40.4 %all-gather.5.cloned.1.call-start = ((), (), s32[]{:S(2)}) async-start(), calls=%async_computation.6 | async-start | bytes 1474560 | tf_op jit(solution)/shard_map/all_gather | solution.py:835
  8.5 26.6 %copy-start.5 = (bf16[128,1024]{1,0:T(8,128)(2,1)}, bf16[128,1024]{1,0:T(8,128)(2,1)S(1)}, u32[]{:S(2)}) copy-start(bf16[128,1024]{1,0:T(8,128)(2,1)S(1)} %get-tuple-element.208.refs_2_) | copy-start | bytes 786436
  10.6 36.2 %collective-permute-start = (bf16[128,1024]{1,0:T(8,128)(2,1)S(1)}, bf16[128,1024]{1,0:T(8,128)(2,1)S(1)}, u32[]{:S(2)}, u32[]{:S(2)}) collective-permute-start(bf16[128,1024]{1,0:T(8,128)(2,1)S(1)} %get-tuple-element.208.refs_2_), channel_id=1, source_target_pairs={{0,1},{1,0},{2,3},{3,2},{4,5},{5,4},{6,7},{7,6},{8,9},{9,8},{10,11... | collective-permute-start | bytes 786440 | tf_op jit(solution)/shard_map/ppermute | solution.py:711
  13.6 33.2 %collective-permute-start.1 = (bf16[128,1024]{1,0:T(8,128)(2,1)S(1)}, bf16[128,1024]{1,0:T(8,128)(2,1)S(1)}, u32[]{:S(2)}, u32[]{:S(2)}) collective-permute-start(bf16[128,1024]{1,0:T(8,128)(2,1)S(1)} %get-tuple-element.208.refs_2_), channel_id=1, source_target_pairs={{0,2},{1,3},{2,0},{3,1},{4,6},{5,7},{6,4},{7,5},{8,10},{9,11},{10,... | collective-permute-start | bytes 786440 | tf_op jit(solution)/shard_map/ppermute | solution.py:711
  17.0 11.8 %all-to-all-start = ((bf16[4,32,1152]{2,1,0:T(8,128)(2,1)}), bf16[4,32,1152]{2,1,0:T(8,128)(2,1)S(1)}, u32[]{:S(2)}, u32[]{:S(2)}) async-start(bf16[4,32,1152]{2,1,0:T(8,128)(2,1)} %shard_map.237), calls=%async_computation | async-start | bytes 589824 | tf_op jit(solution)/shard_map/all_to_all | solution.py:837
  20.5 65.6 %all-gather.7.cloned.1.call-start = ((), (), s32[]{:S(2)}) async-start(), calls=%async_computation.7 | async-start | bytes 2359296 | tf_op jit(solution)/shard_map/all_gather | solution.py:856
  28.8 6.2 %collective-permute-start.3 = (bf16[128,640]{1,0:T(8,128)(2,1)S(1)}, bf16[128,640]{1,0:T(8,128)(2,1)S(1)}, u32[]{:S(2)}, u32[]{:S(2)}) collective-permute-start(bf16[128,640]{1,0:T(8,128)(2,1)S(1)} %slice_add_fusion), channel_id=1, source_target_pairs={{0,8},{4,12},{8,0},{12,4},{16,24},{20,28},{24,16},{28,20},{1,9},{5... | collective-permute-start | bytes 491528 | tf_op jit(solution)/shard_map/ppermute | solution.py:711
  30.5 13.1 %collective-permute-start.4 = (bf16[128,640]{1,0:T(8,128)(2,1)S(1)}, bf16[128,640]{1,0:T(8,128)(2,1)S(1)}, u32[]{:S(2)}, u32[]{:S(2)}) collective-permute-start(bf16[128,640]{1,0:T(8,128)(2,1)S(1)} %slice_add_fusion), channel_id=1, source_target_pairs={{0,16},{4,20},{8,24},{12,28},{16,0},{20,4},{24,8},{28,12},{1,17},{... | collective-permute-start | bytes 491528 | tf_op jit(solution)/shard_map/ppermute | solution.py:711
  33.1 10.5 %collective-permute-start.5 = (bf16[128,640]{1,0:T(8,128)(2,1)S(1)}, bf16[128,640]{1,0:T(8,128)(2,1)S(1)}, u32[]{:S(2)}, u32[]{:S(2)}) collective-permute-start(bf16[128,640]{1,0:T(8,128)(2,1)S(1)} %slice_add_fusion), channel_id=1, source_target_pairs={{0,24},{4,28},{8,16},{12,20},{16,8},{20,12},{24,0},{28,4},{1,25},{... | collective-permute-start | bytes 491528 | tf_op jit(solution)/shard_map/ppermute | solution.py:711
  35.1 11.7 %collective-permute-start.2 = (bf16[128,1024]{1,0:T(8,128)(2,1)S(1)}, bf16[128,1024]{1,0:T(8,128)(2,1)S(1)}, u32[]{:S(2)}, u32[]{:S(2)}) collective-permute-start(bf16[128,1024]{1,0:T(8,128)(2,1)S(1)} %get-tuple-element.208.refs_2_), channel_id=1, source_target_pairs={{0,3},{1,2},{2,1},{3,0},{4,7},{5,6},{6,5},{7,4},{8,11},{9,10},{10,... | collective-permute-start | bytes 786440 | tf_op jit(solution)/shard_map/ppermute | solution.py:711
  43.7 3.9 %copy-start.1 = (bf16[4,128,640]{2,1,0:T(8,128)(2,1)}, bf16[4,128,640]{2,1,0:T(8,128)(2,1)S(1)}, u32[]{:S(2)}) copy-start(bf16[4,128,640]{2,1,0:T(8,128)(2,1)S(1)} %pad_maximum_fusion.refs_6_) | copy-start | bytes 1966084
  43.7 3.9 %collective-permute-start.6 = (bf16[4,128,640]{2,1,0:T(8,128)(2,1)S(1)}, bf16[4,128,640]{2,1,0:T(8,128)(2,1)S(1)}, u32[]{:S(2)}, u32[]{:S(2)}) collective-permute-start(bf16[4,128,640]{2,1,0:T(8,128)(2,1)S(1)} %pad_maximum_fusion.refs_6_), channel_id=1, source_target_pairs={{0,4},{4,0},{8,12},{12,8},{16,20},{20,16},{24,28},{28,24},{1,5},{5... | collective-permute-start | bytes 1966088 | tf_op jit(solution)/shard_map/ppermute | solution.py:711
  46.8 0.8 copy-start.9
  47.6 0.8 copy-start.6
  58.4 12.0 %collective-permute-start.7 = (bf16[96,1024]{1,0:T(8,128)(2,1)}, bf16[96,1024]{1,0:T(8,128)(2,1)S(1)}, u32[]{:S(2)}, u32[]{:S(2)}) collective-permute-start(bf16[96,1024]{1,0:T(8,128)(2,1)} %get-tuple-element.80), channel_id=1, source_target_pairs={{0,1},{1,0},{2,3},{3,2},{4,5},{5,4},{6,7},{7,6},{8,9},{9,8},{10,11... | collective-permute-start | bytes 589832 | tf_op jit(solution)/shard_map/ppermute | solution.py:711
  59.2 11.1 %collective-permute-start.8 = (bf16[96,1024]{1,0:T(8,128)(2,1)}, bf16[96,1024]{1,0:T(8,128)(2,1)S(1)}, u32[]{:S(2)}, u32[]{:S(2)}) collective-permute-start(bf16[96,1024]{1,0:T(8,128)(2,1)} %get-tuple-element.80), channel_id=1, source_target_pairs={{0,2},{1,3},{2,0},{3,1},{4,6},{5,7},{6,4},{7,5},{8,10},{9,11},{10,... | collective-permute-start | bytes 589832 | tf_op jit(solution)/shard_map/ppermute | solution.py:711
  59.7 10.7 %collective-permute-start.9 = (bf16[96,1024]{1,0:T(8,128)(2,1)}, bf16[96,1024]{1,0:T(8,128)(2,1)S(1)}, u32[]{:S(2)}, u32[]{:S(2)}) collective-permute-start(bf16[96,1024]{1,0:T(8,128)(2,1)} %get-tuple-element.80), channel_id=1, source_target_pairs={{0,3},{1,2},{2,1},{3,0},{4,7},{5,6},{6,5},{7,4},{8,11},{9,10},{10,... | collective-permute-start | bytes 589832 | tf_op jit(solution)/shard_map/ppermute | solution.py:711
  64.3 41.1 %all-to-all-start.2 = ((bf16[4,64,1024]{2,1,0:T(8,128)(2,1)}), bf16[4,64,1024]{2,1,0:T(8,128)(2,1)S(1)}, u32[]{:S(2)}, u32[]{:S(2)}) async-start(bf16[4,64,1024]{2,1,0:T(8,128)(2,1)} %bitcast.122), calls=%async_computation.2 | async-start | bytes 1048576 | tf_op jit(solution)/shard_map/all_to_all | solution.py:890
  67.8 201.6 %reduce-scatter.2.cloned.1.call-start = ((), (), s32[]{:S(2)}) async-start(), calls=%async_computation.5 | async-start | bytes 4718592 | tf_op jit(solution)/shard_map/reduce_scatter | solution.py:1025
  68.9 1.5 copy-start.21
  70.3 13.8 %copy-start.27 = (f32[1,128]{1,0:T(1,128)S(1)}, f32[1,128]{1,0:T(1,128)}, u32[]{:S(2)}) copy-start(f32[1,128]{1,0:T(1,128)} %get-tuple-element.105) | copy-start | bytes 1540
  101.9 22.2 %collective-permute-start.10 = (bf16[128,1024]{1,0:T(8,128)(2,1)}, bf16[128,1024]{1,0:T(8,128)(2,1)S(1)}, u32[]{:S(2)}, u32[]{:S(2)}) collective-permute-start(bf16[128,1024]{1,0:T(8,128)(2,1)} %get-tuple-element.89), channel_id=1, source_target_pairs={{0,1},{1,0},{2,3},{3,2},{4,5},{5,4},{6,7},{7,6},{8,9},{9,8},{10,11... | collective-permute-start | bytes 786440 | tf_op jit(solution)/shard_map/ppermute | solution.py:711
  103.7 20.7 %collective-permute-start.11 = (bf16[128,1024]{1,0:T(8,128)(2,1)}, bf16[128,1024]{1,0:T(8,128)(2,1)S(1)}, u32[]{:S(2)}, u32[]{:S(2)}) collective-permute-start(bf16[128,1024]{1,0:T(8,128)(2,1)} %get-tuple-element.90), channel_id=1, source_target_pairs={{0,2},{1,3},{2,0},{3,1},{4,6},{5,7},{6,4},{7,5},{8,10},{9,11},{10,... | collective-permute-start | bytes 786440 | tf_op jit(solution)/shard_map/ppermute | solution.py:711
  105.2 19.2 %collective-permute-start.12 = (bf16[128,1024]{1,0:T(8,128)(2,1)}, bf16[128,1024]{1,0:T(8,128)(2,1)S(1)}, u32[]{:S(2)}, u32[]{:S(2)}) collective-permute-start(bf16[128,1024]{1,0:T(8,128)(2,1)} %get-tuple-element.91), channel_id=1, source_target_pairs={{0,3},{1,2},{2,1},{3,0},{4,7},{5,6},{6,5},{7,4},{8,11},{9,10},{10,... | collective-permute-start | bytes 786440 | tf_op jit(solution)/shard_map/ppermute | solution.py:711
  105.6 18.8 %copy-start.14 = (bf16[128,1024]{1,0:T(8,128)(2,1)S(1)}, bf16[128,1024]{1,0:T(8,128)(2,1)}, u32[]{:S(2)}) copy-start(bf16[128,1024]{1,0:T(8,128)(2,1)} %get-tuple-element.88) | copy-start | bytes 786436
  120.8 9.5 %collective-permute-start.13 = (bf16[128,1024]{1,0:T(8,128)(2,1)}, bf16[128,1024]{1,0:T(8,128)(2,1)S(1)}, u32[]{:S(2)}, u32[]{:S(2)}) collective-permute-start(bf16[128,1024]{1,0:T(8,128)(2,1)} %get-tuple-element.100), channel_id=1, source_target_pairs={{0,1},{1,0},{2,3},{3,2},{4,5},{5,4},{6,7},{7,6},{8,9},{9,8},{10,11... | collective-permute-start | bytes 786440 | tf_op jit(solution)/shard_map/ppermute | solution.py:711
  122.6 15.1 %collective-permute-start.14 = (bf16[128,1024]{1,0:T(8,128)(2,1)}, bf16[128,1024]{1,0:T(8,128)(2,1)S(1)}, u32[]{:S(2)}, u32[]{:S(2)}) collective-permute-start(bf16[128,1024]{1,0:T(8,128)(2,1)} %get-tuple-element.101), channel_id=1, source_target_pairs={{0,2},{1,3},{2,0},{3,1},{4,6},{5,7},{6,4},{7,5},{8,10},{9,11},{10,... | collective-permute-start | bytes 786440 | tf_op jit(solution)/shard_map/ppermute | solution.py:711
  124.1 13.6 %collective-permute-start.15 = (bf16[128,1024]{1,0:T(8,128)(2,1)}, bf16[128,1024]{1,0:T(8,128)(2,1)S(1)}, u32[]{:S(2)}, u32[]{:S(2)}) collective-permute-start(bf16[128,1024]{1,0:T(8,128)(2,1)} %get-tuple-element.102), channel_id=1, source_target_pairs={{0,3},{1,2},{2,1},{3,0},{4,7},{5,6},{6,5},{7,4},{8,11},{9,10},{10,... | collective-permute-start | bytes 786440 | tf_op jit(solution)/shard_map/ppermute | solution.py:711
  124.4 13.3 %copy-start.13 = (bf16[128,1024]{1,0:T(8,128)(2,1)S(1)}, bf16[128,1024]{1,0:T(8,128)(2,1)}, u32[]{:S(2)}) copy-start(bf16[128,1024]{1,0:T(8,128)(2,1)} %get-tuple-element.99) | copy-start | bytes 786436
  124.8 13.3 %copy-start.4 = (bf16[128,1024]{1,0:T(8,128)(2,1)}, bf16[128,1024]{1,0:T(8,128)(2,1)S(1)}, u32[]{:S(2)}) copy-start(bf16[128,1024]{1,0:T(8,128)(2,1)S(1)} %get-tuple-element.201.refs_8_) | copy-start | bytes 786436
  124.8 16.8 %collective-permute-start.19 = (bf16[128,1024]{1,0:T(8,128)(2,1)S(1)}, bf16[128,1024]{1,0:T(8,128)(2,1)S(1)}, u32[]{:S(2)}, u32[]{:S(2)}) collective-permute-start(bf16[128,1024]{1,0:T(8,128)(2,1)S(1)} %get-tuple-element.201.refs_8_), channel_id=1, source_target_pairs={{0,1},{1,0},{2,3},{3,2},{4,5},{5,4},{6,7},{7,6},{8,9},{9,8},{10,11... | collective-permute-start | bytes 786440 | tf_op jit(solution)/shard_map/ppermute | solution.py:711
  126.6 22.1 %collective-permute-start.20 = (bf16[128,1024]{1,0:T(8,128)(2,1)S(1)}, bf16[128,1024]{1,0:T(8,128)(2,1)S(1)}, u32[]{:S(2)}, u32[]{:S(2)}) collective-permute-start(bf16[128,1024]{1,0:T(8,128)(2,1)S(1)} %get-tuple-element.201.refs_8_), channel_id=1, source_target_pairs={{0,2},{1,3},{2,0},{3,1},{4,6},{5,7},{6,4},{7,5},{8,10},{9,11},{10,... | collective-permute-start | bytes 786440 | tf_op jit(solution)/shard_map/ppermute | solution.py:711
  130.3 18.4 %collective-permute-start.21 = (bf16[128,1024]{1,0:T(8,128)(2,1)S(1)}, bf16[128,1024]{1,0:T(8,128)(2,1)S(1)}, u32[]{:S(2)}, u32[]{:S(2)}) collective-permute-start(bf16[128,1024]{1,0:T(8,128)(2,1)S(1)} %get-tuple-element.201.refs_8_), channel_id=1, source_target_pairs={{0,3},{1,2},{2,1},{3,0},{4,7},{5,6},{6,5},{7,4},{8,11},{9,10},{10,... | collective-permute-start | bytes 786440 | tf_op jit(solution)/shard_map/ppermute | solution.py:711
  138.1 21.0 %copy-start.3 = (bf16[128,1024]{1,0:T(8,128)(2,1)}, bf16[128,1024]{1,0:T(8,128)(2,1)S(1)}, u32[]{:S(2)}) copy-start(bf16[128,1024]{1,0:T(8,128)(2,1)S(1)} %get-tuple-element.203.refs_8_) | copy-start | bytes 786436
  138.1 21.0 %collective-permute-start.16 = (bf16[128,1024]{1,0:T(8,128)(2,1)S(1)}, bf16[128,1024]{1,0:T(8,128)(2,1)S(1)}, u32[]{:S(2)}, u32[]{:S(2)}) collective-permute-start(bf16[128,1024]{1,0:T(8,128)(2,1)S(1)} %get-tuple-element.203.refs_8_), channel_id=1, source_target_pairs={{0,1},{1,0},{2,3},{3,2},{4,5},{5,4},{6,7},{7,6},{8,9},{9,8},{10,11... | collective-permute-start | bytes 786440 | tf_op jit(solution)/shard_map/ppermute | solution.py:711
  139.3 19.8 %collective-permute-start.17 = (bf16[128,1024]{1,0:T(8,128)(2,1)S(1)}, bf16[128,1024]{1,0:T(8,128)(2,1)S(1)}, u32[]{:S(2)}, u32[]{:S(2)}) collective-permute-start(bf16[128,1024]{1,0:T(8,128)(2,1)S(1)} %get-tuple-element.203.refs_8_), channel_id=1, source_target_pairs={{0,2},{1,3},{2,0},{3,1},{4,6},{5,7},{6,4},{7,5},{8,10},{9,11},{10,... | collective-permute-start | bytes 786440 | tf_op jit(solution)/shard_map/ppermute | solution.py:711
  141.6 7.1 %copy-start.16 = (bf16[128,1024]{1,0:T(8,128)(2,1)}, bf16[128,1024]{1,0:T(8,128)(2,1)S(1)}, u32[]{:S(2)}) copy-start(bf16[128,1024]{1,0:T(8,128)(2,1)S(1)} %collective-permute-done.19.refs_9_) | copy-start | bytes 786436
  141.6 17.5 %collective-permute-start.18 = (bf16[128,1024]{1,0:T(8,128)(2,1)S(1)}, bf16[128,1024]{1,0:T(8,128)(2,1)S(1)}, u32[]{:S(2)}, u32[]{:S(2)}) collective-permute-start(bf16[128,1024]{1,0:T(8,128)(2,1)S(1)} %get-tuple-element.203.refs_8_), channel_id=1, source_target_pairs={{0,3},{1,2},{2,1},{3,0},{4,7},{5,6},{6,5},{7,4},{8,11},{9,10},{10,... | collective-permute-start | bytes 786440 | tf_op jit(solution)/shard_map/ppermute | solution.py:711
  159.1 0.8 copy-start.12
  219.5 8.5 %collective-permute-start.22 = (bf16[1024,128]{1,0:T(8,128)(2,1)}, bf16[1024,128]{1,0:T(8,128)(2,1)S(1)}, u32[]{:S(2)}, u32[]{:S(2)}) collective-permute-start(bf16[1024,128]{1,0:T(8,128)(2,1)} %get-tuple-element.117.refs_1_), channel_id=1, source_target_pairs={{0,1},{1,0},{2,3},{3,2},{4,5},{5,4},{6,7},{7,6},{8,9},{9,8},{10,11... | collective-permute-start | bytes 786440 | tf_op jit(solution)/shard_map/ppermute | solution.py:711
  220.8 9.4 %collective-permute-start.23 = (bf16[1024,128]{1,0:T(8,128)(2,1)}, bf16[1024,128]{1,0:T(8,128)(2,1)S(1)}, u32[]{:S(2)}, u32[]{:S(2)}) collective-permute-start(bf16[1024,128]{1,0:T(8,128)(2,1)} %get-tuple-element.117.refs_1_), channel_id=1, source_target_pairs={{0,2},{1,3},{2,0},{3,1},{4,6},{5,7},{6,4},{7,5},{8,10},{9,11},{10,... | collective-permute-start | bytes 786440 | tf_op jit(solution)/shard_map/ppermute | solution.py:711
  221.7 8.5 %collective-permute-start.24 = (bf16[1024,128]{1,0:T(8,128)(2,1)}, bf16[1024,128]{1,0:T(8,128)(2,1)S(1)}, u32[]{:S(2)}, u32[]{:S(2)}) collective-permute-start(bf16[1024,128]{1,0:T(8,128)(2,1)} %get-tuple-element.117.refs_1_), channel_id=1, source_target_pairs={{0,3},{1,2},{2,1},{3,0},{4,7},{5,6},{6,5},{7,4},{8,11},{9,10},{10,... | collective-permute-start | bytes 786440 | tf_op jit(solution)/shard_map/ppermute | solution.py:711
  223.9 20.5 %all-to-all-start.1 = ((bf16[4,64,1024]{2,1,0:T(8,128)(2,1)}), bf16[4,64,1024]{2,1,0:T(8,128)(2,1)S(1)}, u32[]{:S(2)}, u32[]{:S(2)}) async-start(bf16[4,64,1024]{2,1,0:T(8,128)(2,1)} %pad_maximum_fusion.2), calls=%async_computation.1 | async-start | bytes 1048576 | tf_op jit(solution)/shard_map/all_to_all | solution.py:1014
  228.0 2.2 copy-start.15
  231.0 13.2 %copy-start = (bf16[1,256,1024]{2,1,0:T(8,128)(2,1)S(1)}, bf16[1,256,1024]{2,1,0:T(8,128)(2,1)}, u32[]{:S(2)}) copy-start(bf16[1,256,1024]{2,1,0:T(8,128)(2,1)} %param.14) | copy-start | bytes 1572868
  244.1 3.5 %collective-permute-start.25 = (bf16[4,176,512]{2,1,0:T(8,128)(2,1)}, bf16[4,176,512]{2,1,0:T(8,128)(2,1)S(1)}, u32[]{:S(2)}, u32[]{:S(2)}) collective-permute-start(bf16[4,176,512]{2,1,0:T(8,128)(2,1)} %get-tuple-element.127), channel_id=1, source_target_pairs={{0,4},{4,0},{8,12},{12,8},{16,20},{20,16},{24,28},{28,24},{1,5},{5... | collective-permute-start | bytes 2162696 | tf_op jit(solution)/shard_map/ppermute | solution.py:711
  244.4 31.8 %collective-permute-start.29 = (bf16[256,1024]{1,0:T(8,128)(2,1)}, bf16[256,1024]{1,0:T(8,128)(2,1)S(1)}, u32[]{:S(2)}, u32[]{:S(2)}) collective-permute-start(bf16[256,1024]{1,0:T(8,128)(2,1)} %get-tuple-element.132), channel_id=1, source_target_pairs={{0,1},{1,0},{2,3},{3,2},{4,5},{5,4},{6,7},{7,6},{8,9},{9,8},{10,11... | collective-permute-start | bytes 1572872 | tf_op jit(solution)/shard_map/ppermute | solution.py:711
  245.3 31.0 %collective-permute-start.30 = (bf16[256,1024]{1,0:T(8,128)(2,1)}, bf16[256,1024]{1,0:T(8,128)(2,1)S(1)}, u32[]{:S(2)}, u32[]{:S(2)}) collective-permute-start(bf16[256,1024]{1,0:T(8,128)(2,1)} %get-tuple-element.133), channel_id=1, source_target_pairs={{0,2},{1,3},{2,0},{3,1},{4,6},{5,7},{6,4},{7,5},{8,10},{9,11},{10,... | collective-permute-start | bytes 1572872 | tf_op jit(solution)/shard_map/ppermute | solution.py:711
  249.4 26.9 %copy-start.2 = (bf16[256,1024]{1,0:T(8,128)(2,1)S(1)}, bf16[256,1024]{1,0:T(8,128)(2,1)}, u32[]{:S(2)}) copy-start(bf16[256,1024]{1,0:T(8,128)(2,1)} %get-tuple-element.131) | copy-start | bytes 1572868
  249.4 26.9 %copy-start.25 = (f32[1,1024]{1,0:T(1,128)S(1)}, f32[1,1024]{1,0:T(1,128)}, u32[]{:S(2)}) copy-start(f32[1,1024]{1,0:T(1,128)} %get-tuple-element.135) | copy-start | bytes 12292
  249.5 9.6 %collective-permute-start.26 = (bf16[176,512]{1,0:T(8,128)(2,1)S(1)}, bf16[176,512]{1,0:T(8,128)(2,1)S(1)}, u32[]{:S(2)}, u32[]{:S(2)}) collective-permute-start(bf16[176,512]{1,0:T(8,128)(2,1)S(1)} %get-tuple-element.198), channel_id=1, source_target_pairs={{0,8},{4,12},{8,0},{12,4},{16,24},{20,28},{24,16},{28,20},{1,9},{5... | collective-permute-start | bytes 540680 | tf_op jit(solution)/shard_map/ppermute | solution.py:711
  250.7 16.6 %collective-permute-start.27 = (bf16[176,512]{1,0:T(8,128)(2,1)S(1)}, bf16[176,512]{1,0:T(8,128)(2,1)S(1)}, u32[]{:S(2)}, u32[]{:S(2)}) collective-permute-start(bf16[176,512]{1,0:T(8,128)(2,1)S(1)} %get-tuple-element.199), channel_id=1, source_target_pairs={{0,16},{4,20},{8,24},{12,28},{16,0},{20,4},{24,8},{28,12},{1,17},{... | collective-permute-start | bytes 540680 | tf_op jit(solution)/shard_map/ppermute | solution.py:711
  254.2 13.1 %collective-permute-start.28 = (bf16[176,512]{1,0:T(8,128)(2,1)S(1)}, bf16[176,512]{1,0:T(8,128)(2,1)S(1)}, u32[]{:S(2)}, u32[]{:S(2)}) collective-permute-start(bf16[176,512]{1,0:T(8,128)(2,1)S(1)} %get-tuple-element.200), channel_id=1, source_target_pairs={{0,24},{4,28},{8,16},{12,20},{16,8},{20,12},{24,0},{28,4},{1,25},{... | collective-permute-start | bytes 540680 | tf_op jit(solution)/shard_map/ppermute | solution.py:711
  259.1 17.2 %collective-permute-start.31 = (bf16[256,1024]{1,0:T(8,128)(2,1)}, bf16[256,1024]{1,0:T(8,128)(2,1)S(1)}, u32[]{:S(2)}, u32[]{:S(2)}) collective-permute-start(bf16[256,1024]{1,0:T(8,128)(2,1)} %get-tuple-element.134), channel_id=1, source_target_pairs={{0,3},{1,2},{2,1},{3,0},{4,7},{5,6},{6,5},{7,4},{8,11},{9,10},{10,... | collective-permute-start | bytes 1572872 | tf_op jit(solution)/shard_map/ppermute | solution.py:711
  271.1 5.8 %slice-start = ((f32[1,256,512]{2,1,0:T(8,128)}), f32[1,128,512]{2,1,0:T(8,128)S(1)}, s32[]{:S(2)}) async-start(f32[1,256,512]{2,1,0:T(8,128)} %reduce-scatter.2.cloned.1.call-done), calls=%async_computation.8 | async-start | bytes 524288 | tf_op jit(solution)/shard_map/slice | solution.py:1107
  271.1 9.6 %all-to-all-start.3 = ((bf16[4,32,1024]{2,1,0:T(8,128)(2,1)}), bf16[4,32,1024]{2,1,0:T(8,128)(2,1)}, u32[]{:S(2)}, u32[]{:S(2)}) async-start(bf16[4,32,1024]{2,1,0:T(8,128)(2,1)} %pad_maximum_fusion.6), calls=%async_computation.4 | async-start | bytes 524288 | tf_op jit(solution)/shard_map/all_to_all | solution.py:1103
  (8 other events, 6.1 us)
Sparse Core Ops, SparseCore 0:
  10.7 35.2 all-gather.4
  47.7 29.8 all-gather.6
  175.9 50.9 reduce-scatter.1
